TPU v7x, 256 devices: a whole 4x4x8 slice. The times are simulated.
256 devices in a mesh: blk: 32 (over y, z_hi, core), head: 8 (over x, z_lo).
Axes of the slice: x: 4, y: 4, z: 8 (z_hi: 4, z_lo: 2; z = z_hi * 2 + z_lo), core: 2. Of those that a mesh axis runs over, the one named last changes fastest.
Arguments:
- queries: bfloat16 [8192, 40, 128], P('blk', 'head'), may hold values from -8 to 8
- new_keys: bfloat16 [8192, 8, 128], P('blk', 'head'), may hold values from -6.5 to 6.5
- new_values: bfloat16 [8192, 8, 128], P('blk', 'head'), may hold values from -6 to 6
- cache_keys: bfloat16 [192, 128, 8, 128], P('blk', None, 'head'), may hold values from -6 to 6
- cache_values: bfloat16 [192, 128, 8, 128], P('blk', None, 'head'), may hold values from -6 to 6
- out_weight: bfloat16 [5120, 5120], P('blk', 'head'), may hold values from -0.078125 to 0.078125
- cache_len: int32 [8], replicated, may hold values from 128 to 6144, as said below
- span_len: int32 [8], replicated, may hold values from 128 to 2048, as said below
- block_table: int32 [8, 64], replicated, may hold values from 0 to 191, as said below
- window: int32 [8], replicated, may hold values from 2048 to 4096, as said below
Outputs:
- attn_output: bfloat16 [8192, 5120], P('blk', 'head')
- new_cache_keys: bfloat16 [192, 128, 8, 128], P('blk', None, 'head')
- new_cache_values: bfloat16 [192, 128, 8, 128], P('blk', None, 'head')
Inputs may be any that keep to these rules, and one draw needn't show every extreme that they name: `cache_len`: multiples of 128; two requests hold 6144 tokens each, the other six fewer. `span_len`: multiples of 128 that sum to 8192; some request's is 2048. `block_table`: row r lists, in order of position, the slots of the cache_len[r] // 128 cached blocks of request r and then of the span_len[r] // 128 blocks of its span; every slot of the cache appears exactly once among these entries; a slot whose index modulo 6 is below 4 holds a cached block, the others receive blocks of the spans. Later entries of a row are arbitrary slots and unused. Some request's window is 4096.
All inputs are finite; a program needn't handle non-finite values.
Results may differ from a plain program's by a relative error of at most 0.015.
Values may be sent and summed in bfloat16 or wider, within the bound.
No kernel may reach another device: no remote copies, remote signals or barrier semaphores. Data moves between devices by JAX's collectives and lax.ppermute only.
A program may use at most 128 MiB of HBM per device.

v0:
```python
import functools
import math

import jax
import jax.numpy as jnp
from jax import lax
from jax.experimental import pallas as pl
from jax.experimental.pallas import tpu as pltpu
from jax.sharding import PartitionSpec as P

NY, NZ, NC = 4, 4, 2
SINK = 4
LOWEST = -1e30
FLOOR = -1e25
FAR = 1 << 29
SHIFTS = (0, 1, -1, 2)


def blk_perm(dy, dz, dc):
    pairs = []
    for y in range(NY):
        for z in range(NZ):
            for c in range(NC):
                src = (y * NZ + z) * NC + c
                dst = ((y + dy) % NY * NZ + (z + dz) % NZ) * NC + (c + dc) % NC
                pairs.append((src, dst))
    return pairs


def shift(value, dy=0, dz=0, dc=0):
    return lax.ppermute(value, "blk", blk_perm(dy, dz, dc))


def lookup(table_row, wanted):
    places = jnp.arange(table_row.shape[0], dtype=jnp.int32)
    return jnp.sum(jnp.where(places[None, :] == wanted[:, None], table_row[None, :], 0), axis=1)


def block_start(global_block, span_len, cache_len, block_size):
    lower = jnp.arange(span_len.shape[0], dtype=jnp.int32)
    span_end = jnp.sum(jnp.where(lower[:, None] >= lower[None, :], span_len[None, :], 0), axis=1)
    first_token = global_block * block_size
    request = jnp.sum((first_token[:, None] >= span_end[None, :]).astype(jnp.int32), axis=1)
    return (request, lookup(cache_len - span_end + span_len, request) + first_token)


def table_entry(block_table, request, logical):
    row_ids = jnp.arange(block_table.shape[0], dtype=jnp.int32)
    col_ids = jnp.arange(block_table.shape[1], dtype=jnp.int32)
    match = (row_ids[None, :, None] == request[:, None, None]) & (
        col_ids[None, None, :] == logical[:, None, None]
    )
    return jnp.sum(jnp.where(match, block_table[None], 0), axis=(1, 2))


def slot_owner(block_table, limit, slot_ids):
    row_ids = jnp.arange(block_table.shape[0], dtype=jnp.int32)
    col_ids = jnp.arange(block_table.shape[1], dtype=jnp.int32)
    match = (block_table[None] == slot_ids[:, None, None]) & (
        col_ids[None, None, :] < limit[None, :, None]
    )
    packed = row_ids[:, None] * 4096 + col_ids[None, :] + 1
    found = jnp.sum(jnp.where(match, packed[None], 0), axis=(1, 2))
    place = jnp.maximum(found - 1, 0)
    return (place // 4096, place % 4096, found > 0)


def pack_kernel(ck, cv, nk, nv, out, sem):
    old = 4
    new = nk.shape[0]
    copies = [
        pltpu.make_async_copy(ck.at[pl.ds(0, old)], out.at[pl.ds(0, old)], sem.at[0]),
        pltpu.make_async_copy(nk, out.at[pl.ds(old, new)], sem.at[1]),
        pltpu.make_async_copy(cv.at[pl.ds(0, old)], out.at[pl.ds(old + new, old)], sem.at[2]),
        pltpu.make_async_copy(nv, out.at[pl.ds(2 * old + new, new)], sem.at[3]),
    ]
    for copy in copies:
        copy.start()
    for copy in copies:
        copy.wait()


def pack(ck, cv, nk, nv):
    anywhere = pl.BlockSpec(memory_space=pl.ANY)
    return pl.pallas_call(
        pack_kernel,
        out_shape=jax.ShapeDtypeStruct((2 * ck.shape[0],) + ck.shape[1:], ck.dtype),
        in_specs=[anywhere] * 4,
        out_specs=anywhere,
        scratch_shapes=[pltpu.SemaphoreType.DMA((4,))],
        name="pack",
    )(ck, cv, nk, nv)


def attend_kernel(
    log_scale,
    nkv,
    nq,
    count,
    chosen,
    partial_view,
    first_key,
    first_query,
    reach,
    moves,
    *refs,
):
    kv_in = refs[:nkv]
    q_in = refs[nkv : nkv + nq]
    out_refs = refs[nkv + nq : nkv + 2 * nq]
    move_refs = refs[nkv + 2 * nq : nkv + 3 * nq]
    kv, queries, scores, high, total, result, in_sem, out_sem, move_sem = refs[nkv + 3 * nq :]
    slots = kv_in[0].shape[0]
    half = slots // 2
    heads, rows, width = q_in[0].shape
    size = kv_in[0].shape[1]
    per = rows // size
    wide = heads * size
    longest = chosen.shape[0] // (nq * per)
    loads = []
    for a in range(nkv):
        loads.append(
            pltpu.make_async_copy(kv_in[a], kv.at[pl.ds(a * slots, slots)], in_sem.at[a])
        )
    for r in range(nq):
        loads.append(pltpu.make_async_copy(q_in[r], queries.at[r], in_sem.at[nkv + r]))
    for load in loads:
        load.start()
    for load in loads:
        load.wait()

    def place(j):
        return j // half * slots + j % half

    sends = []
    for r in range(nq):
        for s in range(per):
            at = place(moves[r * per + s])
            for side in range(2):
                sends.append(
                    pltpu.make_async_copy(
                        kv.at[at + side * half],
                        move_refs[r].at[2 * s + side],
                        move_sem.at[(r * per + s) * 2 + side],
                    )
                )
    for send in sends:
        send.start()

    row_ids = lax.broadcasted_iota(jnp.int32, (size, width), 0)
    col_ids = lax.broadcasted_iota(jnp.int32, (size, width), 1)
    ones = jnp.ones((2 * size, width), jnp.bfloat16)

    def one_block(i, unused):
        r = i // per
        s = i % per
        begin = pl.multiple_of(s * size, size)
        query = jnp.concatenate(
            [queries[r, h, pl.ds(begin, size), :] for h in range(heads)], axis=0
        )
        pairs = (count[i] + 1) // 2
        high[...] = jnp.full_like(high, LOWEST)

        def score(t, unused):
            at = i * longest + 2 * t
            keys = jnp.concatenate([kv[place(chosen[at])], kv[place(chosen[at + 1])]], axis=0)
            raw = lax.dot_general(
                query, keys, (((1,), (1,)), ((), ())), preferred_element_type=jnp.float32
            )
            edge = partial_view[at] + partial_view[at + 1]

            @pl.when(edge > 0)
            def _():
                for side in range(2):
                    key_pos = first_key[at + side] + col_ids
                    distance = first_query[i] + row_ids - key_pos
                    allowed = (distance >= 0) & ((distance < reach[i]) | (key_pos < SINK))
                    bias = jnp.where(allowed, 0.0, LOWEST)
                    for h in range(heads):
                        lines = slice(h * size, (h + 1) * size)
                        part = raw[lines, side * size : (side + 1) * size]
                        part = jnp.where(bias < 0.0, LOWEST, part)
                        scores[t, lines, side * size : (side + 1) * size] = part
                        high[lines, :] = jnp.maximum(high[lines, :], part)

            @pl.when(edge == 0)
            def _():
                scores[t] = raw
                high[...] = jnp.maximum(
                    high[...], jnp.maximum(raw[:, :size], raw[:, size:])
                )

            return unused

        lax.fori_loop(0, pairs, score, 0)
        top = jnp.maximum(jnp.max(high[...], axis=1, keepdims=True), FLOOR)
        high[...] = jnp.broadcast_to(top, high.shape)
        total[...] = jnp.zeros_like(total)

        def blend(t, unused):
            at = i * longest + 2 * t
            values = jnp.concatenate(
                [kv[place(chosen[at]) + half], kv[place(chosen[at + 1]) + half]], axis=0
            )
            values = jnp.concatenate([values, ones], axis=1)
            level = high[...]
            level = jnp.concatenate([level, level], axis=1)
            weights = jnp.exp2((scores[t] - level) * log_scale).astype(jnp.bfloat16)
            total[...] += jnp.dot(weights, values, preferred_element_type=jnp.float32)
            return unused

        lax.fori_loop(0, pairs, blend, 0)
        summed = total[:, width:]
        live = summed > 0.0
        safe = jnp.where(live, summed, 1.0)
        result[i, 0:wide, :] = (total[:, :width] / safe).astype(jnp.bfloat16)
        level = jnp.where(live, high[...] * log_scale + jnp.log2(safe), LOWEST)
        line_ids = lax.broadcasted_iota(jnp.int32, (16, width), 0)
        stats = jnp.zeros((16, width), jnp.float32)
        for h in range(heads):
            tile = level[h * size : (h + 1) * size, :]
            row = jnp.sum(jnp.where(row_ids == col_ids, tile, 0.0), axis=0, keepdims=True)
            for part in range(3):
                piece = row.astype(jnp.bfloat16).astype(jnp.float32)
                row = row - piece
                stats = jnp.where(line_ids == part * heads + h, piece, stats)
        result[i, wide : wide + 16, :] = stats.astype(jnp.bfloat16)
        return unused

    lax.fori_loop(0, nq * per, one_block, 0)
    backs = []
    for r in range(nq):
        backs.append(
            pltpu.make_async_copy(result.at[pl.ds(r * per, per)], out_refs[r], out_sem.at[r])
        )
    for back in backs:
        back.start()
    for send in sends:
        send.wait()
    for back in backs:
        back.wait()


def attend(meta, kv_parts, q_parts, log_scale):
    slots, size, width = kv_parts[0].shape
    heads, rows, _ = q_parts[0].shape
    nkv, nq, per = len(kv_parts), len(q_parts), rows // size
    wide = heads * size
    longest = meta[1].shape[0] // (nq * per)
    smem = pl.BlockSpec(memory_space=pltpu.SMEM)
    anywhere = pl.BlockSpec(memory_space=pl.ANY)
    parts = jax.ShapeDtypeStruct((per, wide + 16, width), jnp.bfloat16)
    moved = jax.ShapeDtypeStruct((2 * per, size, width), jnp.bfloat16)
    return pl.pallas_call(
        functools.partial(attend_kernel, log_scale, nkv, nq),
        out_shape=(parts,) * nq + (moved,) * nq,
        in_specs=[smem] * len(meta) + [anywhere] * (nkv + nq),
        out_specs=(anywhere,) * (2 * nq),
        scratch_shapes=[
            pltpu.VMEM((nkv * slots, size, width), jnp.bfloat16),
            pltpu.VMEM((nq, heads, rows, width), jnp.bfloat16),
            pltpu.VMEM((longest // 2, wide, 2 * size), jnp.float32),
            pltpu.VMEM((wide, size), jnp.float32),
            pltpu.VMEM((wide, 2 * width), jnp.float32),
            pltpu.VMEM((nq * per, wide + 16, width), jnp.bfloat16),
            pltpu.SemaphoreType.DMA((nkv + nq,)),
            pltpu.SemaphoreType.DMA((nq,)),
            pltpu.SemaphoreType.DMA((2 * nq * per,)),
        ],
        compiler_params=pltpu.CompilerParams(vmem_limit_bytes=40 << 20),
        cost_estimate=pl.CostEstimate(
            flops=5_000_000_000, bytes_accessed=8_000_000, transcendentals=8_000_000
        ),
        name="attend",
    )(*meta, *kv_parts, *q_parts)


def merge_kernel(heads, *refs):
    parts = refs[:-1]
    out = refs[-1]
    per, lines, width = parts[0].shape
    size = (lines - 16) // heads
    row_ids = lax.broadcasted_iota(jnp.int32, (size, width), 0)
    col_ids = lax.broadcasted_iota(jnp.int32, (size, width), 1)
    for s in range(per):
        levels = []
        for part in parts:
            stats = part[s, heads * size :, :].astype(jnp.float32)
            levels.append(
                stats[0:heads] + stats[heads : 2 * heads] + stats[2 * heads : 3 * heads]
            )
        top = functools.reduce(jnp.maximum, levels)
        shares = [jnp.exp2(level - top) for level in levels]
        whole = functools.reduce(jnp.add, shares)
        shares = [share / whole for share in shares]
        for h in range(heads):
            mixed = jnp.zeros((size, width), jnp.float32)
            for part, share in zip(parts, shares):
                spread = jnp.where(row_ids == col_ids, share[h : h + 1, :], 0.0)
                column = jnp.sum(spread, axis=1, keepdims=True)
                mixed += column * part[s, h * size : (h + 1) * size, :].astype(jnp.float32)
            out[s * size : (s + 1) * size, h * width : (h + 1) * width] = mixed.astype(
                jnp.bfloat16
            )


def merge(parts, heads):
    per, lines, width = parts[0].shape
    size = (lines - 16) // heads
    return pl.pallas_call(
        functools.partial(merge_kernel, heads),
        out_shape=jax.ShapeDtypeStruct((per * size, heads * width), jnp.bfloat16),
        name="merge",
    )(*parts)


def refill_kernel(nq, source, ck, cv, *refs):
    moved = refs[:nq]
    new_ck, new_cv, sem = refs[nq:]
    old = 4
    per = ck.shape[0] - old
    keeps = [
        pltpu.make_async_copy(ck.at[pl.ds(0, old)], new_ck.at[pl.ds(0, old)], sem.at[0]),
        pltpu.make_async_copy(cv.at[pl.ds(0, old)], new_cv.at[pl.ds(0, old)], sem.at[1]),
    ]
    for keep in keeps:
        keep.start()
    for s in range(per):
        for r in range(nq):

            @pl.when(source[s] == r)
            def _():
                fills = [
                    pltpu.make_async_copy(moved[r].at[2 * s], new_ck.at[old + s], sem.at[2]),
                    pltpu.make_async_copy(moved[r].at[2 * s + 1], new_cv.at[old + s], sem.at[3]),
                ]
                for fill in fills:
                    fill.start()
                for fill in fills:
                    fill.wait()

    for keep in keeps:
        keep.wait()


def refill(source, ck, cv, moved):
    anywhere = pl.BlockSpec(memory_space=pl.ANY)
    shape = jax.ShapeDtypeStruct(ck.shape, ck.dtype)
    return pl.pallas_call(
        functools.partial(refill_kernel, len(moved)),
        out_shape=(shape, shape),
        in_specs=[pl.BlockSpec(memory_space=pltpu.SMEM)] + [anywhere] * (2 + len(moved)),
        out_specs=(anywhere, anywhere),
        scratch_shapes=[pltpu.SemaphoreType.DMA((4,))],
        name="refill",
    )(source, ck, cv, *moved)


def plan(device, per, slots, size, cache_len, span_len, block_table, window):
    old = slots - per
    c = device % NC
    z = device // NC % NZ
    y = device // (NC * NZ)
    ring = jnp.array([-k for k in SHIFTS], jnp.int32)
    q_dev = ((y + ring) % NY * NZ + z) * NC + c
    pair = jnp.arange(NC, dtype=jnp.int32)
    k_dev = ((y * NZ + (z + ring[:, None]) % NZ) * NC + (c + pair[None, :]) % NC).reshape(-1)
    slot = jnp.arange(slots, dtype=jnp.int32)
    step = jnp.arange(per, dtype=jnp.int32)
    q_ids = (q_dev[:, None] * per + step[None, :]).reshape(-1)
    q_request, q_first = block_start(q_ids, span_len, cache_len, size)
    q_window = lookup(window, q_request)
    within = jnp.tile(slot, k_dev.shape[0])
    owner = jnp.repeat(k_dev, slots)
    is_old = within < old
    o_request, o_logical, o_live = slot_owner(block_table, cache_len // size, owner * slots + within)
    n_request, n_first = block_start(
        owner * per + jnp.maximum(within - old, 0), span_len, cache_len, size
    )
    k_request = jnp.where(is_old, o_request, n_request)
    k_first = jnp.where(is_old, o_logical * size, n_first)
    live = jnp.where(is_old, o_live, True)
    last = q_first + size - 1
    seen = (
        live[None, :]
        & (q_request[:, None] == k_request[None, :])
        & (k_first[None, :] <= last[:, None])
        & (
            (k_first[None, :] < SINK)
            | (q_first[:, None] - (k_first[None, :] + size - 1) < q_window[:, None])
        )
    )
    inside = (k_first[None, :] + size - 1 <= q_first[:, None]) & (
        last[:, None] - k_first[None, :] < q_window[:, None]
    )
    total = k_first.shape[0]
    ids = jnp.arange(total, dtype=jnp.int32)
    hits = seen.astype(jnp.int32)
    count = jnp.sum(hits, axis=1)
    rank = jnp.sum(jnp.where(ids[None, None, :] < ids[None, :, None], hits[:, None, :], 0), axis=2)
    at = seen[:, None, :] & (rank[:, None, :] == ids[None, :, None])
    pick = lambda x: jnp.sum(jnp.where(at, x, 0), axis=2)
    filled = ids[None, :] < count[:, None]
    chosen = pick(ids[None, None, :])
    edge = jnp.where(filled, pick(1 - inside.astype(jnp.int32)[:, None, :]), 1)
    first_key = jnp.where(filled, pick(k_first[None, None, :]), FAR)
    targets = table_entry(block_table, n_request, n_first // size)
    wanted = (q_dev[:, None] * slots + old + step[None, :]).reshape(-1)
    hit = (targets[None, :] == wanted[:, None]) & ~is_old[None, :]
    moves = jnp.sum(jnp.where(hit, ids[None, :], 0), axis=1)
    all_new = jnp.arange(NY * NZ * NC * per, dtype=jnp.int32)
    a_request, a_first = block_start(all_new, span_len, cache_len, size)
    a_target = table_entry(block_table, a_request, a_first // size)
    mine = a_target[None, :] == (device * slots + old + step)[:, None]
    from_y = jnp.sum(jnp.where(mine, (all_new // (per * NC * NZ))[None, :], 0), axis=1)
    ahead = (from_y - y) % NY
    source = jnp.where(ahead == NY - 1, 2, jnp.where(ahead == 2, 3, ahead))
    meta = (
        count,
        chosen.reshape(-1),
        edge.reshape(-1),
        first_key.reshape(-1),
        q_first,
        q_window,
        moves,
    )
    return meta, source


def shards(
    queries,
    new_keys,
    new_values,
    cache_keys,
    cache_values,
    out_weight,
    cache_len,
    span_len,
    block_table,
    window,
):
    device = lax.axis_index("blk")
    tokens, heads, width = queries.shape
    slots, size = cache_keys.shape[:2]
    per = tokens // size
    log_scale = math.log2(math.e) / math.sqrt(width)
    ck = cache_keys.reshape(slots, size, width)
    cv = cache_values.reshape(slots, size, width)
    own_kv = pack(
        ck, cv, new_keys.reshape(per, size, width), new_values.reshape(per, size, width)
    )
    own_q = jnp.transpose(queries, (1, 0, 2))
    lines = [own_kv] + [shift(own_kv, dz=k) for k in SHIFTS[1:]]
    q_parts = [own_q] + [shift(own_q, dy=k) for k in SHIFTS[1:]]
    kv_parts = []
    for part in lines:
        kv_parts += [part, shift(part, dc=1)]
    weight = lax.all_gather(out_weight, "blk", axis=0, tiled=True)
    meta, source = plan(device, per, slots, size, cache_len, span_len, block_table, window)
    outs = attend(meta, kv_parts, q_parts, log_scale)
    parts, moved = outs[: len(SHIFTS)], outs[len(SHIFTS) :]
    parts = [parts[0]] + [shift(p, dy=-k) for p, k in zip(parts[1:], SHIFTS[1:])]
    moved = [moved[0]] + [shift(p, dy=-k) for p, k in zip(moved[1:], SHIFTS[1:])]
    attention = merge(parts, heads)
    partial_out = lax.dot_general(
        attention, weight, (((1,), (1,)), ((), ())), preferred_element_type=jnp.float32
    ).astype(jnp.bfloat16)
    n_head = lax.axis_size("head")
    blocks = jnp.moveaxis(partial_out.reshape(tokens, n_head, -1), 1, 0)
    arrived = lax.all_to_all(blocks, "head", split_axis=0, concat_axis=0, tiled=True)
    attn_output = arrived.astype(jnp.float32).sum(axis=0).astype(jnp.bfloat16)
    new_ck, new_cv = refill(source, ck, cv, moved)
    return (
        attn_output,
        new_ck.reshape(cache_keys.shape),
        new_cv.reshape(cache_values.shape),
    )


def solution(mesh):
    placed = (
        P("blk", "head", None),
        P("blk", "head", None),
        P("blk", "head", None),
        P("blk", None, "head", None),
        P("blk", None, "head", None),
        P("blk", "head"),
        P(),
        P(),
        P(),
        P(),
    )
    return jax.shard_map(
        shards,
        mesh=mesh,
        in_specs=placed,
        out_specs=(P("blk", "head"), P("blk", None, "head", None), P("blk", None, "head", None)),
        check_vma=False,
    )
```

profile of v0, /device:TPU:6, one launch (start us, length us, event | category | flops | bytes accessed | tf_op | source)
XLA Modules:
  0.0 188.3 jit_solution(13419992635348338060)
XLA Ops:
  7.9 13.1 %pack.1.refs_0_ = bf16[12,128,128]{2,1,0:T(8,128)(2,1)} custom-call(bf16[6,128,128]{2,1,0:T(8,128)(2,1)} %bitcast.26, bf16[6,128,128]{2,1,0:T(8,128)(2,1)} %bitcast.28, bf16[2,128,128]{2,1,0:T(8,128)(2,1)} %bitcast.30, bf16[2,128,128]{2,1,0:T(8,128)(2,1)} %bitcast.31), custom_call_target="tpu_custom_call" | custom-call | tf_op jit(solution)/shard_map/pack/pallas_call | solution.py:85
  21.0 3.3 %collective-permute-start.1 = (bf16[12,128,128]{2,1,0:T(8,128)(2,1)}, bf16[12,128,128]{2,1,0:T(8,128)(2,1)S(1)}, u32[]{:S(2)}, u32[]{:S(2)}) collective-permute-start(bf16[12,128,128]{2,1,0:T(8,128)(2,1)} %pack.1.refs_0_), channel_id=1, source_target_pairs={{0,16},{8,24},{16,32},{24,40},{32,48},{40,56},{48,0},{56,8},{64,80... | collective-permute-start | bytes 1179656 | tf_op jit(solution)/shard_map/ppermute | solution.py:31
  24.3 3.1 %collective-permute-start.3 = (bf16[12,128,128]{2,1,0:T(8,128)(2,1)}, bf16[12,128,128]{2,1,0:T(8,128)(2,1)S(1)}, u32[]{:S(2)}, u32[]{:S(2)}) collective-permute-start(bf16[12,128,128]{2,1,0:T(8,128)(2,1)} %pack.1.refs_0_), channel_id=1, source_target_pairs={{0,48},{8,56},{16,0},{24,8},{32,16},{40,24},{48,32},{56,40},{64,11... | collective-permute-start | bytes 1179656 | tf_op jit(solution)/shard_map/ppermute | solution.py:31
  27.4 4.9 %collective-permute-start.5 = (bf16[12,128,128]{2,1,0:T(8,128)(2,1)}, bf16[12,128,128]{2,1,0:T(8,128)(2,1)S(1)}, u32[]{:S(2)}, u32[]{:S(2)}) collective-permute-start(bf16[12,128,128]{2,1,0:T(8,128)(2,1)} %pack.1.refs_0_), channel_id=1, source_target_pairs={{0,32},{8,40},{16,48},{24,56},{32,0},{40,8},{48,16},{56,24},{64,96... | collective-permute-start | bytes 1179656 | tf_op jit(solution)/shard_map/ppermute | solution.py:31
  32.4 1.6 collective-permute-start.7
  33.9 1.7 collective-permute-start.8
  39.0 0.9 select_reduce_fusion.10
  40.1 2.6 %select_reduce_fusion.1 = (s32[48]{0:T(128)S(1)}, s32[48]{0:T(128)S(1)}) fusion(s32[8,64]{1,0:T(8,128)} %param.19, pred[48,64]{1,0:T(8,128)(4,1)S(1)} %iota_compare_fusion.2, pred[48,8]{1,0:T(8,128)(4,1)S(1)} %copy.21, s32[8,64]{1,0:T(8,128)S(1)} %add_add_fusion, pred[8,64]{1,0:T(8,128)(4,1)S(1)} %iota_compare_fusion.9, s32[48]{0:T(128)S(1)} %add.376), kind=kLoop, calls=%fused_computation.3 | loop fusion | flops 171936 | bytes 8640 | tf_op jit(solution)/shard_map/reduce_sum | solution.py:53
  43.8 2.1 %collective-permute-done.1.refs_2_ = bf16[12,128,128]{2,1,0:T(8,128)(2,1)S(1)} collective-permute-done((bf16[12,128,128]{2,1,0:T(8,128)(2,1)}, bf16[12,128,128]{2,1,0:T(8,128)(2,1)S(1)}, u32[]{:S(2)}, u32[]{:S(2)}) %collective-permute-start.1) | collective-permute-done | bytes 393248 | tf_op jit(solution)/shard_map/ppermute | solution.py:31
  45.9 17.6 %collective-permute-done.3.refs_4_ = bf16[12,128,128]{2,1,0:T(8,128)(2,1)S(1)} collective-permute-done((bf16[12,128,128]{2,1,0:T(8,128)(2,1)}, bf16[12,128,128]{2,1,0:T(8,128)(2,1)S(1)}, u32[]{:S(2)}, u32[]{:S(2)}) %collective-permute-start.3) | collective-permute-done | bytes 393248 | tf_op jit(solution)/shard_map/ppermute | solution.py:31
  64.3 3.9 %collective-permute-start.9 = (bf16[5,256,128]{2,1,0:T(8,128)(2,1)}, bf16[5,256,128]{2,1,0:T(8,128)(2,1)}, u32[]{:S(2)}, u32[]{:S(2)}) collective-permute-start(bf16[5,256,128]{2,1,0:T(8,128)(2,1)} %bitcast.22), channel_id=1, source_target_pairs={{0,128},{8,136},{16,144},{24,152},{32,160},{40,168},{48,176},{56,1... | collective-permute-start | bytes 983048 | tf_op jit(solution)/shard_map/ppermute | solution.py:31
  68.7 12.4 %collective-permute-done.9.refs_11_ = bf16[5,256,128]{2,1,0:T(8,128)(2,1)} collective-permute-done((bf16[5,256,128]{2,1,0:T(8,128)(2,1)}, bf16[5,256,128]{2,1,0:T(8,128)(2,1)}, u32[]{:S(2)}, u32[]{:S(2)}) %collective-permute-start.9) | collective-permute-done | bytes 327712 | tf_op jit(solution)/shard_map/ppermute | solution.py:31
  81.2 1.0 copy-done
  82.2 1.0 copy-done.3
  83.1 17.9 %attend.1 = (bf16[2,656,128]{2,1,0:T(8,128)(2,1)S(1)}, bf16[2,656,128]{2,1,0:T(8,128)(2,1)S(1)}, bf16[2,656,128]{2,1,0:T(8,128)(2,1)S(1)}, bf16[2,656,128]{2,1,0...) custom-call(s32[8]{0:T(128)S(1)} %convert_reduce_fusion.3.count, ...), custom_call_target="tpu_custom_call" | custom-call | flops 5000000000 | bytes 8000000 | tf_op jit(solution)/shard_map/attend/pallas_call | solution.py:254
  104.4 0.9 collective-permute-start.10
  105.3 3.2 %collective-permute-start.11 = (bf16[2,656,128]{2,1,0:T(8,128)(2,1)S(1)}, bf16[2,656,128]{2,1,0:T(8,128)(2,1)S(1)}, u32[]{:S(2)}, u32[]{:S(2)}) collective-permute-start(bf16[2,656,128]{2,1,0:T(8,128)(2,1)S(1)} %get-tuple-element.15), channel_id=1, source_target_pairs={{0,64},{8,72},{16,80},{24,88},{32,96},{40,104},{48,112},{56,120},{... | collective-permute-start | bytes 1007624 | tf_op jit(solution)/shard_map/ppermute | solution.py:31
  108.5 8.2 %collective-permute-start.12 = (bf16[2,656,128]{2,1,0:T(8,128)(2,1)S(1)}, bf16[2,656,128]{2,1,0:T(8,128)(2,1)S(1)}, u32[]{:S(2)}, u32[]{:S(2)}) collective-permute-start(bf16[2,656,128]{2,1,0:T(8,128)(2,1)S(1)} %get-tuple-element.16), channel_id=1, source_target_pairs={{0,128},{8,136},{16,144},{24,152},{32,160},{40,168},{48,176},{56,1... | collective-permute-start | bytes 1007624 | tf_op jit(solution)/shard_map/ppermute | solution.py:31
  116.7 6.4 %collective-permute-done.11.refs_2_ = bf16[2,656,128]{2,1,0:T(8,128)(2,1)S(1)} collective-permute-done((bf16[2,656,128]{2,1,0:T(8,128)(2,1)S(1)}, bf16[2,656,128]{2,1,0:T(8,128)(2,1)S(1)}, u32[]{:S(2)}, u32[]{:S(2)}) %collective-permute-start.11) | collective-permute-done | bytes 335904 | tf_op jit(solution)/shard_map/ppermute | solution.py:31
  123.1 6.9 %collective-permute-done.12.refs_3_ = bf16[2,656,128]{2,1,0:T(8,128)(2,1)S(1)} collective-permute-done((bf16[2,656,128]{2,1,0:T(8,128)(2,1)S(1)}, bf16[2,656,128]{2,1,0:T(8,128)(2,1)S(1)}, u32[]{:S(2)}, u32[]{:S(2)}) %collective-permute-start.12) | collective-permute-done | bytes 335904 | tf_op jit(solution)/shard_map/ppermute | solution.py:31
  130.8 2.8 %merge.1 = bf16[256,640]{1,0:T(8,128)(2,1)} custom-call(bf16[2,656,128]{2,1,0:T(8,128)(2,1)} %copy-done.1, bf16[2,656,128]{2,1,0:T(8,128)(2,1)} %copy-done.10, bf16[2,656,128]{2,1,0:T(8,128)(2,1)} %copy-done.11, bf16[2,656,128]{2,1,0:T(8,128)(2,1)} %copy-done.12), custom_call_target="tpu_custom_call" | custom-call | tf_op jit(solution)/shard_map/merge/pallas_call | solution.py:310
  133.6 5.2 %convolution_convert_fusion = bf16[256,5120]{1,0:T(8,128)(2,1)S(1)} fusion(bf16[256,640]{1,0:T(8,128)(2,1)} %merge.1, bf16[5120,640]{1,0:T(8,128)(2,1)} %all-gather.2.cloned.1.call-done), kind=kOutput, calls=%fused_computation | convolution fusion | flops 1679032320 | bytes 9502720 | tf_op jit(solution)/shard_map/dot_general | solution.py:465
  138.9 1.8 copy.28
  140.7 12.2 %all-to-all-start = ((bf16[8,256,640]{2,1,0:T(8,128)(2,1)}), bf16[8,256,640]{2,1,0:T(8,128)(2,1)S(1)}, u32[]{:S(2)}, u32[]{:S(2)}) async-start(bf16[8,256,640]{2,1,0:T(8,128)(2,1)} %bitcast.24), calls=%async_computation | async-start | bytes 5242880 | tf_op jit(solution)/shard_map/all_to_all | solution.py:470
  153.2 1.3 select_reduce_fusion
  154.8 2.0 %collective-permute-start.14 = (bf16[4,128,128]{2,1,0:T(8,128)(2,1)S(1)}, bf16[4,128,128]{2,1,0:T(8,128)(2,1)S(1)}, u32[]{:S(2)}, u32[]{:S(2)}) collective-permute-start(bf16[4,128,128]{2,1,0:T(8,128)(2,1)S(1)} %copy-done.7), channel_id=1, source_target_pairs={{0,64},{8,72},{16,80},{24,88},{32,96},{40,104},{48,112},{56,120},{... | collective-permute-start | bytes 393224 | tf_op jit(solution)/shard_map/ppermute | solution.py:31
  157.8 1.9 %collective-permute-done.13.refs_1_ = bf16[4,128,128]{2,1,0:T(8,128)(2,1)S(1)} collective-permute-done((bf16[4,128,128]{2,1,0:T(8,128)(2,1)S(1)}, bf16[4,128,128]{2,1,0:T(8,128)(2,1)S(1)}, u32[]{:S(2)}, u32[]{:S(2)}) %collective-permute-start.13) | collective-permute-done | bytes 131104 | tf_op jit(solution)/shard_map/ppermute | solution.py:31
  159.8 1.3 collective-permute-done.14.refs_2_
  161.1 2.2 %collective-permute-done.15.refs_3_ = bf16[4,128,128]{2,1,0:T(8,128)(2,1)S(1)} collective-permute-done((bf16[4,128,128]{2,1,0:T(8,128)(2,1)S(1)}, bf16[4,128,128]{2,1,0:T(8,128)(2,1)S(1)}, u32[]{:S(2)}, u32[]{:S(2)}) %collective-permute-start.15) | collective-permute-done | bytes 131104 | tf_op jit(solution)/shard_map/ppermute | solution.py:31
  164.0 14.8 %refill.1 = (bf16[6,128,128]{2,1,0:T(8,128)(2,1)}, bf16[6,128,128]{2,1,0:T(8,128)(2,1)}) custom-call(s32[2]{0:T(128)} %compare_select_fusion.9.source, bf16[6,128,128]{2,1,0:T(8,128)(2,1)} %bitcast.27, bf16[6,128,128]{2,1,0:T(8,128)(2,1)} %bitcast.29, bf16[4,128,128]{2,1,0:T(8,128)(2,1)} %copy-done.2, bf16[4,128,128]{2,1,0:T(8,128)(2,1)} %copy-done.13, ...), custom_call_target="tpu_custom_call" | custom-call | tf_op jit(solution)/shard_map/refill/pallas_call | solution.py:349
  178.8 1.5 all-to-all-done
  180.3 1.2 reduce_sum.196
  (102 shorter events, 13.0 us)
Async XLA Ops:
  7.2 126.5 %all-gather.2.cloned.1.call-start = ((), (), s32[]{:S(2)}) async-start(), calls=%async_computation.1 | async-start | bytes 6758400 | tf_op jit(solution)/shard_map/all_gather | solution.py:458
  21.0 24.9 %collective-permute-start.1 = (bf16[12,128,128]{2,1,0:T(8,128)(2,1)}, bf16[12,128,128]{2,1,0:T(8,128)(2,1)S(1)}, u32[]{:S(2)}, u32[]{:S(2)}) collective-permute-start(bf16[12,128,128]{2,1,0:T(8,128)(2,1)} %pack.1.refs_0_), channel_id=1, source_target_pairs={{0,16},{8,24},{16,32},{24,40},{32,48},{40,56},{48,0},{56,8},{64,80... | collective-permute-start | bytes 1179656 | tf_op jit(solution)/shard_map/ppermute | solution.py:31
  24.3 39.2 %collective-permute-start.3 = (bf16[12,128,128]{2,1,0:T(8,128)(2,1)}, bf16[12,128,128]{2,1,0:T(8,128)(2,1)S(1)}, u32[]{:S(2)}, u32[]{:S(2)}) collective-permute-start(bf16[12,128,128]{2,1,0:T(8,128)(2,1)} %pack.1.refs_0_), channel_id=1, source_target_pairs={{0,48},{8,56},{16,0},{24,8},{32,16},{40,24},{48,32},{56,40},{64,11... | collective-permute-start | bytes 1179656 | tf_op jit(solution)/shard_map/ppermute | solution.py:31
  27.4 36.1 %collective-permute-start.5 = (bf16[12,128,128]{2,1,0:T(8,128)(2,1)}, bf16[12,128,128]{2,1,0:T(8,128)(2,1)S(1)}, u32[]{:S(2)}, u32[]{:S(2)}) collective-permute-start(bf16[12,128,128]{2,1,0:T(8,128)(2,1)} %pack.1.refs_0_), channel_id=1, source_target_pairs={{0,32},{8,40},{16,48},{24,56},{32,0},{40,8},{48,16},{56,24},{64,96... | collective-permute-start | bytes 1179656 | tf_op jit(solution)/shard_map/ppermute | solution.py:31
  32.4 11.3 %collective-permute-start.7 = (bf16[5,256,128]{2,1,0:T(8,128)(2,1)}, bf16[5,256,128]{2,1,0:T(8,128)(2,1)S(1)}, u32[]{:S(2)}, u32[]{:S(2)}) collective-permute-start(bf16[5,256,128]{2,1,0:T(8,128)(2,1)} %bitcast.20), channel_id=1, source_target_pairs={{0,64},{8,72},{16,80},{24,88},{32,96},{40,104},{48,112},{56,120},{... | collective-permute-start | bytes 983048 | tf_op jit(solution)/shard_map/ppermute | solution.py:31
  33.9 30.3 %collective-permute-start.8 = (bf16[5,256,128]{2,1,0:T(8,128)(2,1)}, bf16[5,256,128]{2,1,0:T(8,128)(2,1)S(1)}, u32[]{:S(2)}, u32[]{:S(2)}) collective-permute-start(bf16[5,256,128]{2,1,0:T(8,128)(2,1)} %bitcast.21), channel_id=1, source_target_pairs={{0,192},{8,200},{16,208},{24,216},{32,224},{40,232},{48,240},{56,2... | collective-permute-start | bytes 983048 | tf_op jit(solution)/shard_map/ppermute | solution.py:31
  43.7 37.5 %collective-permute-start = (bf16[12,128,128]{2,1,0:T(8,128)(2,1)}, bf16[12,128,128]{2,1,0:T(8,128)(2,1)S(1)}, u32[]{:S(2)}, u32[]{:S(2)}) collective-permute-start(bf16[12,128,128]{2,1,0:T(8,128)(2,1)} %pack.1.refs_0_), channel_id=1, source_target_pairs={{0,8},{8,0},{16,24},{24,16},{32,40},{40,32},{48,56},{56,48},{64,72... | collective-permute-start | bytes 1179656 | tf_op jit(solution)/shard_map/ppermute | solution.py:31
  45.9 35.2 %collective-permute-start.2 = (bf16[12,128,128]{2,1,0:T(8,128)(2,1)S(1)}, bf16[12,128,128]{2,1,0:T(8,128)(2,1)S(1)}, u32[]{:S(2)}, u32[]{:S(2)}) collective-permute-start(bf16[12,128,128]{2,1,0:T(8,128)(2,1)S(1)} %collective-permute-done.1.refs_2_), channel_id=1, source_target_pairs={{0,8},{8,0},{16,24},{24,16},{32,40},{40,32},{48,56},{56,48},{64,72... | collective-permute-start | bytes 1179656 | tf_op jit(solution)/shard_map/ppermute | solution.py:31
  63.5 17.6 %collective-permute-start.4 = (bf16[12,128,128]{2,1,0:T(8,128)(2,1)S(1)}, bf16[12,128,128]{2,1,0:T(8,128)(2,1)S(1)}, u32[]{:S(2)}, u32[]{:S(2)}) collective-permute-start(bf16[12,128,128]{2,1,0:T(8,128)(2,1)S(1)} %collective-permute-done.3.refs_4_), channel_id=1, source_target_pairs={{0,8},{8,0},{16,24},{24,16},{32,40},{40,32},{48,56},{56,48},{64,72... | collective-permute-start | bytes 1179656 | tf_op jit(solution)/shard_map/ppermute | solution.py:31
  63.5 17.6 %collective-permute-start.6 = (bf16[12,128,128]{2,1,0:T(8,128)(2,1)S(1)}, bf16[12,128,128]{2,1,0:T(8,128)(2,1)S(1)}, u32[]{:S(2)}, u32[]{:S(2)}) collective-permute-start(bf16[12,128,128]{2,1,0:T(8,128)(2,1)S(1)} %collective-permute-done.5.refs_6_), channel_id=1, source_target_pairs={{0,8},{8,0},{16,24},{24,16},{32,40},{40,32},{48,56},{56,48},{64,72... | collective-permute-start | bytes 1179656 | tf_op jit(solution)/shard_map/ppermute | solution.py:31
  64.3 16.9 %collective-permute-start.9 = (bf16[5,256,128]{2,1,0:T(8,128)(2,1)}, bf16[5,256,128]{2,1,0:T(8,128)(2,1)}, u32[]{:S(2)}, u32[]{:S(2)}) collective-permute-start(bf16[5,256,128]{2,1,0:T(8,128)(2,1)} %bitcast.22), channel_id=1, source_target_pairs={{0,128},{8,136},{16,144},{24,152},{32,160},{40,168},{48,176},{56,1... | collective-permute-start | bytes 983048 | tf_op jit(solution)/shard_map/ppermute | solution.py:31
  81.1 1.0 copy-start
  82.2 1.0 copy-start.3
  101.0 0.7 copy-start.1
  103.1 0.7 copy-start.6
  104.4 12.3 %collective-permute-start.10 = (bf16[2,656,128]{2,1,0:T(8,128)(2,1)S(1)}, bf16[2,656,128]{2,1,0:T(8,128)(2,1)S(1)}, u32[]{:S(2)}, u32[]{:S(2)}) collective-permute-start(bf16[2,656,128]{2,1,0:T(8,128)(2,1)S(1)} %get-tuple-element.14), channel_id=1, source_target_pairs={{0,192},{8,200},{16,208},{24,216},{32,224},{40,232},{48,240},{56,2... | collective-permute-start | bytes 1007624 | tf_op jit(solution)/shard_map/ppermute | solution.py:31
  105.3 17.9 %collective-permute-start.11 = (bf16[2,656,128]{2,1,0:T(8,128)(2,1)S(1)}, bf16[2,656,128]{2,1,0:T(8,128)(2,1)S(1)}, u32[]{:S(2)}, u32[]{:S(2)}) collective-permute-start(bf16[2,656,128]{2,1,0:T(8,128)(2,1)S(1)} %get-tuple-element.15), channel_id=1, source_target_pairs={{0,64},{8,72},{16,80},{24,88},{32,96},{40,104},{48,112},{56,120},{... | collective-permute-start | bytes 1007624 | tf_op jit(solution)/shard_map/ppermute | solution.py:31
  108.5 21.6 %collective-permute-start.12 = (bf16[2,656,128]{2,1,0:T(8,128)(2,1)S(1)}, bf16[2,656,128]{2,1,0:T(8,128)(2,1)S(1)}, u32[]{:S(2)}, u32[]{:S(2)}) collective-permute-start(bf16[2,656,128]{2,1,0:T(8,128)(2,1)S(1)} %get-tuple-element.16), channel_id=1, source_target_pairs={{0,128},{8,136},{16,144},{24,152},{32,160},{40,168},{48,176},{56,1... | collective-permute-start | bytes 1007624 | tf_op jit(solution)/shard_map/ppermute | solution.py:31
  116.7 13.4 %copy-start.10 = (bf16[2,656,128]{2,1,0:T(8,128)(2,1)}, bf16[2,656,128]{2,1,0:T(8,128)(2,1)S(1)}, u32[]{:S(2)}) copy-start(bf16[2,656,128]{2,1,0:T(8,128)(2,1)S(1)} %collective-permute-done.10.refs_1_) | copy-start | bytes 1007620
  123.1 6.9 %copy-start.11 = (bf16[2,656,128]{2,1,0:T(8,128)(2,1)}, bf16[2,656,128]{2,1,0:T(8,128)(2,1)S(1)}, u32[]{:S(2)}) copy-start(bf16[2,656,128]{2,1,0:T(8,128)(2,1)S(1)} %collective-permute-done.11.refs_2_) | copy-start | bytes 1007620
  130.1 0.7 copy-start.12
  138.9 14.4 %copy-start.16 = (s32[8,64]{1,0:T(8,128)S(1)}, s32[8,64]{1,0:T(8,128)}, u32[]{:S(2)}) copy-start(s32[8,64]{1,0:T(8,128)} %param.19) | copy-start | bytes 6148
  138.9 15.9 %copy-start.9 = (bf16[4,128,128]{2,1,0:T(8,128)(2,1)S(1)}, bf16[4,128,128]{2,1,0:T(8,128)(2,1)}, u32[]{:S(2)}) copy-start(bf16[4,128,128]{2,1,0:T(8,128)(2,1)} %copy-done.8) | copy-start | bytes 393220
  138.9 16.0 %copy-start.7 = (bf16[4,128,128]{2,1,0:T(8,128)(2,1)S(1)}, bf16[4,128,128]{2,1,0:T(8,128)(2,1)}, u32[]{:S(2)}) copy-start(bf16[4,128,128]{2,1,0:T(8,128)(2,1)} %copy-done.6) | copy-start | bytes 393220
  138.9 18.0 %copy-start.5 = (bf16[4,128,128]{2,1,0:T(8,128)(2,1)S(1)}, bf16[4,128,128]{2,1,0:T(8,128)(2,1)}, u32[]{:S(2)}) copy-start(bf16[4,128,128]{2,1,0:T(8,128)(2,1)} %copy-done.4) | copy-start | bytes 393220
  140.7 39.7 %all-to-all-start = ((bf16[8,256,640]{2,1,0:T(8,128)(2,1)}), bf16[8,256,640]{2,1,0:T(8,128)(2,1)S(1)}, u32[]{:S(2)}, u32[]{:S(2)}) async-start(bf16[8,256,640]{2,1,0:T(8,128)(2,1)} %bitcast.24), calls=%async_computation | async-start | bytes 5242880 | tf_op jit(solution)/shard_map/all_to_all | solution.py:470
  154.7 5.0 %collective-permute-start.13 = (bf16[4,128,128]{2,1,0:T(8,128)(2,1)S(1)}, bf16[4,128,128]{2,1,0:T(8,128)(2,1)S(1)}, u32[]{:S(2)}, u32[]{:S(2)}) collective-permute-start(bf16[4,128,128]{2,1,0:T(8,128)(2,1)S(1)} %copy-done.9), channel_id=1, source_target_pairs={{0,192},{8,200},{16,208},{24,216},{32,224},{40,232},{48,240},{56,2... | collective-permute-start | bytes 393224 | tf_op jit(solution)/shard_map/ppermute | solution.py:31
  154.8 6.3 %collective-permute-start.14 = (bf16[4,128,128]{2,1,0:T(8,128)(2,1)S(1)}, bf16[4,128,128]{2,1,0:T(8,128)(2,1)S(1)}, u32[]{:S(2)}, u32[]{:S(2)}) collective-permute-start(bf16[4,128,128]{2,1,0:T(8,128)(2,1)S(1)} %copy-done.7), channel_id=1, source_target_pairs={{0,64},{8,72},{16,80},{24,88},{32,96},{40,104},{48,112},{56,120},{... | collective-permute-start | bytes 393224 | tf_op jit(solution)/shard_map/ppermute | solution.py:31
  156.8 6.5 %collective-permute-start.15 = (bf16[4,128,128]{2,1,0:T(8,128)(2,1)S(1)}, bf16[4,128,128]{2,1,0:T(8,128)(2,1)S(1)}, u32[]{:S(2)}, u32[]{:S(2)}) collective-permute-start(bf16[4,128,128]{2,1,0:T(8,128)(2,1)S(1)} %copy-done.5), channel_id=1, source_target_pairs={{0,128},{8,136},{16,144},{24,152},{32,160},{40,168},{48,176},{56,1... | collective-permute-start | bytes 393224 | tf_op jit(solution)/shard_map/ppermute | solution.py:31
  159.8 3.5 %copy-start.13 = (bf16[4,128,128]{2,1,0:T(8,128)(2,1)}, bf16[4,128,128]{2,1,0:T(8,128)(2,1)S(1)}, u32[]{:S(2)}) copy-start(bf16[4,128,128]{2,1,0:T(8,128)(2,1)S(1)} %collective-permute-done.13.refs_1_) | copy-start | bytes 393220
  161.1 2.2 %copy-start.14 = (bf16[4,128,128]{2,1,0:T(8,128)(2,1)}, bf16[4,128,128]{2,1,0:T(8,128)(2,1)S(1)}, u32[]{:S(2)}) copy-start(bf16[4,128,128]{2,1,0:T(8,128)(2,1)S(1)} %collective-permute-done.14.refs_2_) | copy-start | bytes 393220
  163.3 0.7 copy-start.15
  (3 other events, 2.0 us)
Sparse Core Ops, SparseCore 0:
  10.5 91.4 all-gather.1
where the time goes:
time: 190 us; the launch traced here: 188 us
  waiting for transfers between devices  53.3 us (28%)
  Pallas kernels  48.6 us (26%)
  starting transfers between devices  46.2 us (24%)
  between operations  14.3 us (8%)
  other arithmetic  11.3 us (6%)
  local copies, waits for them, and re-layouts  9.53 us (5%)
  matrix products  5.21 us (3%)
    ppermute x16, waiting for transfers between devices, shift(): return lax.ppermute(value, 'blk', blk_perm(dy, dz, dc))  51.1 us
    ppermute x16, starting transfers between devices, shift(): return lax.ppermute(value, 'blk', blk_perm(dy, dz, dc))  34 us
    pallas_call x1, Pallas kernels, attend(): pl.pallas_call(functools.partial(attend_kernel, log_scale, nkv, nq), out_...  17.9 us
    pallas_call x1, Pallas kernels, refill(): pl.pallas_call(functools.partial(refill_kernel, len(moved)), out_shape=(s...  14.8 us
    pallas_call x1, Pallas kernels, pack(): pl.pallas_call(pack_kernel, out_shape=jax.ShapeDtypeStruct((2 * ck.shape[...  13.1 us
    all_to_all x1, starting transfers between devices, shards(): lax.all_to_all(blocks, 'head', split_axis=0, concat_axis=0, tiled=True)  12.2 us
    unnamed x34, local copies, waits for them, and re-layouts  6.74 us
    dot_general x1, matrix products, shards(): lax.dot_general(attention, weight, (((1,), (1,)), ((), ())), preferred_el...  5.21 us
  transfers between devices with their start and end apart: 18, of which 9 were waited for; matrix products, arithmetic and copies ran while one was open for 6% of the time, Pallas kernels for 26%

commit v1 on v0

--- a/solution.py
+++ b/solution.py
@@ -65,29 +65,19 @@
     return (place // 4096, place % 4096, found > 0)
 
 
-def pack_kernel(ck, cv, nk, nv, out, sem):
-    old = 4
+def pack_kernel(ck, cv, nk, nv, out):
     new = nk.shape[0]
-    copies = [
-        pltpu.make_async_copy(ck.at[pl.ds(0, old)], out.at[pl.ds(0, old)], sem.at[0]),
-        pltpu.make_async_copy(nk, out.at[pl.ds(old, new)], sem.at[1]),
-        pltpu.make_async_copy(cv.at[pl.ds(0, old)], out.at[pl.ds(old + new, old)], sem.at[2]),
-        pltpu.make_async_copy(nv, out.at[pl.ds(2 * old + new, new)], sem.at[3]),
-    ]
-    for copy in copies:
-        copy.start()
-    for copy in copies:
-        copy.wait()
+    old = ck.shape[0] - new
+    out[0:old] = ck[0:old]
+    out[old : old + new] = nk[...]
+    out[old + new : 2 * old + new] = cv[0:old]
+    out[2 * old + new :] = nv[...]
 
 
 def pack(ck, cv, nk, nv):
-    anywhere = pl.BlockSpec(memory_space=pl.ANY)
     return pl.pallas_call(
         pack_kernel,
         out_shape=jax.ShapeDtypeStruct((2 * ck.shape[0],) + ck.shape[1:], ck.dtype),
-        in_specs=[anywhere] * 4,
-        out_specs=anywhere,
-        scratch_shapes=[pltpu.SemaphoreType.DMA((4,))],
         name="pack",
     )(ck, cv, nk, nv)
 
@@ -98,7 +88,7 @@
     nq,
     count,
     chosen,
-    partial_view,
+    edges,
     first_key,
     first_query,
     reach,
@@ -161,38 +151,36 @@
         pairs = (count[i] + 1) // 2
         high[...] = jnp.full_like(high, LOWEST)
 
-        def score(t, unused):
+        def raw_scores(t):
             at = i * longest + 2 * t
             keys = jnp.concatenate([kv[place(chosen[at])], kv[place(chosen[at + 1])]], axis=0)
-            raw = lax.dot_general(
+            return lax.dot_general(
                 query, keys, (((1,), (1,)), ((), ())), preferred_element_type=jnp.float32
             )
-            edge = partial_view[at] + partial_view[at + 1]
-
-            @pl.when(edge > 0)
-            def _():
-                for side in range(2):
-                    key_pos = first_key[at + side] + col_ids
-                    distance = first_query[i] + row_ids - key_pos
-                    allowed = (distance >= 0) & ((distance < reach[i]) | (key_pos < SINK))
-                    bias = jnp.where(allowed, 0.0, LOWEST)
-                    for h in range(heads):
-                        lines = slice(h * size, (h + 1) * size)
-                        part = raw[lines, side * size : (side + 1) * size]
-                        part = jnp.where(bias < 0.0, LOWEST, part)
-                        scores[t, lines, side * size : (side + 1) * size] = part
-                        high[lines, :] = jnp.maximum(high[lines, :], part)
-
-            @pl.when(edge == 0)
-            def _():
-                scores[t] = raw
-                high[...] = jnp.maximum(
-                    high[...], jnp.maximum(raw[:, :size], raw[:, size:])
-                )
-
+
+        def score_edge(t, unused):
+            raw = raw_scores(t)
+            for side in range(2):
+                key_pos = first_key[i * longest + 2 * t + side] + col_ids
+                distance = first_query[i] + row_ids - key_pos
+                allowed = (distance >= 0) & ((distance < reach[i]) | (key_pos < SINK))
+                hidden = jnp.where(allowed, 0.0, LOWEST)
+                for h in range(heads):
+                    lines = slice(h * size, (h + 1) * size)
+                    part = raw[lines, side * size : (side + 1) * size]
+                    part = jnp.where(hidden < 0.0, LOWEST, part)
+                    scores[t, lines, side * size : (side + 1) * size] = part
+                    high[lines, :] = jnp.maximum(high[lines, :], part)
             return unused
 
-        lax.fori_loop(0, pairs, score, 0)
+        def score_full(t, unused):
+            raw = raw_scores(t)
+            scores[t] = raw
+            high[...] = jnp.maximum(high[...], jnp.maximum(raw[:, :size], raw[:, size:]))
+            return unused
+
+        lax.fori_loop(0, edges[i], score_edge, 0)
+        lax.fori_loop(edges[i], pairs, score_full, 0)
         top = jnp.maximum(jnp.max(high[...], axis=1, keepdims=True), FLOOR)
         high[...] = jnp.broadcast_to(top, high.shape)
         total[...] = jnp.zeros_like(total)
@@ -211,19 +199,26 @@
 
         lax.fori_loop(0, pairs, blend, 0)
         summed = total[:, width:]
-        live = summed > 0.0
-        safe = jnp.where(live, summed, 1.0)
+        safe = jnp.where(summed > 0.0, summed, 1.0)
         result[i, 0:wide, :] = (total[:, :width] / safe).astype(jnp.bfloat16)
-        level = jnp.where(live, high[...] * log_scale + jnp.log2(safe), LOWEST)
         line_ids = lax.broadcasted_iota(jnp.int32, (16, width), 0)
-        stats = jnp.zeros((16, width), jnp.float32)
+        tops = jnp.zeros((16, width), jnp.float32)
+        sums = jnp.zeros((16, width), jnp.float32)
         for h in range(heads):
-            tile = level[h * size : (h + 1) * size, :]
-            row = jnp.sum(jnp.where(row_ids == col_ids, tile, 0.0), axis=0, keepdims=True)
-            for part in range(3):
-                piece = row.astype(jnp.bfloat16).astype(jnp.float32)
-                row = row - piece
-                stats = jnp.where(line_ids == part * heads + h, piece, stats)
+            lines = slice(h * size, (h + 1) * size)
+            row = jnp.sum(jnp.where(row_ids == col_ids, high[lines, :], 0.0), axis=0, keepdims=True)
+            tops = jnp.where(line_ids % heads == h, row, tops)
+            row = jnp.sum(
+                jnp.where(row_ids == col_ids, total[lines, width:], 0.0), axis=0, keepdims=True
+            )
+            sums = jnp.where(line_ids % heads == h, row, sums)
+        live = sums > 0.0
+        level = tops * log_scale + jnp.log2(jnp.where(live, sums, 1.0))
+        level = jnp.where(live, level, LOWEST)
+        first = level.astype(jnp.bfloat16).astype(jnp.float32)
+        second = (level - first).astype(jnp.bfloat16).astype(jnp.float32)
+        third = level - first - second
+        stats = jnp.where(line_ids < heads, first, jnp.where(line_ids < 2 * heads, second, third))
         result[i, wide : wide + 16, :] = stats.astype(jnp.bfloat16)
         return unused
 
@@ -255,7 +250,7 @@
         functools.partial(attend_kernel, log_scale, nkv, nq),
         out_shape=(parts,) * nq + (moved,) * nq,
         in_specs=[smem] * len(meta) + [anywhere] * (nkv + nq),
-        out_specs=(anywhere,) * (2 * nq),
+        out_specs=(pl.BlockSpec(memory_space=pltpu.HBM),) * (2 * nq),
         scratch_shapes=[
             pltpu.VMEM((nkv * slots, size, width), jnp.bfloat16),
             pltpu.VMEM((nq, heads, rows, width), jnp.bfloat16),
@@ -316,42 +311,28 @@
 
 def refill_kernel(nq, source, ck, cv, *refs):
     moved = refs[:nq]
-    new_ck, new_cv, sem = refs[nq:]
-    old = 4
-    per = ck.shape[0] - old
-    keeps = [
-        pltpu.make_async_copy(ck.at[pl.ds(0, old)], new_ck.at[pl.ds(0, old)], sem.at[0]),
-        pltpu.make_async_copy(cv.at[pl.ds(0, old)], new_cv.at[pl.ds(0, old)], sem.at[1]),
-    ]
-    for keep in keeps:
-        keep.start()
+    new_ck, new_cv = refs[nq:]
+    per = moved[0].shape[0] // 2
+    old = ck.shape[0] - per
+    new_ck[0:old] = ck[0:old]
+    new_cv[0:old] = cv[0:old]
     for s in range(per):
         for r in range(nq):
 
             @pl.when(source[s] == r)
             def _():
-                fills = [
-                    pltpu.make_async_copy(moved[r].at[2 * s], new_ck.at[old + s], sem.at[2]),
-                    pltpu.make_async_copy(moved[r].at[2 * s + 1], new_cv.at[old + s], sem.at[3]),
-                ]
-                for fill in fills:
-                    fill.start()
-                for fill in fills:
-                    fill.wait()
-
-    for keep in keeps:
-        keep.wait()
+                new_ck[old + s] = moved[r][2 * s]
+                new_cv[old + s] = moved[r][2 * s + 1]
 
 
 def refill(source, ck, cv, moved):
-    anywhere = pl.BlockSpec(memory_space=pl.ANY)
     shape = jax.ShapeDtypeStruct(ck.shape, ck.dtype)
+    whole = pl.BlockSpec(memory_space=pltpu.VMEM)
     return pl.pallas_call(
         functools.partial(refill_kernel, len(moved)),
         out_shape=(shape, shape),
-        in_specs=[pl.BlockSpec(memory_space=pltpu.SMEM)] + [anywhere] * (2 + len(moved)),
-        out_specs=(anywhere, anywhere),
-        scratch_shapes=[pltpu.SemaphoreType.DMA((4,))],
+        in_specs=[pl.BlockSpec(memory_space=pltpu.SMEM)] + [whole] * (2 + len(moved)),
+        out_specs=(whole, whole),
         name="refill",
     )(source, ck, cv, *moved)
 
@@ -396,14 +377,19 @@
     total = k_first.shape[0]
     ids = jnp.arange(total, dtype=jnp.int32)
     hits = seen.astype(jnp.int32)
+    rim = (seen & ~inside).astype(jnp.int32)
     count = jnp.sum(hits, axis=1)
-    rank = jnp.sum(jnp.where(ids[None, None, :] < ids[None, :, None], hits[:, None, :], 0), axis=2)
+    rims = jnp.sum(rim, axis=1)
+    odd = count % 2
+    before = ids[None, None, :] < ids[None, :, None]
+    rim_rank = jnp.sum(jnp.where(before, rim[:, None, :], 0), axis=2)
+    rank = jnp.sum(jnp.where(before, hits[:, None, :], 0), axis=2)
+    rank = odd[:, None] + jnp.where(rim > 0, rim_rank, rims[:, None] + rank - rim_rank)
     at = seen[:, None, :] & (rank[:, None, :] == ids[None, :, None])
-    pick = lambda x: jnp.sum(jnp.where(at, x, 0), axis=2)
-    filled = ids[None, :] < count[:, None]
-    chosen = pick(ids[None, None, :])
-    edge = jnp.where(filled, pick(1 - inside.astype(jnp.int32)[:, None, :]), 1)
-    first_key = jnp.where(filled, pick(k_first[None, None, :]), FAR)
+    packed = jnp.sum(jnp.where(at, (k_first * total + ids)[None, None, :] + 1, 0), axis=2)
+    chosen = jnp.maximum(packed - 1, 0) % total
+    first_key = jnp.where(packed > 0, jnp.maximum(packed - 1, 0) // total, FAR)
+    edges = (odd + rims + 1) // 2
     targets = table_entry(block_table, n_request, n_first // size)
     wanted = (q_dev[:, None] * slots + old + step[None, :]).reshape(-1)
     hit = (targets[None, :] == wanted[:, None]) & ~is_old[None, :]
@@ -418,7 +404,7 @@
     meta = (
         count,
         chosen.reshape(-1),
-        edge.reshape(-1),
+        edges,
         first_key.reshape(-1),
         q_first,
         q_window,

time: 190 us -> 172 us (0.905)
  the two profiles are of different devices: /device:TPU:6 before, /device:TPU:192 now
where the time goes in v1:
time: 172 us; the launch traced here: 170 us
  waiting for transfers between devices  81.8 us (48%)
  Pallas kernels  25.4 us (15%)
  starting transfers between devices  23.4 us (14%)
  between operations  14.3 us (8%)
  other arithmetic  11.2 us (7%)
  local copies, waits for them, and re-layouts  9.11 us (5%)
  matrix products  5.21 us (3%)
    ppermute x16, waiting for transfers between devices, shift(): return lax.ppermute(value, 'blk', blk_perm(dy, dz, dc))  62.3 us
    ppermute x16, starting transfers between devices, shift(): return lax.ppermute(value, 'blk', blk_perm(dy, dz, dc))  19.1 us
    all_to_all x1, waiting for transfers between devices, shards(): lax.all_to_all(blocks, 'head', split_axis=0, concat_axis=0, tiled=True)  18.7 us
    pallas_call x1, Pallas kernels, attend(): pl.pallas_call(functools.partial(attend_kernel, log_scale, nkv, nq), out_...  18.6 us
    unnamed x38, local copies, waits for them, and re-layouts  6.23 us
    dot_general x1, matrix products, shards(): lax.dot_general(attention, weight, (((1,), (1,)), ((), ())), preferred_el...  5.21 us
    all_to_all x1, starting transfers between devices, shards(): lax.all_to_all(blocks, 'head', split_axis=0, concat_axis=0, tiled=True)  4.29 us
    reduce_sum x2, other arithmetic, table_entry(): return jnp.sum(jnp.where(match, block_table[None], 0), axis=(1, 2))  3.89 us
  transfers between devices with their start and end apart: 18, of which 9 were waited for; matrix products, arithmetic and copies ran while one was open for 7% of the time, Pallas kernels for 15%

profile of v1, /device:TPU:192, one launch (start us, length us, event | category | flops | bytes accessed | tf_op | source)
XLA Modules:
  0.0 170.4 jit_solution(3251984511635928216)
XLA Ops:
  7.9 1.9 %pack.1.refs_0_ = bf16[12,128,128]{2,1,0:T(8,128)(2,1)} custom-call(bf16[6,128,128]{2,1,0:T(8,128)(2,1)} %bitcast.26, bf16[6,128,128]{2,1,0:T(8,128)(2,1)} %bitcast.28, bf16[2,128,128]{2,1,0:T(8,128)(2,1)} %bitcast.30, bf16[2,128,128]{2,1,0:T(8,128)(2,1)} %bitcast.31), custom_call_target="tpu_custom_call" | custom-call | tf_op jit(solution)/shard_map/pack/pallas_call | solution.py:78
  9.8 2.9 %collective-permute-start.3 = (bf16[12,128,128]{2,1,0:T(8,128)(2,1)}, bf16[12,128,128]{2,1,0:T(8,128)(2,1)S(1)}, u32[]{:S(2)}, u32[]{:S(2)}) collective-permute-start(bf16[12,128,128]{2,1,0:T(8,128)(2,1)} %pack.1.refs_0_), channel_id=1, source_target_pairs={{0,48},{8,56},{16,0},{24,8},{32,16},{40,24},{48,32},{56,40},{64,11... | collective-permute-start | bytes 1179656 | tf_op jit(solution)/shard_map/ppermute | solution.py:31
  12.7 2.1 %collective-permute-start.5 = (bf16[12,128,128]{2,1,0:T(8,128)(2,1)}, bf16[12,128,128]{2,1,0:T(8,128)(2,1)S(1)}, u32[]{:S(2)}, u32[]{:S(2)}) collective-permute-start(bf16[12,128,128]{2,1,0:T(8,128)(2,1)} %pack.1.refs_0_), channel_id=1, source_target_pairs={{0,32},{8,40},{16,48},{24,56},{32,0},{40,8},{48,16},{56,24},{64,96... | collective-permute-start | bytes 1179656 | tf_op jit(solution)/shard_map/ppermute | solution.py:31
  14.8 1.6 collective-permute-start.7
  16.4 1.7 collective-permute-start.8
  19.0 0.8 select_reduce_fusion.11
  21.5 0.9 select_reduce_fusion.9
  22.6 2.6 %select_reduce_fusion.1 = (s32[48]{0:T(128)S(1)}, s32[48]{0:T(128)S(1)}) fusion(s32[8,64]{1,0:T(8,128)} %param.19, pred[48,64]{1,0:T(8,128)(4,1)S(1)} %iota_compare_fusion.2, pred[48,8]{1,0:T(8,128)(4,1)S(1)} %copy.21, s32[8,64]{1,0:T(8,128)S(1)} %add_add_fusion, pred[8,64]{1,0:T(8,128)(4,1)S(1)} %iota_compare_fusion.8, s32[48]{0:T(128)S(1)} %add.446), kind=kLoop, calls=%fused_computation.3 | loop fusion | flops 171936 | bytes 8640 | tf_op jit(solution)/shard_map/reduce_sum | solution.py:53
  26.9 21.2 %collective-permute-done.3.refs_4_ = bf16[12,128,128]{2,1,0:T(8,128)(2,1)S(1)} collective-permute-done((bf16[12,128,128]{2,1,0:T(8,128)(2,1)}, bf16[12,128,128]{2,1,0:T(8,128)(2,1)S(1)}, u32[]{:S(2)}, u32[]{:S(2)}) %collective-permute-start.3) | collective-permute-done | bytes 393248 | tf_op jit(solution)/shard_map/ppermute | solution.py:31
  48.1 7.5 %collective-permute-done.5.refs_6_ = bf16[12,128,128]{2,1,0:T(8,128)(2,1)S(1)} collective-permute-done((bf16[12,128,128]{2,1,0:T(8,128)(2,1)}, bf16[12,128,128]{2,1,0:T(8,128)(2,1)S(1)}, u32[]{:S(2)}, u32[]{:S(2)}) %collective-permute-start.5) | collective-permute-done | bytes 393248 | tf_op jit(solution)/shard_map/ppermute | solution.py:31
  56.0 3.3 %collective-permute-start.9 = (bf16[5,256,128]{2,1,0:T(8,128)(2,1)}, bf16[5,256,128]{2,1,0:T(8,128)(2,1)S(1)}, u32[]{:S(2)}, u32[]{:S(2)}) collective-permute-start(bf16[5,256,128]{2,1,0:T(8,128)(2,1)} %bitcast.22), channel_id=1, source_target_pairs={{0,128},{8,136},{16,144},{24,152},{32,160},{40,168},{48,176},{56,1... | collective-permute-start | bytes 983048 | tf_op jit(solution)/shard_map/ppermute | solution.py:31
  59.5 8.9 %collective-permute-done.9.refs_11_ = bf16[5,256,128]{2,1,0:T(8,128)(2,1)S(1)} collective-permute-done((bf16[5,256,128]{2,1,0:T(8,128)(2,1)}, bf16[5,256,128]{2,1,0:T(8,128)(2,1)S(1)}, u32[]{:S(2)}, u32[]{:S(2)}) %collective-permute-start.9) | collective-permute-done | bytes 327712 | tf_op jit(solution)/shard_map/ppermute | solution.py:31
  68.5 1.0 copy-done
  69.4 1.0 copy-done.3
  70.4 18.6 %attend.1 = (bf16[2,656,128]{2,1,0:T(8,128)(2,1)S(1)}, bf16[2,656,128]{2,1,0:T(8,128)(2,1)S(1)}, bf16[2,656,128]{2,1,0:T(8,128)(2,1)S(1)}, bf16[2,656,128]{2,1,0...) custom-call(s32[8]{0:T(128)S(1)} %convert_reduce_fusion.3.count, ...), custom_call_target="tpu_custom_call" | custom-call | flops 5000000000 | bytes 8000000 | tf_op jit(solution)/shard_map/attend/pallas_call | solution.py:249
  89.1 0.7 copy-done.1
  91.8 3.7 %collective-permute-start.10 = (bf16[2,656,128]{2,1,0:T(8,128)(2,1)S(1)}, bf16[2,656,128]{2,1,0:T(8,128)(2,1)S(1)}, u32[]{:S(2)}, u32[]{:S(2)}) collective-permute-start(bf16[2,656,128]{2,1,0:T(8,128)(2,1)S(1)} %get-tuple-element.14), channel_id=1, source_target_pairs={{0,192},{8,200},{16,208},{24,216},{32,224},{40,232},{48,240},{56,2... | collective-permute-start | bytes 1007624 | tf_op jit(solution)/shard_map/ppermute | solution.py:31
  95.5 1.5 collective-permute-start.12
  96.9 13.7 %collective-permute-done.10.refs_1_ = bf16[2,656,128]{2,1,0:T(8,128)(2,1)S(1)} collective-permute-done((bf16[2,656,128]{2,1,0:T(8,128)(2,1)S(1)}, bf16[2,656,128]{2,1,0:T(8,128)(2,1)S(1)}, u32[]{:S(2)}, u32[]{:S(2)}) %collective-permute-start.10) | collective-permute-done | bytes 335904 | tf_op jit(solution)/shard_map/ppermute | solution.py:31
  110.7 3.9 %collective-permute-done.11.refs_2_ = bf16[2,656,128]{2,1,0:T(8,128)(2,1)S(1)} collective-permute-done((bf16[2,656,128]{2,1,0:T(8,128)(2,1)S(1)}, bf16[2,656,128]{2,1,0:T(8,128)(2,1)S(1)}, u32[]{:S(2)}, u32[]{:S(2)}) %collective-permute-start.11) | collective-permute-done | bytes 335904 | tf_op jit(solution)/shard_map/ppermute | solution.py:31
  114.5 0.7 copy-done.9
  115.4 2.8 %merge.1 = bf16[256,640]{1,0:T(8,128)(2,1)} custom-call(bf16[2,656,128]{2,1,0:T(8,128)(2,1)} %copy-done.1, bf16[2,656,128]{2,1,0:T(8,128)(2,1)} %copy-done.8, bf16[2,656,128]{2,1,0:T(8,128)(2,1)} %copy-done.9, bf16[2,656,128]{2,1,0:T(8,128)(2,1)} %copy-done.10), custom_call_target="tpu_custom_call" | custom-call | tf_op jit(solution)/shard_map/merge/pallas_call | solution.py:305
  118.2 5.2 %convolution_convert_fusion = bf16[256,5120]{1,0:T(8,128)(2,1)S(1)} fusion(bf16[256,640]{1,0:T(8,128)(2,1)} %merge.1, bf16[5120,640]{1,0:T(8,128)(2,1)} %all-gather.2.cloned.1.call-done), kind=kOutput, calls=%fused_computation | convolution fusion | flops 1679032320 | bytes 9502720 | tf_op jit(solution)/shard_map/dot_general | solution.py:451
  123.5 1.8 %copy.28 = bf16[32,8,8,640]{3,2,0,1:T(8,128)(2,1)} copy(bf16[32,8,8,640]{3,2,1,0:T(8,128)(2,1)S(1)} %bitcast.25) | data formatting | bytes 5242880 | tf_op jit(solution)/shard_map/reshape | solution.py:455
  125.3 4.3 %all-to-all-start = ((bf16[8,256,640]{2,1,0:T(8,128)(2,1)}), bf16[8,256,640]{2,1,0:T(8,128)(2,1)S(1)}, u32[]{:S(2)}, u32[]{:S(2)}) async-start(bf16[8,256,640]{2,1,0:T(8,128)(2,1)} %bitcast.24), calls=%async_computation | async-start | bytes 5242880 | tf_op jit(solution)/shard_map/all_to_all | solution.py:456
  130.0 1.3 select_reduce_fusion
  131.6 2.0 %collective-permute-start.14 = (bf16[4,128,128]{2,1,0:T(8,128)(2,1)S(1)}, bf16[4,128,128]{2,1,0:T(8,128)(2,1)S(1)}, u32[]{:S(2)}, u32[]{:S(2)}) collective-permute-start(bf16[4,128,128]{2,1,0:T(8,128)(2,1)S(1)} %copy-done.5), channel_id=1, source_target_pairs={{0,64},{8,72},{16,80},{24,88},{32,96},{40,104},{48,112},{56,120},{... | collective-permute-start | bytes 393224 | tf_op jit(solution)/shard_map/ppermute | solution.py:31
  134.2 3.6 %collective-permute-done.13.refs_1_ = bf16[4,128,128]{2,1,0:T(8,128)(2,1)S(1)} collective-permute-done((bf16[4,128,128]{2,1,0:T(8,128)(2,1)S(1)}, bf16[4,128,128]{2,1,0:T(8,128)(2,1)S(1)}, u32[]{:S(2)}, u32[]{:S(2)}) %collective-permute-start.13) | collective-permute-done | bytes 131104 | tf_op jit(solution)/shard_map/ppermute | solution.py:31
  137.8 3.2 %collective-permute-done.14.refs_2_ = bf16[4,128,128]{2,1,0:T(8,128)(2,1)S(1)} collective-permute-done((bf16[4,128,128]{2,1,0:T(8,128)(2,1)S(1)}, bf16[4,128,128]{2,1,0:T(8,128)(2,1)S(1)}, u32[]{:S(2)}, u32[]{:S(2)}) %collective-permute-start.14) | collective-permute-done | bytes 131104 | tf_op jit(solution)/shard_map/ppermute | solution.py:31
  141.6 2.1 %refill.1 = (bf16[6,128,128]{2,1,0:T(8,128)(2,1)}, bf16[6,128,128]{2,1,0:T(8,128)(2,1)}) custom-call(s32[2]{0:T(128)} %compare_select_fusion.11.source, bf16[6,128,128]{2,1,0:T(8,128)(2,1)} %bitcast.27, bf16[6,128,128]{2,1,0:T(8,128)(2,1)} %bitcast.29, bf16[4,128,128]{2,1,0:T(8,128)(2,1)} %copy-done.2, bf16[4,128,128]{2,1,0:T(8,128)(2,1)} %copy-done.11, ...), custom_call_target="tpu_custom_call" | custom-call | tf_op jit(solution)/shard_map/refill/pallas_call | solution.py:331
  143.7 18.7 %all-to-all-done = bf16[8,256,640]{2,1,0:T(8,128)(2,1)S(1)} async-done(((bf16[8,256,640]{2,1,0:T(8,128)(2,1)}), bf16[8,256,640]{2,1,0:T(8,128)(2,1)S(1)}, u32[]{:S(2)}, u32[]{:S(2)}) %all-to-all-start) | async-done | bytes 2621472 | tf_op jit(solution)/shard_map/all_to_all | solution.py:456
  162.4 1.2 reduce_sum.196
  (112 shorter events, 9.9 us)
Async XLA Ops:
  7.2 111.1 %all-gather.2.cloned.1.call-start = ((), (), s32[]{:S(2)}) async-start(), calls=%async_computation.1 | async-start | bytes 6758400 | tf_op jit(solution)/shard_map/all_gather | solution.py:444
  9.8 17.0 %collective-permute-start.1 = (bf16[12,128,128]{2,1,0:T(8,128)(2,1)}, bf16[12,128,128]{2,1,0:T(8,128)(2,1)S(1)}, u32[]{:S(2)}, u32[]{:S(2)}) collective-permute-start(bf16[12,128,128]{2,1,0:T(8,128)(2,1)} %pack.1.refs_0_), channel_id=1, source_target_pairs={{0,16},{8,24},{16,32},{24,40},{32,48},{40,56},{48,0},{56,8},{64,80... | collective-permute-start | bytes 1179656 | tf_op jit(solution)/shard_map/ppermute | solution.py:31
  9.8 38.3 %collective-permute-start.3 = (bf16[12,128,128]{2,1,0:T(8,128)(2,1)}, bf16[12,128,128]{2,1,0:T(8,128)(2,1)S(1)}, u32[]{:S(2)}, u32[]{:S(2)}) collective-permute-start(bf16[12,128,128]{2,1,0:T(8,128)(2,1)} %pack.1.refs_0_), channel_id=1, source_target_pairs={{0,48},{8,56},{16,0},{24,8},{32,16},{40,24},{48,32},{56,40},{64,11... | collective-permute-start | bytes 1179656 | tf_op jit(solution)/shard_map/ppermute | solution.py:31
  12.7 42.9 %collective-permute-start.5 = (bf16[12,128,128]{2,1,0:T(8,128)(2,1)}, bf16[12,128,128]{2,1,0:T(8,128)(2,1)S(1)}, u32[]{:S(2)}, u32[]{:S(2)}) collective-permute-start(bf16[12,128,128]{2,1,0:T(8,128)(2,1)} %pack.1.refs_0_), channel_id=1, source_target_pairs={{0,32},{8,40},{16,48},{24,56},{32,0},{40,8},{48,16},{56,24},{64,96... | collective-permute-start | bytes 1179656 | tf_op jit(solution)/shard_map/ppermute | solution.py:31
  14.8 11.5 %collective-permute-start.7 = (bf16[5,256,128]{2,1,0:T(8,128)(2,1)}, bf16[5,256,128]{2,1,0:T(8,128)(2,1)S(1)}, u32[]{:S(2)}, u32[]{:S(2)}) collective-permute-start(bf16[5,256,128]{2,1,0:T(8,128)(2,1)} %bitcast.20), channel_id=1, source_target_pairs={{0,64},{8,72},{16,80},{24,88},{32,96},{40,104},{48,112},{56,120},{... | collective-permute-start | bytes 983048 | tf_op jit(solution)/shard_map/ppermute | solution.py:31
  16.4 39.7 %collective-permute-start.8 = (bf16[5,256,128]{2,1,0:T(8,128)(2,1)}, bf16[5,256,128]{2,1,0:T(8,128)(2,1)S(1)}, u32[]{:S(2)}, u32[]{:S(2)}) collective-permute-start(bf16[5,256,128]{2,1,0:T(8,128)(2,1)} %bitcast.21), channel_id=1, source_target_pairs={{0,192},{8,200},{16,208},{24,216},{32,224},{40,232},{48,240},{56,2... | collective-permute-start | bytes 983048 | tf_op jit(solution)/shard_map/ppermute | solution.py:31
  19.8 1.5 copy-start.17
  21.2 1.2 copy-start.15
  26.3 42.2 %collective-permute-start = (bf16[12,128,128]{2,1,0:T(8,128)(2,1)}, bf16[12,128,128]{2,1,0:T(8,128)(2,1)S(1)}, u32[]{:S(2)}, u32[]{:S(2)}) collective-permute-start(bf16[12,128,128]{2,1,0:T(8,128)(2,1)} %pack.1.refs_0_), channel_id=1, source_target_pairs={{0,8},{8,0},{16,24},{24,16},{32,40},{40,32},{48,56},{56,48},{64,72... | collective-permute-start | bytes 1179656 | tf_op jit(solution)/shard_map/ppermute | solution.py:31
  26.7 41.7 %collective-permute-start.2 = (bf16[12,128,128]{2,1,0:T(8,128)(2,1)S(1)}, bf16[12,128,128]{2,1,0:T(8,128)(2,1)S(1)}, u32[]{:S(2)}, u32[]{:S(2)}) collective-permute-start(bf16[12,128,128]{2,1,0:T(8,128)(2,1)S(1)} %collective-permute-done.1.refs_2_), channel_id=1, source_target_pairs={{0,8},{8,0},{16,24},{24,16},{32,40},{40,32},{48,56},{56,48},{64,72... | collective-permute-start | bytes 1179656 | tf_op jit(solution)/shard_map/ppermute | solution.py:31
  48.1 20.3 %collective-permute-start.4 = (bf16[12,128,128]{2,1,0:T(8,128)(2,1)S(1)}, bf16[12,128,128]{2,1,0:T(8,128)(2,1)S(1)}, u32[]{:S(2)}, u32[]{:S(2)}) collective-permute-start(bf16[12,128,128]{2,1,0:T(8,128)(2,1)S(1)} %collective-permute-done.3.refs_4_), channel_id=1, source_target_pairs={{0,8},{8,0},{16,24},{24,16},{32,40},{40,32},{48,56},{56,48},{64,72... | collective-permute-start | bytes 1179656 | tf_op jit(solution)/shard_map/ppermute | solution.py:31
  55.6 12.9 %collective-permute-start.6 = (bf16[12,128,128]{2,1,0:T(8,128)(2,1)S(1)}, bf16[12,128,128]{2,1,0:T(8,128)(2,1)S(1)}, u32[]{:S(2)}, u32[]{:S(2)}) collective-permute-start(bf16[12,128,128]{2,1,0:T(8,128)(2,1)S(1)} %collective-permute-done.5.refs_6_), channel_id=1, source_target_pairs={{0,8},{8,0},{16,24},{24,16},{32,40},{40,32},{48,56},{56,48},{64,72... | collective-permute-start | bytes 1179656 | tf_op jit(solution)/shard_map/ppermute | solution.py:31
  56.0 12.4 %collective-permute-start.9 = (bf16[5,256,128]{2,1,0:T(8,128)(2,1)}, bf16[5,256,128]{2,1,0:T(8,128)(2,1)S(1)}, u32[]{:S(2)}, u32[]{:S(2)}) collective-permute-start(bf16[5,256,128]{2,1,0:T(8,128)(2,1)} %bitcast.22), channel_id=1, source_target_pairs={{0,128},{8,136},{16,144},{24,152},{32,160},{40,168},{48,176},{56,1... | collective-permute-start | bytes 983048 | tf_op jit(solution)/shard_map/ppermute | solution.py:31
  68.4 1.0 copy-start
  69.4 1.0 copy-start.3
  89.0 0.7 copy-start.1
  91.8 18.9 %collective-permute-start.10 = (bf16[2,656,128]{2,1,0:T(8,128)(2,1)S(1)}, bf16[2,656,128]{2,1,0:T(8,128)(2,1)S(1)}, u32[]{:S(2)}, u32[]{:S(2)}) collective-permute-start(bf16[2,656,128]{2,1,0:T(8,128)(2,1)S(1)} %get-tuple-element.14), channel_id=1, source_target_pairs={{0,192},{8,200},{16,208},{24,216},{32,224},{40,232},{48,240},{56,2... | collective-permute-start | bytes 1007624 | tf_op jit(solution)/shard_map/ppermute | solution.py:31
  95.5 19.1 %collective-permute-start.11 = (bf16[2,656,128]{2,1,0:T(8,128)(2,1)S(1)}, bf16[2,656,128]{2,1,0:T(8,128)(2,1)S(1)}, u32[]{:S(2)}, u32[]{:S(2)}) collective-permute-start(bf16[2,656,128]{2,1,0:T(8,128)(2,1)S(1)} %get-tuple-element.15), channel_id=1, source_target_pairs={{0,64},{8,72},{16,80},{24,88},{32,96},{40,104},{48,112},{56,120},{... | collective-permute-start | bytes 1007624 | tf_op jit(solution)/shard_map/ppermute | solution.py:31
  95.5 19.1 %collective-permute-start.12 = (bf16[2,656,128]{2,1,0:T(8,128)(2,1)S(1)}, bf16[2,656,128]{2,1,0:T(8,128)(2,1)S(1)}, u32[]{:S(2)}, u32[]{:S(2)}) collective-permute-start(bf16[2,656,128]{2,1,0:T(8,128)(2,1)S(1)} %get-tuple-element.16), channel_id=1, source_target_pairs={{0,128},{8,136},{16,144},{24,152},{32,160},{40,168},{48,176},{56,1... | collective-permute-start | bytes 1007624 | tf_op jit(solution)/shard_map/ppermute | solution.py:31
  110.6 3.9 %copy-start.8 = (bf16[2,656,128]{2,1,0:T(8,128)(2,1)}, bf16[2,656,128]{2,1,0:T(8,128)(2,1)S(1)}, u32[]{:S(2)}) copy-start(bf16[2,656,128]{2,1,0:T(8,128)(2,1)S(1)} %collective-permute-done.10.refs_1_) | copy-start | bytes 1007620
  114.5 0.7 copy-start.9
  114.5 0.8 copy-start.10
  123.4 6.1 %copy-start.18 = (s32[8]{0:T(128)S(1)}, s32[8]{0:T(128)}, u32[]{:S(2)}) copy-start(s32[8]{0:T(128)} %copy-done.17) | copy-start | bytes 100
  123.5 6.3 %copy-start.16 = (s32[8]{0:T(128)S(1)}, s32[8]{0:T(128)}, u32[]{:S(2)}) copy-start(s32[8]{0:T(128)} %copy-done.15) | copy-start | bytes 100
  123.5 6.5 %copy-start.14 = (s32[8,64]{1,0:T(8,128)S(1)}, s32[8,64]{1,0:T(8,128)}, u32[]{:S(2)}) copy-start(s32[8,64]{1,0:T(8,128)} %param.19) | copy-start | bytes 6148
  123.5 8.0 %copy-start.7 = (bf16[4,128,128]{2,1,0:T(8,128)(2,1)S(1)}, bf16[4,128,128]{2,1,0:T(8,128)(2,1)}, u32[]{:S(2)}) copy-start(bf16[4,128,128]{2,1,0:T(8,128)(2,1)} %copy-done.6) | copy-start | bytes 393220
  123.5 8.1 %copy-start.5 = (bf16[4,128,128]{2,1,0:T(8,128)(2,1)S(1)}, bf16[4,128,128]{2,1,0:T(8,128)(2,1)}, u32[]{:S(2)}) copy-start(bf16[4,128,128]{2,1,0:T(8,128)(2,1)} %copy-done.4) | copy-start | bytes 393220
  125.3 37.2 %all-to-all-start = ((bf16[8,256,640]{2,1,0:T(8,128)(2,1)}), bf16[8,256,640]{2,1,0:T(8,128)(2,1)S(1)}, u32[]{:S(2)}, u32[]{:S(2)}) async-start(bf16[8,256,640]{2,1,0:T(8,128)(2,1)} %bitcast.24), calls=%async_computation | async-start | bytes 5242880 | tf_op jit(solution)/shard_map/all_to_all | solution.py:456
  131.5 6.3 %collective-permute-start.13 = (bf16[4,128,128]{2,1,0:T(8,128)(2,1)S(1)}, bf16[4,128,128]{2,1,0:T(8,128)(2,1)S(1)}, u32[]{:S(2)}, u32[]{:S(2)}) collective-permute-start(bf16[4,128,128]{2,1,0:T(8,128)(2,1)S(1)} %copy-done.7), channel_id=1, source_target_pairs={{0,192},{8,200},{16,208},{24,216},{32,224},{40,232},{48,240},{56,2... | collective-permute-start | bytes 393224 | tf_op jit(solution)/shard_map/ppermute | solution.py:31
  131.6 9.3 %collective-permute-start.14 = (bf16[4,128,128]{2,1,0:T(8,128)(2,1)S(1)}, bf16[4,128,128]{2,1,0:T(8,128)(2,1)S(1)}, u32[]{:S(2)}, u32[]{:S(2)}) collective-permute-start(bf16[4,128,128]{2,1,0:T(8,128)(2,1)S(1)} %copy-done.5), channel_id=1, source_target_pairs={{0,64},{8,72},{16,80},{24,88},{32,96},{40,104},{48,112},{56,120},{... | collective-permute-start | bytes 393224 | tf_op jit(solution)/shard_map/ppermute | solution.py:31
  133.6 7.3 %collective-permute-start.15 = (bf16[4,128,128]{2,1,0:T(8,128)(2,1)S(1)}, bf16[4,128,128]{2,1,0:T(8,128)(2,1)S(1)}, u32[]{:S(2)}, u32[]{:S(2)}) collective-permute-start(bf16[4,128,128]{2,1,0:T(8,128)(2,1)S(1)} %get-tuple-element.20), channel_id=1, source_target_pairs={{0,128},{8,136},{16,144},{24,152},{32,160},{40,168},{48,176},{56,1... | collective-permute-start | bytes 393224 | tf_op jit(solution)/shard_map/ppermute | solution.py:31
  137.8 3.2 %copy-start.11 = (bf16[4,128,128]{2,1,0:T(8,128)(2,1)}, bf16[4,128,128]{2,1,0:T(8,128)(2,1)S(1)}, u32[]{:S(2)}) copy-start(bf16[4,128,128]{2,1,0:T(8,128)(2,1)S(1)} %collective-permute-done.13.refs_1_) | copy-start | bytes 393220
  (5 other events, 3.3 us)
Sparse Core Ops, SparseCore 0:
  10.5 86.3 all-gather.1

commit v2 on v1

--- a/solution.py
+++ b/solution.py
@@ -9,6 +9,7 @@
 from jax.sharding import PartitionSpec as P
 
 NY, NZ, NC = 4, 4, 2
+NX, NL = 4, 2
 SINK = 4
 LOWEST = -1e30
 FLOOR = -1e25
@@ -29,6 +30,19 @@
 
 def shift(value, dy=0, dz=0, dc=0):
     return lax.ppermute(value, "blk", blk_perm(dy, dz, dc))
+
+
+def head_shift(value, dx=0, dz=0):
+    pairs = []
+    for x in range(NX):
+        for z in range(NL):
+            pairs.append((x * NL + z, (x + dx) % NX * NL + (z + dz) % NL))
+    return lax.ppermute(value, "head", pairs)
+
+
+def ring_place(distance):
+    distance = distance % len(SHIFTS)
+    return jnp.where(distance == 3, 2, jnp.where(distance == 2, 3, distance))
 
 
 def lookup(table_row, wanted):
@@ -250,7 +264,7 @@
         functools.partial(attend_kernel, log_scale, nkv, nq),
         out_shape=(parts,) * nq + (moved,) * nq,
         in_specs=[smem] * len(meta) + [anywhere] * (nkv + nq),
-        out_specs=(pl.BlockSpec(memory_space=pltpu.HBM),) * (2 * nq),
+        out_specs=(anywhere,) * (2 * nq),
         scratch_shapes=[
             pltpu.VMEM((nkv * slots, size, width), jnp.bfloat16),
             pltpu.VMEM((nq, heads, rows, width), jnp.bfloat16),
@@ -262,7 +276,7 @@
             pltpu.SemaphoreType.DMA((nq,)),
             pltpu.SemaphoreType.DMA((2 * nq * per,)),
         ],
-        compiler_params=pltpu.CompilerParams(vmem_limit_bytes=40 << 20),
+        compiler_params=pltpu.CompilerParams(vmem_limit_bytes=56 << 20),
         cost_estimate=pl.CostEstimate(
             flops=5_000_000_000, bytes_accessed=8_000_000, transcendentals=8_000_000
         ),
@@ -270,17 +284,34 @@
     )(*meta, *kv_parts, *q_parts)
 
 
-def merge_kernel(heads, *refs):
-    parts = refs[:-1]
-    out = refs[-1]
-    per, lines, width = parts[0].shape
+def finish_kernel(heads, nparts, nw, pieces, *refs):
+    part_in = refs[:nparts]
+    w_in = refs[nparts : nparts + nw]
+    first_out = refs[nparts + nw : nparts + nw + NX]
+    second_out = refs[nparts + nw + NX : nparts + nw + NX + NL]
+    parts, weight, mixed_rows, first, second, part_sem, w_sem, a_sem, b_sem = refs[
+        nparts + nw + NX + NL :
+    ]
+    group = w_in[0].shape[0]
+    per, lines, width = part_in[0].shape
     size = (lines - 16) // heads
+    part_loads = [
+        pltpu.make_async_copy(part_in[r], parts.at[r], part_sem.at[r]) for r in range(nparts)
+    ]
+    w_loads = [
+        pltpu.make_async_copy(w_in[a], weight.at[pl.ds(a * group, group)], w_sem.at[a])
+        for a in range(nw)
+    ]
+    for load in part_loads + w_loads:
+        load.start()
+    for load in part_loads:
+        load.wait()
     row_ids = lax.broadcasted_iota(jnp.int32, (size, width), 0)
     col_ids = lax.broadcasted_iota(jnp.int32, (size, width), 1)
     for s in range(per):
         levels = []
-        for part in parts:
-            stats = part[s, heads * size :, :].astype(jnp.float32)
+        for r in range(nparts):
+            stats = parts[r, s, heads * size :, :].astype(jnp.float32)
             levels.append(
                 stats[0:heads] + stats[heads : 2 * heads] + stats[2 * heads : 3 * heads]
             )
@@ -290,49 +321,109 @@
         shares = [share / whole for share in shares]
         for h in range(heads):
             mixed = jnp.zeros((size, width), jnp.float32)
-            for part, share in zip(parts, shares):
-                spread = jnp.where(row_ids == col_ids, share[h : h + 1, :], 0.0)
+            for r in range(nparts):
+                spread = jnp.where(row_ids == col_ids, shares[r][h : h + 1, :], 0.0)
                 column = jnp.sum(spread, axis=1, keepdims=True)
-                mixed += column * part[s, h * size : (h + 1) * size, :].astype(jnp.float32)
-            out[s * size : (s + 1) * size, h * width : (h + 1) * width] = mixed.astype(
+                mixed += column * parts[r, s, h * size : (h + 1) * size, :].astype(jnp.float32)
+            mixed_rows[s * size : (s + 1) * size, h * width : (h + 1) * width] = mixed.astype(
                 jnp.bfloat16
             )
-
-
-def merge(parts, heads):
+    for load in w_loads:
+        load.wait()
+    sends = []
+    for r in reversed(range(NX)):
+        for z in range(NL):
+            at = (r * NL + z) * group
+            rows = jnp.concatenate([weight[pieces[at + q]] for q in range(group)], axis=0)
+            product = lax.dot_general(
+                mixed_rows[...], rows, (((1,), (1,)), ((), ())), preferred_element_type=jnp.float32
+            ).astype(jnp.bfloat16)
+            first[r, z] = product[:size]
+            second[z, r] = product[size:]
+        sends.append(pltpu.make_async_copy(first.at[r], first_out[r], a_sem.at[r]))
+        sends[-1].start()
+    for z in range(NL):
+        sends.append(pltpu.make_async_copy(second.at[z], second_out[z], b_sem.at[z]))
+        sends[-1].start()
+    for send in sends:
+        send.wait()
+
+
+def finish(pieces, parts, w_parts, heads):
     per, lines, width = parts[0].shape
     size = (lines - 16) // heads
+    group, rows, depth = w_parts[0].shape
+    columns = group * rows
+    nparts, nw = len(parts), len(w_parts)
+    anywhere = pl.BlockSpec(memory_space=pl.ANY)
+    first = jax.ShapeDtypeStruct((NL, size, columns), jnp.bfloat16)
+    second = jax.ShapeDtypeStruct((NX, size, columns), jnp.bfloat16)
     return pl.pallas_call(
-        functools.partial(merge_kernel, heads),
-        out_shape=jax.ShapeDtypeStruct((per * size, heads * width), jnp.bfloat16),
-        name="merge",
-    )(*parts)
+        functools.partial(finish_kernel, heads, nparts, nw),
+        out_shape=(first,) * NX + (second,) * NL,
+        in_specs=[pl.BlockSpec(memory_space=pltpu.SMEM)] + [anywhere] * (nparts + nw),
+        out_specs=(anywhere,) * (NX + NL),
+        scratch_shapes=[
+            pltpu.VMEM((nparts, per, lines, width), jnp.bfloat16),
+            pltpu.VMEM((nw * group, rows, depth), jnp.bfloat16),
+            pltpu.VMEM((per * size, heads * width), jnp.bfloat16),
+            pltpu.VMEM((NX, NL, size, columns), jnp.bfloat16),
+            pltpu.VMEM((NL, NX, size, columns), jnp.bfloat16),
+            pltpu.SemaphoreType.DMA((nparts,)),
+            pltpu.SemaphoreType.DMA((nw,)),
+            pltpu.SemaphoreType.DMA((NX,)),
+            pltpu.SemaphoreType.DMA((NL,)),
+        ],
+        compiler_params=pltpu.CompilerParams(vmem_limit_bytes=24 << 20),
+        cost_estimate=pl.CostEstimate(
+            flops=2_000_000_000, bytes_accessed=12_000_000, transcendentals=10_000
+        ),
+        name="finish",
+    )(pieces, *parts, *w_parts)
+
+
+def piece_table(device, head, group):
+    c = device % NC
+    z = device // NC % NZ
+    y = device // (NC * NZ)
+    steps = jnp.array(SHIFTS, jnp.int32)
+    target = (head // NL + steps[:, None]) % NX * NL + (head + jnp.arange(NL)[None, :]) % NL
+    owner = (target.reshape(-1)[:, None] * group + jnp.arange(group)[None, :]).reshape(-1)
+    place = ring_place(y - owner // (NC * NZ)) * NC + (c + owner) % NC
+    return (place * NZ + ring_place(z - owner // NC % NZ)).astype(jnp.int32)
 
 
 def refill_kernel(nq, source, ck, cv, *refs):
-    moved = refs[:nq]
-    new_ck, new_cv = refs[nq:]
-    per = moved[0].shape[0] // 2
+    moved_in = refs[:nq]
+    new_ck, new_cv, moved, sem = refs[nq:]
+    per = moved_in[0].shape[0] // 2
     old = ck.shape[0] - per
+    loads = [pltpu.make_async_copy(moved_in[r], moved.at[r], sem.at[r]) for r in range(nq)]
+    for load in loads:
+        load.start()
     new_ck[0:old] = ck[0:old]
     new_cv[0:old] = cv[0:old]
+    for load in loads:
+        load.wait()
     for s in range(per):
-        for r in range(nq):
-
-            @pl.when(source[s] == r)
-            def _():
-                new_ck[old + s] = moved[r][2 * s]
-                new_cv[old + s] = moved[r][2 * s + 1]
+        new_ck[old + s] = moved[source[s], 2 * s]
+        new_cv[old + s] = moved[source[s], 2 * s + 1]
 
 
 def refill(source, ck, cv, moved):
     shape = jax.ShapeDtypeStruct(ck.shape, ck.dtype)
     whole = pl.BlockSpec(memory_space=pltpu.VMEM)
+    anywhere = pl.BlockSpec(memory_space=pl.ANY)
+    nq = len(moved)
     return pl.pallas_call(
-        functools.partial(refill_kernel, len(moved)),
+        functools.partial(refill_kernel, nq),
         out_shape=(shape, shape),
-        in_specs=[pl.BlockSpec(memory_space=pltpu.SMEM)] + [whole] * (2 + len(moved)),
+        in_specs=[pl.BlockSpec(memory_space=pltpu.SMEM)] + [whole] * 2 + [anywhere] * nq,
         out_specs=(whole, whole),
+        scratch_shapes=[
+            pltpu.VMEM((nq,) + moved[0].shape, moved[0].dtype),
+            pltpu.SemaphoreType.DMA((nq,)),
+        ],
         name="refill",
     )(source, ck, cv, *moved)
 
@@ -399,8 +490,7 @@
     a_target = table_entry(block_table, a_request, a_first // size)
     mine = a_target[None, :] == (device * slots + old + step)[:, None]
     from_y = jnp.sum(jnp.where(mine, (all_new // (per * NC * NZ))[None, :], 0), axis=1)
-    ahead = (from_y - y) % NY
-    source = jnp.where(ahead == NY - 1, 2, jnp.where(ahead == 2, 3, ahead))
+    source = ring_place(from_y - y)
     meta = (
         count,
         chosen.reshape(-1),
@@ -426,35 +516,48 @@
     window,
 ):
     device = lax.axis_index("blk")
+    head = lax.axis_index("head")
     tokens, heads, width = queries.shape
     slots, size = cache_keys.shape[:2]
     per = tokens // size
     log_scale = math.log2(math.e) / math.sqrt(width)
     ck = cache_keys.reshape(slots, size, width)
     cv = cache_values.reshape(slots, size, width)
+    own_q = jnp.transpose(queries, (1, 0, 2))
+    w_line = [out_weight] + [shift(out_weight, dz=k) for k in SHIFTS[1:]]
     own_kv = pack(
         ck, cv, new_keys.reshape(per, size, width), new_values.reshape(per, size, width)
     )
-    own_q = jnp.transpose(queries, (1, 0, 2))
     lines = [own_kv] + [shift(own_kv, dz=k) for k in SHIFTS[1:]]
     q_parts = [own_q] + [shift(own_q, dy=k) for k in SHIFTS[1:]]
     kv_parts = []
     for part in lines:
         kv_parts += [part, shift(part, dc=1)]
-    weight = lax.all_gather(out_weight, "blk", axis=0, tiled=True)
+    w_four = jnp.stack(w_line)
+    w_far = [shift(w_four, dy=k) for k in SHIFTS[1:]]
+    w_parts = [w_four, shift(w_four, dc=1)]
     meta, source = plan(device, per, slots, size, cache_len, span_len, block_table, window)
     outs = attend(meta, kv_parts, q_parts, log_scale)
     parts, moved = outs[: len(SHIFTS)], outs[len(SHIFTS) :]
+    for part in lax.optimization_barrier((*w_far, parts[0]))[:-1]:
+        w_parts += [part, shift(part, dc=1)]
     parts = [parts[0]] + [shift(p, dy=-k) for p, k in zip(parts[1:], SHIFTS[1:])]
     moved = [moved[0]] + [shift(p, dy=-k) for p, k in zip(moved[1:], SHIFTS[1:])]
-    attention = merge(parts, heads)
-    partial_out = lax.dot_general(
-        attention, weight, (((1,), (1,)), ((), ())), preferred_element_type=jnp.float32
-    ).astype(jnp.bfloat16)
-    n_head = lax.axis_size("head")
-    blocks = jnp.moveaxis(partial_out.reshape(tokens, n_head, -1), 1, 0)
-    arrived = lax.all_to_all(blocks, "head", split_axis=0, concat_axis=0, tiled=True)
-    attn_output = arrived.astype(jnp.float32).sum(axis=0).astype(jnp.bfloat16)
+    pieces = piece_table(device, head, heads * width // out_weight.shape[0])
+    shares = finish(pieces, parts, w_parts, heads)
+    first, second = shares[:NX], shares[NX:]
+    first = [first[0]] + [head_shift(p, dx=k) for p, k in zip(first[1:], SHIFTS[1:])]
+    second_sum = second[0].astype(jnp.float32) + head_shift(second[1], dz=1).astype(jnp.float32)
+    first_sum = functools.reduce(jnp.add, [p.astype(jnp.float32) for p in first])
+    second_out = second_sum[0]
+    for r in range(1, NX):
+        second_out += head_shift(second_sum[r].astype(jnp.bfloat16), dx=SHIFTS[r]).astype(
+            jnp.float32
+        )
+    first_out = first_sum[0] + head_shift(first_sum[1].astype(jnp.bfloat16), dz=1).astype(
+        jnp.float32
+    )
+    attn_output = jnp.concatenate([first_out, second_out], axis=0).astype(jnp.bfloat16)
     new_ck, new_cv = refill(source, ck, cv, moved)
     return (
         attn_output,

time: 172 us -> 174 us (1.012)
  the two profiles are of different devices: /device:TPU:192 before, /device:TPU:6 now
where the time goes in v2:
time: 174 us
  waiting for transfers between devices  67.1 us (39%)
  starting transfers between devices  57.7 us (33%)
  Pallas kernels  29 us (17%)
  other arithmetic  14.2 us (8%)
  local copies, waits for them, and re-layouts  4.9 us (3%)
    ppermute x26, waiting for transfers between devices, shift(): return lax.ppermute(value, 'blk', blk_perm(dy, dz, dc))  53.1 us
    ppermute x26, starting transfers between devices, shift(): return lax.ppermute(value, 'blk', blk_perm(dy, dz, dc))  50.5 us
    pallas_call x1, Pallas kernels, attend(): pl.pallas_call(functools.partial(attend_kernel, log_scale, nkv, nq), out_...  17.2 us
    ppermute x8, waiting for transfers between devices, head_shift(): return lax.ppermute(value, 'head', pairs)  14 us
    ppermute x8, starting transfers between devices, head_shift(): return lax.ppermute(value, 'head', pairs)  7.15 us
    pallas_call x1, Pallas kernels, finish(): pl.pallas_call(functools.partial(finish_kernel, heads, nparts, nw), out_s...  7.08 us
    reduce_sum x2, other arithmetic, table_entry(): return jnp.sum(jnp.where(match, block_table[None], 0), axis=(1, 2))  3.89 us
    unnamed x40, local copies, waits for them, and re-layouts  3.55 us
  transfers between devices with their start and end apart: 34, of which 13 were waited for; matrix products, arithmetic and copies ran while one was open for 8% of the time, Pallas kernels for 17%

profile of v2, /device:TPU:6, one launch (start us, length us, event | category | flops | bytes accessed | tf_op | source)
XLA Modules:
  0.0 174.1 jit_solution(12016077018569656780)
XLA Ops:
  0.7 3.3 %collective-permute-start.13 = (bf16[160,640]{1,0:T(8,128)(2,1)}, bf16[160,640]{1,0:T(8,128)(2,1)S(1)}, u32[]{:S(2)}, u32[]{:S(2)}) collective-permute-start(bf16[160,640]{1,0:T(8,128)(2,1)} %param.17), channel_id=1, source_target_pairs={{0,16},{8,24},{16,32},{24,40},{32,48},{40,56},{48,0},{56,8},{64,80... | collective-permute-start | bytes 614408 | tf_op jit(solution)/shard_map/ppermute | solution.py:32
  4.0 5.4 %collective-permute-start.15 = (bf16[160,640]{1,0:T(8,128)(2,1)}, bf16[160,640]{1,0:T(8,128)(2,1)S(1)}, u32[]{:S(2)}, u32[]{:S(2)}) collective-permute-start(bf16[160,640]{1,0:T(8,128)(2,1)} %param.17), channel_id=1, source_target_pairs={{0,32},{8,40},{16,48},{24,56},{32,0},{40,8},{48,16},{56,24},{64,96... | collective-permute-start | bytes 614408 | tf_op jit(solution)/shard_map/ppermute | solution.py:32
  9.4 2.7 %collective-permute-start.14 = (bf16[160,640]{1,0:T(8,128)(2,1)}, bf16[160,640]{1,0:T(8,128)(2,1)S(1)}, u32[]{:S(2)}, u32[]{:S(2)}) collective-permute-start(bf16[160,640]{1,0:T(8,128)(2,1)} %param.17), channel_id=1, source_target_pairs={{0,48},{8,56},{16,0},{24,8},{32,16},{40,24},{48,32},{56,40},{64,11... | collective-permute-start | bytes 614408 | tf_op jit(solution)/shard_map/ppermute | solution.py:32
  12.1 3.2 %collective-permute-start.9 = (bf16[5,256,128]{2,1,0:T(8,128)(2,1)}, bf16[5,256,128]{2,1,0:T(8,128)(2,1)S(1)}, u32[]{:S(2)}, u32[]{:S(2)}) collective-permute-start(bf16[5,256,128]{2,1,0:T(8,128)(2,1)} %bitcast.49), channel_id=1, source_target_pairs={{0,128},{8,136},{16,144},{24,152},{32,160},{40,168},{48,176},{56,1... | collective-permute-start | bytes 983048 | tf_op jit(solution)/shard_map/ppermute | solution.py:32
  15.3 1.8 %pack.1.refs_0_ = bf16[12,128,128]{2,1,0:T(8,128)(2,1)} custom-call(bf16[6,128,128]{2,1,0:T(8,128)(2,1)} %bitcast.39, bf16[6,128,128]{2,1,0:T(8,128)(2,1)} %bitcast.41, bf16[2,128,128]{2,1,0:T(8,128)(2,1)} %bitcast.47, bf16[2,128,128]{2,1,0:T(8,128)(2,1)} %bitcast.48), custom_call_target="tpu_custom_call" | custom-call | tf_op jit(solution)/shard_map/pack/pallas_call | solution.py:92
  21.5 2.6 %select_reduce_fusion.1 = (s32[48]{0:T(128)S(1)}, s32[48]{0:T(128)S(1)}) fusion(s32[8,64]{1,0:T(8,128)} %param.20, pred[48,64]{1,0:T(8,128)(4,1)S(1)} %iota_compare_fusion.2, pred[48,8]{1,0:T(8,128)(4,1)S(1)} %copy.19, s32[8,64]{1,0:T(8,128)S(1)} %add_add_fusion, pred[8,64]{1,0:T(8,128)(4,1)S(1)} %iota_compare_fusion.8, s32[48]{0:T(128)S(1)} %add.594), kind=kLoop, calls=%fused_computation.14 | loop fusion | flops 171936 | bytes 8640 | tf_op jit(solution)/shard_map/reduce_sum | solution.py:67
  28.4 14.5 %collective-permute-start.3 = (bf16[12,128,128]{2,1,0:T(8,128)(2,1)}, bf16[12,128,128]{2,1,0:T(8,128)(2,1)}, u32[]{:S(2)}, u32[]{:S(2)}) collective-permute-start(bf16[12,128,128]{2,1,0:T(8,128)(2,1)} %pack.1.refs_0_), channel_id=1, source_target_pairs={{0,48},{8,56},{16,0},{24,8},{32,16},{40,24},{48,32},{56,40},{64,11... | collective-permute-start | bytes 1179656 | tf_op jit(solution)/shard_map/ppermute | solution.py:32
  42.9 10.6 %collective-permute-done.14 = bf16[160,640]{1,0:T(8,128)(2,1)S(1)} collective-permute-done((bf16[160,640]{1,0:T(8,128)(2,1)}, bf16[160,640]{1,0:T(8,128)(2,1)S(1)}, u32[]{:S(2)}, u32[]{:S(2)}) %collective-permute-start.14) | collective-permute-done | bytes 204832 | tf_op jit(solution)/shard_map/ppermute | solution.py:32
  53.5 2.0 %collective-permute-start.1 = (bf16[12,128,128]{2,1,0:T(8,128)(2,1)}, bf16[12,128,128]{2,1,0:T(8,128)(2,1)}, u32[]{:S(2)}, u32[]{:S(2)}) collective-permute-start(bf16[12,128,128]{2,1,0:T(8,128)(2,1)} %pack.1.refs_0_), channel_id=1, source_target_pairs={{0,16},{8,24},{16,32},{24,40},{32,48},{40,56},{48,0},{56,8},{64,80... | collective-permute-start | bytes 1179656 | tf_op jit(solution)/shard_map/ppermute | solution.py:32
  56.2 1.7 collective-permute-start.7
  58.0 9.3 %collective-permute-done.7.refs_9_ = bf16[5,256,128]{2,1,0:T(8,128)(2,1)S(1)} collective-permute-done((bf16[5,256,128]{2,1,0:T(8,128)(2,1)S(1)}, bf16[5,256,128]{2,1,0:T(8,128)(2,1)S(1)}, u32[]{:S(2)}, u32[]{:S(2)}) %collective-permute-start.7) | collective-permute-done | bytes 327712 | tf_op jit(solution)/shard_map/ppermute | solution.py:32
  67.2 1.9 %collective-permute-start.19 = (bf16[4,160,640]{2,1,0:T(8,128)(2,1)S(1)}, bf16[4,160,640]{2,1,0:T(8,128)(2,1)S(1)}, u32[]{:S(2)}, u32[]{:S(2)}) collective-permute-start(bf16[4,160,640]{2,1,0:T(8,128)(2,1)S(1)} %pad_maximum_fusion.refs_4_), channel_id=1, source_target_pairs={{0,128},{8,136},{16,144},{24,152},{32,160},{40,168},{48,176},{56,1... | collective-permute-start | bytes 2457608 | tf_op jit(solution)/shard_map/ppermute | solution.py:32
  74.3 17.2 %attend.1 = (bf16[2,656,128]{2,1,0:T(8,128)(2,1)}, bf16[2,656,128]{2,1,0:T(8,128)(2,1)}, bf16[2,656,128]{2,1,0:T(8,128)(2,1)}, bf16[2,656,128]{2,1,0:T(8,128)(2,...) custom-call(s32[8]{0:T(128)} %copy-done.11, ...), custom_call_target="tpu_custom_call" | custom-call | flops 5000000000 | bytes 8000000 | tf_op jit(solution)/shard_map/attend/pallas_call | solution.py:263
  91.5 13.4 %collective-permute-done.18.refs_8_ = bf16[4,160,640]{2,1,0:T(8,128)(2,1)S(1)} collective-permute-done((bf16[4,160,640]{2,1,0:T(8,128)(2,1)S(1)}, bf16[4,160,640]{2,1,0:T(8,128)(2,1)S(1)}, u32[]{:S(2)}, u32[]{:S(2)}) %collective-permute-start.18) | collective-permute-done | bytes 819232 | tf_op jit(solution)/shard_map/ppermute | solution.py:32
  106.6 1.8 %collective-permute-start.10 = (bf16[2,656,128]{2,1,0:T(8,128)(2,1)}, bf16[2,656,128]{2,1,0:T(8,128)(2,1)S(1)}, u32[]{:S(2)}, u32[]{:S(2)}) collective-permute-start(bf16[2,656,128]{2,1,0:T(8,128)(2,1)} %get-tuple-element.23), channel_id=1, source_target_pairs={{0,192},{8,200},{16,208},{24,216},{32,224},{40,232},{48,240},{56,2... | collective-permute-start | bytes 1007624 | tf_op jit(solution)/shard_map/ppermute | solution.py:32
  110.2 7.0 %collective-permute-done.10.refs_1_ = bf16[2,656,128]{2,1,0:T(8,128)(2,1)S(1)} collective-permute-done((bf16[2,656,128]{2,1,0:T(8,128)(2,1)}, bf16[2,656,128]{2,1,0:T(8,128)(2,1)S(1)}, u32[]{:S(2)}, u32[]{:S(2)}) %collective-permute-start.10) | collective-permute-done | bytes 335904 | tf_op jit(solution)/shard_map/ppermute | solution.py:32
  117.2 1.9 %collective-permute-start.12 = (bf16[2,656,128]{2,1,0:T(8,128)(2,1)}, bf16[2,656,128]{2,1,0:T(8,128)(2,1)S(1)}, u32[]{:S(2)}, u32[]{:S(2)}) collective-permute-start(bf16[2,656,128]{2,1,0:T(8,128)(2,1)} %get-tuple-element.25), channel_id=1, source_target_pairs={{0,128},{8,136},{16,144},{24,152},{32,160},{40,168},{48,176},{56,1... | collective-permute-start | bytes 1007624 | tf_op jit(solution)/shard_map/ppermute | solution.py:32
  119.1 2.2 %collective-permute-done.11.refs_2_ = bf16[2,656,128]{2,1,0:T(8,128)(2,1)S(1)} collective-permute-done((bf16[2,656,128]{2,1,0:T(8,128)(2,1)}, bf16[2,656,128]{2,1,0:T(8,128)(2,1)S(1)}, u32[]{:S(2)}, u32[]{:S(2)}) %collective-permute-start.11) | collective-permute-done | bytes 335904 | tf_op jit(solution)/shard_map/ppermute | solution.py:32
  121.3 7.2 %collective-permute-done.12.refs_3_ = bf16[2,656,128]{2,1,0:T(8,128)(2,1)S(1)} collective-permute-done((bf16[2,656,128]{2,1,0:T(8,128)(2,1)}, bf16[2,656,128]{2,1,0:T(8,128)(2,1)S(1)}, u32[]{:S(2)}, u32[]{:S(2)}) %collective-permute-start.12) | collective-permute-done | bytes 335904 | tf_op jit(solution)/shard_map/ppermute | solution.py:32
  128.5 1.6 collective-permute-start.32
  131.1 7.1 %finish.1 = (bf16[2,128,640]{2,1,0:T(8,128)(2,1)S(1)}, bf16[2,128,640]{2,1,0:T(8,128)(2,1)}, bf16[2,128,640]{2,1,0:T(8,128)(2,1)}, bf16[2,128,640]{2,1,0:T(8,128...) custom-call(s32[32]{0:T(128)S(1)} %fusion.32.pieces, bf16[2,656,128]{2,1,0:T(8,128)(2,1)S(1)} %copy-done.2, ...), custom_call_target="tpu_custom_call" | custom-call | flops 2000000000 | bytes 12000000 | tf_op jit(solution)/shard_map/finish/pallas_call | solution.py:361
  140.3 1.5 collective-permute-start.24
  141.8 1.4 collective-permute-start.25
  143.4 4.1 %collective-permute-start.33 = (bf16[4,128,128]{2,1,0:T(8,128)(2,1)S(1)}, bf16[4,128,128]{2,1,0:T(8,128)(2,1)S(1)}, u32[]{:S(2)}, u32[]{:S(2)}) collective-permute-start(bf16[4,128,128]{2,1,0:T(8,128)(2,1)S(1)} %copy-done.18), channel_id=1, source_target_pairs={{0,128},{8,136},{16,144},{24,152},{32,160},{40,168},{48,176},{56,1... | collective-permute-start | bytes 393224 | tf_op jit(solution)/shard_map/ppermute | solution.py:32
  148.1 2.4 %collective-permute-done.33.refs_3_ = bf16[4,128,128]{2,1,0:T(8,128)(2,1)S(1)} collective-permute-done((bf16[4,128,128]{2,1,0:T(8,128)(2,1)S(1)}, bf16[4,128,128]{2,1,0:T(8,128)(2,1)S(1)}, u32[]{:S(2)}, u32[]{:S(2)}) %collective-permute-start.33) | collective-permute-done | bytes 131104 | tf_op jit(solution)/shard_map/ppermute | solution.py:32
  151.1 2.9 %refill.1 = (bf16[6,128,128]{2,1,0:T(8,128)(2,1)}, bf16[6,128,128]{2,1,0:T(8,128)(2,1)}) custom-call(s32[2]{0:T(128)} %compare_select_fusion.25.source, bf16[6,128,128]{2,1,0:T(8,128)(2,1)} %bitcast.40, bf16[6,128,128]{2,1,0:T(8,128)(2,1)} %bitcast.42, bf16[4,128,128]{2,1,0:T(8,128)(2,1)} %get-tuple-element.35.refs_0_, bf16[4,128,128]{2,1,0:T(8,128)(2,1)} %copy-done.5, ...), custom_call_target="tpu_custom_call" | custom-call | tf_op jit(solution)/shard_map/refill/pallas_call | solution.py:418
  154.0 1.5 collective-permute-done.24
  156.8 5.4 %collective-permute-done.27 = bf16[4,128,640]{2,1,0:T(8,128)(2,1)S(1)} collective-permute-done((bf16[4,128,640]{2,1,0:T(8,128)(2,1)}, bf16[4,128,640]{2,1,0:T(8,128)(2,1)S(1)}, u32[]{:S(2)}, u32[]{:S(2)}) %collective-permute-start.27) | collective-permute-done | bytes 655392 | tf_op jit(solution)/shard_map/ppermute | solution.py:40
  162.5 2.2 %collective-permute-start.28 = (bf16[128,640]{1,0:T(8,128)(2,1)S(1)}, bf16[128,640]{1,0:T(8,128)(2,1)S(1)}, u32[]{:S(2)}, u32[]{:S(2)}) collective-permute-start(bf16[128,640]{1,0:T(8,128)(2,1)S(1)} %get-tuple-element.69), channel_id=1, source_target_pairs={{0,2},{1,3},{2,4},{3,5},{4,6},{5,7},{6,0},{7,1},{8,10},{9,11},{10,... | collective-permute-start | bytes 491528 | tf_op jit(solution)/shard_map/ppermute | solution.py:40
  166.1 3.1 %collective-permute-done.28 = bf16[128,640]{1,0:T(8,128)(2,1)S(1)} collective-permute-done((bf16[128,640]{1,0:T(8,128)(2,1)S(1)}, bf16[128,640]{1,0:T(8,128)(2,1)S(1)}, u32[]{:S(2)}, u32[]{:S(2)}) %collective-permute-start.28) | collective-permute-done | bytes 163872 | tf_op jit(solution)/shard_map/ppermute | solution.py:40
  169.3 2.3 %collective-permute-done.30 = bf16[128,640]{1,0:T(8,128)(2,1)S(1)} collective-permute-done((bf16[128,640]{1,0:T(8,128)(2,1)S(1)}, bf16[128,640]{1,0:T(8,128)(2,1)S(1)}, u32[]{:S(2)}, u32[]{:S(2)}) %collective-permute-start.30) | collective-permute-done | bytes 163872 | tf_op jit(solution)/shard_map/ppermute | solution.py:40
  171.6 1.7 collective-permute-done.29
  (157 shorter events, 26.1 us)
Async XLA Ops:
  0.7 26.5 %collective-permute-start.13 = (bf16[160,640]{1,0:T(8,128)(2,1)}, bf16[160,640]{1,0:T(8,128)(2,1)S(1)}, u32[]{:S(2)}, u32[]{:S(2)}) collective-permute-start(bf16[160,640]{1,0:T(8,128)(2,1)} %param.17), channel_id=1, source_target_pairs={{0,16},{8,24},{16,32},{24,40},{32,48},{40,56},{48,0},{56,8},{64,80... | collective-permute-start | bytes 614408 | tf_op jit(solution)/shard_map/ppermute | solution.py:32
  4.0 24.4 %collective-permute-start.15 = (bf16[160,640]{1,0:T(8,128)(2,1)}, bf16[160,640]{1,0:T(8,128)(2,1)S(1)}, u32[]{:S(2)}, u32[]{:S(2)}) collective-permute-start(bf16[160,640]{1,0:T(8,128)(2,1)} %param.17), channel_id=1, source_target_pairs={{0,32},{8,40},{16,48},{24,56},{32,0},{40,8},{48,16},{56,24},{64,96... | collective-permute-start | bytes 614408 | tf_op jit(solution)/shard_map/ppermute | solution.py:32
  9.4 44.1 %collective-permute-start.14 = (bf16[160,640]{1,0:T(8,128)(2,1)}, bf16[160,640]{1,0:T(8,128)(2,1)S(1)}, u32[]{:S(2)}, u32[]{:S(2)}) collective-permute-start(bf16[160,640]{1,0:T(8,128)(2,1)} %param.17), channel_id=1, source_target_pairs={{0,48},{8,56},{16,0},{24,8},{32,16},{40,24},{48,32},{56,40},{64,11... | collective-permute-start | bytes 614408 | tf_op jit(solution)/shard_map/ppermute | solution.py:32
  12.1 43.5 %collective-permute-start.9 = (bf16[5,256,128]{2,1,0:T(8,128)(2,1)}, bf16[5,256,128]{2,1,0:T(8,128)(2,1)S(1)}, u32[]{:S(2)}, u32[]{:S(2)}) collective-permute-start(bf16[5,256,128]{2,1,0:T(8,128)(2,1)} %bitcast.49), channel_id=1, source_target_pairs={{0,128},{8,136},{16,144},{24,152},{32,160},{40,168},{48,176},{56,1... | collective-permute-start | bytes 983048 | tf_op jit(solution)/shard_map/ppermute | solution.py:32
  17.1 38.5 %collective-permute-start.5 = (bf16[12,128,128]{2,1,0:T(8,128)(2,1)}, bf16[12,128,128]{2,1,0:T(8,128)(2,1)}, u32[]{:S(2)}, u32[]{:S(2)}) collective-permute-start(bf16[12,128,128]{2,1,0:T(8,128)(2,1)} %pack.1.refs_0_), channel_id=1, source_target_pairs={{0,32},{8,40},{16,48},{24,56},{32,0},{40,8},{48,16},{56,24},{64,96... | collective-permute-start | bytes 1179656 | tf_op jit(solution)/shard_map/ppermute | solution.py:32
  27.2 29.0 %collective-permute-start.8 = (bf16[5,256,128]{2,1,0:T(8,128)(2,1)S(1)}, bf16[5,256,128]{2,1,0:T(8,128)(2,1)S(1)}, u32[]{:S(2)}, u32[]{:S(2)}) collective-permute-start(bf16[5,256,128]{2,1,0:T(8,128)(2,1)S(1)} %bitcast.51), channel_id=1, source_target_pairs={{0,192},{8,200},{16,208},{24,216},{32,224},{40,232},{48,240},{56,2... | collective-permute-start | bytes 983048 | tf_op jit(solution)/shard_map/ppermute | solution.py:32
  28.4 40.8 %collective-permute-start.3 = (bf16[12,128,128]{2,1,0:T(8,128)(2,1)}, bf16[12,128,128]{2,1,0:T(8,128)(2,1)}, u32[]{:S(2)}, u32[]{:S(2)}) collective-permute-start(bf16[12,128,128]{2,1,0:T(8,128)(2,1)} %pack.1.refs_0_), channel_id=1, source_target_pairs={{0,48},{8,56},{16,0},{24,8},{32,16},{40,24},{48,32},{56,40},{64,11... | collective-permute-start | bytes 1179656 | tf_op jit(solution)/shard_map/ppermute | solution.py:32
  53.5 16.7 %collective-permute-start.1 = (bf16[12,128,128]{2,1,0:T(8,128)(2,1)}, bf16[12,128,128]{2,1,0:T(8,128)(2,1)}, u32[]{:S(2)}, u32[]{:S(2)}) collective-permute-start(bf16[12,128,128]{2,1,0:T(8,128)(2,1)} %pack.1.refs_0_), channel_id=1, source_target_pairs={{0,16},{8,24},{16,32},{24,40},{32,48},{40,56},{48,0},{56,8},{64,80... | collective-permute-start | bytes 1179656 | tf_op jit(solution)/shard_map/ppermute | solution.py:32
  55.6 15.6 %collective-permute-start = (bf16[12,128,128]{2,1,0:T(8,128)(2,1)}, bf16[12,128,128]{2,1,0:T(8,128)(2,1)S(1)}, u32[]{:S(2)}, u32[]{:S(2)}) collective-permute-start(bf16[12,128,128]{2,1,0:T(8,128)(2,1)} %pack.1.refs_0_), channel_id=1, source_target_pairs={{0,8},{8,0},{16,24},{24,16},{32,40},{40,32},{48,56},{56,48},{64,72... | collective-permute-start | bytes 1179656 | tf_op jit(solution)/shard_map/ppermute | solution.py:32
  55.6 15.6 %collective-permute-start.6 = (bf16[12,128,128]{2,1,0:T(8,128)(2,1)}, bf16[12,128,128]{2,1,0:T(8,128)(2,1)S(1)}, u32[]{:S(2)}, u32[]{:S(2)}) collective-permute-start(bf16[12,128,128]{2,1,0:T(8,128)(2,1)} %collective-permute-done.5.refs_6_), channel_id=1, source_target_pairs={{0,8},{8,0},{16,24},{24,16},{32,40},{40,32},{48,56},{56,48},{64,72... | collective-permute-start | bytes 1179656 | tf_op jit(solution)/shard_map/ppermute | solution.py:32
  56.2 11.1 %collective-permute-start.7 = (bf16[5,256,128]{2,1,0:T(8,128)(2,1)S(1)}, bf16[5,256,128]{2,1,0:T(8,128)(2,1)S(1)}, u32[]{:S(2)}, u32[]{:S(2)}) collective-permute-start(bf16[5,256,128]{2,1,0:T(8,128)(2,1)S(1)} %bitcast.52), channel_id=1, source_target_pairs={{0,64},{8,72},{16,80},{24,88},{32,96},{40,104},{48,112},{56,120},{... | collective-permute-start | bytes 983048 | tf_op jit(solution)/shard_map/ppermute | solution.py:32
  67.2 24.2 %collective-permute-start.19 = (bf16[4,160,640]{2,1,0:T(8,128)(2,1)S(1)}, bf16[4,160,640]{2,1,0:T(8,128)(2,1)S(1)}, u32[]{:S(2)}, u32[]{:S(2)}) collective-permute-start(bf16[4,160,640]{2,1,0:T(8,128)(2,1)S(1)} %pad_maximum_fusion.refs_4_), channel_id=1, source_target_pairs={{0,128},{8,136},{16,144},{24,152},{32,160},{40,168},{48,176},{56,1... | collective-permute-start | bytes 2457608 | tf_op jit(solution)/shard_map/ppermute | solution.py:32
  69.2 35.8 %collective-permute-start.18 = (bf16[4,160,640]{2,1,0:T(8,128)(2,1)S(1)}, bf16[4,160,640]{2,1,0:T(8,128)(2,1)S(1)}, u32[]{:S(2)}, u32[]{:S(2)}) collective-permute-start(bf16[4,160,640]{2,1,0:T(8,128)(2,1)S(1)} %pad_maximum_fusion.refs_4_), channel_id=1, source_target_pairs={{0,192},{8,200},{16,208},{24,216},{32,224},{40,232},{48,240},{56,2... | collective-permute-start | bytes 2457608 | tf_op jit(solution)/shard_map/ppermute | solution.py:32
  70.2 35.7 %collective-permute-start.17 = (bf16[4,160,640]{2,1,0:T(8,128)(2,1)S(1)}, bf16[4,160,640]{2,1,0:T(8,128)(2,1)S(1)}, u32[]{:S(2)}, u32[]{:S(2)}) collective-permute-start(bf16[4,160,640]{2,1,0:T(8,128)(2,1)S(1)} %pad_maximum_fusion.refs_4_), channel_id=1, source_target_pairs={{0,64},{8,72},{16,80},{24,88},{32,96},{40,104},{48,112},{56,120},{... | collective-permute-start | bytes 2457608 | tf_op jit(solution)/shard_map/ppermute | solution.py:32
  73.9 35.9 %collective-permute-start.16 = (bf16[4,160,640]{2,1,0:T(8,128)(2,1)S(1)}, bf16[4,160,640]{2,1,0:T(8,128)(2,1)}, u32[]{:S(2)}, u32[]{:S(2)}) collective-permute-start(bf16[4,160,640]{2,1,0:T(8,128)(2,1)S(1)} %pad_maximum_fusion.refs_4_), channel_id=1, source_target_pairs={{0,8},{8,0},{16,24},{24,16},{32,40},{40,32},{48,56},{56,48},{64,72... | collective-permute-start | bytes 2457608 | tf_op jit(solution)/shard_map/ppermute | solution.py:32
  105.9 24.2 %collective-permute-start.20 = (bf16[4,160,640]{2,1,0:T(8,128)(2,1)S(1)}, bf16[4,160,640]{2,1,0:T(8,128)(2,1)}, u32[]{:S(2)}, u32[]{:S(2)}) collective-permute-start(bf16[4,160,640]{2,1,0:T(8,128)(2,1)S(1)} %collective-permute-done.17.refs_6_), channel_id=1, source_target_pairs={{0,8},{8,0},{16,24},{24,16},{32,40},{40,32},{48,56},{56,48},{64,72... | collective-permute-start | bytes 2457608 | tf_op jit(solution)/shard_map/ppermute | solution.py:32
  105.9 24.2 %collective-permute-start.21 = (bf16[4,160,640]{2,1,0:T(8,128)(2,1)S(1)}, bf16[4,160,640]{2,1,0:T(8,128)(2,1)}, u32[]{:S(2)}, u32[]{:S(2)}) collective-permute-start(bf16[4,160,640]{2,1,0:T(8,128)(2,1)S(1)} %collective-permute-done.18.refs_8_), channel_id=1, source_target_pairs={{0,8},{8,0},{16,24},{24,16},{32,40},{40,32},{48,56},{56,48},{64,72... | collective-permute-start | bytes 2457608 | tf_op jit(solution)/shard_map/ppermute | solution.py:32
  106.4 23.7 %collective-permute-start.22 = (bf16[4,160,640]{2,1,0:T(8,128)(2,1)S(1)}, bf16[4,160,640]{2,1,0:T(8,128)(2,1)}, u32[]{:S(2)}, u32[]{:S(2)}) collective-permute-start(bf16[4,160,640]{2,1,0:T(8,128)(2,1)S(1)} %collective-permute-done.19.refs_10_), channel_id=1, source_target_pairs={{0,8},{8,0},{16,24},{24,16},{32,40},{40,32},{48,56},{56,48},{64,72... | collective-permute-start | bytes 2457608 | tf_op jit(solution)/shard_map/ppermute | solution.py:32
  106.6 10.6 %collective-permute-start.10 = (bf16[2,656,128]{2,1,0:T(8,128)(2,1)}, bf16[2,656,128]{2,1,0:T(8,128)(2,1)S(1)}, u32[]{:S(2)}, u32[]{:S(2)}) collective-permute-start(bf16[2,656,128]{2,1,0:T(8,128)(2,1)} %get-tuple-element.23), channel_id=1, source_target_pairs={{0,192},{8,200},{16,208},{24,216},{32,224},{40,232},{48,240},{56,2... | collective-permute-start | bytes 1007624 | tf_op jit(solution)/shard_map/ppermute | solution.py:32
  109.8 11.5 %collective-permute-start.11 = (bf16[2,656,128]{2,1,0:T(8,128)(2,1)}, bf16[2,656,128]{2,1,0:T(8,128)(2,1)S(1)}, u32[]{:S(2)}, u32[]{:S(2)}) collective-permute-start(bf16[2,656,128]{2,1,0:T(8,128)(2,1)} %get-tuple-element.24), channel_id=1, source_target_pairs={{0,64},{8,72},{16,80},{24,88},{32,96},{40,104},{48,112},{56,120},{... | collective-permute-start | bytes 1007624 | tf_op jit(solution)/shard_map/ppermute | solution.py:32
  117.2 11.3 %collective-permute-start.12 = (bf16[2,656,128]{2,1,0:T(8,128)(2,1)}, bf16[2,656,128]{2,1,0:T(8,128)(2,1)S(1)}, u32[]{:S(2)}, u32[]{:S(2)}) collective-permute-start(bf16[2,656,128]{2,1,0:T(8,128)(2,1)} %get-tuple-element.25), channel_id=1, source_target_pairs={{0,128},{8,136},{16,144},{24,152},{32,160},{40,168},{48,176},{56,1... | collective-permute-start | bytes 1007624 | tf_op jit(solution)/shard_map/ppermute | solution.py:32
  121.3 22.1 %collective-permute-start.31 = (bf16[4,128,128]{2,1,0:T(8,128)(2,1)}, bf16[4,128,128]{2,1,0:T(8,128)(2,1)S(1)}, u32[]{:S(2)}, u32[]{:S(2)}) collective-permute-start(bf16[4,128,128]{2,1,0:T(8,128)(2,1)} %get-tuple-element.36), channel_id=1, source_target_pairs={{0,192},{8,200},{16,208},{24,216},{32,224},{40,232},{48,240},{56,2... | collective-permute-start | bytes 393224 | tf_op jit(solution)/shard_map/ppermute | solution.py:32
  128.5 19.0 %collective-permute-start.32 = (bf16[4,128,128]{2,1,0:T(8,128)(2,1)}, bf16[4,128,128]{2,1,0:T(8,128)(2,1)S(1)}, u32[]{:S(2)}, u32[]{:S(2)}) collective-permute-start(bf16[4,128,128]{2,1,0:T(8,128)(2,1)} %get-tuple-element.37), channel_id=1, source_target_pairs={{0,64},{8,72},{16,80},{24,88},{32,96},{40,104},{48,112},{56,120},{... | collective-permute-start | bytes 393224 | tf_op jit(solution)/shard_map/ppermute | solution.py:32
  139.8 14.2 %collective-permute-start.23 = (bf16[2,128,640]{2,1,0:T(8,128)(2,1)}, bf16[2,128,640]{2,1,0:T(8,128)(2,1)S(1)}, u32[]{:S(2)}, u32[]{:S(2)}) collective-permute-start(bf16[2,128,640]{2,1,0:T(8,128)(2,1)} %get-tuple-element.30), channel_id=1, source_target_pairs={{0,2},{1,3},{2,4},{3,5},{4,6},{5,7},{6,0},{7,1},{8,10},{9,11},{10,... | collective-permute-start | bytes 983048 | tf_op jit(solution)/shard_map/ppermute | solution.py:40
  140.3 15.3 %collective-permute-start.24 = (bf16[2,128,640]{2,1,0:T(8,128)(2,1)}, bf16[2,128,640]{2,1,0:T(8,128)(2,1)S(1)}, u32[]{:S(2)}, u32[]{:S(2)}) collective-permute-start(bf16[2,128,640]{2,1,0:T(8,128)(2,1)} %get-tuple-element.31), channel_id=1, source_target_pairs={{0,6},{1,7},{2,0},{3,1},{4,2},{5,3},{6,4},{7,5},{8,14},{9,15},{10,... | collective-permute-start | bytes 983048 | tf_op jit(solution)/shard_map/ppermute | solution.py:40
  141.8 13.7 %collective-permute-start.25 = (bf16[2,128,640]{2,1,0:T(8,128)(2,1)}, bf16[2,128,640]{2,1,0:T(8,128)(2,1)S(1)}, u32[]{:S(2)}, u32[]{:S(2)}) collective-permute-start(bf16[2,128,640]{2,1,0:T(8,128)(2,1)} %get-tuple-element.32), channel_id=1, source_target_pairs={{0,4},{1,5},{2,6},{3,7},{4,0},{5,1},{6,2},{7,3},{8,12},{9,13},{10,... | collective-permute-start | bytes 983048 | tf_op jit(solution)/shard_map/ppermute | solution.py:40
  143.4 7.0 %collective-permute-start.33 = (bf16[4,128,128]{2,1,0:T(8,128)(2,1)S(1)}, bf16[4,128,128]{2,1,0:T(8,128)(2,1)S(1)}, u32[]{:S(2)}, u32[]{:S(2)}) collective-permute-start(bf16[4,128,128]{2,1,0:T(8,128)(2,1)S(1)} %copy-done.18), channel_id=1, source_target_pairs={{0,128},{8,136},{16,144},{24,152},{32,160},{40,168},{48,176},{56,1... | collective-permute-start | bytes 393224 | tf_op jit(solution)/shard_map/ppermute | solution.py:32
  147.5 14.7 %collective-permute-start.27 = (bf16[4,128,640]{2,1,0:T(8,128)(2,1)}, bf16[4,128,640]{2,1,0:T(8,128)(2,1)S(1)}, u32[]{:S(2)}, u32[]{:S(2)}) collective-permute-start(bf16[4,128,640]{2,1,0:T(8,128)(2,1)} %get-tuple-element.34), channel_id=1, source_target_pairs={{0,1},{1,0},{2,3},{3,2},{4,5},{5,4},{6,7},{7,6},{8,9},{9,8},{10,11... | collective-permute-start | bytes 1966088 | tf_op jit(solution)/shard_map/ppermute | solution.py:40
  156.7 9.4 %collective-permute-start.26 = (bf16[128,640]{1,0:T(8,128)(2,1)S(1)}, bf16[128,640]{1,0:T(8,128)(2,1)S(1)}, u32[]{:S(2)}, u32[]{:S(2)}) collective-permute-start(bf16[128,640]{1,0:T(8,128)(2,1)S(1)} %fusion.7), channel_id=1, source_target_pairs={{0,1},{1,0},{2,3},{3,2},{4,5},{5,4},{6,7},{7,6},{8,9},{9,8},{10,11... | collective-permute-start | bytes 491528 | tf_op jit(solution)/shard_map/ppermute | solution.py:40
  162.5 6.8 %collective-permute-start.28 = (bf16[128,640]{1,0:T(8,128)(2,1)S(1)}, bf16[128,640]{1,0:T(8,128)(2,1)S(1)}, u32[]{:S(2)}, u32[]{:S(2)}) collective-permute-start(bf16[128,640]{1,0:T(8,128)(2,1)S(1)} %get-tuple-element.69), channel_id=1, source_target_pairs={{0,2},{1,3},{2,4},{3,5},{4,6},{5,7},{6,0},{7,1},{8,10},{9,11},{10,... | collective-permute-start | bytes 491528 | tf_op jit(solution)/shard_map/ppermute | solution.py:40
  164.6 6.9 %collective-permute-start.30 = (bf16[128,640]{1,0:T(8,128)(2,1)S(1)}, bf16[128,640]{1,0:T(8,128)(2,1)S(1)}, u32[]{:S(2)}, u32[]{:S(2)}) collective-permute-start(bf16[128,640]{1,0:T(8,128)(2,1)S(1)} %get-tuple-element.70), channel_id=1, source_target_pairs={{0,4},{1,5},{2,6},{3,7},{4,0},{5,1},{6,2},{7,3},{8,12},{9,13},{10,... | collective-permute-start | bytes 491528 | tf_op jit(solution)/shard_map/ppermute | solution.py:40
  165.8 7.5 %collective-permute-start.29 = (bf16[128,640]{1,0:T(8,128)(2,1)S(1)}, bf16[128,640]{1,0:T(8,128)(2,1)S(1)}, u32[]{:S(2)}, u32[]{:S(2)}) collective-permute-start(bf16[128,640]{1,0:T(8,128)(2,1)S(1)} %get-tuple-element.71), channel_id=1, source_target_pairs={{0,6},{1,7},{2,0},{3,1},{4,2},{5,3},{6,4},{7,5},{8,14},{9,15},{10,... | collective-permute-start | bytes 491528 | tf_op jit(solution)/shard_map/ppermute | solution.py:40
  (22 other events, 337.6 us)

commit v3 on v2

--- a/solution.py
+++ b/solution.py
@@ -30,6 +30,14 @@
 
 def shift(value, dy=0, dz=0, dc=0):
     return lax.ppermute(value, "blk", blk_perm(dy, dz, dc))
+
+
+def after(value, *earlier):
+    return lax.optimization_barrier((value, *earlier))[0]
+
+
+def in_hbm(value):
+    return pltpu.with_memory_space_constraint(value, pltpu.HBM)
 
 
 def head_shift(value, dx=0, dz=0):
@@ -116,6 +124,7 @@
     kv, queries, scores, high, total, result, in_sem, out_sem, move_sem = refs[nkv + 3 * nq :]
     slots = kv_in[0].shape[0]
     half = slots // 2
+    begins = [sum(ref.shape[0] for ref in kv_in[:a]) for a in range(nkv)]
     heads, rows, width = q_in[0].shape
     size = kv_in[0].shape[1]
     per = rows // size
@@ -124,7 +133,9 @@
     loads = []
     for a in range(nkv):
         loads.append(
-            pltpu.make_async_copy(kv_in[a], kv.at[pl.ds(a * slots, slots)], in_sem.at[a])
+            pltpu.make_async_copy(
+                kv_in[a], kv.at[pl.ds(begins[a], kv_in[a].shape[0])], in_sem.at[a]
+            )
         )
     for r in range(nq):
         loads.append(pltpu.make_async_copy(q_in[r], queries.at[r], in_sem.at[nkv + r]))
@@ -251,7 +262,7 @@
 
 
 def attend(meta, kv_parts, q_parts, log_scale):
-    slots, size, width = kv_parts[0].shape
+    _, size, width = kv_parts[0].shape
     heads, rows, _ = q_parts[0].shape
     nkv, nq, per = len(kv_parts), len(q_parts), rows // size
     wide = heads * size
@@ -266,7 +277,7 @@
         in_specs=[smem] * len(meta) + [anywhere] * (nkv + nq),
         out_specs=(anywhere,) * (2 * nq),
         scratch_shapes=[
-            pltpu.VMEM((nkv * slots, size, width), jnp.bfloat16),
+            pltpu.VMEM((sum(p.shape[0] for p in kv_parts), size, width), jnp.bfloat16),
             pltpu.VMEM((nq, heads, rows, width), jnp.bfloat16),
             pltpu.VMEM((longest // 2, wide, 2 * size), jnp.float32),
             pltpu.VMEM((wide, size), jnp.float32),
@@ -525,28 +536,40 @@
     cv = cache_values.reshape(slots, size, width)
     own_q = jnp.transpose(queries, (1, 0, 2))
     w_line = [out_weight] + [shift(out_weight, dz=k) for k in SHIFTS[1:]]
+    q_near = [shift(own_q, dy=k) for k in SHIFTS[1:3]]
     own_kv = pack(
         ck, cv, new_keys.reshape(per, size, width), new_values.reshape(per, size, width)
     )
-    lines = [own_kv] + [shift(own_kv, dz=k) for k in SHIFTS[1:]]
-    q_parts = [own_q] + [shift(own_q, dy=k) for k in SHIFTS[1:]]
+    own_kv = after(own_kv, *w_line[1:], *q_near)
+    kv_near = [shift(own_kv, dz=k) for k in SHIFTS[1:3]]
+    q_parts = [own_q, *q_near, shift(after(own_q, *q_near), dy=SHIFTS[3])]
+    w_four = jnp.stack(w_line)
+    w_near = [shift(w_four, dy=k) for k in SHIFTS[1:3]]
+    far = [
+        shift(kv_near[0][:slots], dz=SHIFTS[1]),
+        shift(kv_near[1][slots:], dz=SHIFTS[2]),
+    ]
+    w_far = [*w_near, shift(after(w_four, *w_near), dy=SHIFTS[3])]
     kv_parts = []
-    for part in lines:
+    for part in (own_kv, *kv_near):
         kv_parts += [part, shift(part, dc=1)]
-    w_four = jnp.stack(w_line)
-    w_far = [shift(w_four, dy=k) for k in SHIFTS[1:]]
-    w_parts = [w_four, shift(w_four, dc=1)]
+    kv_parts += far + [shift(part, dc=1) for part in far]
+    w_parts = []
+    for part in (w_four, *w_near):
+        w_parts += [part, shift(part, dc=1)]
     meta, source = plan(device, per, slots, size, cache_len, span_len, block_table, window)
     outs = attend(meta, kv_parts, q_parts, log_scale)
     parts, moved = outs[: len(SHIFTS)], outs[len(SHIFTS) :]
-    for part in lax.optimization_barrier((*w_far, parts[0]))[:-1]:
-        w_parts += [part, shift(part, dc=1)]
     parts = [parts[0]] + [shift(p, dy=-k) for p, k in zip(parts[1:], SHIFTS[1:])]
-    moved = [moved[0]] + [shift(p, dy=-k) for p, k in zip(moved[1:], SHIFTS[1:])]
+    w_far[2] = after(w_far[2], *parts[1:])
+    w_parts += [w_far[2], shift(w_far[2], dc=1)]
     pieces = piece_table(device, head, heads * width // out_weight.shape[0])
-    shares = finish(pieces, parts, w_parts, heads)
+    shares = finish(pieces, [in_hbm(p) for p in parts], w_parts, heads)
     first, second = shares[:NX], shares[NX:]
     first = [first[0]] + [head_shift(p, dx=k) for p, k in zip(first[1:], SHIFTS[1:])]
+    moved = [moved[0]] + [
+        shift(after(p, first[1]), dy=-k) for p, k in zip(moved[1:], SHIFTS[1:])
+    ]
     second_sum = second[0].astype(jnp.float32) + head_shift(second[1], dz=1).astype(jnp.float32)
     first_sum = functools.reduce(jnp.add, [p.astype(jnp.float32) for p in first])
     second_out = second_sum[0]

time: 174 us -> 157 us (0.902); the launches traced: 174 us -> 155 us
  waiting for transfers between devices: 67.1 us -> 48.9 us
  Pallas kernels: 29 us -> 31.3 us
    ppermute x26 -> x28, waiting for transfers between devices: 53.1 us -> 30.2 us  [shift(): return lax.ppermute(value, 'blk', blk_perm(dy, dz, dc))]
    ppermute x8, waiting for transfers between devices: 14 us -> 18.7 us  [head_shift(): return lax.ppermute(value, 'head', pairs)]
    unnamed x40 -> x46, local copies, waits for them, and re-layouts: 3.55 us -> 2.33 us
    ppermute x26 -> x28, starting transfers between devices: 50.5 us -> 50.6 us  [shift(): return lax.ppermute(value, 'blk', blk_perm(dy, dz, dc))]
  transfers between devices with their start and end apart: 34 -> 36, of which waited for: 13 -> 11; matrix products, arithmetic and copies ran while one was open for 8% -> 9% of each run, Pallas kernels for 17% -> 15%
where the time goes in v3:
time: 157 us; the launch traced here: 155 us
  starting transfers between devices  56.3 us (36%)
  waiting for transfers between devices  48.9 us (31%)
  Pallas kernels  31.3 us (20%)
  other arithmetic  13.3 us (8%)
  local copies, waits for them, and re-layouts  3.7 us (2%)
    ppermute x28, starting transfers between devices, shift(): return lax.ppermute(value, 'blk', blk_perm(dy, dz, dc))  50.6 us
    ppermute x28, waiting for transfers between devices, shift(): return lax.ppermute(value, 'blk', blk_perm(dy, dz, dc))  30.2 us
    pallas_call x1, Pallas kernels, attend(): pl.pallas_call(functools.partial(attend_kernel, log_scale, nkv, nq), out_...  18.8 us
    ppermute x8, waiting for transfers between devices, head_shift(): return lax.ppermute(value, 'head', pairs)  18.7 us
    pallas_call x1, Pallas kernels, finish(): pl.pallas_call(functools.partial(finish_kernel, heads, nparts, nw), out_s...  7.8 us
    ppermute x8, starting transfers between devices, head_shift(): return lax.ppermute(value, 'head', pairs)  5.71 us
    reduce_sum x2, other arithmetic, table_entry(): return jnp.sum(jnp.where(match, block_table[None], 0), axis=(1, 2))  3.89 us
  transfers between devices with their start and end apart: 36, of which 11 were waited for; matrix products, arithmetic and copies ran while one was open for 9% of the time, Pallas kernels for 15%

profile of v3, /device:TPU:6, one launch (start us, length us, event | category | flops | bytes accessed | tf_op | source)
XLA Modules:
  0.0 154.7 jit_solution(5110256421571913975)
XLA Ops:
  0.6 6.4 %collective-permute-start.1 = (bf16[160,640]{1,0:T(8,128)(2,1)}, bf16[160,640]{1,0:T(8,128)(2,1)S(1)}, u32[]{:S(2)}, u32[]{:S(2)}) collective-permute-start(bf16[160,640]{1,0:T(8,128)(2,1)} %param.17), channel_id=1, source_target_pairs={{0,48},{8,56},{16,0},{24,8},{32,16},{40,24},{48,32},{56,40},{64,11... | collective-permute-start | bytes 614408 | tf_op jit(solution)/shard_map/ppermute | solution.py:32
  7.0 3.8 %collective-permute-start.2 = (bf16[160,640]{1,0:T(8,128)(2,1)}, bf16[160,640]{1,0:T(8,128)(2,1)S(1)}, u32[]{:S(2)}, u32[]{:S(2)}) collective-permute-start(bf16[160,640]{1,0:T(8,128)(2,1)} %param.17), channel_id=1, source_target_pairs={{0,32},{8,40},{16,48},{24,56},{32,0},{40,8},{48,16},{56,24},{64,96... | collective-permute-start | bytes 614408 | tf_op jit(solution)/shard_map/ppermute | solution.py:32
  10.8 3.0 %collective-permute-start.4 = (bf16[5,256,128]{2,1,0:T(8,128)(2,1)}, bf16[5,256,128]{2,1,0:T(8,128)(2,1)S(1)}, u32[]{:S(2)}, u32[]{:S(2)}) collective-permute-start(bf16[5,256,128]{2,1,0:T(8,128)(2,1)} %bitcast.4.refs_10_), channel_id=1, source_target_pairs={{0,192},{8,200},{16,208},{24,216},{32,224},{40,232},{48,240},{56,2... | collective-permute-start | bytes 983048 | tf_op jit(solution)/shard_map/ppermute | solution.py:32
  17.2 2.6 %select_reduce_fusion.1 = (s32[48]{0:T(128)S(1)}, s32[48]{0:T(128)S(1)}) fusion(s32[8,64]{1,0:T(8,128)} %param.20, pred[48,64]{1,0:T(8,128)(4,1)S(1)} %iota_compare_fusion.2, pred[48,8]{1,0:T(8,128)(4,1)S(1)} %copy.19, s32[8,64]{1,0:T(8,128)S(1)} %add_add_fusion, pred[8,64]{1,0:T(8,128)(4,1)S(1)} %iota_compare_fusion.8, s32[48]{0:T(128)S(1)} %add.594), kind=kLoop, calls=%fused_computation.14 | loop fusion | flops 171936 | bytes 8640 | tf_op jit(solution)/shard_map/reduce_sum | solution.py:75
  23.0 1.8 %pack.1.refs_0_ = bf16[12,128,128]{2,1,0:T(8,128)(2,1)} custom-call(bf16[6,128,128]{2,1,0:T(8,128)(2,1)} %bitcast.39, bf16[6,128,128]{2,1,0:T(8,128)(2,1)} %bitcast.41, bf16[2,128,128]{2,1,0:T(8,128)(2,1)} %bitcast.47, bf16[2,128,128]{2,1,0:T(8,128)(2,1)} %bitcast.48), custom_call_target="tpu_custom_call" | custom-call | tf_op jit(solution)/shard_map/pack/pallas_call | solution.py:100
  25.7 3.3 %collective-permute-start.21 = (bf16[4,160,640]{2,1,0:T(8,128)(2,1)S(1)}, bf16[4,160,640]{2,1,0:T(8,128)(2,1)S(1)}, u32[]{:S(2)}, u32[]{:S(2)}) collective-permute-start(bf16[4,160,640]{2,1,0:T(8,128)(2,1)S(1)} %pad_maximum_fusion.refs_4_), channel_id=1, source_target_pairs={{0,192},{8,200},{16,208},{24,216},{32,224},{40,232},{48,240},{56,2... | collective-permute-start | bytes 2457608 | tf_op jit(solution)/shard_map/ppermute | solution.py:32
  29.0 4.7 %collective-permute-start.8 = (bf16[12,128,128]{2,1,0:T(8,128)(2,1)S(1)}, bf16[12,128,128]{2,1,0:T(8,128)(2,1)S(1)}, u32[]{:S(2)}, u32[]{:S(2)}) collective-permute-start(bf16[12,128,128]{2,1,0:T(8,128)(2,1)S(1)} %copy-done.2), channel_id=1, source_target_pairs={{0,48},{8,56},{16,0},{24,8},{32,16},{40,24},{48,32},{56,40},{64,11... | collective-permute-start | bytes 1179656 | tf_op jit(solution)/shard_map/ppermute | solution.py:32
  34.3 2.3 %collective-permute-start.14 = (bf16[5,256,128]{2,1,0:T(8,128)(2,1)}, bf16[5,256,128]{2,1,0:T(8,128)(2,1)S(1)}, u32[]{:S(2)}, u32[]{:S(2)}) collective-permute-start(bf16[5,256,128]{2,1,0:T(8,128)(2,1)} %bitcast.4.refs_10_), channel_id=1, source_target_pairs={{0,128},{8,136},{16,144},{24,152},{32,160},{40,168},{48,176},{56,1... | collective-permute-start | bytes 983048 | tf_op jit(solution)/shard_map/ppermute | solution.py:32
  36.7 15.6 %collective-permute-done.8.refs_4_ = bf16[12,128,128]{2,1,0:T(8,128)(2,1)S(1)} collective-permute-done((bf16[12,128,128]{2,1,0:T(8,128)(2,1)S(1)}, bf16[12,128,128]{2,1,0:T(8,128)(2,1)S(1)}, u32[]{:S(2)}, u32[]{:S(2)}) %collective-permute-start.8) | collective-permute-done | bytes 393248 | tf_op jit(solution)/shard_map/ppermute | solution.py:32
  52.3 1.7 %collective-permute-start.11 = (bf16[6,128,128]{2,1,0:T(8,128)(2,1)S(1)}, bf16[6,128,128]{2,1,0:T(8,128)(2,1)S(1)}, u32[]{:S(2)}, u32[]{:S(2)}) collective-permute-start(bf16[6,128,128]{2,1,0:T(8,128)(2,1)S(1)} %slice.37), channel_id=1, source_target_pairs={{0,48},{8,56},{16,0},{24,8},{32,16},{40,24},{48,32},{56,40},{64,11... | collective-permute-start | bytes 589832 | tf_op jit(solution)/shard_map/ppermute | solution.py:32
  54.0 1.4 collective-permute-start.10
  56.2 4.1 %collective-permute-done.11.refs_7_ = bf16[6,128,128]{2,1,0:T(8,128)(2,1)S(1)} collective-permute-done((bf16[6,128,128]{2,1,0:T(8,128)(2,1)S(1)}, bf16[6,128,128]{2,1,0:T(8,128)(2,1)S(1)}, u32[]{:S(2)}, u32[]{:S(2)}) %collective-permute-start.11) | collective-permute-done | bytes 196640 | tf_op jit(solution)/shard_map/ppermute | solution.py:32
  60.3 2.4 %collective-permute-done.10.refs_6_ = bf16[6,128,128]{2,1,0:T(8,128)(2,1)} collective-permute-done((bf16[6,128,128]{2,1,0:T(8,128)(2,1)S(1)}, bf16[6,128,128]{2,1,0:T(8,128)(2,1)}, u32[]{:S(2)}, u32[]{:S(2)}) %collective-permute-start.10) | collective-permute-done | bytes 196640 | tf_op jit(solution)/shard_map/ppermute | solution.py:32
  64.2 1.9 %collective-permute-start.23 = (bf16[4,160,640]{2,1,0:T(8,128)(2,1)S(1)}, bf16[4,160,640]{2,1,0:T(8,128)(2,1)S(1)}, u32[]{:S(2)}, u32[]{:S(2)}) collective-permute-start(bf16[4,160,640]{2,1,0:T(8,128)(2,1)S(1)} %pad_maximum_fusion.refs_4_), channel_id=1, source_target_pairs={{0,128},{8,136},{16,144},{24,152},{32,160},{40,168},{48,176},{56,1... | collective-permute-start | bytes 2457608 | tf_op jit(solution)/shard_map/ppermute | solution.py:32
  66.3 18.8 %attend.1 = (bf16[2,656,128]{2,1,0:T(8,128)(2,1)}, bf16[2,656,128]{2,1,0:T(8,128)(2,1)}, bf16[2,656,128]{2,1,0:T(8,128)(2,1)}, bf16[2,656,128]{2,1,0:T(8,128)(2,...) custom-call(s32[8]{0:T(128)} %copy-done.15, ...), custom_call_target="tpu_custom_call" | custom-call | flops 5000000000 | bytes 8000000 | tf_op jit(solution)/shard_map/attend/pallas_call | solution.py:274
  85.2 2.0 %collective-permute-start.16 = (bf16[2,656,128]{2,1,0:T(8,128)(2,1)}, bf16[2,656,128]{2,1,0:T(8,128)(2,1)S(1)}, u32[]{:S(2)}, u32[]{:S(2)}) collective-permute-start(bf16[2,656,128]{2,1,0:T(8,128)(2,1)} %get-tuple-element.30), channel_id=1, source_target_pairs={{0,64},{8,72},{16,80},{24,88},{32,96},{40,104},{48,112},{56,120},{... | collective-permute-start | bytes 1007624 | tf_op jit(solution)/shard_map/ppermute | solution.py:32
  87.3 3.4 %collective-permute-start.18 = (bf16[4,160,640]{2,1,0:T(8,128)(2,1)S(1)}, bf16[4,160,640]{2,1,0:T(8,128)(2,1)}, u32[]{:S(2)}, u32[]{:S(2)}) collective-permute-start(bf16[4,160,640]{2,1,0:T(8,128)(2,1)S(1)} %pad_maximum_fusion.refs_4_), channel_id=1, source_target_pairs={{0,8},{8,0},{16,24},{24,16},{32,40},{40,32},{48,56},{56,48},{64,72... | collective-permute-start | bytes 2457608 | tf_op jit(solution)/shard_map/ppermute | solution.py:32
  90.7 2.4 %collective-permute-done.15.refs_1_ = bf16[2,656,128]{2,1,0:T(8,128)(2,1)S(1)} collective-permute-done((bf16[2,656,128]{2,1,0:T(8,128)(2,1)}, bf16[2,656,128]{2,1,0:T(8,128)(2,1)S(1)}, u32[]{:S(2)}, u32[]{:S(2)}) %collective-permute-start.15) | collective-permute-done | bytes 335904 | tf_op jit(solution)/shard_map/ppermute | solution.py:32
  93.1 6.2 %collective-permute-start.22 = (bf16[4,160,640]{2,1,0:T(8,128)(2,1)S(1)}, bf16[4,160,640]{2,1,0:T(8,128)(2,1)}, u32[]{:S(2)}, u32[]{:S(2)}) collective-permute-start(bf16[4,160,640]{2,1,0:T(8,128)(2,1)S(1)} %collective-permute-done.21.refs_8_), channel_id=1, source_target_pairs={{0,8},{8,0},{16,24},{24,16},{32,40},{40,32},{48,56},{56,48},{64,72... | collective-permute-start | bytes 2457608 | tf_op jit(solution)/shard_map/ppermute | solution.py:32
  99.3 5.2 %collective-permute-start.20 = (bf16[4,160,640]{2,1,0:T(8,128)(2,1)S(1)}, bf16[4,160,640]{2,1,0:T(8,128)(2,1)}, u32[]{:S(2)}, u32[]{:S(2)}) collective-permute-start(bf16[4,160,640]{2,1,0:T(8,128)(2,1)S(1)} %collective-permute-done.19.refs_6_), channel_id=1, source_target_pairs={{0,8},{8,0},{16,24},{24,16},{32,40},{40,32},{48,56},{56,48},{64,72... | collective-permute-start | bytes 2457608 | tf_op jit(solution)/shard_map/ppermute | solution.py:32
  107.8 7.8 %finish.1 = (bf16[2,128,640]{2,1,0:T(8,128)(2,1)S(1)}, bf16[2,128,640]{2,1,0:T(8,128)(2,1)S(1)}, bf16[2,128,640]{2,1,0:T(8,128)(2,1)S(1)}, bf16[2,128,640]{2,1,0...) custom-call(s32[32]{0:T(128)S(1)} %fusion.32.pieces, ...), custom_call_target="tpu_custom_call" | custom-call | flops 2000000000 | bytes 12000000 | tf_op jit(solution)/shard_map/finish/pallas_call | solution.py:372
  116.9 1.6 %collective-permute-start.26 = (bf16[2,128,640]{2,1,0:T(8,128)(2,1)S(1)}, bf16[2,128,640]{2,1,0:T(8,128)(2,1)S(1)}, u32[]{:S(2)}, u32[]{:S(2)}) collective-permute-start(bf16[2,128,640]{2,1,0:T(8,128)(2,1)S(1)} %get-tuple-element.36), channel_id=1, source_target_pairs={{0,6},{1,7},{2,0},{3,1},{4,2},{5,3},{6,4},{7,5},{8,14},{9,15},{10,... | collective-permute-start | bytes 983048 | tf_op jit(solution)/shard_map/ppermute | solution.py:48
  118.5 1.4 collective-permute-start.27
  120.7 6.2 %collective-permute-done.25 = bf16[2,128,640]{2,1,0:T(8,128)(2,1)S(1)} collective-permute-done((bf16[2,128,640]{2,1,0:T(8,128)(2,1)S(1)}, bf16[2,128,640]{2,1,0:T(8,128)(2,1)S(1)}, u32[]{:S(2)}, u32[]{:S(2)}) %collective-permute-start.25) | collective-permute-done | bytes 327712 | tf_op jit(solution)/shard_map/ppermute | solution.py:48
  127.5 1.5 collective-permute-start.34
  129.0 5.8 %collective-permute-done.26 = bf16[2,128,640]{2,1,0:T(8,128)(2,1)S(1)} collective-permute-done((bf16[2,128,640]{2,1,0:T(8,128)(2,1)S(1)}, bf16[2,128,640]{2,1,0:T(8,128)(2,1)S(1)}, u32[]{:S(2)}, u32[]{:S(2)}) %collective-permute-start.26) | collective-permute-done | bytes 327712 | tf_op jit(solution)/shard_map/ppermute | solution.py:48
  136.6 4.8 %collective-permute-done.35.refs_3_ = bf16[4,128,128]{2,1,0:T(8,128)(2,1)S(1)} collective-permute-done((bf16[4,128,128]{2,1,0:T(8,128)(2,1)S(1)}, bf16[4,128,128]{2,1,0:T(8,128)(2,1)S(1)}, u32[]{:S(2)}, u32[]{:S(2)}) %collective-permute-start.35) | collective-permute-done | bytes 131104 | tf_op jit(solution)/shard_map/ppermute | solution.py:32
  142.0 2.9 %refill.1 = (bf16[6,128,128]{2,1,0:T(8,128)(2,1)}, bf16[6,128,128]{2,1,0:T(8,128)(2,1)}) custom-call(s32[2]{0:T(128)} %compare_select_fusion.25.source, bf16[6,128,128]{2,1,0:T(8,128)(2,1)} %bitcast.40, bf16[6,128,128]{2,1,0:T(8,128)(2,1)} %bitcast.42, bf16[4,128,128]{2,1,0:T(8,128)(2,1)} %get-tuple-element.40.refs_0_, bf16[4,128,128]{2,1,0:T(8,128)(2,1)} %copy-done.7, ...), custom_call_target="tpu_custom_call" | custom-call | tf_op jit(solution)/shard_map/refill/pallas_call | solution.py:429
  145.3 1.9 %collective-permute-start.31 = (bf16[128,640]{1,0:T(8,128)(2,1)S(1)}, bf16[128,640]{1,0:T(8,128)(2,1)S(1)}, u32[]{:S(2)}, u32[]{:S(2)}) collective-permute-start(bf16[128,640]{1,0:T(8,128)(2,1)S(1)} %get-tuple-element.79), channel_id=1, source_target_pairs={{0,6},{1,7},{2,0},{3,1},{4,2},{5,3},{6,4},{7,5},{8,14},{9,15},{10,... | collective-permute-start | bytes 491528 | tf_op jit(solution)/shard_map/ppermute | solution.py:48
  147.3 3.3 %collective-permute-done.30 = bf16[128,640]{1,0:T(8,128)(2,1)S(1)} collective-permute-done((bf16[128,640]{1,0:T(8,128)(2,1)S(1)}, bf16[128,640]{1,0:T(8,128)(2,1)S(1)}, u32[]{:S(2)}, u32[]{:S(2)}) %collective-permute-start.30) | collective-permute-done | bytes 163872 | tf_op jit(solution)/shard_map/ppermute | solution.py:48
  150.5 1.7 %collective-permute-done.32 = bf16[128,640]{1,0:T(8,128)(2,1)S(1)} collective-permute-done((bf16[128,640]{1,0:T(8,128)(2,1)S(1)}, bf16[128,640]{1,0:T(8,128)(2,1)S(1)}, u32[]{:S(2)}, u32[]{:S(2)}) %collective-permute-start.32) | collective-permute-done | bytes 163872 | tf_op jit(solution)/shard_map/ppermute | solution.py:48
  152.2 1.7 %collective-permute-done.31 = bf16[128,640]{1,0:T(8,128)(2,1)S(1)} collective-permute-done((bf16[128,640]{1,0:T(8,128)(2,1)S(1)}, bf16[128,640]{1,0:T(8,128)(2,1)S(1)}, u32[]{:S(2)}, u32[]{:S(2)}) %collective-permute-start.31) | collective-permute-done | bytes 163872 | tf_op jit(solution)/shard_map/ppermute | solution.py:48
  (169 shorter events, 20.1 us)
Async XLA Ops:
  0.6 24.8 %collective-permute-start.1 = (bf16[160,640]{1,0:T(8,128)(2,1)}, bf16[160,640]{1,0:T(8,128)(2,1)S(1)}, u32[]{:S(2)}, u32[]{:S(2)}) collective-permute-start(bf16[160,640]{1,0:T(8,128)(2,1)} %param.17), channel_id=1, source_target_pairs={{0,48},{8,56},{16,0},{24,8},{32,16},{40,24},{48,32},{56,40},{64,11... | collective-permute-start | bytes 614408 | tf_op jit(solution)/shard_map/ppermute | solution.py:32
  7.0 18.5 %collective-permute-start = (bf16[160,640]{1,0:T(8,128)(2,1)}, bf16[160,640]{1,0:T(8,128)(2,1)S(1)}, u32[]{:S(2)}, u32[]{:S(2)}) collective-permute-start(bf16[160,640]{1,0:T(8,128)(2,1)} %param.17), channel_id=1, source_target_pairs={{0,16},{8,24},{16,32},{24,40},{32,48},{40,56},{48,0},{56,8},{64,80... | collective-permute-start | bytes 614408 | tf_op jit(solution)/shard_map/ppermute | solution.py:32
  7.0 18.5 %collective-permute-start.2 = (bf16[160,640]{1,0:T(8,128)(2,1)}, bf16[160,640]{1,0:T(8,128)(2,1)S(1)}, u32[]{:S(2)}, u32[]{:S(2)}) collective-permute-start(bf16[160,640]{1,0:T(8,128)(2,1)} %param.17), channel_id=1, source_target_pairs={{0,32},{8,40},{16,48},{24,56},{32,0},{40,8},{48,16},{56,24},{64,96... | collective-permute-start | bytes 614408 | tf_op jit(solution)/shard_map/ppermute | solution.py:32
  10.8 18.1 %collective-permute-start.4 = (bf16[5,256,128]{2,1,0:T(8,128)(2,1)}, bf16[5,256,128]{2,1,0:T(8,128)(2,1)S(1)}, u32[]{:S(2)}, u32[]{:S(2)}) collective-permute-start(bf16[5,256,128]{2,1,0:T(8,128)(2,1)} %bitcast.4.refs_10_), channel_id=1, source_target_pairs={{0,192},{8,200},{16,208},{24,216},{32,224},{40,232},{48,240},{56,2... | collective-permute-start | bytes 983048 | tf_op jit(solution)/shard_map/ppermute | solution.py:32
  13.8 15.1 %collective-permute-start.3 = (bf16[5,256,128]{2,1,0:T(8,128)(2,1)}, bf16[5,256,128]{2,1,0:T(8,128)(2,1)}, u32[]{:S(2)}, u32[]{:S(2)}) collective-permute-start(bf16[5,256,128]{2,1,0:T(8,128)(2,1)} %bitcast.4.refs_10_), channel_id=1, source_target_pairs={{0,64},{8,72},{16,80},{24,88},{32,96},{40,104},{48,112},{56,120},{... | collective-permute-start | bytes 983048 | tf_op jit(solution)/shard_map/ppermute | solution.py:32
  25.7 37.1 %collective-permute-start.21 = (bf16[4,160,640]{2,1,0:T(8,128)(2,1)S(1)}, bf16[4,160,640]{2,1,0:T(8,128)(2,1)S(1)}, u32[]{:S(2)}, u32[]{:S(2)}) collective-permute-start(bf16[4,160,640]{2,1,0:T(8,128)(2,1)S(1)} %pad_maximum_fusion.refs_4_), channel_id=1, source_target_pairs={{0,192},{8,200},{16,208},{24,216},{32,224},{40,232},{48,240},{56,2... | collective-permute-start | bytes 2457608 | tf_op jit(solution)/shard_map/ppermute | solution.py:32
  29.0 34.4 %collective-permute-start.19 = (bf16[4,160,640]{2,1,0:T(8,128)(2,1)S(1)}, bf16[4,160,640]{2,1,0:T(8,128)(2,1)S(1)}, u32[]{:S(2)}, u32[]{:S(2)}) collective-permute-start(bf16[4,160,640]{2,1,0:T(8,128)(2,1)S(1)} %pad_maximum_fusion.refs_4_), channel_id=1, source_target_pairs={{0,64},{8,72},{16,80},{24,88},{32,96},{40,104},{48,112},{56,120},{... | collective-permute-start | bytes 2457608 | tf_op jit(solution)/shard_map/ppermute | solution.py:32
  29.0 23.3 %collective-permute-start.8 = (bf16[12,128,128]{2,1,0:T(8,128)(2,1)S(1)}, bf16[12,128,128]{2,1,0:T(8,128)(2,1)S(1)}, u32[]{:S(2)}, u32[]{:S(2)}) collective-permute-start(bf16[12,128,128]{2,1,0:T(8,128)(2,1)S(1)} %copy-done.2), channel_id=1, source_target_pairs={{0,48},{8,56},{16,0},{24,8},{32,16},{40,24},{48,32},{56,40},{64,11... | collective-permute-start | bytes 1179656 | tf_op jit(solution)/shard_map/ppermute | solution.py:32
  33.7 20.3 %collective-permute-start.6 = (bf16[12,128,128]{2,1,0:T(8,128)(2,1)S(1)}, bf16[12,128,128]{2,1,0:T(8,128)(2,1)S(1)}, u32[]{:S(2)}, u32[]{:S(2)}) collective-permute-start(bf16[12,128,128]{2,1,0:T(8,128)(2,1)S(1)} %copy-done.2), channel_id=1, source_target_pairs={{0,16},{8,24},{16,32},{24,40},{32,48},{40,56},{48,0},{56,8},{64,80... | collective-permute-start | bytes 1179656 | tf_op jit(solution)/shard_map/ppermute | solution.py:32
  34.3 21.1 %collective-permute-start.14 = (bf16[5,256,128]{2,1,0:T(8,128)(2,1)}, bf16[5,256,128]{2,1,0:T(8,128)(2,1)S(1)}, u32[]{:S(2)}, u32[]{:S(2)}) collective-permute-start(bf16[5,256,128]{2,1,0:T(8,128)(2,1)} %bitcast.4.refs_10_), channel_id=1, source_target_pairs={{0,128},{8,136},{16,144},{24,152},{32,160},{40,168},{48,176},{56,1... | collective-permute-start | bytes 983048 | tf_op jit(solution)/shard_map/ppermute | solution.py:32
  52.3 8.0 %collective-permute-start.11 = (bf16[6,128,128]{2,1,0:T(8,128)(2,1)S(1)}, bf16[6,128,128]{2,1,0:T(8,128)(2,1)S(1)}, u32[]{:S(2)}, u32[]{:S(2)}) collective-permute-start(bf16[6,128,128]{2,1,0:T(8,128)(2,1)S(1)} %slice.37), channel_id=1, source_target_pairs={{0,48},{8,56},{16,0},{24,8},{32,16},{40,24},{48,32},{56,40},{64,11... | collective-permute-start | bytes 589832 | tf_op jit(solution)/shard_map/ppermute | solution.py:32
  54.0 8.7 %collective-permute-start.10 = (bf16[6,128,128]{2,1,0:T(8,128)(2,1)S(1)}, bf16[6,128,128]{2,1,0:T(8,128)(2,1)}, u32[]{:S(2)}, u32[]{:S(2)}) collective-permute-start(bf16[6,128,128]{2,1,0:T(8,128)(2,1)S(1)} %slice.36), channel_id=1, source_target_pairs={{0,16},{8,24},{16,32},{24,40},{32,48},{40,56},{48,0},{56,8},{64,80... | collective-permute-start | bytes 589832 | tf_op jit(solution)/shard_map/ppermute | solution.py:32
  55.4 8.8 %collective-permute-start.5 = (bf16[12,128,128]{2,1,0:T(8,128)(2,1)S(1)}, bf16[12,128,128]{2,1,0:T(8,128)(2,1)}, u32[]{:S(2)}, u32[]{:S(2)}) collective-permute-start(bf16[12,128,128]{2,1,0:T(8,128)(2,1)S(1)} %copy-done.2), channel_id=1, source_target_pairs={{0,8},{8,0},{16,24},{24,16},{32,40},{40,32},{48,56},{56,48},{64,72... | collective-permute-start | bytes 1179656 | tf_op jit(solution)/shard_map/ppermute | solution.py:32
  60.3 6.0 %collective-permute-start.9 = (bf16[12,128,128]{2,1,0:T(8,128)(2,1)}, bf16[12,128,128]{2,1,0:T(8,128)(2,1)}, u32[]{:S(2)}, u32[]{:S(2)}) collective-permute-start(bf16[12,128,128]{2,1,0:T(8,128)(2,1)} %copy-done.10), channel_id=1, source_target_pairs={{0,8},{8,0},{16,24},{24,16},{32,40},{40,32},{48,56},{56,48},{64,72... | collective-permute-start | bytes 1179656 | tf_op jit(solution)/shard_map/ppermute | solution.py:32
  64.2 40.3 %collective-permute-start.23 = (bf16[4,160,640]{2,1,0:T(8,128)(2,1)S(1)}, bf16[4,160,640]{2,1,0:T(8,128)(2,1)S(1)}, u32[]{:S(2)}, u32[]{:S(2)}) collective-permute-start(bf16[4,160,640]{2,1,0:T(8,128)(2,1)S(1)} %pad_maximum_fusion.refs_4_), channel_id=1, source_target_pairs={{0,128},{8,136},{16,144},{24,152},{32,160},{40,168},{48,176},{56,1... | collective-permute-start | bytes 2457608 | tf_op jit(solution)/shard_map/ppermute | solution.py:32
  85.1 8.0 %collective-permute-start.15 = (bf16[2,656,128]{2,1,0:T(8,128)(2,1)}, bf16[2,656,128]{2,1,0:T(8,128)(2,1)S(1)}, u32[]{:S(2)}, u32[]{:S(2)}) collective-permute-start(bf16[2,656,128]{2,1,0:T(8,128)(2,1)} %get-tuple-element.29), channel_id=1, source_target_pairs={{0,192},{8,200},{16,208},{24,216},{32,224},{40,232},{48,240},{56,2... | collective-permute-start | bytes 1007624 | tf_op jit(solution)/shard_map/ppermute | solution.py:32
  85.2 14.1 %collective-permute-start.16 = (bf16[2,656,128]{2,1,0:T(8,128)(2,1)}, bf16[2,656,128]{2,1,0:T(8,128)(2,1)S(1)}, u32[]{:S(2)}, u32[]{:S(2)}) collective-permute-start(bf16[2,656,128]{2,1,0:T(8,128)(2,1)} %get-tuple-element.30), channel_id=1, source_target_pairs={{0,64},{8,72},{16,80},{24,88},{32,96},{40,104},{48,112},{56,120},{... | collective-permute-start | bytes 1007624 | tf_op jit(solution)/shard_map/ppermute | solution.py:32
  87.2 17.3 %collective-permute-start.17 = (bf16[2,656,128]{2,1,0:T(8,128)(2,1)}, bf16[2,656,128]{2,1,0:T(8,128)(2,1)S(1)}, u32[]{:S(2)}, u32[]{:S(2)}) collective-permute-start(bf16[2,656,128]{2,1,0:T(8,128)(2,1)} %get-tuple-element.31), channel_id=1, source_target_pairs={{0,128},{8,136},{16,144},{24,152},{32,160},{40,168},{48,176},{56,1... | collective-permute-start | bytes 1007624 | tf_op jit(solution)/shard_map/ppermute | solution.py:32
  87.3 19.6 %collective-permute-start.18 = (bf16[4,160,640]{2,1,0:T(8,128)(2,1)S(1)}, bf16[4,160,640]{2,1,0:T(8,128)(2,1)}, u32[]{:S(2)}, u32[]{:S(2)}) collective-permute-start(bf16[4,160,640]{2,1,0:T(8,128)(2,1)S(1)} %pad_maximum_fusion.refs_4_), channel_id=1, source_target_pairs={{0,8},{8,0},{16,24},{24,16},{32,40},{40,32},{48,56},{56,48},{64,72... | collective-permute-start | bytes 2457608 | tf_op jit(solution)/shard_map/ppermute | solution.py:32
  93.1 13.7 %collective-permute-start.22 = (bf16[4,160,640]{2,1,0:T(8,128)(2,1)S(1)}, bf16[4,160,640]{2,1,0:T(8,128)(2,1)}, u32[]{:S(2)}, u32[]{:S(2)}) collective-permute-start(bf16[4,160,640]{2,1,0:T(8,128)(2,1)S(1)} %collective-permute-done.21.refs_8_), channel_id=1, source_target_pairs={{0,8},{8,0},{16,24},{24,16},{32,40},{40,32},{48,56},{56,48},{64,72... | collective-permute-start | bytes 2457608 | tf_op jit(solution)/shard_map/ppermute | solution.py:32
  99.3 7.6 %collective-permute-start.20 = (bf16[4,160,640]{2,1,0:T(8,128)(2,1)S(1)}, bf16[4,160,640]{2,1,0:T(8,128)(2,1)}, u32[]{:S(2)}, u32[]{:S(2)}) collective-permute-start(bf16[4,160,640]{2,1,0:T(8,128)(2,1)S(1)} %collective-permute-done.19.refs_6_), channel_id=1, source_target_pairs={{0,8},{8,0},{16,24},{24,16},{32,40},{40,32},{48,56},{56,48},{64,72... | collective-permute-start | bytes 2457608 | tf_op jit(solution)/shard_map/ppermute | solution.py:32
  116.4 10.5 %collective-permute-start.25 = (bf16[2,128,640]{2,1,0:T(8,128)(2,1)S(1)}, bf16[2,128,640]{2,1,0:T(8,128)(2,1)S(1)}, u32[]{:S(2)}, u32[]{:S(2)}) collective-permute-start(bf16[2,128,640]{2,1,0:T(8,128)(2,1)S(1)} %get-tuple-element.35), channel_id=1, source_target_pairs={{0,2},{1,3},{2,4},{3,5},{4,6},{5,7},{6,0},{7,1},{8,10},{9,11},{10,... | collective-permute-start | bytes 983048 | tf_op jit(solution)/shard_map/ppermute | solution.py:48
  116.9 17.9 %collective-permute-start.26 = (bf16[2,128,640]{2,1,0:T(8,128)(2,1)S(1)}, bf16[2,128,640]{2,1,0:T(8,128)(2,1)S(1)}, u32[]{:S(2)}, u32[]{:S(2)}) collective-permute-start(bf16[2,128,640]{2,1,0:T(8,128)(2,1)S(1)} %get-tuple-element.36), channel_id=1, source_target_pairs={{0,6},{1,7},{2,0},{3,1},{4,2},{5,3},{6,4},{7,5},{8,14},{9,15},{10,... | collective-permute-start | bytes 983048 | tf_op jit(solution)/shard_map/ppermute | solution.py:48
  118.5 17.8 %collective-permute-start.27 = (bf16[2,128,640]{2,1,0:T(8,128)(2,1)S(1)}, bf16[2,128,640]{2,1,0:T(8,128)(2,1)S(1)}, u32[]{:S(2)}, u32[]{:S(2)}) collective-permute-start(bf16[2,128,640]{2,1,0:T(8,128)(2,1)S(1)} %get-tuple-element.37), channel_id=1, source_target_pairs={{0,4},{1,5},{2,6},{3,7},{4,0},{5,1},{6,2},{7,3},{8,12},{9,13},{10,... | collective-permute-start | bytes 983048 | tf_op jit(solution)/shard_map/ppermute | solution.py:48
  120.1 24.8 %collective-permute-start.29 = (bf16[4,128,640]{2,1,0:T(8,128)(2,1)}, bf16[4,128,640]{2,1,0:T(8,128)(2,1)S(1)}, u32[]{:S(2)}, u32[]{:S(2)}) collective-permute-start(bf16[4,128,640]{2,1,0:T(8,128)(2,1)} %get-tuple-element.39), channel_id=1, source_target_pairs={{0,1},{1,0},{2,3},{3,2},{4,5},{5,4},{6,7},{7,6},{8,9},{9,8},{10,11... | collective-permute-start | bytes 1966088 | tf_op jit(solution)/shard_map/ppermute | solution.py:48
  127.0 9.5 %collective-permute-start.33 = (bf16[4,128,128]{2,1,0:T(8,128)(2,1)S(1)}, bf16[4,128,128]{2,1,0:T(8,128)(2,1)S(1)}, u32[]{:S(2)}, u32[]{:S(2)}) collective-permute-start(bf16[4,128,128]{2,1,0:T(8,128)(2,1)S(1)} %copy-done.21), channel_id=1, source_target_pairs={{0,192},{8,200},{16,208},{24,216},{32,224},{40,232},{48,240},{56,2... | collective-permute-start | bytes 393224 | tf_op jit(solution)/shard_map/ppermute | solution.py:32
  127.5 9.0 %collective-permute-start.34 = (bf16[4,128,128]{2,1,0:T(8,128)(2,1)S(1)}, bf16[4,128,128]{2,1,0:T(8,128)(2,1)S(1)}, u32[]{:S(2)}, u32[]{:S(2)}) collective-permute-start(bf16[4,128,128]{2,1,0:T(8,128)(2,1)S(1)} %copy-done.20), channel_id=1, source_target_pairs={{0,64},{8,72},{16,80},{24,88},{32,96},{40,104},{48,112},{56,120},{... | collective-permute-start | bytes 393224 | tf_op jit(solution)/shard_map/ppermute | solution.py:32
  134.8 6.5 %collective-permute-start.35 = (bf16[4,128,128]{2,1,0:T(8,128)(2,1)S(1)}, bf16[4,128,128]{2,1,0:T(8,128)(2,1)S(1)}, u32[]{:S(2)}, u32[]{:S(2)}) collective-permute-start(bf16[4,128,128]{2,1,0:T(8,128)(2,1)S(1)} %copy-done.19), channel_id=1, source_target_pairs={{0,128},{8,136},{16,144},{24,152},{32,160},{40,168},{48,176},{56,1... | collective-permute-start | bytes 393224 | tf_op jit(solution)/shard_map/ppermute | solution.py:32
  136.4 10.8 %collective-permute-start.28 = (bf16[128,640]{1,0:T(8,128)(2,1)S(1)}, bf16[128,640]{1,0:T(8,128)(2,1)S(1)}, u32[]{:S(2)}, u32[]{:S(2)}) collective-permute-start(bf16[128,640]{1,0:T(8,128)(2,1)S(1)} %fusion.7), channel_id=1, source_target_pairs={{0,1},{1,0},{2,3},{3,2},{4,5},{5,4},{6,7},{7,6},{8,9},{9,8},{10,11... | collective-permute-start | bytes 491528 | tf_op jit(solution)/shard_map/ppermute | solution.py:48
  145.1 5.4 %collective-permute-start.30 = (bf16[128,640]{1,0:T(8,128)(2,1)S(1)}, bf16[128,640]{1,0:T(8,128)(2,1)S(1)}, u32[]{:S(2)}, u32[]{:S(2)}) collective-permute-start(bf16[128,640]{1,0:T(8,128)(2,1)S(1)} %get-tuple-element.77), channel_id=1, source_target_pairs={{0,2},{1,3},{2,4},{3,5},{4,6},{5,7},{6,0},{7,1},{8,10},{9,11},{10,... | collective-permute-start | bytes 491528 | tf_op jit(solution)/shard_map/ppermute | solution.py:48
  145.2 7.0 %collective-permute-start.32 = (bf16[128,640]{1,0:T(8,128)(2,1)S(1)}, bf16[128,640]{1,0:T(8,128)(2,1)S(1)}, u32[]{:S(2)}, u32[]{:S(2)}) collective-permute-start(bf16[128,640]{1,0:T(8,128)(2,1)S(1)} %get-tuple-element.78), channel_id=1, source_target_pairs={{0,4},{1,5},{2,6},{3,7},{4,0},{5,1},{6,2},{7,3},{8,12},{9,13},{10,... | collective-permute-start | bytes 491528 | tf_op jit(solution)/shard_map/ppermute | solution.py:48
  145.3 8.6 %collective-permute-start.31 = (bf16[128,640]{1,0:T(8,128)(2,1)S(1)}, bf16[128,640]{1,0:T(8,128)(2,1)S(1)}, u32[]{:S(2)}, u32[]{:S(2)}) collective-permute-start(bf16[128,640]{1,0:T(8,128)(2,1)S(1)} %get-tuple-element.79), channel_id=1, source_target_pairs={{0,6},{1,7},{2,0},{3,1},{4,2},{5,3},{6,4},{7,5},{8,14},{9,15},{10,... | collective-permute-start | bytes 491528 | tf_op jit(solution)/shard_map/ppermute | solution.py:48
  (27 other events, 229.6 us)

commit v4 on v3

--- a/solution.py
+++ b/solution.py
@@ -247,14 +247,13 @@
         result[i, wide : wide + 16, :] = stats.astype(jnp.bfloat16)
         return unused
 
-    lax.fori_loop(0, nq * per, one_block, 0)
     backs = []
-    for r in range(nq):
+    for r in reversed(range(nq)):
+        lax.fori_loop(r * per, (r + 1) * per, one_block, 0)
         backs.append(
             pltpu.make_async_copy(result.at[pl.ds(r * per, per)], out_refs[r], out_sem.at[r])
         )
-    for back in backs:
-        back.start()
+        backs[-1].start()
     for send in sends:
         send.wait()
     for back in backs:
@@ -544,6 +543,7 @@
     kv_near = [shift(own_kv, dz=k) for k in SHIFTS[1:3]]
     q_parts = [own_q, *q_near, shift(after(own_q, *q_near), dy=SHIFTS[3])]
     w_four = jnp.stack(w_line)
+    w_four = after(w_four, q_parts[3])
     w_near = [shift(w_four, dy=k) for k in SHIFTS[1:3]]
     far = [
         shift(kv_near[0][:slots], dz=SHIFTS[1]),
@@ -567,20 +567,24 @@
     shares = finish(pieces, [in_hbm(p) for p in parts], w_parts, heads)
     first, second = shares[:NX], shares[NX:]
     first = [first[0]] + [head_shift(p, dx=k) for p, k in zip(first[1:], SHIFTS[1:])]
-    moved = [moved[0]] + [
-        shift(after(p, first[1]), dy=-k) for p, k in zip(moved[1:], SHIFTS[1:])
-    ]
+    moved = list(moved)
+    for r in (1, 2):
+        moved[r] = shift(after(moved[r], first[1]), dy=-SHIFTS[r])
+    moved[3] = shift(after(moved[3], moved[1]), dy=-SHIFTS[3])
     second_sum = second[0].astype(jnp.float32) + head_shift(second[1], dz=1).astype(jnp.float32)
     first_sum = functools.reduce(jnp.add, [p.astype(jnp.float32) for p in first])
-    second_out = second_sum[0]
-    for r in range(1, NX):
-        second_out += head_shift(second_sum[r].astype(jnp.bfloat16), dx=SHIFTS[r]).astype(
-            jnp.float32
-        )
+    second_sum = after(second_sum, moved[1], moved[2])
+    second_far = [
+        head_shift(second_sum[r].astype(jnp.bfloat16), dx=SHIFTS[r]) for r in range(1, NX)
+    ]
+    second_out = functools.reduce(
+        jnp.add, [p.astype(jnp.float32) for p in second_far], second_sum[0]
+    )
     first_out = first_sum[0] + head_shift(first_sum[1].astype(jnp.bfloat16), dz=1).astype(
         jnp.float32
     )
     attn_output = jnp.concatenate([first_out, second_out], axis=0).astype(jnp.bfloat16)
+    moved[1] = after(moved[1], second_far[0])
     new_ck, new_cv = refill(source, ck, cv, moved)
     return (
         attn_output,

time: 157 us -> 150 us (0.955); the launches traced: 155 us -> 151 us
  starting transfers between devices: 56.3 us -> 53.4 us
  waiting for transfers between devices: 48.9 us -> 47.2 us
    ppermute x28, starting transfers between devices: 50.6 us -> 46.1 us  [shift(): return lax.ppermute(value, 'blk', blk_perm(dy, dz, dc))]
    ppermute x28, waiting for transfers between devices: 30.2 us -> 27.4 us  [shift(): return lax.ppermute(value, 'blk', blk_perm(dy, dz, dc))]
  transfers between devices with their start and end apart: 36 -> 36, of which waited for: 11 -> 13; matrix products, arithmetic and copies ran while one was open for 9% -> 10% of each run, Pallas kernels for 15% -> 14%
where the time goes in v4:
time: 150 us; the launch traced here: 151 us
  starting transfers between devices  53.4 us (36%)
  waiting for transfers between devices  47.2 us (31%)
  Pallas kernels  31.5 us (21%)
  other arithmetic  13.3 us (9%)
  local copies, waits for them, and re-layouts  3.75 us (2%)
    ppermute x28, starting transfers between devices, shift(): return lax.ppermute(value, 'blk', blk_perm(dy, dz, dc))  46.1 us
    ppermute x28, waiting for transfers between devices, shift(): return lax.ppermute(value, 'blk', blk_perm(dy, dz, dc))  27.4 us
    ppermute x8, waiting for transfers between devices, head_shift(): return lax.ppermute(value, 'head', pairs)  19.8 us
    pallas_call x1, Pallas kernels, attend(): pl.pallas_call(functools.partial(attend_kernel, log_scale, nkv, nq), out_...  19.5 us
    ppermute x8, starting transfers between devices, head_shift(): return lax.ppermute(value, 'head', pairs)  7.28 us
    pallas_call x1, Pallas kernels, finish(): pl.pallas_call(functools.partial(finish_kernel, heads, nparts, nw), out_s...  7.22 us
    reduce_sum x2, other arithmetic, table_entry(): return jnp.sum(jnp.where(match, block_table[None], 0), axis=(1, 2))  3.89 us
  transfers between devices with their start and end apart: 36, of which 13 were waited for; matrix products, arithmetic and copies ran while one was open for 10% of the time, Pallas kernels for 14%

profile of v4, /device:TPU:6, one launch (start us, length us, event | category | flops | bytes accessed | tf_op | source)
XLA Modules:
  0.0 150.5 jit_solution(6187766764786507722)
XLA Ops:
  0.7 6.4 %collective-permute-start.1 = (bf16[160,640]{1,0:T(8,128)(2,1)}, bf16[160,640]{1,0:T(8,128)(2,1)S(1)}, u32[]{:S(2)}, u32[]{:S(2)}) collective-permute-start(bf16[160,640]{1,0:T(8,128)(2,1)} %param.17), channel_id=1, source_target_pairs={{0,48},{8,56},{16,0},{24,8},{32,16},{40,24},{48,32},{56,40},{64,11... | collective-permute-start | bytes 614408 | tf_op jit(solution)/shard_map/ppermute | solution.py:32
  7.0 3.8 %collective-permute-start.2 = (bf16[160,640]{1,0:T(8,128)(2,1)}, bf16[160,640]{1,0:T(8,128)(2,1)S(1)}, u32[]{:S(2)}, u32[]{:S(2)}) collective-permute-start(bf16[160,640]{1,0:T(8,128)(2,1)} %param.17), channel_id=1, source_target_pairs={{0,32},{8,40},{16,48},{24,56},{32,0},{40,8},{48,16},{56,24},{64,96... | collective-permute-start | bytes 614408 | tf_op jit(solution)/shard_map/ppermute | solution.py:32
  10.9 3.0 %collective-permute-start.4 = (bf16[5,256,128]{2,1,0:T(8,128)(2,1)}, bf16[5,256,128]{2,1,0:T(8,128)(2,1)S(1)}, u32[]{:S(2)}, u32[]{:S(2)}) collective-permute-start(bf16[5,256,128]{2,1,0:T(8,128)(2,1)} %bitcast.47), channel_id=1, source_target_pairs={{0,192},{8,200},{16,208},{24,216},{32,224},{40,232},{48,240},{56,2... | collective-permute-start | bytes 983048 | tf_op jit(solution)/shard_map/ppermute | solution.py:32
  17.2 2.6 %select_reduce_fusion.1 = (s32[48]{0:T(128)S(1)}, s32[48]{0:T(128)S(1)}) fusion(s32[8,64]{1,0:T(8,128)} %param.20, pred[48,64]{1,0:T(8,128)(4,1)S(1)} %iota_compare_fusion.2, pred[48,8]{1,0:T(8,128)(4,1)S(1)} %copy.19, s32[8,64]{1,0:T(8,128)S(1)} %add_add_fusion, pred[8,64]{1,0:T(8,128)(4,1)S(1)} %iota_compare_fusion.8, s32[48]{0:T(128)S(1)} %add.594), kind=kLoop, calls=%fused_computation.13 | loop fusion | flops 171936 | bytes 8640 | tf_op jit(solution)/shard_map/reduce_sum | solution.py:75
  23.0 1.8 %pack.1.refs_0_ = bf16[12,128,128]{2,1,0:T(8,128)(2,1)} custom-call(bf16[6,128,128]{2,1,0:T(8,128)(2,1)} %bitcast.37, bf16[6,128,128]{2,1,0:T(8,128)(2,1)} %bitcast.39, bf16[2,128,128]{2,1,0:T(8,128)(2,1)} %bitcast.45, bf16[2,128,128]{2,1,0:T(8,128)(2,1)} %bitcast.46), custom_call_target="tpu_custom_call" | custom-call | tf_op jit(solution)/shard_map/pack/pallas_call | solution.py:100
  24.9 2.3 %collective-permute-start.14 = (bf16[5,256,128]{2,1,0:T(8,128)(2,1)S(1)}, bf16[5,256,128]{2,1,0:T(8,128)(2,1)S(1)}, u32[]{:S(2)}, u32[]{:S(2)}) collective-permute-start(bf16[5,256,128]{2,1,0:T(8,128)(2,1)S(1)} %bitcast.50), channel_id=1, source_target_pairs={{0,128},{8,136},{16,144},{24,152},{32,160},{40,168},{48,176},{56,1... | collective-permute-start | bytes 983048 | tf_op jit(solution)/shard_map/ppermute | solution.py:32
  27.4 3.2 %collective-permute-start.8 = (bf16[12,128,128]{2,1,0:T(8,128)(2,1)S(1)}, bf16[12,128,128]{2,1,0:T(8,128)(2,1)S(1)}, u32[]{:S(2)}, u32[]{:S(2)}) collective-permute-start(bf16[12,128,128]{2,1,0:T(8,128)(2,1)S(1)} %copy-done), channel_id=1, source_target_pairs={{0,48},{8,56},{16,0},{24,8},{32,16},{40,24},{48,32},{56,40},{64,11... | collective-permute-start | bytes 1179656 | tf_op jit(solution)/shard_map/ppermute | solution.py:32
  31.2 3.6 %collective-permute-done.14.refs_13_ = bf16[5,256,128]{2,1,0:T(8,128)(2,1)S(1)} collective-permute-done((bf16[5,256,128]{2,1,0:T(8,128)(2,1)S(1)}, bf16[5,256,128]{2,1,0:T(8,128)(2,1)S(1)}, u32[]{:S(2)}, u32[]{:S(2)}) %collective-permute-start.14) | collective-permute-done | bytes 327712 | tf_op jit(solution)/shard_map/ppermute | solution.py:32
  35.6 2.9 %collective-permute-start.21 = (bf16[4,160,640]{2,1,0:T(8,128)(2,1)S(1)}, bf16[4,160,640]{2,1,0:T(8,128)(2,1)S(1)}, u32[]{:S(2)}, u32[]{:S(2)}) collective-permute-start(bf16[4,160,640]{2,1,0:T(8,128)(2,1)S(1)} %pad_maximum_fusion.refs_4_), channel_id=1, source_target_pairs={{0,192},{8,200},{16,208},{24,216},{32,224},{40,232},{48,240},{56,2... | collective-permute-start | bytes 2457608 | tf_op jit(solution)/shard_map/ppermute | solution.py:32
  39.2 10.0 %collective-permute-done.8.refs_4_ = bf16[12,128,128]{2,1,0:T(8,128)(2,1)S(1)} collective-permute-done((bf16[12,128,128]{2,1,0:T(8,128)(2,1)S(1)}, bf16[12,128,128]{2,1,0:T(8,128)(2,1)S(1)}, u32[]{:S(2)}, u32[]{:S(2)}) %collective-permute-start.8) | collective-permute-done | bytes 393248 | tf_op jit(solution)/shard_map/ppermute | solution.py:32
  49.2 2.8 %collective-permute-start.11 = (bf16[6,128,128]{2,1,0:T(8,128)(2,1)S(1)}, bf16[6,128,128]{2,1,0:T(8,128)(2,1)S(1)}, u32[]{:S(2)}, u32[]{:S(2)}) collective-permute-start(bf16[6,128,128]{2,1,0:T(8,128)(2,1)S(1)} %slice.37), channel_id=1, source_target_pairs={{0,48},{8,56},{16,0},{24,8},{32,16},{40,24},{48,32},{56,40},{64,11... | collective-permute-start | bytes 589832 | tf_op jit(solution)/shard_map/ppermute | solution.py:32
  52.4 2.6 %collective-permute-start.10 = (bf16[6,128,128]{2,1,0:T(8,128)(2,1)S(1)}, bf16[6,128,128]{2,1,0:T(8,128)(2,1)}, u32[]{:S(2)}, u32[]{:S(2)}) collective-permute-start(bf16[6,128,128]{2,1,0:T(8,128)(2,1)S(1)} %slice.36), channel_id=1, source_target_pairs={{0,16},{8,24},{16,32},{24,40},{32,48},{40,56},{48,0},{56,8},{64,80... | collective-permute-start | bytes 589832 | tf_op jit(solution)/shard_map/ppermute | solution.py:32
  55.2 4.8 %collective-permute-done.11.refs_7_ = bf16[6,128,128]{2,1,0:T(8,128)(2,1)S(1)} collective-permute-done((bf16[6,128,128]{2,1,0:T(8,128)(2,1)S(1)}, bf16[6,128,128]{2,1,0:T(8,128)(2,1)S(1)}, u32[]{:S(2)}, u32[]{:S(2)}) %collective-permute-start.11) | collective-permute-done | bytes 196640 | tf_op jit(solution)/shard_map/ppermute | solution.py:32
  62.3 1.6 %collective-permute-start.23 = (bf16[4,160,640]{2,1,0:T(8,128)(2,1)S(1)}, bf16[4,160,640]{2,1,0:T(8,128)(2,1)S(1)}, u32[]{:S(2)}, u32[]{:S(2)}) collective-permute-start(bf16[4,160,640]{2,1,0:T(8,128)(2,1)S(1)} %pad_maximum_fusion.refs_4_), channel_id=1, source_target_pairs={{0,128},{8,136},{16,144},{24,152},{32,160},{40,168},{48,176},{56,1... | collective-permute-start | bytes 2457608 | tf_op jit(solution)/shard_map/ppermute | solution.py:32
  64.1 19.5 %attend.1 = (bf16[2,656,128]{2,1,0:T(8,128)(2,1)}, bf16[2,656,128]{2,1,0:T(8,128)(2,1)}, bf16[2,656,128]{2,1,0:T(8,128)(2,1)}, bf16[2,656,128]{2,1,0:T(8,128)(2,...) custom-call(s32[8]{0:T(128)} %copy-done.13, ...), custom_call_target="tpu_custom_call" | custom-call | flops 5000000000 | bytes 8000000 | tf_op jit(solution)/shard_map/attend/pallas_call | solution.py:273
  83.7 2.0 %collective-permute-start.16 = (bf16[2,656,128]{2,1,0:T(8,128)(2,1)}, bf16[2,656,128]{2,1,0:T(8,128)(2,1)S(1)}, u32[]{:S(2)}, u32[]{:S(2)}) collective-permute-start(bf16[2,656,128]{2,1,0:T(8,128)(2,1)} %get-tuple-element.33), channel_id=1, source_target_pairs={{0,64},{8,72},{16,80},{24,88},{32,96},{40,104},{48,112},{56,120},{... | collective-permute-start | bytes 1007624 | tf_op jit(solution)/shard_map/ppermute | solution.py:32
  86.0 2.6 %collective-permute-start.18 = (bf16[4,160,640]{2,1,0:T(8,128)(2,1)S(1)}, bf16[4,160,640]{2,1,0:T(8,128)(2,1)}, u32[]{:S(2)}, u32[]{:S(2)}) collective-permute-start(bf16[4,160,640]{2,1,0:T(8,128)(2,1)S(1)} %pad_maximum_fusion.refs_4_), channel_id=1, source_target_pairs={{0,8},{8,0},{16,24},{24,16},{32,40},{40,32},{48,56},{56,48},{64,72... | collective-permute-start | bytes 2457608 | tf_op jit(solution)/shard_map/ppermute | solution.py:32
  88.6 3.5 %collective-permute-done.15.refs_1_ = bf16[2,656,128]{2,1,0:T(8,128)(2,1)S(1)} collective-permute-done((bf16[2,656,128]{2,1,0:T(8,128)(2,1)}, bf16[2,656,128]{2,1,0:T(8,128)(2,1)S(1)}, u32[]{:S(2)}, u32[]{:S(2)}) %collective-permute-start.15) | collective-permute-done | bytes 335904 | tf_op jit(solution)/shard_map/ppermute | solution.py:32
  92.1 5.1 %collective-permute-start.22 = (bf16[4,160,640]{2,1,0:T(8,128)(2,1)S(1)}, bf16[4,160,640]{2,1,0:T(8,128)(2,1)}, u32[]{:S(2)}, u32[]{:S(2)}) collective-permute-start(bf16[4,160,640]{2,1,0:T(8,128)(2,1)S(1)} %collective-permute-done.21.refs_8_), channel_id=1, source_target_pairs={{0,8},{8,0},{16,24},{24,16},{32,40},{40,32},{48,56},{56,48},{64,72... | collective-permute-start | bytes 2457608 | tf_op jit(solution)/shard_map/ppermute | solution.py:32
  97.2 3.4 %collective-permute-done.16.refs_2_ = bf16[2,656,128]{2,1,0:T(8,128)(2,1)S(1)} collective-permute-done((bf16[2,656,128]{2,1,0:T(8,128)(2,1)}, bf16[2,656,128]{2,1,0:T(8,128)(2,1)S(1)}, u32[]{:S(2)}, u32[]{:S(2)}) %collective-permute-start.16) | collective-permute-done | bytes 335904 | tf_op jit(solution)/shard_map/ppermute | solution.py:32
  100.6 2.3 %collective-permute-start.20 = (bf16[4,160,640]{2,1,0:T(8,128)(2,1)S(1)}, bf16[4,160,640]{2,1,0:T(8,128)(2,1)}, u32[]{:S(2)}, u32[]{:S(2)}) collective-permute-start(bf16[4,160,640]{2,1,0:T(8,128)(2,1)S(1)} %collective-permute-done.19.refs_6_), channel_id=1, source_target_pairs={{0,8},{8,0},{16,24},{24,16},{32,40},{40,32},{48,56},{56,48},{64,72... | collective-permute-start | bytes 2457608 | tf_op jit(solution)/shard_map/ppermute | solution.py:32
  106.2 7.2 %finish.1 = (bf16[2,128,640]{2,1,0:T(8,128)(2,1)S(1)}, bf16[2,128,640]{2,1,0:T(8,128)(2,1)S(1)}, bf16[2,128,640]{2,1,0:T(8,128)(2,1)S(1)}, bf16[2,128,640]{2,1,0...) custom-call(s32[32]{0:T(128)S(1)} %fusion.31.pieces, ...), custom_call_target="tpu_custom_call" | custom-call | flops 2000000000 | bytes 12000000 | tf_op jit(solution)/shard_map/finish/pallas_call | solution.py:371
  114.0 1.5 %collective-permute-start.26 = (bf16[2,128,640]{2,1,0:T(8,128)(2,1)S(1)}, bf16[2,128,640]{2,1,0:T(8,128)(2,1)S(1)}, u32[]{:S(2)}, u32[]{:S(2)}) collective-permute-start(bf16[2,128,640]{2,1,0:T(8,128)(2,1)S(1)} %get-tuple-element.40), channel_id=1, source_target_pairs={{0,6},{1,7},{2,0},{3,1},{4,2},{5,3},{6,4},{7,5},{8,14},{9,15},{10,... | collective-permute-start | bytes 983048 | tf_op jit(solution)/shard_map/ppermute | solution.py:48
  117.8 6.2 %collective-permute-done.25 = bf16[2,128,640]{2,1,0:T(8,128)(2,1)S(1)} collective-permute-done((bf16[2,128,640]{2,1,0:T(8,128)(2,1)S(1)}, bf16[2,128,640]{2,1,0:T(8,128)(2,1)S(1)}, u32[]{:S(2)}, u32[]{:S(2)}) %collective-permute-start.25) | collective-permute-done | bytes 327712 | tf_op jit(solution)/shard_map/ppermute | solution.py:48
  124.6 1.5 %collective-permute-start.31 = (bf16[4,128,128]{2,1,0:T(8,128)(2,1)S(1)}, bf16[4,128,128]{2,1,0:T(8,128)(2,1)S(1)}, u32[]{:S(2)}, u32[]{:S(2)}) collective-permute-start(bf16[4,128,128]{2,1,0:T(8,128)(2,1)S(1)} %copy-done.20), channel_id=1, source_target_pairs={{0,64},{8,72},{16,80},{24,88},{32,96},{40,104},{48,112},{56,120},{... | collective-permute-start | bytes 393224 | tf_op jit(solution)/shard_map/ppermute | solution.py:32
  126.1 5.8 %collective-permute-done.26 = bf16[2,128,640]{2,1,0:T(8,128)(2,1)S(1)} collective-permute-done((bf16[2,128,640]{2,1,0:T(8,128)(2,1)S(1)}, bf16[2,128,640]{2,1,0:T(8,128)(2,1)S(1)}, u32[]{:S(2)}, u32[]{:S(2)}) %collective-permute-start.26) | collective-permute-done | bytes 327712 | tf_op jit(solution)/shard_map/ppermute | solution.py:48
  134.5 1.8 %collective-permute-start.32 = (bf16[128,640]{1,0:T(8,128)(2,1)S(1)}, bf16[128,640]{1,0:T(8,128)(2,1)S(1)}, u32[]{:S(2)}, u32[]{:S(2)}) collective-permute-start(bf16[128,640]{1,0:T(8,128)(2,1)S(1)} %get-tuple-element.81), channel_id=1, source_target_pairs={{0,2},{1,3},{2,4},{3,5},{4,6},{5,7},{6,0},{7,1},{8,10},{9,11},{10,... | collective-permute-start | bytes 491528 | tf_op jit(solution)/shard_map/ppermute | solution.py:48
  136.3 1.8 %collective-permute-start.34 = (bf16[128,640]{1,0:T(8,128)(2,1)S(1)}, bf16[128,640]{1,0:T(8,128)(2,1)S(1)}, u32[]{:S(2)}, u32[]{:S(2)}) collective-permute-start(bf16[128,640]{1,0:T(8,128)(2,1)S(1)} %get-tuple-element.82), channel_id=1, source_target_pairs={{0,4},{1,5},{2,6},{3,7},{4,0},{5,1},{6,2},{7,3},{8,12},{9,13},{10,... | collective-permute-start | bytes 491528 | tf_op jit(solution)/shard_map/ppermute | solution.py:48
  138.1 4.1 %collective-permute-done.32 = bf16[128,640]{1,0:T(8,128)(2,1)S(1)} collective-permute-done((bf16[128,640]{1,0:T(8,128)(2,1)S(1)}, bf16[128,640]{1,0:T(8,128)(2,1)S(1)}, u32[]{:S(2)}, u32[]{:S(2)}) %collective-permute-start.32) | collective-permute-done | bytes 163872 | tf_op jit(solution)/shard_map/ppermute | solution.py:48
  142.2 2.0 %collective-permute-done.34 = bf16[128,640]{1,0:T(8,128)(2,1)S(1)} collective-permute-done((bf16[128,640]{1,0:T(8,128)(2,1)S(1)}, bf16[128,640]{1,0:T(8,128)(2,1)S(1)}, u32[]{:S(2)}, u32[]{:S(2)}) %collective-permute-start.34) | collective-permute-done | bytes 163872 | tf_op jit(solution)/shard_map/ppermute | solution.py:48
  144.2 1.7 %collective-permute-done.33 = bf16[128,640]{1,0:T(8,128)(2,1)S(1)} collective-permute-done((bf16[128,640]{1,0:T(8,128)(2,1)S(1)}, bf16[128,640]{1,0:T(8,128)(2,1)S(1)}, u32[]{:S(2)}, u32[]{:S(2)}) %collective-permute-start.33) | collective-permute-done | bytes 163872 | tf_op jit(solution)/shard_map/ppermute | solution.py:48
  147.4 2.9 %refill.1 = (bf16[6,128,128]{2,1,0:T(8,128)(2,1)}, bf16[6,128,128]{2,1,0:T(8,128)(2,1)}) custom-call(s32[2]{0:T(128)} %compare_select_fusion.25.source, bf16[6,128,128]{2,1,0:T(8,128)(2,1)} %bitcast.38, bf16[6,128,128]{2,1,0:T(8,128)(2,1)} %bitcast.40, bf16[4,128,128]{2,1,0:T(8,128)(2,1)} %get-tuple-element.49.refs_0_, bf16[4,128,128]{2,1,0:T(8,128)(2,1)} %copy-done.5, ...), custom_call_target="tpu_custom_call" | custom-call | tf_op jit(solution)/shard_map/refill/pallas_call | solution.py:428
  (170 shorter events, 22.7 us)
Async XLA Ops:
  0.7 26.5 %collective-permute-start.1 = (bf16[160,640]{1,0:T(8,128)(2,1)}, bf16[160,640]{1,0:T(8,128)(2,1)S(1)}, u32[]{:S(2)}, u32[]{:S(2)}) collective-permute-start(bf16[160,640]{1,0:T(8,128)(2,1)} %param.17), channel_id=1, source_target_pairs={{0,48},{8,56},{16,0},{24,8},{32,16},{40,24},{48,32},{56,40},{64,11... | collective-permute-start | bytes 614408 | tf_op jit(solution)/shard_map/ppermute | solution.py:32
  7.0 20.2 %collective-permute-start = (bf16[160,640]{1,0:T(8,128)(2,1)}, bf16[160,640]{1,0:T(8,128)(2,1)S(1)}, u32[]{:S(2)}, u32[]{:S(2)}) collective-permute-start(bf16[160,640]{1,0:T(8,128)(2,1)} %param.17), channel_id=1, source_target_pairs={{0,16},{8,24},{16,32},{24,40},{32,48},{40,56},{48,0},{56,8},{64,80... | collective-permute-start | bytes 614408 | tf_op jit(solution)/shard_map/ppermute | solution.py:32
  7.0 20.2 %collective-permute-start.2 = (bf16[160,640]{1,0:T(8,128)(2,1)}, bf16[160,640]{1,0:T(8,128)(2,1)S(1)}, u32[]{:S(2)}, u32[]{:S(2)}) collective-permute-start(bf16[160,640]{1,0:T(8,128)(2,1)} %param.17), channel_id=1, source_target_pairs={{0,32},{8,40},{16,48},{24,56},{32,0},{40,8},{48,16},{56,24},{64,96... | collective-permute-start | bytes 614408 | tf_op jit(solution)/shard_map/ppermute | solution.py:32
  10.9 14.0 %collective-permute-start.4 = (bf16[5,256,128]{2,1,0:T(8,128)(2,1)}, bf16[5,256,128]{2,1,0:T(8,128)(2,1)S(1)}, u32[]{:S(2)}, u32[]{:S(2)}) collective-permute-start(bf16[5,256,128]{2,1,0:T(8,128)(2,1)} %bitcast.47), channel_id=1, source_target_pairs={{0,192},{8,200},{16,208},{24,216},{32,224},{40,232},{48,240},{56,2... | collective-permute-start | bytes 983048 | tf_op jit(solution)/shard_map/ppermute | solution.py:32
  13.9 11.0 %collective-permute-start.3 = (bf16[5,256,128]{2,1,0:T(8,128)(2,1)}, bf16[5,256,128]{2,1,0:T(8,128)(2,1)S(1)}, u32[]{:S(2)}, u32[]{:S(2)}) collective-permute-start(bf16[5,256,128]{2,1,0:T(8,128)(2,1)} %bitcast.48), channel_id=1, source_target_pairs={{0,64},{8,72},{16,80},{24,88},{32,96},{40,104},{48,112},{56,120},{... | collective-permute-start | bytes 983048 | tf_op jit(solution)/shard_map/ppermute | solution.py:32
  24.9 9.9 %collective-permute-start.14 = (bf16[5,256,128]{2,1,0:T(8,128)(2,1)S(1)}, bf16[5,256,128]{2,1,0:T(8,128)(2,1)S(1)}, u32[]{:S(2)}, u32[]{:S(2)}) collective-permute-start(bf16[5,256,128]{2,1,0:T(8,128)(2,1)S(1)} %bitcast.50), channel_id=1, source_target_pairs={{0,128},{8,136},{16,144},{24,152},{32,160},{40,168},{48,176},{56,1... | collective-permute-start | bytes 983048 | tf_op jit(solution)/shard_map/ppermute | solution.py:32
  27.4 21.8 %collective-permute-start.8 = (bf16[12,128,128]{2,1,0:T(8,128)(2,1)S(1)}, bf16[12,128,128]{2,1,0:T(8,128)(2,1)S(1)}, u32[]{:S(2)}, u32[]{:S(2)}) collective-permute-start(bf16[12,128,128]{2,1,0:T(8,128)(2,1)S(1)} %copy-done), channel_id=1, source_target_pairs={{0,48},{8,56},{16,0},{24,8},{32,16},{40,24},{48,32},{56,40},{64,11... | collective-permute-start | bytes 1179656 | tf_op jit(solution)/shard_map/ppermute | solution.py:32
  30.6 21.8 %collective-permute-start.6 = (bf16[12,128,128]{2,1,0:T(8,128)(2,1)S(1)}, bf16[12,128,128]{2,1,0:T(8,128)(2,1)S(1)}, u32[]{:S(2)}, u32[]{:S(2)}) collective-permute-start(bf16[12,128,128]{2,1,0:T(8,128)(2,1)S(1)} %copy-done), channel_id=1, source_target_pairs={{0,16},{8,24},{16,32},{24,40},{32,48},{40,56},{48,0},{56,8},{64,80... | collective-permute-start | bytes 1179656 | tf_op jit(solution)/shard_map/ppermute | solution.py:32
  35.6 25.2 %collective-permute-start.21 = (bf16[4,160,640]{2,1,0:T(8,128)(2,1)S(1)}, bf16[4,160,640]{2,1,0:T(8,128)(2,1)S(1)}, u32[]{:S(2)}, u32[]{:S(2)}) collective-permute-start(bf16[4,160,640]{2,1,0:T(8,128)(2,1)S(1)} %pad_maximum_fusion.refs_4_), channel_id=1, source_target_pairs={{0,192},{8,200},{16,208},{24,216},{32,224},{40,232},{48,240},{56,2... | collective-permute-start | bytes 2457608 | tf_op jit(solution)/shard_map/ppermute | solution.py:32
  38.5 22.9 %collective-permute-start.19 = (bf16[4,160,640]{2,1,0:T(8,128)(2,1)S(1)}, bf16[4,160,640]{2,1,0:T(8,128)(2,1)S(1)}, u32[]{:S(2)}, u32[]{:S(2)}) collective-permute-start(bf16[4,160,640]{2,1,0:T(8,128)(2,1)S(1)} %pad_maximum_fusion.refs_4_), channel_id=1, source_target_pairs={{0,64},{8,72},{16,80},{24,88},{32,96},{40,104},{48,112},{56,120},{... | collective-permute-start | bytes 2457608 | tf_op jit(solution)/shard_map/ppermute | solution.py:32
  49.2 10.8 %collective-permute-start.11 = (bf16[6,128,128]{2,1,0:T(8,128)(2,1)S(1)}, bf16[6,128,128]{2,1,0:T(8,128)(2,1)S(1)}, u32[]{:S(2)}, u32[]{:S(2)}) collective-permute-start(bf16[6,128,128]{2,1,0:T(8,128)(2,1)S(1)} %slice.37), channel_id=1, source_target_pairs={{0,48},{8,56},{16,0},{24,8},{32,16},{40,24},{48,32},{56,40},{64,11... | collective-permute-start | bytes 589832 | tf_op jit(solution)/shard_map/ppermute | solution.py:32
  52.4 8.4 %collective-permute-start.10 = (bf16[6,128,128]{2,1,0:T(8,128)(2,1)S(1)}, bf16[6,128,128]{2,1,0:T(8,128)(2,1)}, u32[]{:S(2)}, u32[]{:S(2)}) collective-permute-start(bf16[6,128,128]{2,1,0:T(8,128)(2,1)S(1)} %slice.36), channel_id=1, source_target_pairs={{0,16},{8,24},{16,32},{24,40},{32,48},{40,56},{48,0},{56,8},{64,80... | collective-permute-start | bytes 589832 | tf_op jit(solution)/shard_map/ppermute | solution.py:32
  55.0 7.2 %collective-permute-start.5 = (bf16[12,128,128]{2,1,0:T(8,128)(2,1)S(1)}, bf16[12,128,128]{2,1,0:T(8,128)(2,1)}, u32[]{:S(2)}, u32[]{:S(2)}) collective-permute-start(bf16[12,128,128]{2,1,0:T(8,128)(2,1)S(1)} %copy-done), channel_id=1, source_target_pairs={{0,8},{8,0},{16,24},{24,16},{32,40},{40,32},{48,56},{56,48},{64,72... | collective-permute-start | bytes 1179656 | tf_op jit(solution)/shard_map/ppermute | solution.py:32
  60.0 4.0 %collective-permute-start.9 = (bf16[12,128,128]{2,1,0:T(8,128)(2,1)}, bf16[12,128,128]{2,1,0:T(8,128)(2,1)}, u32[]{:S(2)}, u32[]{:S(2)}) collective-permute-start(bf16[12,128,128]{2,1,0:T(8,128)(2,1)} %copy-done.8), channel_id=1, source_target_pairs={{0,8},{8,0},{16,24},{24,16},{32,40},{40,32},{48,56},{56,48},{64,72... | collective-permute-start | bytes 1179656 | tf_op jit(solution)/shard_map/ppermute | solution.py:32
  62.3 40.7 %collective-permute-start.23 = (bf16[4,160,640]{2,1,0:T(8,128)(2,1)S(1)}, bf16[4,160,640]{2,1,0:T(8,128)(2,1)S(1)}, u32[]{:S(2)}, u32[]{:S(2)}) collective-permute-start(bf16[4,160,640]{2,1,0:T(8,128)(2,1)S(1)} %pad_maximum_fusion.refs_4_), channel_id=1, source_target_pairs={{0,128},{8,136},{16,144},{24,152},{32,160},{40,168},{48,176},{56,1... | collective-permute-start | bytes 2457608 | tf_op jit(solution)/shard_map/ppermute | solution.py:32
  83.6 8.6 %collective-permute-start.15 = (bf16[2,656,128]{2,1,0:T(8,128)(2,1)}, bf16[2,656,128]{2,1,0:T(8,128)(2,1)S(1)}, u32[]{:S(2)}, u32[]{:S(2)}) collective-permute-start(bf16[2,656,128]{2,1,0:T(8,128)(2,1)} %get-tuple-element.32), channel_id=1, source_target_pairs={{0,192},{8,200},{16,208},{24,216},{32,224},{40,232},{48,240},{56,2... | collective-permute-start | bytes 1007624 | tf_op jit(solution)/shard_map/ppermute | solution.py:32
  83.7 17.0 %collective-permute-start.16 = (bf16[2,656,128]{2,1,0:T(8,128)(2,1)}, bf16[2,656,128]{2,1,0:T(8,128)(2,1)S(1)}, u32[]{:S(2)}, u32[]{:S(2)}) collective-permute-start(bf16[2,656,128]{2,1,0:T(8,128)(2,1)} %get-tuple-element.33), channel_id=1, source_target_pairs={{0,64},{8,72},{16,80},{24,88},{32,96},{40,104},{48,112},{56,120},{... | collective-permute-start | bytes 1007624 | tf_op jit(solution)/shard_map/ppermute | solution.py:32
  85.7 17.3 %collective-permute-start.17 = (bf16[2,656,128]{2,1,0:T(8,128)(2,1)}, bf16[2,656,128]{2,1,0:T(8,128)(2,1)S(1)}, u32[]{:S(2)}, u32[]{:S(2)}) collective-permute-start(bf16[2,656,128]{2,1,0:T(8,128)(2,1)} %get-tuple-element.34), channel_id=1, source_target_pairs={{0,128},{8,136},{16,144},{24,152},{32,160},{40,168},{48,176},{56,1... | collective-permute-start | bytes 1007624 | tf_op jit(solution)/shard_map/ppermute | solution.py:32
  86.0 19.3 %collective-permute-start.18 = (bf16[4,160,640]{2,1,0:T(8,128)(2,1)S(1)}, bf16[4,160,640]{2,1,0:T(8,128)(2,1)}, u32[]{:S(2)}, u32[]{:S(2)}) collective-permute-start(bf16[4,160,640]{2,1,0:T(8,128)(2,1)S(1)} %pad_maximum_fusion.refs_4_), channel_id=1, source_target_pairs={{0,8},{8,0},{16,24},{24,16},{32,40},{40,32},{48,56},{56,48},{64,72... | collective-permute-start | bytes 2457608 | tf_op jit(solution)/shard_map/ppermute | solution.py:32
  92.1 13.2 %collective-permute-start.22 = (bf16[4,160,640]{2,1,0:T(8,128)(2,1)S(1)}, bf16[4,160,640]{2,1,0:T(8,128)(2,1)}, u32[]{:S(2)}, u32[]{:S(2)}) collective-permute-start(bf16[4,160,640]{2,1,0:T(8,128)(2,1)S(1)} %collective-permute-done.21.refs_8_), channel_id=1, source_target_pairs={{0,8},{8,0},{16,24},{24,16},{32,40},{40,32},{48,56},{56,48},{64,72... | collective-permute-start | bytes 2457608 | tf_op jit(solution)/shard_map/ppermute | solution.py:32
  100.6 4.7 %collective-permute-start.20 = (bf16[4,160,640]{2,1,0:T(8,128)(2,1)S(1)}, bf16[4,160,640]{2,1,0:T(8,128)(2,1)}, u32[]{:S(2)}, u32[]{:S(2)}) collective-permute-start(bf16[4,160,640]{2,1,0:T(8,128)(2,1)S(1)} %collective-permute-done.19.refs_6_), channel_id=1, source_target_pairs={{0,8},{8,0},{16,24},{24,16},{32,40},{40,32},{48,56},{56,48},{64,72... | collective-permute-start | bytes 2457608 | tf_op jit(solution)/shard_map/ppermute | solution.py:32
  113.4 10.6 %collective-permute-start.25 = (bf16[2,128,640]{2,1,0:T(8,128)(2,1)S(1)}, bf16[2,128,640]{2,1,0:T(8,128)(2,1)S(1)}, u32[]{:S(2)}, u32[]{:S(2)}) collective-permute-start(bf16[2,128,640]{2,1,0:T(8,128)(2,1)S(1)} %get-tuple-element.39), channel_id=1, source_target_pairs={{0,2},{1,3},{2,4},{3,5},{4,6},{5,7},{6,0},{7,1},{8,10},{9,11},{10,... | collective-permute-start | bytes 983048 | tf_op jit(solution)/shard_map/ppermute | solution.py:48
  114.0 17.9 %collective-permute-start.26 = (bf16[2,128,640]{2,1,0:T(8,128)(2,1)S(1)}, bf16[2,128,640]{2,1,0:T(8,128)(2,1)S(1)}, u32[]{:S(2)}, u32[]{:S(2)}) collective-permute-start(bf16[2,128,640]{2,1,0:T(8,128)(2,1)S(1)} %get-tuple-element.40), channel_id=1, source_target_pairs={{0,6},{1,7},{2,0},{3,1},{4,2},{5,3},{6,4},{7,5},{8,14},{9,15},{10,... | collective-permute-start | bytes 983048 | tf_op jit(solution)/shard_map/ppermute | solution.py:48
  115.6 16.4 %collective-permute-start.27 = (bf16[2,128,640]{2,1,0:T(8,128)(2,1)S(1)}, bf16[2,128,640]{2,1,0:T(8,128)(2,1)S(1)}, u32[]{:S(2)}, u32[]{:S(2)}) collective-permute-start(bf16[2,128,640]{2,1,0:T(8,128)(2,1)S(1)} %get-tuple-element.41), channel_id=1, source_target_pairs={{0,4},{1,5},{2,6},{3,7},{4,0},{5,1},{6,2},{7,3},{8,12},{9,13},{10,... | collective-permute-start | bytes 983048 | tf_op jit(solution)/shard_map/ppermute | solution.py:48
  117.2 16.6 %collective-permute-start.29 = (bf16[4,128,640]{2,1,0:T(8,128)(2,1)S(1)}, bf16[4,128,640]{2,1,0:T(8,128)(2,1)S(1)}, u32[]{:S(2)}, u32[]{:S(2)}) collective-permute-start(bf16[4,128,640]{2,1,0:T(8,128)(2,1)S(1)} %get-tuple-element.43), channel_id=1, source_target_pairs={{0,1},{1,0},{2,3},{3,2},{4,5},{5,4},{6,7},{7,6},{8,9},{9,8},{10,11... | collective-permute-start | bytes 1966088 | tf_op jit(solution)/shard_map/ppermute | solution.py:48
  124.1 8.2 %collective-permute-start.30 = (bf16[4,128,128]{2,1,0:T(8,128)(2,1)S(1)}, bf16[4,128,128]{2,1,0:T(8,128)(2,1)S(1)}, u32[]{:S(2)}, u32[]{:S(2)}) collective-permute-start(bf16[4,128,128]{2,1,0:T(8,128)(2,1)S(1)} %copy-done.21), channel_id=1, source_target_pairs={{0,192},{8,200},{16,208},{24,216},{32,224},{40,232},{48,240},{56,2... | collective-permute-start | bytes 393224 | tf_op jit(solution)/shard_map/ppermute | solution.py:32
  124.6 9.3 %collective-permute-start.31 = (bf16[4,128,128]{2,1,0:T(8,128)(2,1)S(1)}, bf16[4,128,128]{2,1,0:T(8,128)(2,1)S(1)}, u32[]{:S(2)}, u32[]{:S(2)}) collective-permute-start(bf16[4,128,128]{2,1,0:T(8,128)(2,1)S(1)} %copy-done.20), channel_id=1, source_target_pairs={{0,64},{8,72},{16,80},{24,88},{32,96},{40,104},{48,112},{56,120},{... | collective-permute-start | bytes 393224 | tf_op jit(solution)/shard_map/ppermute | solution.py:32
  132.1 6.0 %collective-permute-start.28 = (bf16[128,640]{1,0:T(8,128)(2,1)S(1)}, bf16[128,640]{1,0:T(8,128)(2,1)S(1)}, u32[]{:S(2)}, u32[]{:S(2)}) collective-permute-start(bf16[128,640]{1,0:T(8,128)(2,1)S(1)} %fusion.6), channel_id=1, source_target_pairs={{0,1},{1,0},{2,3},{3,2},{4,5},{5,4},{6,7},{7,6},{8,9},{9,8},{10,11... | collective-permute-start | bytes 491528 | tf_op jit(solution)/shard_map/ppermute | solution.py:48
  132.3 14.5 %collective-permute-start.35 = (bf16[4,128,128]{2,1,0:T(8,128)(2,1)S(1)}, bf16[4,128,128]{2,1,0:T(8,128)(2,1)S(1)}, u32[]{:S(2)}, u32[]{:S(2)}) collective-permute-start(bf16[4,128,128]{2,1,0:T(8,128)(2,1)S(1)} %copy-done.19), channel_id=1, source_target_pairs={{0,128},{8,136},{16,144},{24,152},{32,160},{40,168},{48,176},{56,1... | collective-permute-start | bytes 393224 | tf_op jit(solution)/shard_map/ppermute | solution.py:32
  134.5 7.7 %collective-permute-start.32 = (bf16[128,640]{1,0:T(8,128)(2,1)S(1)}, bf16[128,640]{1,0:T(8,128)(2,1)S(1)}, u32[]{:S(2)}, u32[]{:S(2)}) collective-permute-start(bf16[128,640]{1,0:T(8,128)(2,1)S(1)} %get-tuple-element.81), channel_id=1, source_target_pairs={{0,2},{1,3},{2,4},{3,5},{4,6},{5,7},{6,0},{7,1},{8,10},{9,11},{10,... | collective-permute-start | bytes 491528 | tf_op jit(solution)/shard_map/ppermute | solution.py:48
  136.3 7.9 %collective-permute-start.34 = (bf16[128,640]{1,0:T(8,128)(2,1)S(1)}, bf16[128,640]{1,0:T(8,128)(2,1)S(1)}, u32[]{:S(2)}, u32[]{:S(2)}) collective-permute-start(bf16[128,640]{1,0:T(8,128)(2,1)S(1)} %get-tuple-element.82), channel_id=1, source_target_pairs={{0,4},{1,5},{2,6},{3,7},{4,0},{5,1},{6,2},{7,3},{8,12},{9,13},{10,... | collective-permute-start | bytes 491528 | tf_op jit(solution)/shard_map/ppermute | solution.py:48
  138.1 7.8 %collective-permute-start.33 = (bf16[128,640]{1,0:T(8,128)(2,1)S(1)}, bf16[128,640]{1,0:T(8,128)(2,1)S(1)}, u32[]{:S(2)}, u32[]{:S(2)}) collective-permute-start(bf16[128,640]{1,0:T(8,128)(2,1)S(1)} %get-tuple-element.83), channel_id=1, source_target_pairs={{0,6},{1,7},{2,0},{3,1},{4,2},{5,3},{6,4},{7,5},{8,14},{9,15},{10,... | collective-permute-start | bytes 491528 | tf_op jit(solution)/shard_map/ppermute | solution.py:48
  (27 other events, 241.1 us)

commit v5 on v4

--- a/solution.py
+++ b/solution.py
@@ -554,15 +554,21 @@
     for part in (own_kv, *kv_near):
         kv_parts += [part, shift(part, dc=1)]
     kv_parts += far + [shift(part, dc=1) for part in far]
+    meta, source = plan(device, per, slots, size, cache_len, span_len, block_table, window)
+    half = len(SHIFTS) // 2
+    late, early = [
+        [x[a * x.shape[0] // 2 : (a + 1) * x.shape[0] // 2] for x in meta] for a in range(2)
+    ]
+    far_outs = attend(early, kv_parts, q_parts[half:], log_scale)
+    far_parts = [shift(p, dy=-k) for p, k in zip(far_outs[:half], SHIFTS[half:])]
+    late[0] = after(late[0], far_outs[0])
+    near_outs = attend(late, kv_parts, q_parts[:half], log_scale)
+    parts = [near_outs[0], shift(near_outs[1], dy=-SHIFTS[1])] + far_parts
+    moved = near_outs[half:] + far_outs[half:]
     w_parts = []
-    for part in (w_four, *w_near):
+    for i, part in enumerate((w_four, *w_far)):
+        part = after(part, near_outs[0]) if i < 3 else after(part, *parts[1:])
         w_parts += [part, shift(part, dc=1)]
-    meta, source = plan(device, per, slots, size, cache_len, span_len, block_table, window)
-    outs = attend(meta, kv_parts, q_parts, log_scale)
-    parts, moved = outs[: len(SHIFTS)], outs[len(SHIFTS) :]
-    parts = [parts[0]] + [shift(p, dy=-k) for p, k in zip(parts[1:], SHIFTS[1:])]
-    w_far[2] = after(w_far[2], *parts[1:])
-    w_parts += [w_far[2], shift(w_far[2], dc=1)]
     pieces = piece_table(device, head, heads * width // out_weight.shape[0])
     shares = finish(pieces, [in_hbm(p) for p in parts], w_parts, heads)
     first, second = shares[:NX], shares[NX:]
@@ -577,15 +583,15 @@
     second_far = [
         head_shift(second_sum[r].astype(jnp.bfloat16), dx=SHIFTS[r]) for r in range(1, NX)
     ]
+    first_far = head_shift(first_sum[1].astype(jnp.bfloat16), dz=1)
+    moved[1] = after(moved[1], first_far)
+    new_ck, new_cv = refill(source, ck, cv, moved)
+    second_far = lax.optimization_barrier((*second_far, new_ck, new_cv))[: NX - 1]
     second_out = functools.reduce(
         jnp.add, [p.astype(jnp.float32) for p in second_far], second_sum[0]
     )
-    first_out = first_sum[0] + head_shift(first_sum[1].astype(jnp.bfloat16), dz=1).astype(
-        jnp.float32
-    )
+    first_out = first_sum[0] + first_far.astype(jnp.float32)
     attn_output = jnp.concatenate([first_out, second_out], axis=0).astype(jnp.bfloat16)
-    moved[1] = after(moved[1], second_far[0])
-    new_ck, new_cv = refill(source, ck, cv, moved)
     return (
         attn_output,
         new_ck.reshape(cache_keys.shape),

time: 150 us -> 166 us (1.11); the launches traced: 151 us -> 163 us
  local copies, waits for them, and re-layouts: 3.75 us -> 8.86 us
  waiting for transfers between devices: 47.2 us -> 50.9 us
  starting transfers between devices: 53.4 us -> 55.8 us
  Pallas kernels: 31.5 us -> 33.7 us
    ppermute x28, waiting for transfers between devices: 27.4 us -> 41.8 us  [shift(): return lax.ppermute(value, 'blk', blk_perm(dy, dz, dc))]
    ppermute x8, waiting for transfers between devices: 19.8 us -> 9.07 us  [head_shift(): return lax.ppermute(value, 'head', pairs)]
    slice x0 -> x10, local copies, waits for them, and re-layouts: none -> 5.2 us  [shards(): x[a * x.shape[0] // 2:(a + 1) * x.shape[0] // 2]]
    pallas_call x1 -> x2, Pallas kernels: 19.5 us -> 21.8 us  [attend(): pl.pallas_call(functools.partial(attend_kernel, log_scale, nkv, nq), out_...]
  transfers between devices with their start and end apart: 36 -> 36, of which waited for: 13 -> 14; matrix products, arithmetic and copies ran while one was open for 10% -> 11% of each run, Pallas kernels for 14% -> 16%
where the time goes in v5:
time: 166 us; the launch traced here: 163 us
  starting transfers between devices  55.8 us (34%)
  waiting for transfers between devices  50.9 us (31%)
  Pallas kernels  33.7 us (20%)
  other arithmetic  12.2 us (7%)
  local copies, waits for them, and re-layouts  8.86 us (5%)
    ppermute x28, starting transfers between devices, shift(): return lax.ppermute(value, 'blk', blk_perm(dy, dz, dc))  47.3 us
    ppermute x28, waiting for transfers between devices, shift(): return lax.ppermute(value, 'blk', blk_perm(dy, dz, dc))  41.8 us
    pallas_call x2, Pallas kernels, attend(): pl.pallas_call(functools.partial(attend_kernel, log_scale, nkv, nq), out_...  21.8 us
    ppermute x8, waiting for transfers between devices, head_shift(): return lax.ppermute(value, 'head', pairs)  9.07 us
    ppermute x8, starting transfers between devices, head_shift(): return lax.ppermute(value, 'head', pairs)  8.51 us
    pallas_call x1, Pallas kernels, finish(): pl.pallas_call(functools.partial(finish_kernel, heads, nparts, nw), out_s...  7.22 us
    slice x10, local copies, waits for them, and re-layouts, shards(): x[a * x.shape[0] // 2:(a + 1) * x.shape[0] // 2]  5.2 us
    reduce_sum x2, other arithmetic, table_entry(): return jnp.sum(jnp.where(match, block_table[None], 0), axis=(1, 2))  3.89 us
  transfers between devices with their start and end apart: 36, of which 14 were waited for; matrix products, arithmetic and copies ran while one was open for 11% of the time, Pallas kernels for 16%

profile of v5, /device:TPU:6, one launch (start us, length us, event | category | flops | bytes accessed | tf_op | source)
XLA Modules:
  0.0 162.6 jit_solution(2150249982041520327)
XLA Ops:
  0.7 6.4 %collective-permute-start.1 = (bf16[160,640]{1,0:T(8,128)(2,1)}, bf16[160,640]{1,0:T(8,128)(2,1)S(1)}, u32[]{:S(2)}, u32[]{:S(2)}) collective-permute-start(bf16[160,640]{1,0:T(8,128)(2,1)} %param.17), channel_id=1, source_target_pairs={{0,48},{8,56},{16,0},{24,8},{32,16},{40,24},{48,32},{56,40},{64,11... | collective-permute-start | bytes 614408 | tf_op jit(solution)/shard_map/ppermute | solution.py:32
  7.0 3.8 %collective-permute-start.2 = (bf16[160,640]{1,0:T(8,128)(2,1)}, bf16[160,640]{1,0:T(8,128)(2,1)S(1)}, u32[]{:S(2)}, u32[]{:S(2)}) collective-permute-start(bf16[160,640]{1,0:T(8,128)(2,1)} %param.17), channel_id=1, source_target_pairs={{0,32},{8,40},{16,48},{24,56},{32,0},{40,8},{48,16},{56,24},{64,96... | collective-permute-start | bytes 614408 | tf_op jit(solution)/shard_map/ppermute | solution.py:32
  10.8 3.0 %collective-permute-start.4 = (bf16[5,256,128]{2,1,0:T(8,128)(2,1)}, bf16[5,256,128]{2,1,0:T(8,128)(2,1)S(1)}, u32[]{:S(2)}, u32[]{:S(2)}) collective-permute-start(bf16[5,256,128]{2,1,0:T(8,128)(2,1)} %bitcast.47), channel_id=1, source_target_pairs={{0,192},{8,200},{16,208},{24,216},{32,224},{40,232},{48,240},{56,2... | collective-permute-start | bytes 983048 | tf_op jit(solution)/shard_map/ppermute | solution.py:32
  17.2 2.6 %select_reduce_fusion.1 = (s32[48]{0:T(128)S(1)}, s32[48]{0:T(128)S(1)}) fusion(s32[8,64]{1,0:T(8,128)} %param.20, pred[48,64]{1,0:T(8,128)(4,1)S(1)} %iota_compare_fusion.2, pred[48,8]{1,0:T(8,128)(4,1)S(1)} %copy.19, s32[8,64]{1,0:T(8,128)S(1)} %add_add_fusion, pred[8,64]{1,0:T(8,128)(4,1)S(1)} %iota_compare_fusion.8, s32[48]{0:T(128)S(1)} %add.596), kind=kLoop, calls=%fused_computation.13 | loop fusion | flops 171936 | bytes 8640 | tf_op jit(solution)/shard_map/reduce_sum | solution.py:75
  23.5 1.8 %pack.1.refs_0_ = bf16[12,128,128]{2,1,0:T(8,128)(2,1)} custom-call(bf16[6,128,128]{2,1,0:T(8,128)(2,1)} %bitcast.37, bf16[6,128,128]{2,1,0:T(8,128)(2,1)} %bitcast.39, bf16[2,128,128]{2,1,0:T(8,128)(2,1)} %bitcast.45, bf16[2,128,128]{2,1,0:T(8,128)(2,1)} %bitcast.46), custom_call_target="tpu_custom_call" | custom-call | tf_op jit(solution)/shard_map/pack/pallas_call | solution.py:100
  25.4 5.0 %collective-permute-start.8 = (bf16[12,128,128]{2,1,0:T(8,128)(2,1)}, bf16[12,128,128]{2,1,0:T(8,128)(2,1)S(1)}, u32[]{:S(2)}, u32[]{:S(2)}) collective-permute-start(bf16[12,128,128]{2,1,0:T(8,128)(2,1)} %pack.1.refs_0_), channel_id=1, source_target_pairs={{0,48},{8,56},{16,0},{24,8},{32,16},{40,24},{48,32},{56,40},{64,11... | collective-permute-start | bytes 1179656 | tf_op jit(solution)/shard_map/ppermute | solution.py:32
  32.0 3.3 %collective-permute-start.14 = (bf16[5,256,128]{2,1,0:T(8,128)(2,1)S(1)}, bf16[5,256,128]{2,1,0:T(8,128)(2,1)S(1)}, u32[]{:S(2)}, u32[]{:S(2)}) collective-permute-start(bf16[5,256,128]{2,1,0:T(8,128)(2,1)S(1)} %bitcast.50), channel_id=1, source_target_pairs={{0,128},{8,136},{16,144},{24,152},{32,160},{40,168},{48,176},{56,1... | collective-permute-start | bytes 983048 | tf_op jit(solution)/shard_map/ppermute | solution.py:32
  35.3 12.0 %collective-permute-done.8.refs_4_ = bf16[12,128,128]{2,1,0:T(8,128)(2,1)S(1)} collective-permute-done((bf16[12,128,128]{2,1,0:T(8,128)(2,1)}, bf16[12,128,128]{2,1,0:T(8,128)(2,1)S(1)}, u32[]{:S(2)}, u32[]{:S(2)}) %collective-permute-start.8) | collective-permute-done | bytes 393248 | tf_op jit(solution)/shard_map/ppermute | solution.py:32
  47.3 1.5 collective-permute-start.11
  51.9 4.3 %collective-permute-start.21 = (bf16[4,160,640]{2,1,0:T(8,128)(2,1)S(1)}, bf16[4,160,640]{2,1,0:T(8,128)(2,1)S(1)}, u32[]{:S(2)}, u32[]{:S(2)}) collective-permute-start(bf16[4,160,640]{2,1,0:T(8,128)(2,1)S(1)} %pad_maximum_fusion.refs_4_), channel_id=1, source_target_pairs={{0,192},{8,200},{16,208},{24,216},{32,224},{40,232},{48,240},{56,2... | collective-permute-start | bytes 2457608 | tf_op jit(solution)/shard_map/ppermute | solution.py:32
  57.3 3.4 %collective-permute-done.10.refs_6_ = bf16[6,128,128]{2,1,0:T(8,128)(2,1)} collective-permute-done((bf16[6,128,128]{2,1,0:T(8,128)(2,1)S(1)}, bf16[6,128,128]{2,1,0:T(8,128)(2,1)}, u32[]{:S(2)}, u32[]{:S(2)}) %collective-permute-start.10) | collective-permute-done | bytes 196640 | tf_op jit(solution)/shard_map/ppermute | solution.py:32
  66.1 12.5 %attend.2 = (bf16[2,656,128]{2,1,0:T(8,128)(2,1)}, bf16[2,656,128]{2,1,0:T(8,128)(2,1)}, bf16[4,128,128]{2,1,0:T(8,128)(2,1)}, bf16[4,128,128]{2,1,0:T(8,128)(2,1)}) custom-call(s32[4]{0:T(128)} %get-tuple-element.117.count, s32[192]{0:T(256)} %slice.85.chosen, s32[4]{0:T(128)} %get-tuple-element.114.edges, s32[192]{0:T(256)} %slice.88.first_key, ...), custom_call_target="tpu_custom_call" | custom-call | flops 5000000000 | bytes 8000000 | tf_op jit(solution)/shard_map/attend/pallas_call | solution.py:273
  78.7 5.4 %collective-permute-start.23 = (bf16[4,160,640]{2,1,0:T(8,128)(2,1)S(1)}, bf16[4,160,640]{2,1,0:T(8,128)(2,1)S(1)}, u32[]{:S(2)}, u32[]{:S(2)}) collective-permute-start(bf16[4,160,640]{2,1,0:T(8,128)(2,1)S(1)} %pad_maximum_fusion.refs_4_), channel_id=1, source_target_pairs={{0,128},{8,136},{16,144},{24,152},{32,160},{40,168},{48,176},{56,1... | collective-permute-start | bytes 2457608 | tf_op jit(solution)/shard_map/ppermute | solution.py:32
  84.2 9.2 %attend.3 = (bf16[2,656,128]{2,1,0:T(8,128)(2,1)}, bf16[2,656,128]{2,1,0:T(8,128)(2,1)}, bf16[4,128,128]{2,1,0:T(8,128)(2,1)}, bf16[4,128,128]{2,1,0:T(8,128)(2,1)}) custom-call(s32[4]{0:T(128)} %get-tuple-element.39.count, s32[192]{0:T(256)} %slice.95.chosen, s32[4]{0:T(128)} %get-tuple-element.113.edges, s32[192]{0:T(256)} %slice.98.first_key, ...), custom_call_target="tpu_custom_call" | custom-call | flops 5000000000 | bytes 8000000 | tf_op jit(solution)/shard_map/attend/pallas_call | solution.py:273
  93.4 2.1 %collective-permute-start.15 = (bf16[2,656,128]{2,1,0:T(8,128)(2,1)}, bf16[2,656,128]{2,1,0:T(8,128)(2,1)}, u32[]{:S(2)}, u32[]{:S(2)}) collective-permute-start(bf16[2,656,128]{2,1,0:T(8,128)(2,1)} %get-tuple-element.41), channel_id=1, source_target_pairs={{0,192},{8,200},{16,208},{24,216},{32,224},{40,232},{48,240},{56,2... | collective-permute-start | bytes 1007624 | tf_op jit(solution)/shard_map/ppermute | solution.py:32
  95.6 14.9 %collective-permute-done.15.refs_1_ = bf16[2,656,128]{2,1,0:T(8,128)(2,1)} collective-permute-done((bf16[2,656,128]{2,1,0:T(8,128)(2,1)}, bf16[2,656,128]{2,1,0:T(8,128)(2,1)}, u32[]{:S(2)}, u32[]{:S(2)}) %collective-permute-start.15) | collective-permute-done | bytes 335904 | tf_op jit(solution)/shard_map/ppermute | solution.py:32
  110.5 2.8 %collective-permute-done.17.refs_3_ = bf16[2,656,128]{2,1,0:T(8,128)(2,1)} collective-permute-done((bf16[2,656,128]{2,1,0:T(8,128)(2,1)}, bf16[2,656,128]{2,1,0:T(8,128)(2,1)}, u32[]{:S(2)}, u32[]{:S(2)}) %collective-permute-start.17) | collective-permute-done | bytes 335904 | tf_op jit(solution)/shard_map/ppermute | solution.py:32
  113.3 1.8 %collective-permute-done.16.refs_2_ = bf16[2,656,128]{2,1,0:T(8,128)(2,1)} collective-permute-done((bf16[2,656,128]{2,1,0:T(8,128)(2,1)}, bf16[2,656,128]{2,1,0:T(8,128)(2,1)}, u32[]{:S(2)}, u32[]{:S(2)}) %collective-permute-start.16) | collective-permute-done | bytes 335904 | tf_op jit(solution)/shard_map/ppermute | solution.py:32
  115.8 1.8 %collective-permute-done.24.refs_11_ = bf16[4,160,640]{2,1,0:T(8,128)(2,1)} collective-permute-done((bf16[4,160,640]{2,1,0:T(8,128)(2,1)S(1)}, bf16[4,160,640]{2,1,0:T(8,128)(2,1)}, u32[]{:S(2)}, u32[]{:S(2)}) %collective-permute-start.24) | collective-permute-done | bytes 819232 | tf_op jit(solution)/shard_map/ppermute | solution.py:32
  117.6 7.2 %finish.1 = (bf16[2,128,640]{2,1,0:T(8,128)(2,1)S(1)}, bf16[2,128,640]{2,1,0:T(8,128)(2,1)S(1)}, bf16[2,128,640]{2,1,0:T(8,128)(2,1)S(1)}, bf16[2,128,640]{2,1,0...) custom-call(s32[32]{0:T(128)S(1)} %fusion.30.pieces, ...), custom_call_target="tpu_custom_call" | custom-call | flops 2000000000 | bytes 12000000 | tf_op jit(solution)/shard_map/finish/pallas_call | solution.py:371
  125.4 1.5 collective-permute-start.26
  127.0 1.4 collective-permute-start.27
  128.4 1.3 select_reduce_fusion
  130.0 5.5 %collective-permute-done.25 = bf16[2,128,640]{2,1,0:T(8,128)(2,1)S(1)} collective-permute-done((bf16[2,128,640]{2,1,0:T(8,128)(2,1)S(1)}, bf16[2,128,640]{2,1,0:T(8,128)(2,1)S(1)}, u32[]{:S(2)}, u32[]{:S(2)}) %collective-permute-start.25) | collective-permute-done | bytes 327712 | tf_op jit(solution)/shard_map/ppermute | solution.py:48
  135.5 4.3 %collective-permute-start.30 = (bf16[4,128,128]{2,1,0:T(8,128)(2,1)S(1)}, bf16[4,128,128]{2,1,0:T(8,128)(2,1)S(1)}, u32[]{:S(2)}, u32[]{:S(2)}) collective-permute-start(bf16[4,128,128]{2,1,0:T(8,128)(2,1)S(1)} %copy-done.16), channel_id=1, source_target_pairs={{0,192},{8,200},{16,208},{24,216},{32,224},{40,232},{48,240},{56,2... | collective-permute-start | bytes 393224 | tf_op jit(solution)/shard_map/ppermute | solution.py:32
  139.7 3.4 %collective-permute-done.26 = bf16[2,128,640]{2,1,0:T(8,128)(2,1)S(1)} collective-permute-done((bf16[2,128,640]{2,1,0:T(8,128)(2,1)S(1)}, bf16[2,128,640]{2,1,0:T(8,128)(2,1)S(1)}, u32[]{:S(2)}, u32[]{:S(2)}) %collective-permute-start.26) | collective-permute-done | bytes 327712 | tf_op jit(solution)/shard_map/ppermute | solution.py:48
  143.9 2.0 %collective-permute-start.31 = (bf16[4,128,128]{2,1,0:T(8,128)(2,1)S(1)}, bf16[4,128,128]{2,1,0:T(8,128)(2,1)S(1)}, u32[]{:S(2)}, u32[]{:S(2)}) collective-permute-start(bf16[4,128,128]{2,1,0:T(8,128)(2,1)S(1)} %copy-done.15), channel_id=1, source_target_pairs={{0,64},{8,72},{16,80},{24,88},{32,96},{40,104},{48,112},{56,120},{... | collective-permute-start | bytes 393224 | tf_op jit(solution)/shard_map/ppermute | solution.py:32
  145.9 3.8 %collective-permute-start.35 = (bf16[4,128,128]{2,1,0:T(8,128)(2,1)S(1)}, bf16[4,128,128]{2,1,0:T(8,128)(2,1)S(1)}, u32[]{:S(2)}, u32[]{:S(2)}) collective-permute-start(bf16[4,128,128]{2,1,0:T(8,128)(2,1)S(1)} %copy-done.14), channel_id=1, source_target_pairs={{0,128},{8,136},{16,144},{24,152},{32,160},{40,168},{48,176},{56,1... | collective-permute-start | bytes 393224 | tf_op jit(solution)/shard_map/ppermute | solution.py:32
  149.9 2.6 %collective-permute-done.31.refs_2_ = bf16[4,128,128]{2,1,0:T(8,128)(2,1)S(1)} collective-permute-done((bf16[4,128,128]{2,1,0:T(8,128)(2,1)S(1)}, bf16[4,128,128]{2,1,0:T(8,128)(2,1)S(1)}, u32[]{:S(2)}, u32[]{:S(2)}) %collective-permute-start.31) | collective-permute-done | bytes 131104 | tf_op jit(solution)/shard_map/ppermute | solution.py:32
  153.2 1.6 collective-permute-start.34
  154.8 3.2 %collective-permute-start.32 = (bf16[128,640]{1,0:T(8,128)(2,1)S(1)}, bf16[128,640]{1,0:T(8,128)(2,1)S(1)}, u32[]{:S(2)}, u32[]{:S(2)}) collective-permute-start(bf16[128,640]{1,0:T(8,128)(2,1)S(1)} %get-tuple-element.97), channel_id=1, source_target_pairs={{0,2},{1,3},{2,4},{3,5},{4,6},{5,7},{6,0},{7,1},{8,10},{9,11},{10,... | collective-permute-start | bytes 491528 | tf_op jit(solution)/shard_map/ppermute | solution.py:48
  158.7 2.9 %refill.1 = (bf16[6,128,128]{2,1,0:T(8,128)(2,1)}, bf16[6,128,128]{2,1,0:T(8,128)(2,1)}) custom-call(s32[2]{0:T(128)} %compare_select_fusion.25.source, bf16[6,128,128]{2,1,0:T(8,128)(2,1)} %bitcast.38, bf16[6,128,128]{2,1,0:T(8,128)(2,1)} %bitcast.40, bf16[4,128,128]{2,1,0:T(8,128)(2,1)} %get-tuple-element.60.refs_0_, bf16[4,128,128]{2,1,0:T(8,128)(2,1)} %copy-done.1, ...), custom_call_target="tpu_custom_call" | custom-call | tf_op jit(solution)/shard_map/refill/pallas_call | solution.py:428
  (163 shorter events, 23.0 us)
Async XLA Ops:
  0.7 24.7 %collective-permute-start.1 = (bf16[160,640]{1,0:T(8,128)(2,1)}, bf16[160,640]{1,0:T(8,128)(2,1)S(1)}, u32[]{:S(2)}, u32[]{:S(2)}) collective-permute-start(bf16[160,640]{1,0:T(8,128)(2,1)} %param.17), channel_id=1, source_target_pairs={{0,48},{8,56},{16,0},{24,8},{32,16},{40,24},{48,32},{56,40},{64,11... | collective-permute-start | bytes 614408 | tf_op jit(solution)/shard_map/ppermute | solution.py:32
  7.0 18.4 %collective-permute-start = (bf16[160,640]{1,0:T(8,128)(2,1)}, bf16[160,640]{1,0:T(8,128)(2,1)S(1)}, u32[]{:S(2)}, u32[]{:S(2)}) collective-permute-start(bf16[160,640]{1,0:T(8,128)(2,1)} %param.17), channel_id=1, source_target_pairs={{0,16},{8,24},{16,32},{24,40},{32,48},{40,56},{48,0},{56,8},{64,80... | collective-permute-start | bytes 614408 | tf_op jit(solution)/shard_map/ppermute | solution.py:32
  7.0 18.4 %collective-permute-start.2 = (bf16[160,640]{1,0:T(8,128)(2,1)}, bf16[160,640]{1,0:T(8,128)(2,1)S(1)}, u32[]{:S(2)}, u32[]{:S(2)}) collective-permute-start(bf16[160,640]{1,0:T(8,128)(2,1)} %param.17), channel_id=1, source_target_pairs={{0,32},{8,40},{16,48},{24,56},{32,0},{40,8},{48,16},{56,24},{64,96... | collective-permute-start | bytes 614408 | tf_op jit(solution)/shard_map/ppermute | solution.py:32
  10.8 14.5 %collective-permute-start.4 = (bf16[5,256,128]{2,1,0:T(8,128)(2,1)}, bf16[5,256,128]{2,1,0:T(8,128)(2,1)S(1)}, u32[]{:S(2)}, u32[]{:S(2)}) collective-permute-start(bf16[5,256,128]{2,1,0:T(8,128)(2,1)} %bitcast.47), channel_id=1, source_target_pairs={{0,192},{8,200},{16,208},{24,216},{32,224},{40,232},{48,240},{56,2... | collective-permute-start | bytes 983048 | tf_op jit(solution)/shard_map/ppermute | solution.py:32
  13.9 11.6 %collective-permute-start.3 = (bf16[5,256,128]{2,1,0:T(8,128)(2,1)}, bf16[5,256,128]{2,1,0:T(8,128)(2,1)S(1)}, u32[]{:S(2)}, u32[]{:S(2)}) collective-permute-start(bf16[5,256,128]{2,1,0:T(8,128)(2,1)} %bitcast.48), channel_id=1, source_target_pairs={{0,64},{8,72},{16,80},{24,88},{32,96},{40,104},{48,112},{56,120},{... | collective-permute-start | bytes 983048 | tf_op jit(solution)/shard_map/ppermute | solution.py:32
  25.4 21.9 %collective-permute-start.8 = (bf16[12,128,128]{2,1,0:T(8,128)(2,1)}, bf16[12,128,128]{2,1,0:T(8,128)(2,1)S(1)}, u32[]{:S(2)}, u32[]{:S(2)}) collective-permute-start(bf16[12,128,128]{2,1,0:T(8,128)(2,1)} %pack.1.refs_0_), channel_id=1, source_target_pairs={{0,48},{8,56},{16,0},{24,8},{32,16},{40,24},{48,32},{56,40},{64,11... | collective-permute-start | bytes 1179656 | tf_op jit(solution)/shard_map/ppermute | solution.py:32
  30.4 19.1 %collective-permute-start.6 = (bf16[12,128,128]{2,1,0:T(8,128)(2,1)}, bf16[12,128,128]{2,1,0:T(8,128)(2,1)S(1)}, u32[]{:S(2)}, u32[]{:S(2)}) collective-permute-start(bf16[12,128,128]{2,1,0:T(8,128)(2,1)} %pack.1.refs_0_), channel_id=1, source_target_pairs={{0,16},{8,24},{16,32},{24,40},{32,48},{40,56},{48,0},{56,8},{64,80... | collective-permute-start | bytes 1179656 | tf_op jit(solution)/shard_map/ppermute | solution.py:32
  31.8 24.5 %collective-permute-start.5 = (bf16[12,128,128]{2,1,0:T(8,128)(2,1)}, bf16[12,128,128]{2,1,0:T(8,128)(2,1)S(1)}, u32[]{:S(2)}, u32[]{:S(2)}) collective-permute-start(bf16[12,128,128]{2,1,0:T(8,128)(2,1)} %pack.1.refs_0_), channel_id=1, source_target_pairs={{0,8},{8,0},{16,24},{24,16},{32,40},{40,32},{48,56},{56,48},{64,72... | collective-permute-start | bytes 1179656 | tf_op jit(solution)/shard_map/ppermute | solution.py:32
  32.0 19.2 %collective-permute-start.14 = (bf16[5,256,128]{2,1,0:T(8,128)(2,1)S(1)}, bf16[5,256,128]{2,1,0:T(8,128)(2,1)S(1)}, u32[]{:S(2)}, u32[]{:S(2)}) collective-permute-start(bf16[5,256,128]{2,1,0:T(8,128)(2,1)S(1)} %bitcast.50), channel_id=1, source_target_pairs={{0,128},{8,136},{16,144},{24,152},{32,160},{40,168},{48,176},{56,1... | collective-permute-start | bytes 983048 | tf_op jit(solution)/shard_map/ppermute | solution.py:32
  47.3 9.9 %collective-permute-start.11 = (bf16[6,128,128]{2,1,0:T(8,128)(2,1)S(1)}, bf16[6,128,128]{2,1,0:T(8,128)(2,1)S(1)}, u32[]{:S(2)}, u32[]{:S(2)}) collective-permute-start(bf16[6,128,128]{2,1,0:T(8,128)(2,1)S(1)} %slice.109), channel_id=1, source_target_pairs={{0,48},{8,56},{16,0},{24,8},{32,16},{40,24},{48,32},{56,40},{64,11... | collective-permute-start | bytes 589832 | tf_op jit(solution)/shard_map/ppermute | solution.py:32
  49.5 11.2 %collective-permute-start.10 = (bf16[6,128,128]{2,1,0:T(8,128)(2,1)S(1)}, bf16[6,128,128]{2,1,0:T(8,128)(2,1)}, u32[]{:S(2)}, u32[]{:S(2)}) collective-permute-start(bf16[6,128,128]{2,1,0:T(8,128)(2,1)S(1)} %slice.108), channel_id=1, source_target_pairs={{0,16},{8,24},{16,32},{24,40},{32,48},{40,56},{48,0},{56,8},{64,80... | collective-permute-start | bytes 589832 | tf_op jit(solution)/shard_map/ppermute | solution.py:32
  51.9 26.8 %collective-permute-start.21 = (bf16[4,160,640]{2,1,0:T(8,128)(2,1)S(1)}, bf16[4,160,640]{2,1,0:T(8,128)(2,1)S(1)}, u32[]{:S(2)}, u32[]{:S(2)}) collective-permute-start(bf16[4,160,640]{2,1,0:T(8,128)(2,1)S(1)} %pad_maximum_fusion.refs_4_), channel_id=1, source_target_pairs={{0,192},{8,200},{16,208},{24,216},{32,224},{40,232},{48,240},{56,2... | collective-permute-start | bytes 2457608 | tf_op jit(solution)/shard_map/ppermute | solution.py:32
  56.2 22.5 %collective-permute-start.19 = (bf16[4,160,640]{2,1,0:T(8,128)(2,1)S(1)}, bf16[4,160,640]{2,1,0:T(8,128)(2,1)S(1)}, u32[]{:S(2)}, u32[]{:S(2)}) collective-permute-start(bf16[4,160,640]{2,1,0:T(8,128)(2,1)S(1)} %pad_maximum_fusion.refs_4_), channel_id=1, source_target_pairs={{0,64},{8,72},{16,80},{24,88},{32,96},{40,104},{48,112},{56,120},{... | collective-permute-start | bytes 2457608 | tf_op jit(solution)/shard_map/ppermute | solution.py:32
  56.2 8.5 %collective-permute-start.9 = (bf16[12,128,128]{2,1,0:T(8,128)(2,1)S(1)}, bf16[12,128,128]{2,1,0:T(8,128)(2,1)}, u32[]{:S(2)}, u32[]{:S(2)}) collective-permute-start(bf16[12,128,128]{2,1,0:T(8,128)(2,1)S(1)} %collective-permute-done.8.refs_4_), channel_id=1, source_target_pairs={{0,8},{8,0},{16,24},{24,16},{32,40},{40,32},{48,56},{56,48},{64,72... | collective-permute-start | bytes 1179656 | tf_op jit(solution)/shard_map/ppermute | solution.py:32
  57.2 8.2 %collective-permute-start.7 = (bf16[12,128,128]{2,1,0:T(8,128)(2,1)S(1)}, bf16[12,128,128]{2,1,0:T(8,128)(2,1)}, u32[]{:S(2)}, u32[]{:S(2)}) collective-permute-start(bf16[12,128,128]{2,1,0:T(8,128)(2,1)S(1)} %collective-permute-done.6.refs_2_), channel_id=1, source_target_pairs={{0,8},{8,0},{16,24},{24,16},{32,40},{40,32},{48,56},{56,48},{64,72... | collective-permute-start | bytes 1179656 | tf_op jit(solution)/shard_map/ppermute | solution.py:32
  78.6 36.5 %collective-permute-start.16 = (bf16[2,656,128]{2,1,0:T(8,128)(2,1)}, bf16[2,656,128]{2,1,0:T(8,128)(2,1)}, u32[]{:S(2)}, u32[]{:S(2)}) collective-permute-start(bf16[2,656,128]{2,1,0:T(8,128)(2,1)} %get-tuple-element.38), channel_id=1, source_target_pairs={{0,64},{8,72},{16,80},{24,88},{32,96},{40,104},{48,112},{56,120},{... | collective-permute-start | bytes 1007624 | tf_op jit(solution)/shard_map/ppermute | solution.py:32
  78.7 36.4 %collective-permute-start.23 = (bf16[4,160,640]{2,1,0:T(8,128)(2,1)S(1)}, bf16[4,160,640]{2,1,0:T(8,128)(2,1)S(1)}, u32[]{:S(2)}, u32[]{:S(2)}) collective-permute-start(bf16[4,160,640]{2,1,0:T(8,128)(2,1)S(1)} %pad_maximum_fusion.refs_4_), channel_id=1, source_target_pairs={{0,128},{8,136},{16,144},{24,152},{32,160},{40,168},{48,176},{56,1... | collective-permute-start | bytes 2457608 | tf_op jit(solution)/shard_map/ppermute | solution.py:32
  93.4 17.1 %collective-permute-start.15 = (bf16[2,656,128]{2,1,0:T(8,128)(2,1)}, bf16[2,656,128]{2,1,0:T(8,128)(2,1)}, u32[]{:S(2)}, u32[]{:S(2)}) collective-permute-start(bf16[2,656,128]{2,1,0:T(8,128)(2,1)} %get-tuple-element.41), channel_id=1, source_target_pairs={{0,192},{8,200},{16,208},{24,216},{32,224},{40,232},{48,240},{56,2... | collective-permute-start | bytes 1007624 | tf_op jit(solution)/shard_map/ppermute | solution.py:32
  95.5 17.8 %collective-permute-start.17 = (bf16[2,656,128]{2,1,0:T(8,128)(2,1)}, bf16[2,656,128]{2,1,0:T(8,128)(2,1)}, u32[]{:S(2)}, u32[]{:S(2)}) collective-permute-start(bf16[2,656,128]{2,1,0:T(8,128)(2,1)} %get-tuple-element.42), channel_id=1, source_target_pairs={{0,128},{8,136},{16,144},{24,152},{32,160},{40,168},{48,176},{56,1... | collective-permute-start | bytes 1007624 | tf_op jit(solution)/shard_map/ppermute | solution.py:32
  95.6 19.9 %collective-permute-start.18 = (bf16[4,160,640]{2,1,0:T(8,128)(2,1)S(1)}, bf16[4,160,640]{2,1,0:T(8,128)(2,1)}, u32[]{:S(2)}, u32[]{:S(2)}) collective-permute-start(bf16[4,160,640]{2,1,0:T(8,128)(2,1)S(1)} %pad_maximum_fusion.refs_4_), channel_id=1, source_target_pairs={{0,8},{8,0},{16,24},{24,16},{32,40},{40,32},{48,56},{56,48},{64,72... | collective-permute-start | bytes 2457608 | tf_op jit(solution)/shard_map/ppermute | solution.py:32
  110.5 5.1 %collective-permute-start.22 = (bf16[4,160,640]{2,1,0:T(8,128)(2,1)S(1)}, bf16[4,160,640]{2,1,0:T(8,128)(2,1)}, u32[]{:S(2)}, u32[]{:S(2)}) collective-permute-start(bf16[4,160,640]{2,1,0:T(8,128)(2,1)S(1)} %collective-permute-done.21.refs_8_), channel_id=1, source_target_pairs={{0,8},{8,0},{16,24},{24,16},{32,40},{40,32},{48,56},{56,48},{64,72... | collective-permute-start | bytes 2457608 | tf_op jit(solution)/shard_map/ppermute | solution.py:32
  124.8 10.6 %collective-permute-start.25 = (bf16[2,128,640]{2,1,0:T(8,128)(2,1)S(1)}, bf16[2,128,640]{2,1,0:T(8,128)(2,1)S(1)}, u32[]{:S(2)}, u32[]{:S(2)}) collective-permute-start(bf16[2,128,640]{2,1,0:T(8,128)(2,1)S(1)} %get-tuple-element.50), channel_id=1, source_target_pairs={{0,2},{1,3},{2,4},{3,5},{4,6},{5,7},{6,0},{7,1},{8,10},{9,11},{10,... | collective-permute-start | bytes 983048 | tf_op jit(solution)/shard_map/ppermute | solution.py:48
  125.4 17.7 %collective-permute-start.26 = (bf16[2,128,640]{2,1,0:T(8,128)(2,1)S(1)}, bf16[2,128,640]{2,1,0:T(8,128)(2,1)S(1)}, u32[]{:S(2)}, u32[]{:S(2)}) collective-permute-start(bf16[2,128,640]{2,1,0:T(8,128)(2,1)S(1)} %get-tuple-element.51), channel_id=1, source_target_pairs={{0,6},{1,7},{2,0},{3,1},{4,2},{5,3},{6,4},{7,5},{8,14},{9,15},{10,... | collective-permute-start | bytes 983048 | tf_op jit(solution)/shard_map/ppermute | solution.py:48
  127.0 16.2 %collective-permute-start.27 = (bf16[2,128,640]{2,1,0:T(8,128)(2,1)S(1)}, bf16[2,128,640]{2,1,0:T(8,128)(2,1)S(1)}, u32[]{:S(2)}, u32[]{:S(2)}) collective-permute-start(bf16[2,128,640]{2,1,0:T(8,128)(2,1)S(1)} %get-tuple-element.52), channel_id=1, source_target_pairs={{0,4},{1,5},{2,6},{3,7},{4,0},{5,1},{6,2},{7,3},{8,12},{9,13},{10,... | collective-permute-start | bytes 983048 | tf_op jit(solution)/shard_map/ppermute | solution.py:48
  129.9 19.9 %collective-permute-start.29 = (bf16[4,128,640]{2,1,0:T(8,128)(2,1)S(1)}, bf16[4,128,640]{2,1,0:T(8,128)(2,1)S(1)}, u32[]{:S(2)}, u32[]{:S(2)}) collective-permute-start(bf16[4,128,640]{2,1,0:T(8,128)(2,1)S(1)} %get-tuple-element.54), channel_id=1, source_target_pairs={{0,1},{1,0},{2,3},{3,2},{4,5},{5,4},{6,7},{7,6},{8,9},{9,8},{10,11... | collective-permute-start | bytes 1966088 | tf_op jit(solution)/shard_map/ppermute | solution.py:48
  135.5 10.5 %collective-permute-start.30 = (bf16[4,128,128]{2,1,0:T(8,128)(2,1)S(1)}, bf16[4,128,128]{2,1,0:T(8,128)(2,1)S(1)}, u32[]{:S(2)}, u32[]{:S(2)}) collective-permute-start(bf16[4,128,128]{2,1,0:T(8,128)(2,1)S(1)} %copy-done.16), channel_id=1, source_target_pairs={{0,192},{8,200},{16,208},{24,216},{32,224},{40,232},{48,240},{56,2... | collective-permute-start | bytes 393224 | tf_op jit(solution)/shard_map/ppermute | solution.py:32
  143.3 6.4 %collective-permute-start.28 = (bf16[128,640]{1,0:T(8,128)(2,1)S(1)}, bf16[128,640]{1,0:T(8,128)(2,1)S(1)}, u32[]{:S(2)}, u32[]{:S(2)}) collective-permute-start(bf16[128,640]{1,0:T(8,128)(2,1)S(1)} %fusion.6), channel_id=1, source_target_pairs={{0,1},{1,0},{2,3},{3,2},{4,5},{5,4},{6,7},{7,6},{8,9},{9,8},{10,11... | collective-permute-start | bytes 491528 | tf_op jit(solution)/shard_map/ppermute | solution.py:48
  143.9 8.6 %collective-permute-start.31 = (bf16[4,128,128]{2,1,0:T(8,128)(2,1)S(1)}, bf16[4,128,128]{2,1,0:T(8,128)(2,1)S(1)}, u32[]{:S(2)}, u32[]{:S(2)}) collective-permute-start(bf16[4,128,128]{2,1,0:T(8,128)(2,1)S(1)} %copy-done.15), channel_id=1, source_target_pairs={{0,64},{8,72},{16,80},{24,88},{32,96},{40,104},{48,112},{56,120},{... | collective-permute-start | bytes 393224 | tf_op jit(solution)/shard_map/ppermute | solution.py:32
  145.9 12.1 %collective-permute-start.35 = (bf16[4,128,128]{2,1,0:T(8,128)(2,1)S(1)}, bf16[4,128,128]{2,1,0:T(8,128)(2,1)S(1)}, u32[]{:S(2)}, u32[]{:S(2)}) collective-permute-start(bf16[4,128,128]{2,1,0:T(8,128)(2,1)S(1)} %copy-done.14), channel_id=1, source_target_pairs={{0,128},{8,136},{16,144},{24,152},{32,160},{40,168},{48,176},{56,1... | collective-permute-start | bytes 393224 | tf_op jit(solution)/shard_map/ppermute | solution.py:32
  153.2 8.4 %collective-permute-start.34 = (bf16[128,640]{1,0:T(8,128)(2,1)S(1)}, bf16[128,640]{1,0:T(8,128)(2,1)S(1)}, u32[]{:S(2)}, u32[]{:S(2)}) collective-permute-start(bf16[128,640]{1,0:T(8,128)(2,1)S(1)} %get-tuple-element.95), channel_id=1, source_target_pairs={{0,4},{1,5},{2,6},{3,7},{4,0},{5,1},{6,2},{7,3},{8,12},{9,13},{10,... | collective-permute-start | bytes 491528 | tf_op jit(solution)/shard_map/ppermute | solution.py:48
  154.8 7.0 %collective-permute-start.33 = (bf16[128,640]{1,0:T(8,128)(2,1)S(1)}, bf16[128,640]{1,0:T(8,128)(2,1)S(1)}, u32[]{:S(2)}, u32[]{:S(2)}) collective-permute-start(bf16[128,640]{1,0:T(8,128)(2,1)S(1)} %get-tuple-element.96), channel_id=1, source_target_pairs={{0,6},{1,7},{2,0},{3,1},{4,2},{5,3},{6,4},{7,5},{8,14},{9,15},{10,... | collective-permute-start | bytes 491528 | tf_op jit(solution)/shard_map/ppermute | solution.py:48
  154.8 7.0 %collective-permute-start.32 = (bf16[128,640]{1,0:T(8,128)(2,1)S(1)}, bf16[128,640]{1,0:T(8,128)(2,1)S(1)}, u32[]{:S(2)}, u32[]{:S(2)}) collective-permute-start(bf16[128,640]{1,0:T(8,128)(2,1)S(1)} %get-tuple-element.97), channel_id=1, source_target_pairs={{0,2},{1,3},{2,4},{3,5},{4,6},{5,7},{6,0},{7,1},{8,10},{9,11},{10,... | collective-permute-start | bytes 491528 | tf_op jit(solution)/shard_map/ppermute | solution.py:48
  (21 other events, 269.0 us)

commit v6 on v5

--- a/solution.py
+++ b/solution.py
@@ -106,6 +106,7 @@
 
 def attend_kernel(
     log_scale,
+    base,
     nkv,
     nq,
     count,
@@ -129,7 +130,7 @@
     size = kv_in[0].shape[1]
     per = rows // size
     wide = heads * size
-    longest = chosen.shape[0] // (nq * per)
+    longest = chosen.shape[0] // count.shape[0]
     loads = []
     for a in range(nkv):
         loads.append(
@@ -150,7 +151,7 @@
     sends = []
     for r in range(nq):
         for s in range(per):
-            at = place(moves[r * per + s])
+            at = place(moves[(base + r) * per + s])
             for side in range(2):
                 sends.append(
                     pltpu.make_async_copy(
@@ -167,7 +168,7 @@
     ones = jnp.ones((2 * size, width), jnp.bfloat16)
 
     def one_block(i, unused):
-        r = i // per
+        r = i // per - base
         s = i % per
         begin = pl.multiple_of(s * size, size)
         query = jnp.concatenate(
@@ -225,7 +226,7 @@
         lax.fori_loop(0, pairs, blend, 0)
         summed = total[:, width:]
         safe = jnp.where(summed > 0.0, summed, 1.0)
-        result[i, 0:wide, :] = (total[:, :width] / safe).astype(jnp.bfloat16)
+        result[i - base * per, 0:wide, :] = (total[:, :width] / safe).astype(jnp.bfloat16)
         line_ids = lax.broadcasted_iota(jnp.int32, (16, width), 0)
         tops = jnp.zeros((16, width), jnp.float32)
         sums = jnp.zeros((16, width), jnp.float32)
@@ -244,12 +245,12 @@
         second = (level - first).astype(jnp.bfloat16).astype(jnp.float32)
         third = level - first - second
         stats = jnp.where(line_ids < heads, first, jnp.where(line_ids < 2 * heads, second, third))
-        result[i, wide : wide + 16, :] = stats.astype(jnp.bfloat16)
+        result[i - base * per, wide : wide + 16, :] = stats.astype(jnp.bfloat16)
         return unused
 
     backs = []
     for r in reversed(range(nq)):
-        lax.fori_loop(r * per, (r + 1) * per, one_block, 0)
+        lax.fori_loop((base + r) * per, (base + r + 1) * per, one_block, 0)
         backs.append(
             pltpu.make_async_copy(result.at[pl.ds(r * per, per)], out_refs[r], out_sem.at[r])
         )
@@ -260,18 +261,18 @@
         back.wait()
 
 
-def attend(meta, kv_parts, q_parts, log_scale):
+def attend(meta, kv_parts, q_parts, log_scale, base):
     _, size, width = kv_parts[0].shape
     heads, rows, _ = q_parts[0].shape
     nkv, nq, per = len(kv_parts), len(q_parts), rows // size
     wide = heads * size
-    longest = meta[1].shape[0] // (nq * per)
+    longest = meta[1].shape[0] // meta[0].shape[0]
     smem = pl.BlockSpec(memory_space=pltpu.SMEM)
     anywhere = pl.BlockSpec(memory_space=pl.ANY)
     parts = jax.ShapeDtypeStruct((per, wide + 16, width), jnp.bfloat16)
     moved = jax.ShapeDtypeStruct((2 * per, size, width), jnp.bfloat16)
     return pl.pallas_call(
-        functools.partial(attend_kernel, log_scale, nkv, nq),
+        functools.partial(attend_kernel, log_scale, base, nkv, nq),
         out_shape=(parts,) * nq + (moved,) * nq,
         in_specs=[smem] * len(meta) + [anywhere] * (nkv + nq),
         out_specs=(anywhere,) * (2 * nq),
@@ -288,7 +289,7 @@
         ],
         compiler_params=pltpu.CompilerParams(vmem_limit_bytes=56 << 20),
         cost_estimate=pl.CostEstimate(
-            flops=5_000_000_000, bytes_accessed=8_000_000, transcendentals=8_000_000
+            flops=3_000_000_000 * nq, bytes_accessed=8_000_000, transcendentals=8_000_000
         ),
         name="attend",
     )(*meta, *kv_parts, *q_parts)
@@ -543,7 +544,6 @@
     kv_near = [shift(own_kv, dz=k) for k in SHIFTS[1:3]]
     q_parts = [own_q, *q_near, shift(after(own_q, *q_near), dy=SHIFTS[3])]
     w_four = jnp.stack(w_line)
-    w_four = after(w_four, q_parts[3])
     w_near = [shift(w_four, dy=k) for k in SHIFTS[1:3]]
     far = [
         shift(kv_near[0][:slots], dz=SHIFTS[1]),
@@ -555,16 +555,15 @@
         kv_parts += [part, shift(part, dc=1)]
     kv_parts += far + [shift(part, dc=1) for part in far]
     meta, source = plan(device, per, slots, size, cache_len, span_len, block_table, window)
-    half = len(SHIFTS) // 2
-    late, early = [
-        [x[a * x.shape[0] // 2 : (a + 1) * x.shape[0] // 2] for x in meta] for a in range(2)
-    ]
-    far_outs = attend(early, kv_parts, q_parts[half:], log_scale)
-    far_parts = [shift(p, dy=-k) for p, k in zip(far_outs[:half], SHIFTS[half:])]
-    late[0] = after(late[0], far_outs[0])
-    near_outs = attend(late, kv_parts, q_parts[:half], log_scale)
-    parts = [near_outs[0], shift(near_outs[1], dy=-SHIFTS[1])] + far_parts
-    moved = near_outs[half:] + far_outs[half:]
+    near = len(SHIFTS) - 1
+    early = (after(meta[0], *w_near), *meta[1:])
+    far_outs = attend(early, kv_parts, q_parts[near:], log_scale, near)
+    far_parts = [shift(far_outs[0], dy=-SHIFTS[near])]
+    late = (after(meta[0], far_outs[0]), *meta[1:])
+    near_outs = attend(late, kv_parts, q_parts[:near], log_scale, 0)
+    parts = [near_outs[0]]
+    parts += [shift(p, dy=-k) for p, k in zip(near_outs[1:near], SHIFTS[1:near])] + far_parts
+    moved = near_outs[near:] + far_outs[1:]
     w_parts = []
     for i, part in enumerate((w_four, *w_far)):
         part = after(part, near_outs[0]) if i < 3 else after(part, *parts[1:])

time: 166 us -> 158 us (0.952)
  the two profiles are of different devices: /device:TPU:6 before, /device:TPU:0 now
where the time goes in v6:
time: 158 us; the launch traced here: 155 us
  starting transfers between devices  55.7 us (35%)
  waiting for transfers between devices  49.6 us (31%)
  Pallas kernels  29.6 us (19%)
  other arithmetic  13.3 us (8%)
  local copies, waits for them, and re-layouts  5.82 us (4%)
    ppermute x28, starting transfers between devices, shift(): return lax.ppermute(value, 'blk', blk_perm(dy, dz, dc))  42.1 us
    ppermute x28, waiting for transfers between devices, shift(): return lax.ppermute(value, 'blk', blk_perm(dy, dz, dc))  39 us
    pallas_call x2, Pallas kernels, attend(): pl.pallas_call(functools.partial(attend_kernel, log_scale, base, nkv, nq)...  17.5 us
    ppermute x8, starting transfers between devices, head_shift(): return lax.ppermute(value, 'head', pairs)  13.5 us
    ppermute x8, waiting for transfers between devices, head_shift(): return lax.ppermute(value, 'head', pairs)  10.7 us
    pallas_call x1, Pallas kernels, finish(): pl.pallas_call(functools.partial(finish_kernel, heads, nparts, nw), out_s...  7.25 us
    reduce_sum x2, other arithmetic, table_entry(): return jnp.sum(jnp.where(match, block_table[None], 0), axis=(1, 2))  3.89 us
  transfers between devices with their start and end apart: 36, of which 17 were waited for; matrix products, arithmetic and copies ran while one was open for 10% of the time, Pallas kernels for 14%

profile of v6, /device:TPU:0, one launch (start us, length us, event | category | flops | bytes accessed | tf_op | source)
XLA Modules:
  0.0 155.1 jit_solution(16482775560404917153)
XLA Ops:
  2.3 5.4 %collective-permute-start.2 = (bf16[160,640]{1,0:T(8,128)(2,1)}, bf16[160,640]{1,0:T(8,128)(2,1)S(1)}, u32[]{:S(2)}, u32[]{:S(2)}) collective-permute-start(bf16[160,640]{1,0:T(8,128)(2,1)} %param.17), channel_id=1, source_target_pairs={{0,32},{8,40},{16,48},{24,56},{32,0},{40,8},{48,16},{56,24},{64,96... | collective-permute-start | bytes 614408 | tf_op jit(solution)/shard_map/ppermute | solution.py:32
  7.6 2.7 %collective-permute-start.1 = (bf16[160,640]{1,0:T(8,128)(2,1)}, bf16[160,640]{1,0:T(8,128)(2,1)S(1)}, u32[]{:S(2)}, u32[]{:S(2)}) collective-permute-start(bf16[160,640]{1,0:T(8,128)(2,1)} %param.17), channel_id=1, source_target_pairs={{0,48},{8,56},{16,0},{24,8},{32,16},{40,24},{48,32},{56,40},{64,11... | collective-permute-start | bytes 614408 | tf_op jit(solution)/shard_map/ppermute | solution.py:32
  10.3 3.0 %collective-permute-start.6 = (bf16[5,256,128]{2,1,0:T(8,128)(2,1)}, bf16[5,256,128]{2,1,0:T(8,128)(2,1)}, u32[]{:S(2)}, u32[]{:S(2)}) collective-permute-start(bf16[5,256,128]{2,1,0:T(8,128)(2,1)} %bitcast.47), channel_id=1, source_target_pairs={{0,192},{8,200},{16,208},{24,216},{32,224},{40,232},{48,240},{56,2... | collective-permute-start | bytes 983048 | tf_op jit(solution)/shard_map/ppermute | solution.py:32
  16.7 2.6 %select_reduce_fusion.1 = (s32[48]{0:T(128)S(1)}, s32[48]{0:T(128)S(1)}) fusion(s32[8,64]{1,0:T(8,128)} %param.20, pred[48,64]{1,0:T(8,128)(4,1)S(1)} %iota_compare_fusion.2, pred[48,8]{1,0:T(8,128)(4,1)S(1)} %copy.19, s32[8,64]{1,0:T(8,128)S(1)} %add_add_fusion, pred[8,64]{1,0:T(8,128)(4,1)S(1)} %iota_compare_fusion.8, s32[48]{0:T(128)S(1)} %add.594), kind=kLoop, calls=%fused_computation.13 | loop fusion | flops 171936 | bytes 8640 | tf_op jit(solution)/shard_map/reduce_sum | solution.py:75
  22.1 1.9 %pack.1.refs_0_ = bf16[12,128,128]{2,1,0:T(8,128)(2,1)} custom-call(bf16[6,128,128]{2,1,0:T(8,128)(2,1)} %bitcast.37, bf16[6,128,128]{2,1,0:T(8,128)(2,1)} %bitcast.39, bf16[2,128,128]{2,1,0:T(8,128)(2,1)} %bitcast.45, bf16[2,128,128]{2,1,0:T(8,128)(2,1)} %bitcast.46), custom_call_target="tpu_custom_call" | custom-call | tf_op jit(solution)/shard_map/pack/pallas_call | solution.py:100
  24.0 2.4 %collective-permute-done.1 = bf16[160,640]{1,0:T(8,128)(2,1)S(1)} collective-permute-done((bf16[160,640]{1,0:T(8,128)(2,1)}, bf16[160,640]{1,0:T(8,128)(2,1)S(1)}, u32[]{:S(2)}, u32[]{:S(2)}) %collective-permute-start.1) | collective-permute-done | bytes 204832 | tf_op jit(solution)/shard_map/ppermute | solution.py:32
  26.6 3.1 %collective-permute-start.4 = (bf16[4,160,640]{2,1,0:T(8,128)(2,1)S(1)}, bf16[4,160,640]{2,1,0:T(8,128)(2,1)S(1)}, u32[]{:S(2)}, u32[]{:S(2)}) collective-permute-start(bf16[4,160,640]{2,1,0:T(8,128)(2,1)S(1)} %pad_maximum_fusion.refs_4_), channel_id=1, source_target_pairs={{0,192},{8,200},{16,208},{24,216},{32,224},{40,232},{48,240},{56,2... | collective-permute-start | bytes 2457608 | tf_op jit(solution)/shard_map/ppermute | solution.py:32
  29.7 3.6 %collective-permute-start.10 = (bf16[12,128,128]{2,1,0:T(8,128)(2,1)S(1)}, bf16[12,128,128]{2,1,0:T(8,128)(2,1)}, u32[]{:S(2)}, u32[]{:S(2)}) collective-permute-start(bf16[12,128,128]{2,1,0:T(8,128)(2,1)S(1)} %copy-done), channel_id=1, source_target_pairs={{0,48},{8,56},{16,0},{24,8},{32,16},{40,24},{48,32},{56,40},{64,11... | collective-permute-start | bytes 1179656 | tf_op jit(solution)/shard_map/ppermute | solution.py:32
  34.3 2.2 %collective-permute-start.16 = (bf16[5,256,128]{2,1,0:T(8,128)(2,1)S(1)}, bf16[5,256,128]{2,1,0:T(8,128)(2,1)S(1)}, u32[]{:S(2)}, u32[]{:S(2)}) collective-permute-start(bf16[5,256,128]{2,1,0:T(8,128)(2,1)S(1)} %bitcast.50), channel_id=1, source_target_pairs={{0,128},{8,136},{16,144},{24,152},{32,160},{40,168},{48,176},{56,1... | collective-permute-start | bytes 983048 | tf_op jit(solution)/shard_map/ppermute | solution.py:32
  36.6 10.3 %collective-permute-done.10.refs_4_ = bf16[12,128,128]{2,1,0:T(8,128)(2,1)} collective-permute-done((bf16[12,128,128]{2,1,0:T(8,128)(2,1)S(1)}, bf16[12,128,128]{2,1,0:T(8,128)(2,1)}, u32[]{:S(2)}, u32[]{:S(2)}) %collective-permute-start.10) | collective-permute-done | bytes 393248 | tf_op jit(solution)/shard_map/ppermute | solution.py:32
  47.8 3.8 %collective-permute-start.13 = (bf16[6,128,128]{2,1,0:T(8,128)(2,1)S(1)}, bf16[6,128,128]{2,1,0:T(8,128)(2,1)S(1)}, u32[]{:S(2)}, u32[]{:S(2)}) collective-permute-start(bf16[6,128,128]{2,1,0:T(8,128)(2,1)S(1)} %slice.37), channel_id=1, source_target_pairs={{0,48},{8,56},{16,0},{24,8},{32,16},{40,24},{48,32},{56,40},{64,11... | collective-permute-start | bytes 589832 | tf_op jit(solution)/shard_map/ppermute | solution.py:32
  52.6 4.2 %collective-permute-done.16.refs_10_ = bf16[5,256,128]{2,1,0:T(8,128)(2,1)S(1)} collective-permute-done((bf16[5,256,128]{2,1,0:T(8,128)(2,1)S(1)}, bf16[5,256,128]{2,1,0:T(8,128)(2,1)S(1)}, u32[]{:S(2)}, u32[]{:S(2)}) %collective-permute-start.16) | collective-permute-done | bytes 327712 | tf_op jit(solution)/shard_map/ppermute | solution.py:32
  57.4 5.5 %collective-permute-done.12.refs_6_ = bf16[6,128,128]{2,1,0:T(8,128)(2,1)S(1)} collective-permute-done((bf16[6,128,128]{2,1,0:T(8,128)(2,1)S(1)}, bf16[6,128,128]{2,1,0:T(8,128)(2,1)S(1)}, u32[]{:S(2)}, u32[]{:S(2)}) %collective-permute-start.12) | collective-permute-done | bytes 196640 | tf_op jit(solution)/shard_map/ppermute | solution.py:32
  65.0 2.1 %collective-permute-start.23 = (bf16[4,160,640]{2,1,0:T(8,128)(2,1)S(1)}, bf16[4,160,640]{2,1,0:T(8,128)(2,1)S(1)}, u32[]{:S(2)}, u32[]{:S(2)}) collective-permute-start(bf16[4,160,640]{2,1,0:T(8,128)(2,1)S(1)} %pad_maximum_fusion.refs_4_), channel_id=1, source_target_pairs={{0,128},{8,136},{16,144},{24,152},{32,160},{40,168},{48,176},{56,1... | collective-permute-start | bytes 2457608 | tf_op jit(solution)/shard_map/ppermute | solution.py:32
  67.8 4.2 %attend.2 = (bf16[2,656,128]{2,1,0:T(8,128)(2,1)}, bf16[4,128,128]{2,1,0:T(8,128)(2,1)}) custom-call(s32[8]{0:T(128)} %copy-done.8, s32[384]{0:T(512)} %get-tuple-element.103.chosen, s32[8]{0:T(128)} %get-tuple-element.86.edges, s32[384]{0:T(512)} %get-tuple-element.102.first_key, s32[8]{0:T(128)} %copy-done.7, s32[8]{0:T(128)} %copy-done.6, ...), custom_call_target="tpu_custom_call" | custom-call | flops 3000000000 | bytes 8000000 | tf_op jit(solution)/shard_map/attend/pallas_call | solution.py:274
  72.0 2.6 %collective-permute-start.19 = (bf16[2,656,128]{2,1,0:T(8,128)(2,1)}, bf16[2,656,128]{2,1,0:T(8,128)(2,1)}, u32[]{:S(2)}, u32[]{:S(2)}) collective-permute-start(bf16[2,656,128]{2,1,0:T(8,128)(2,1)} %get-tuple-element.39), channel_id=1, source_target_pairs={{0,128},{8,136},{16,144},{24,152},{32,160},{40,168},{48,176},{56,1... | collective-permute-start | bytes 1007624 | tf_op jit(solution)/shard_map/ppermute | solution.py:32
  74.6 13.3 %attend.3 = (bf16[2,656,128]{2,1,0:T(8,128)(2,1)}, bf16[2,656,128]{2,1,0:T(8,128)(2,1)}, bf16[2,656,128]{2,1,0:T(8,128)(2,1)}, bf16[4,128,128]{2,1,0:T(8,128)(2,...) custom-call(s32[8]{0:T(128)} %copy-done.8, s32[384]{0:T(512)} %get-tuple-element.103.chosen, ...), custom_call_target="tpu_custom_call" | custom-call | flops 8999999488 | bytes 8000000 | tf_op jit(solution)/shard_map/attend/pallas_call | solution.py:274
  88.0 4.1 %collective-permute-start.17 = (bf16[2,656,128]{2,1,0:T(8,128)(2,1)}, bf16[2,656,128]{2,1,0:T(8,128)(2,1)}, u32[]{:S(2)}, u32[]{:S(2)}) collective-permute-start(bf16[2,656,128]{2,1,0:T(8,128)(2,1)} %get-tuple-element.42), channel_id=1, source_target_pairs={{0,192},{8,200},{16,208},{24,216},{32,224},{40,232},{48,240},{56,2... | collective-permute-start | bytes 1007624 | tf_op jit(solution)/shard_map/ppermute | solution.py:32
  92.3 9.2 %collective-permute-done.17.refs_1_ = bf16[2,656,128]{2,1,0:T(8,128)(2,1)} collective-permute-done((bf16[2,656,128]{2,1,0:T(8,128)(2,1)}, bf16[2,656,128]{2,1,0:T(8,128)(2,1)}, u32[]{:S(2)}, u32[]{:S(2)}) %collective-permute-start.17) | collective-permute-done | bytes 335904 | tf_op jit(solution)/shard_map/ppermute | solution.py:32
  106.3 7.2 %finish.1 = (bf16[2,128,640]{2,1,0:T(8,128)(2,1)S(1)}, bf16[2,128,640]{2,1,0:T(8,128)(2,1)S(1)}, bf16[2,128,640]{2,1,0:T(8,128)(2,1)S(1)}, bf16[2,128,640]{2,1,0...) custom-call(s32[32]{0:T(128)S(1)} %fusion.31.pieces, ...), custom_call_target="tpu_custom_call" | custom-call | flops 2000000000 | bytes 12000000 | tf_op jit(solution)/shard_map/finish/pallas_call | solution.py:372
  115.2 1.8 %collective-permute-start.26 = (bf16[2,128,640]{2,1,0:T(8,128)(2,1)S(1)}, bf16[2,128,640]{2,1,0:T(8,128)(2,1)S(1)}, u32[]{:S(2)}, u32[]{:S(2)}) collective-permute-start(bf16[2,128,640]{2,1,0:T(8,128)(2,1)S(1)} %get-tuple-element.51), channel_id=1, source_target_pairs={{0,6},{1,7},{2,0},{3,1},{4,2},{5,3},{6,4},{7,5},{8,14},{9,15},{10,... | collective-permute-start | bytes 983048 | tf_op jit(solution)/shard_map/ppermute | solution.py:48
  116.9 1.8 %collective-permute-start.27 = (bf16[2,128,640]{2,1,0:T(8,128)(2,1)S(1)}, bf16[2,128,640]{2,1,0:T(8,128)(2,1)S(1)}, u32[]{:S(2)}, u32[]{:S(2)}) collective-permute-start(bf16[2,128,640]{2,1,0:T(8,128)(2,1)S(1)} %get-tuple-element.52), channel_id=1, source_target_pairs={{0,4},{1,5},{2,6},{3,7},{4,0},{5,1},{6,2},{7,3},{8,12},{9,13},{10,... | collective-permute-start | bytes 983048 | tf_op jit(solution)/shard_map/ppermute | solution.py:48
  120.2 2.3 %collective-permute-start.29 = (bf16[4,128,640]{2,1,0:T(8,128)(2,1)S(1)}, bf16[4,128,640]{2,1,0:T(8,128)(2,1)S(1)}, u32[]{:S(2)}, u32[]{:S(2)}) collective-permute-start(bf16[4,128,640]{2,1,0:T(8,128)(2,1)S(1)} %get-tuple-element.54), channel_id=1, source_target_pairs={{0,1},{1,0},{2,3},{3,2},{4,5},{5,4},{6,7},{7,6},{8,9},{9,8},{10,11... | collective-permute-start | bytes 1966088 | tf_op jit(solution)/shard_map/ppermute | solution.py:48
  122.5 2.1 %collective-permute-done.25 = bf16[2,128,640]{2,1,0:T(8,128)(2,1)S(1)} collective-permute-done((bf16[2,128,640]{2,1,0:T(8,128)(2,1)S(1)}, bf16[2,128,640]{2,1,0:T(8,128)(2,1)S(1)}, u32[]{:S(2)}, u32[]{:S(2)}) %collective-permute-start.25) | collective-permute-done | bytes 327712 | tf_op jit(solution)/shard_map/ppermute | solution.py:48
  124.6 2.6 %collective-permute-start.30 = (bf16[4,128,128]{2,1,0:T(8,128)(2,1)S(1)}, bf16[4,128,128]{2,1,0:T(8,128)(2,1)S(1)}, u32[]{:S(2)}, u32[]{:S(2)}) collective-permute-start(bf16[4,128,128]{2,1,0:T(8,128)(2,1)S(1)} %copy-done.17), channel_id=1, source_target_pairs={{0,192},{8,200},{16,208},{24,216},{32,224},{40,232},{48,240},{56,2... | collective-permute-start | bytes 393224 | tf_op jit(solution)/shard_map/ppermute | solution.py:32
  127.3 3.7 %collective-permute-done.26 = bf16[2,128,640]{2,1,0:T(8,128)(2,1)S(1)} collective-permute-done((bf16[2,128,640]{2,1,0:T(8,128)(2,1)S(1)}, bf16[2,128,640]{2,1,0:T(8,128)(2,1)S(1)}, u32[]{:S(2)}, u32[]{:S(2)}) %collective-permute-start.26) | collective-permute-done | bytes 327712 | tf_op jit(solution)/shard_map/ppermute | solution.py:48
  132.8 2.3 %collective-permute-start.28 = (bf16[128,640]{1,0:T(8,128)(2,1)S(1)}, bf16[128,640]{1,0:T(8,128)(2,1)S(1)}, u32[]{:S(2)}, u32[]{:S(2)}) collective-permute-start(bf16[128,640]{1,0:T(8,128)(2,1)S(1)} %fusion.6), channel_id=1, source_target_pairs={{0,1},{1,0},{2,3},{3,2},{4,5},{5,4},{6,7},{7,6},{8,9},{9,8},{10,11... | collective-permute-start | bytes 491528 | tf_op jit(solution)/shard_map/ppermute | solution.py:48
  136.0 3.9 %collective-permute-start.35 = (bf16[4,128,128]{2,1,0:T(8,128)(2,1)S(1)}, bf16[4,128,128]{2,1,0:T(8,128)(2,1)S(1)}, u32[]{:S(2)}, u32[]{:S(2)}) collective-permute-start(bf16[4,128,128]{2,1,0:T(8,128)(2,1)S(1)} %copy-done.15), channel_id=1, source_target_pairs={{0,128},{8,136},{16,144},{24,152},{32,160},{40,168},{48,176},{56,1... | collective-permute-start | bytes 393224 | tf_op jit(solution)/shard_map/ppermute | solution.py:32
  140.4 2.9 %collective-permute-done.31.refs_2_ = bf16[4,128,128]{2,1,0:T(8,128)(2,1)S(1)} collective-permute-done((bf16[4,128,128]{2,1,0:T(8,128)(2,1)S(1)}, bf16[4,128,128]{2,1,0:T(8,128)(2,1)S(1)}, u32[]{:S(2)}, u32[]{:S(2)}) %collective-permute-start.31) | collective-permute-done | bytes 131104 | tf_op jit(solution)/shard_map/ppermute | solution.py:32
  144.8 3.0 %collective-permute-start.33 = (bf16[128,640]{1,0:T(8,128)(2,1)S(1)}, bf16[128,640]{1,0:T(8,128)(2,1)S(1)}, u32[]{:S(2)}, u32[]{:S(2)}) collective-permute-start(bf16[128,640]{1,0:T(8,128)(2,1)S(1)} %get-tuple-element.96), channel_id=1, source_target_pairs={{0,6},{1,7},{2,0},{3,1},{4,2},{5,3},{6,4},{7,5},{8,14},{9,15},{10,... | collective-permute-start | bytes 491528 | tf_op jit(solution)/shard_map/ppermute | solution.py:48
  148.5 2.9 %refill.1 = (bf16[6,128,128]{2,1,0:T(8,128)(2,1)}, bf16[6,128,128]{2,1,0:T(8,128)(2,1)}) custom-call(s32[2]{0:T(128)} %compare_select_fusion.25.source, bf16[6,128,128]{2,1,0:T(8,128)(2,1)} %bitcast.38, bf16[6,128,128]{2,1,0:T(8,128)(2,1)} %bitcast.40, bf16[4,128,128]{2,1,0:T(8,128)(2,1)} %get-tuple-element.60.refs_0_, bf16[4,128,128]{2,1,0:T(8,128)(2,1)} %copy-done.2, ...), custom_call_target="tpu_custom_call" | custom-call | tf_op jit(solution)/shard_map/refill/pallas_call | solution.py:429
  151.6 2.7 %collective-permute-done.32 = bf16[128,640]{1,0:T(8,128)(2,1)S(1)} collective-permute-done((bf16[128,640]{1,0:T(8,128)(2,1)S(1)}, bf16[128,640]{1,0:T(8,128)(2,1)S(1)}, u32[]{:S(2)}, u32[]{:S(2)}) %collective-permute-start.32) | collective-permute-done | bytes 163872 | tf_op jit(solution)/shard_map/ppermute | solution.py:48
  (163 shorter events, 28.5 us)
Async XLA Ops:
  0.6 23.4 %collective-permute-start = (bf16[160,640]{1,0:T(8,128)(2,1)}, bf16[160,640]{1,0:T(8,128)(2,1)S(1)}, u32[]{:S(2)}, u32[]{:S(2)}) collective-permute-start(bf16[160,640]{1,0:T(8,128)(2,1)} %param.17), channel_id=1, source_target_pairs={{0,16},{8,24},{16,32},{24,40},{32,48},{40,56},{48,0},{56,8},{64,80... | collective-permute-start | bytes 614408 | tf_op jit(solution)/shard_map/ppermute | solution.py:32
  2.3 21.8 %collective-permute-start.2 = (bf16[160,640]{1,0:T(8,128)(2,1)}, bf16[160,640]{1,0:T(8,128)(2,1)S(1)}, u32[]{:S(2)}, u32[]{:S(2)}) collective-permute-start(bf16[160,640]{1,0:T(8,128)(2,1)} %param.17), channel_id=1, source_target_pairs={{0,32},{8,40},{16,48},{24,56},{32,0},{40,8},{48,16},{56,24},{64,96... | collective-permute-start | bytes 614408 | tf_op jit(solution)/shard_map/ppermute | solution.py:32
  7.6 18.8 %collective-permute-start.1 = (bf16[160,640]{1,0:T(8,128)(2,1)}, bf16[160,640]{1,0:T(8,128)(2,1)S(1)}, u32[]{:S(2)}, u32[]{:S(2)}) collective-permute-start(bf16[160,640]{1,0:T(8,128)(2,1)} %param.17), channel_id=1, source_target_pairs={{0,48},{8,56},{16,0},{24,8},{32,16},{40,24},{48,32},{56,40},{64,11... | collective-permute-start | bytes 614408 | tf_op jit(solution)/shard_map/ppermute | solution.py:32
  10.3 19.4 %collective-permute-start.6 = (bf16[5,256,128]{2,1,0:T(8,128)(2,1)}, bf16[5,256,128]{2,1,0:T(8,128)(2,1)}, u32[]{:S(2)}, u32[]{:S(2)}) collective-permute-start(bf16[5,256,128]{2,1,0:T(8,128)(2,1)} %bitcast.47), channel_id=1, source_target_pairs={{0,192},{8,200},{16,208},{24,216},{32,224},{40,232},{48,240},{56,2... | collective-permute-start | bytes 983048 | tf_op jit(solution)/shard_map/ppermute | solution.py:32
  13.3 16.3 %collective-permute-start.5 = (bf16[5,256,128]{2,1,0:T(8,128)(2,1)}, bf16[5,256,128]{2,1,0:T(8,128)(2,1)}, u32[]{:S(2)}, u32[]{:S(2)}) collective-permute-start(bf16[5,256,128]{2,1,0:T(8,128)(2,1)} %bitcast.48), channel_id=1, source_target_pairs={{0,64},{8,72},{16,80},{24,88},{32,96},{40,104},{48,112},{56,120},{... | collective-permute-start | bytes 983048 | tf_op jit(solution)/shard_map/ppermute | solution.py:32
  26.6 37.8 %collective-permute-start.4 = (bf16[4,160,640]{2,1,0:T(8,128)(2,1)S(1)}, bf16[4,160,640]{2,1,0:T(8,128)(2,1)S(1)}, u32[]{:S(2)}, u32[]{:S(2)}) collective-permute-start(bf16[4,160,640]{2,1,0:T(8,128)(2,1)S(1)} %pad_maximum_fusion.refs_4_), channel_id=1, source_target_pairs={{0,192},{8,200},{16,208},{24,216},{32,224},{40,232},{48,240},{56,2... | collective-permute-start | bytes 2457608 | tf_op jit(solution)/shard_map/ppermute | solution.py:32
  29.7 34.7 %collective-permute-start.3 = (bf16[4,160,640]{2,1,0:T(8,128)(2,1)S(1)}, bf16[4,160,640]{2,1,0:T(8,128)(2,1)S(1)}, u32[]{:S(2)}, u32[]{:S(2)}) collective-permute-start(bf16[4,160,640]{2,1,0:T(8,128)(2,1)S(1)} %pad_maximum_fusion.refs_4_), channel_id=1, source_target_pairs={{0,64},{8,72},{16,80},{24,88},{32,96},{40,104},{48,112},{56,120},{... | collective-permute-start | bytes 2457608 | tf_op jit(solution)/shard_map/ppermute | solution.py:32
  29.7 17.2 %collective-permute-start.10 = (bf16[12,128,128]{2,1,0:T(8,128)(2,1)S(1)}, bf16[12,128,128]{2,1,0:T(8,128)(2,1)}, u32[]{:S(2)}, u32[]{:S(2)}) collective-permute-start(bf16[12,128,128]{2,1,0:T(8,128)(2,1)S(1)} %copy-done), channel_id=1, source_target_pairs={{0,48},{8,56},{16,0},{24,8},{32,16},{40,24},{48,32},{56,40},{64,11... | collective-permute-start | bytes 1179656 | tf_op jit(solution)/shard_map/ppermute | solution.py:32
  33.3 18.2 %collective-permute-start.8 = (bf16[12,128,128]{2,1,0:T(8,128)(2,1)S(1)}, bf16[12,128,128]{2,1,0:T(8,128)(2,1)}, u32[]{:S(2)}, u32[]{:S(2)}) collective-permute-start(bf16[12,128,128]{2,1,0:T(8,128)(2,1)S(1)} %copy-done), channel_id=1, source_target_pairs={{0,16},{8,24},{16,32},{24,40},{32,48},{40,56},{48,0},{56,8},{64,80... | collective-permute-start | bytes 1179656 | tf_op jit(solution)/shard_map/ppermute | solution.py:32
  34.3 22.6 %collective-permute-start.16 = (bf16[5,256,128]{2,1,0:T(8,128)(2,1)S(1)}, bf16[5,256,128]{2,1,0:T(8,128)(2,1)S(1)}, u32[]{:S(2)}, u32[]{:S(2)}) collective-permute-start(bf16[5,256,128]{2,1,0:T(8,128)(2,1)S(1)} %bitcast.50), channel_id=1, source_target_pairs={{0,128},{8,136},{16,144},{24,152},{32,160},{40,168},{48,176},{56,1... | collective-permute-start | bytes 983048 | tf_op jit(solution)/shard_map/ppermute | solution.py:32
  47.8 9.6 %collective-permute-start.13 = (bf16[6,128,128]{2,1,0:T(8,128)(2,1)S(1)}, bf16[6,128,128]{2,1,0:T(8,128)(2,1)S(1)}, u32[]{:S(2)}, u32[]{:S(2)}) collective-permute-start(bf16[6,128,128]{2,1,0:T(8,128)(2,1)S(1)} %slice.37), channel_id=1, source_target_pairs={{0,48},{8,56},{16,0},{24,8},{32,16},{40,24},{48,32},{56,40},{64,11... | collective-permute-start | bytes 589832 | tf_op jit(solution)/shard_map/ppermute | solution.py:32
  52.5 10.3 %collective-permute-start.12 = (bf16[6,128,128]{2,1,0:T(8,128)(2,1)S(1)}, bf16[6,128,128]{2,1,0:T(8,128)(2,1)S(1)}, u32[]{:S(2)}, u32[]{:S(2)}) collective-permute-start(bf16[6,128,128]{2,1,0:T(8,128)(2,1)S(1)} %slice.36), channel_id=1, source_target_pairs={{0,16},{8,24},{16,32},{24,40},{32,48},{40,56},{48,0},{56,8},{64,80... | collective-permute-start | bytes 589832 | tf_op jit(solution)/shard_map/ppermute | solution.py:32
  56.9 8.1 %collective-permute-start.7 = (bf16[12,128,128]{2,1,0:T(8,128)(2,1)S(1)}, bf16[12,128,128]{2,1,0:T(8,128)(2,1)}, u32[]{:S(2)}, u32[]{:S(2)}) collective-permute-start(bf16[12,128,128]{2,1,0:T(8,128)(2,1)S(1)} %copy-done), channel_id=1, source_target_pairs={{0,8},{8,0},{16,24},{24,16},{32,40},{40,32},{48,56},{56,48},{64,72... | collective-permute-start | bytes 1179656 | tf_op jit(solution)/shard_map/ppermute | solution.py:32
  57.4 9.7 %collective-permute-start.11 = (bf16[12,128,128]{2,1,0:T(8,128)(2,1)}, bf16[12,128,128]{2,1,0:T(8,128)(2,1)}, u32[]{:S(2)}, u32[]{:S(2)}) collective-permute-start(bf16[12,128,128]{2,1,0:T(8,128)(2,1)} %collective-permute-done.10.refs_4_), channel_id=1, source_target_pairs={{0,8},{8,0},{16,24},{24,16},{32,40},{40,32},{48,56},{56,48},{64,72... | collective-permute-start | bytes 1179656 | tf_op jit(solution)/shard_map/ppermute | solution.py:32
  62.8 4.2 %collective-permute-start.9 = (bf16[12,128,128]{2,1,0:T(8,128)(2,1)}, bf16[12,128,128]{2,1,0:T(8,128)(2,1)}, u32[]{:S(2)}, u32[]{:S(2)}) collective-permute-start(bf16[12,128,128]{2,1,0:T(8,128)(2,1)} %collective-permute-done.8.refs_2_), channel_id=1, source_target_pairs={{0,8},{8,0},{16,24},{24,16},{32,40},{40,32},{48,56},{56,48},{64,72... | collective-permute-start | bytes 1179656 | tf_op jit(solution)/shard_map/ppermute | solution.py:32
  65.0 37.7 %collective-permute-start.23 = (bf16[4,160,640]{2,1,0:T(8,128)(2,1)S(1)}, bf16[4,160,640]{2,1,0:T(8,128)(2,1)S(1)}, u32[]{:S(2)}, u32[]{:S(2)}) collective-permute-start(bf16[4,160,640]{2,1,0:T(8,128)(2,1)S(1)} %pad_maximum_fusion.refs_4_), channel_id=1, source_target_pairs={{0,128},{8,136},{16,144},{24,152},{32,160},{40,168},{48,176},{56,1... | collective-permute-start | bytes 2457608 | tf_op jit(solution)/shard_map/ppermute | solution.py:32
  72.0 30.7 %collective-permute-start.19 = (bf16[2,656,128]{2,1,0:T(8,128)(2,1)}, bf16[2,656,128]{2,1,0:T(8,128)(2,1)}, u32[]{:S(2)}, u32[]{:S(2)}) collective-permute-start(bf16[2,656,128]{2,1,0:T(8,128)(2,1)} %get-tuple-element.39), channel_id=1, source_target_pairs={{0,128},{8,136},{16,144},{24,152},{32,160},{40,168},{48,176},{56,1... | collective-permute-start | bytes 1007624 | tf_op jit(solution)/shard_map/ppermute | solution.py:32
  88.0 13.5 %collective-permute-start.17 = (bf16[2,656,128]{2,1,0:T(8,128)(2,1)}, bf16[2,656,128]{2,1,0:T(8,128)(2,1)}, u32[]{:S(2)}, u32[]{:S(2)}) collective-permute-start(bf16[2,656,128]{2,1,0:T(8,128)(2,1)} %get-tuple-element.42), channel_id=1, source_target_pairs={{0,192},{8,200},{16,208},{24,216},{32,224},{40,232},{48,240},{56,2... | collective-permute-start | bytes 1007624 | tf_op jit(solution)/shard_map/ppermute | solution.py:32
  92.1 10.6 %collective-permute-start.18 = (bf16[2,656,128]{2,1,0:T(8,128)(2,1)}, bf16[2,656,128]{2,1,0:T(8,128)(2,1)}, u32[]{:S(2)}, u32[]{:S(2)}) collective-permute-start(bf16[2,656,128]{2,1,0:T(8,128)(2,1)} %get-tuple-element.43), channel_id=1, source_target_pairs={{0,64},{8,72},{16,80},{24,88},{32,96},{40,104},{48,112},{56,120},{... | collective-permute-start | bytes 1007624 | tf_op jit(solution)/shard_map/ppermute | solution.py:32
  92.3 11.4 %collective-permute-start.20 = (bf16[4,160,640]{2,1,0:T(8,128)(2,1)S(1)}, bf16[4,160,640]{2,1,0:T(8,128)(2,1)}, u32[]{:S(2)}, u32[]{:S(2)}) collective-permute-start(bf16[4,160,640]{2,1,0:T(8,128)(2,1)S(1)} %pad_maximum_fusion.refs_4_), channel_id=1, source_target_pairs={{0,8},{8,0},{16,24},{24,16},{32,40},{40,32},{48,56},{56,48},{64,72... | collective-permute-start | bytes 2457608 | tf_op jit(solution)/shard_map/ppermute | solution.py:32
  102.7 3.6 %collective-permute-start.24 = (bf16[4,160,640]{2,1,0:T(8,128)(2,1)S(1)}, bf16[4,160,640]{2,1,0:T(8,128)(2,1)}, u32[]{:S(2)}, u32[]{:S(2)}) collective-permute-start(bf16[4,160,640]{2,1,0:T(8,128)(2,1)S(1)} %collective-permute-done.23.refs_10_), channel_id=1, source_target_pairs={{0,8},{8,0},{16,24},{24,16},{32,40},{40,32},{48,56},{56,48},{64,72... | collective-permute-start | bytes 2457608 | tf_op jit(solution)/shard_map/ppermute | solution.py:32
  113.6 11.0 %collective-permute-start.25 = (bf16[2,128,640]{2,1,0:T(8,128)(2,1)S(1)}, bf16[2,128,640]{2,1,0:T(8,128)(2,1)S(1)}, u32[]{:S(2)}, u32[]{:S(2)}) collective-permute-start(bf16[2,128,640]{2,1,0:T(8,128)(2,1)S(1)} %get-tuple-element.50), channel_id=1, source_target_pairs={{0,2},{1,3},{2,4},{3,5},{4,6},{5,7},{6,0},{7,1},{8,10},{9,11},{10,... | collective-permute-start | bytes 983048 | tf_op jit(solution)/shard_map/ppermute | solution.py:48
  115.2 15.8 %collective-permute-start.26 = (bf16[2,128,640]{2,1,0:T(8,128)(2,1)S(1)}, bf16[2,128,640]{2,1,0:T(8,128)(2,1)S(1)}, u32[]{:S(2)}, u32[]{:S(2)}) collective-permute-start(bf16[2,128,640]{2,1,0:T(8,128)(2,1)S(1)} %get-tuple-element.51), channel_id=1, source_target_pairs={{0,6},{1,7},{2,0},{3,1},{4,2},{5,3},{6,4},{7,5},{8,14},{9,15},{10,... | collective-permute-start | bytes 983048 | tf_op jit(solution)/shard_map/ppermute | solution.py:48
  116.9 15.7 %collective-permute-start.27 = (bf16[2,128,640]{2,1,0:T(8,128)(2,1)S(1)}, bf16[2,128,640]{2,1,0:T(8,128)(2,1)S(1)}, u32[]{:S(2)}, u32[]{:S(2)}) collective-permute-start(bf16[2,128,640]{2,1,0:T(8,128)(2,1)S(1)} %get-tuple-element.52), channel_id=1, source_target_pairs={{0,4},{1,5},{2,6},{3,7},{4,0},{5,1},{6,2},{7,3},{8,12},{9,13},{10,... | collective-permute-start | bytes 983048 | tf_op jit(solution)/shard_map/ppermute | solution.py:48
  120.2 20.0 %collective-permute-start.29 = (bf16[4,128,640]{2,1,0:T(8,128)(2,1)S(1)}, bf16[4,128,640]{2,1,0:T(8,128)(2,1)S(1)}, u32[]{:S(2)}, u32[]{:S(2)}) collective-permute-start(bf16[4,128,640]{2,1,0:T(8,128)(2,1)S(1)} %get-tuple-element.54), channel_id=1, source_target_pairs={{0,1},{1,0},{2,3},{3,2},{4,5},{5,4},{6,7},{7,6},{8,9},{9,8},{10,11... | collective-permute-start | bytes 1966088 | tf_op jit(solution)/shard_map/ppermute | solution.py:48
  124.6 11.3 %collective-permute-start.30 = (bf16[4,128,128]{2,1,0:T(8,128)(2,1)S(1)}, bf16[4,128,128]{2,1,0:T(8,128)(2,1)S(1)}, u32[]{:S(2)}, u32[]{:S(2)}) collective-permute-start(bf16[4,128,128]{2,1,0:T(8,128)(2,1)S(1)} %copy-done.17), channel_id=1, source_target_pairs={{0,192},{8,200},{16,208},{24,216},{32,224},{40,232},{48,240},{56,2... | collective-permute-start | bytes 393224 | tf_op jit(solution)/shard_map/ppermute | solution.py:32
  132.8 7.4 %collective-permute-start.28 = (bf16[128,640]{1,0:T(8,128)(2,1)S(1)}, bf16[128,640]{1,0:T(8,128)(2,1)S(1)}, u32[]{:S(2)}, u32[]{:S(2)}) collective-permute-start(bf16[128,640]{1,0:T(8,128)(2,1)S(1)} %fusion.6), channel_id=1, source_target_pairs={{0,1},{1,0},{2,3},{3,2},{4,5},{5,4},{6,7},{7,6},{8,9},{9,8},{10,11... | collective-permute-start | bytes 491528 | tf_op jit(solution)/shard_map/ppermute | solution.py:48
  135.7 7.6 %collective-permute-start.31 = (bf16[4,128,128]{2,1,0:T(8,128)(2,1)S(1)}, bf16[4,128,128]{2,1,0:T(8,128)(2,1)S(1)}, u32[]{:S(2)}, u32[]{:S(2)}) collective-permute-start(bf16[4,128,128]{2,1,0:T(8,128)(2,1)S(1)} %copy-done.16), channel_id=1, source_target_pairs={{0,64},{8,72},{16,80},{24,88},{32,96},{40,104},{48,112},{56,120},{... | collective-permute-start | bytes 393224 | tf_op jit(solution)/shard_map/ppermute | solution.py:32
  136.0 11.8 %collective-permute-start.35 = (bf16[4,128,128]{2,1,0:T(8,128)(2,1)S(1)}, bf16[4,128,128]{2,1,0:T(8,128)(2,1)S(1)}, u32[]{:S(2)}, u32[]{:S(2)}) collective-permute-start(bf16[4,128,128]{2,1,0:T(8,128)(2,1)S(1)} %copy-done.15), channel_id=1, source_target_pairs={{0,128},{8,136},{16,144},{24,152},{32,160},{40,168},{48,176},{56,1... | collective-permute-start | bytes 393224 | tf_op jit(solution)/shard_map/ppermute | solution.py:32
  144.0 7.4 %collective-permute-start.34 = (bf16[128,640]{1,0:T(8,128)(2,1)S(1)}, bf16[128,640]{1,0:T(8,128)(2,1)S(1)}, u32[]{:S(2)}, u32[]{:S(2)}) collective-permute-start(bf16[128,640]{1,0:T(8,128)(2,1)S(1)} %get-tuple-element.95), channel_id=1, source_target_pairs={{0,4},{1,5},{2,6},{3,7},{4,0},{5,1},{6,2},{7,3},{8,12},{9,13},{10,... | collective-permute-start | bytes 491528 | tf_op jit(solution)/shard_map/ppermute | solution.py:48
  144.8 6.8 %collective-permute-start.33 = (bf16[128,640]{1,0:T(8,128)(2,1)S(1)}, bf16[128,640]{1,0:T(8,128)(2,1)S(1)}, u32[]{:S(2)}, u32[]{:S(2)}) collective-permute-start(bf16[128,640]{1,0:T(8,128)(2,1)S(1)} %get-tuple-element.96), channel_id=1, source_target_pairs={{0,6},{1,7},{2,0},{3,1},{4,2},{5,3},{6,4},{7,5},{8,14},{9,15},{10,... | collective-permute-start | bytes 491528 | tf_op jit(solution)/shard_map/ppermute | solution.py:48
  147.8 6.5 %collective-permute-start.32 = (bf16[128,640]{1,0:T(8,128)(2,1)S(1)}, bf16[128,640]{1,0:T(8,128)(2,1)S(1)}, u32[]{:S(2)}, u32[]{:S(2)}) collective-permute-start(bf16[128,640]{1,0:T(8,128)(2,1)S(1)} %get-tuple-element.97), channel_id=1, source_target_pairs={{0,2},{1,3},{2,4},{3,5},{4,6},{5,7},{6,0},{7,1},{8,10},{9,11},{10,... | collective-permute-start | bytes 491528 | tf_op jit(solution)/shard_map/ppermute | solution.py:48
  (23 other events, 204.4 us)

commit v7 on v4

--- a/solution.py
+++ b/solution.py
@@ -204,13 +204,27 @@
             high[...] = jnp.maximum(high[...], jnp.maximum(raw[:, :size], raw[:, size:]))
             return unused
 
+        def score_two(u, unused):
+            t = edges[i] + 2 * u
+            one = raw_scores(t)
+            two = raw_scores(t + 1)
+            scores[t] = one
+            scores[t + 1] = two
+            best = jnp.maximum(
+                jnp.maximum(one[:, :size], one[:, size:]),
+                jnp.maximum(two[:, :size], two[:, size:]),
+            )
+            high[...] = jnp.maximum(high[...], best)
+            return unused
+
         lax.fori_loop(0, edges[i], score_edge, 0)
-        lax.fori_loop(edges[i], pairs, score_full, 0)
+        lax.fori_loop(0, (pairs - edges[i]) // 2, score_two, 0)
+        lax.fori_loop(pairs - (pairs - edges[i]) % 2, pairs, score_full, 0)
         top = jnp.maximum(jnp.max(high[...], axis=1, keepdims=True), FLOOR)
         high[...] = jnp.broadcast_to(top, high.shape)
         total[...] = jnp.zeros_like(total)
 
-        def blend(t, unused):
+        def product(t):
             at = i * longest + 2 * t
             values = jnp.concatenate(
                 [kv[place(chosen[at]) + half], kv[place(chosen[at + 1]) + half]], axis=0
@@ -219,10 +233,18 @@
             level = high[...]
             level = jnp.concatenate([level, level], axis=1)
             weights = jnp.exp2((scores[t] - level) * log_scale).astype(jnp.bfloat16)
-            total[...] += jnp.dot(weights, values, preferred_element_type=jnp.float32)
+            return jnp.dot(weights, values, preferred_element_type=jnp.float32)
+
+        def blend(t, unused):
+            total[...] += product(t)
             return unused
 
-        lax.fori_loop(0, pairs, blend, 0)
+        def blend_two(u, unused):
+            total[...] += product(2 * u) + product(2 * u + 1)
+            return unused
+
+        lax.fori_loop(0, pairs // 2, blend_two, 0)
+        lax.fori_loop(pairs - pairs % 2, pairs, blend, 0)
         summed = total[:, width:]
         safe = jnp.where(summed > 0.0, summed, 1.0)
         result[i, 0:wide, :] = (total[:, :width] / safe).astype(jnp.bfloat16)

time: 150 us -> 161 us (1.073)
  the two profiles are of different devices: /device:TPU:6 before, /device:TPU:168 now
where the time goes in v7:
time: 161 us; the launch traced here: 158 us
  starting transfers between devices  87 us (54%)
  waiting for transfers between devices  27.4 us (17%)
  Pallas kernels  25.5 us (16%)
  other arithmetic  13.3 us (8%)
  local copies, waits for them, and re-layouts  4.02 us (2%)
    ppermute x28, starting transfers between devices, shift(): return lax.ppermute(value, 'blk', blk_perm(dy, dz, dc))  61.7 us
    ppermute x8, starting transfers between devices, head_shift(): return lax.ppermute(value, 'head', pairs)  25.3 us
    ppermute x28, waiting for transfers between devices, shift(): return lax.ppermute(value, 'blk', blk_perm(dy, dz, dc))  21 us
    pallas_call x1, Pallas kernels, attend(): pl.pallas_call(functools.partial(attend_kernel, log_scale, nkv, nq), out_...  13.5 us
    pallas_call x1, Pallas kernels, finish(): pl.pallas_call(functools.partial(finish_kernel, heads, nparts, nw), out_s...  7.22 us
    ppermute x8, waiting for transfers between devices, head_shift(): return lax.ppermute(value, 'head', pairs)  6.35 us
    reduce_sum x2, other arithmetic, table_entry(): return jnp.sum(jnp.where(match, block_table[None], 0), axis=(1, 2))  3.89 us
  transfers between devices with their start and end apart: 36, of which 10 were waited for; matrix products, arithmetic and copies ran while one was open for 9% of the time, Pallas kernels for 10%

profile of v7, /device:TPU:168, one launch (start us, length us, event | category | flops | bytes accessed | tf_op | source)
XLA Modules:
  0.0 158.5 jit_solution(7274184229094944331)
XLA Ops:
  1.3 2.4 %collective-permute-start = (bf16[160,640]{1,0:T(8,128)(2,1)}, bf16[160,640]{1,0:T(8,128)(2,1)S(1)}, u32[]{:S(2)}, u32[]{:S(2)}) collective-permute-start(bf16[160,640]{1,0:T(8,128)(2,1)} %param.17), channel_id=1, source_target_pairs={{0,16},{8,24},{16,32},{24,40},{32,48},{40,56},{48,0},{56,8},{64,80... | collective-permute-start | bytes 614408 | tf_op jit(solution)/shard_map/ppermute | solution.py:32
  3.7 2.1 %collective-permute-start.2 = (bf16[160,640]{1,0:T(8,128)(2,1)}, bf16[160,640]{1,0:T(8,128)(2,1)S(1)}, u32[]{:S(2)}, u32[]{:S(2)}) collective-permute-start(bf16[160,640]{1,0:T(8,128)(2,1)} %param.17), channel_id=1, source_target_pairs={{0,32},{8,40},{16,48},{24,56},{32,0},{40,8},{48,16},{56,24},{64,96... | collective-permute-start | bytes 614408 | tf_op jit(solution)/shard_map/ppermute | solution.py:32
  6.2 1.6 collective-permute-start.3
  11.1 2.6 %select_reduce_fusion.1 = (s32[48]{0:T(128)S(1)}, s32[48]{0:T(128)S(1)}) fusion(s32[8,64]{1,0:T(8,128)} %param.20, pred[48,64]{1,0:T(8,128)(4,1)S(1)} %iota_compare_fusion.2, pred[48,8]{1,0:T(8,128)(4,1)S(1)} %copy.19, s32[8,64]{1,0:T(8,128)S(1)} %add_add_fusion, pred[8,64]{1,0:T(8,128)(4,1)S(1)} %iota_compare_fusion.8, s32[48]{0:T(128)S(1)} %add.594), kind=kLoop, calls=%fused_computation.13 | loop fusion | flops 171936 | bytes 8640 | tf_op jit(solution)/shard_map/reduce_sum | solution.py:75
  16.9 1.8 %pack.1.refs_0_ = bf16[12,128,128]{2,1,0:T(8,128)(2,1)} custom-call(bf16[6,128,128]{2,1,0:T(8,128)(2,1)} %bitcast.37, bf16[6,128,128]{2,1,0:T(8,128)(2,1)} %bitcast.39, bf16[2,128,128]{2,1,0:T(8,128)(2,1)} %bitcast.45, bf16[2,128,128]{2,1,0:T(8,128)(2,1)} %bitcast.46), custom_call_target="tpu_custom_call" | custom-call | tf_op jit(solution)/shard_map/pack/pallas_call | solution.py:100
  18.8 3.6 %collective-permute-start.14 = (bf16[5,256,128]{2,1,0:T(8,128)(2,1)S(1)}, bf16[5,256,128]{2,1,0:T(8,128)(2,1)S(1)}, u32[]{:S(2)}, u32[]{:S(2)}) collective-permute-start(bf16[5,256,128]{2,1,0:T(8,128)(2,1)S(1)} %bitcast.50), channel_id=1, source_target_pairs={{0,128},{8,136},{16,144},{24,152},{32,160},{40,168},{48,176},{56,1... | collective-permute-start | bytes 983048 | tf_op jit(solution)/shard_map/ppermute | solution.py:32
  22.8 4.1 %collective-permute-start.8 = (bf16[12,128,128]{2,1,0:T(8,128)(2,1)S(1)}, bf16[12,128,128]{2,1,0:T(8,128)(2,1)S(1)}, u32[]{:S(2)}, u32[]{:S(2)}) collective-permute-start(bf16[12,128,128]{2,1,0:T(8,128)(2,1)S(1)} %copy-done), channel_id=1, source_target_pairs={{0,48},{8,56},{16,0},{24,8},{32,16},{40,24},{48,32},{56,40},{64,11... | collective-permute-start | bytes 1179656 | tf_op jit(solution)/shard_map/ppermute | solution.py:32
  26.9 2.1 %collective-permute-done.14.refs_13_ = bf16[5,256,128]{2,1,0:T(8,128)(2,1)S(1)} collective-permute-done((bf16[5,256,128]{2,1,0:T(8,128)(2,1)S(1)}, bf16[5,256,128]{2,1,0:T(8,128)(2,1)S(1)}, u32[]{:S(2)}, u32[]{:S(2)}) %collective-permute-start.14) | collective-permute-done | bytes 327712 | tf_op jit(solution)/shard_map/ppermute | solution.py:32
  29.7 1.5 collective-permute-start.21
  32.4 2.2 %collective-permute-done.8.refs_4_ = bf16[12,128,128]{2,1,0:T(8,128)(2,1)S(1)} collective-permute-done((bf16[12,128,128]{2,1,0:T(8,128)(2,1)S(1)}, bf16[12,128,128]{2,1,0:T(8,128)(2,1)S(1)}, u32[]{:S(2)}, u32[]{:S(2)}) %collective-permute-start.8) | collective-permute-done | bytes 393248 | tf_op jit(solution)/shard_map/ppermute | solution.py:32
  34.6 6.7 %collective-permute-start.11 = (bf16[6,128,128]{2,1,0:T(8,128)(2,1)S(1)}, bf16[6,128,128]{2,1,0:T(8,128)(2,1)S(1)}, u32[]{:S(2)}, u32[]{:S(2)}) collective-permute-start(bf16[6,128,128]{2,1,0:T(8,128)(2,1)S(1)} %slice.37), channel_id=1, source_target_pairs={{0,48},{8,56},{16,0},{24,8},{32,16},{40,24},{48,32},{56,40},{64,11... | collective-permute-start | bytes 589832 | tf_op jit(solution)/shard_map/ppermute | solution.py:32
  42.2 6.0 %collective-permute-done.11.refs_7_ = bf16[6,128,128]{2,1,0:T(8,128)(2,1)S(1)} collective-permute-done((bf16[6,128,128]{2,1,0:T(8,128)(2,1)S(1)}, bf16[6,128,128]{2,1,0:T(8,128)(2,1)S(1)}, u32[]{:S(2)}, u32[]{:S(2)}) %collective-permute-start.11) | collective-permute-done | bytes 196640 | tf_op jit(solution)/shard_map/ppermute | solution.py:32
  48.2 2.7 %collective-permute-done.10.refs_6_ = bf16[6,128,128]{2,1,0:T(8,128)(2,1)} collective-permute-done((bf16[6,128,128]{2,1,0:T(8,128)(2,1)S(1)}, bf16[6,128,128]{2,1,0:T(8,128)(2,1)}, u32[]{:S(2)}, u32[]{:S(2)}) %collective-permute-start.10) | collective-permute-done | bytes 196640 | tf_op jit(solution)/shard_map/ppermute | solution.py:32
  53.8 13.5 %attend.1 = (bf16[2,656,128]{2,1,0:T(8,128)(2,1)}, bf16[2,656,128]{2,1,0:T(8,128)(2,1)}, bf16[2,656,128]{2,1,0:T(8,128)(2,1)}, bf16[2,656,128]{2,1,0:T(8,128)(2,...) custom-call(s32[8]{0:T(128)} %copy-done.13, ...), custom_call_target="tpu_custom_call" | custom-call | flops 5000000000 | bytes 8000000 | tf_op jit(solution)/shard_map/attend/pallas_call | solution.py:295
  67.3 2.6 %collective-permute-start.15 = (bf16[2,656,128]{2,1,0:T(8,128)(2,1)}, bf16[2,656,128]{2,1,0:T(8,128)(2,1)S(1)}, u32[]{:S(2)}, u32[]{:S(2)}) collective-permute-start(bf16[2,656,128]{2,1,0:T(8,128)(2,1)} %get-tuple-element.32), channel_id=1, source_target_pairs={{0,192},{8,200},{16,208},{24,216},{32,224},{40,232},{48,240},{56,2... | collective-permute-start | bytes 1007624 | tf_op jit(solution)/shard_map/ppermute | solution.py:32
  69.9 6.0 %collective-permute-start.17 = (bf16[2,656,128]{2,1,0:T(8,128)(2,1)}, bf16[2,656,128]{2,1,0:T(8,128)(2,1)S(1)}, u32[]{:S(2)}, u32[]{:S(2)}) collective-permute-start(bf16[2,656,128]{2,1,0:T(8,128)(2,1)} %get-tuple-element.34), channel_id=1, source_target_pairs={{0,128},{8,136},{16,144},{24,152},{32,160},{40,168},{48,176},{56,1... | collective-permute-start | bytes 1007624 | tf_op jit(solution)/shard_map/ppermute | solution.py:32
  76.0 5.9 %collective-permute-done.15.refs_1_ = bf16[2,656,128]{2,1,0:T(8,128)(2,1)S(1)} collective-permute-done((bf16[2,656,128]{2,1,0:T(8,128)(2,1)}, bf16[2,656,128]{2,1,0:T(8,128)(2,1)S(1)}, u32[]{:S(2)}, u32[]{:S(2)}) %collective-permute-start.15) | collective-permute-done | bytes 335904 | tf_op jit(solution)/shard_map/ppermute | solution.py:32
  81.9 9.6 %collective-permute-start.22 = (bf16[4,160,640]{2,1,0:T(8,128)(2,1)S(1)}, bf16[4,160,640]{2,1,0:T(8,128)(2,1)}, u32[]{:S(2)}, u32[]{:S(2)}) collective-permute-start(bf16[4,160,640]{2,1,0:T(8,128)(2,1)S(1)} %collective-permute-done.21.refs_8_), channel_id=1, source_target_pairs={{0,8},{8,0},{16,24},{24,16},{32,40},{40,32},{48,56},{56,48},{64,72... | collective-permute-start | bytes 2457608 | tf_op jit(solution)/shard_map/ppermute | solution.py:32
  92.9 1.3 select_reduce_fusion
  95.0 1.2 collective-permute-done.24.refs_11_
  96.2 7.2 %finish.1 = (bf16[2,128,640]{2,1,0:T(8,128)(2,1)S(1)}, bf16[2,128,640]{2,1,0:T(8,128)(2,1)S(1)}, bf16[2,128,640]{2,1,0:T(8,128)(2,1)S(1)}, bf16[2,128,640]{2,1,0...) custom-call(s32[32]{0:T(128)S(1)} %fusion.31.pieces, ...), custom_call_target="tpu_custom_call" | custom-call | flops 2000000000 | bytes 12000000 | tf_op jit(solution)/shard_map/finish/pallas_call | solution.py:393
  103.4 1.6 collective-permute-start.25
  105.0 1.7 %collective-permute-start.26 = (bf16[2,128,640]{2,1,0:T(8,128)(2,1)S(1)}, bf16[2,128,640]{2,1,0:T(8,128)(2,1)S(1)}, u32[]{:S(2)}, u32[]{:S(2)}) collective-permute-start(bf16[2,128,640]{2,1,0:T(8,128)(2,1)S(1)} %get-tuple-element.40), channel_id=1, source_target_pairs={{0,6},{1,7},{2,0},{3,1},{4,2},{5,3},{6,4},{7,5},{8,14},{9,15},{10,... | collective-permute-start | bytes 983048 | tf_op jit(solution)/shard_map/ppermute | solution.py:48
  106.7 1.8 %collective-permute-start.27 = (bf16[2,128,640]{2,1,0:T(8,128)(2,1)S(1)}, bf16[2,128,640]{2,1,0:T(8,128)(2,1)S(1)}, u32[]{:S(2)}, u32[]{:S(2)}) collective-permute-start(bf16[2,128,640]{2,1,0:T(8,128)(2,1)S(1)} %get-tuple-element.41), channel_id=1, source_target_pairs={{0,4},{1,5},{2,6},{3,7},{4,0},{5,1},{6,2},{7,3},{8,12},{9,13},{10,... | collective-permute-start | bytes 983048 | tf_op jit(solution)/shard_map/ppermute | solution.py:48
  108.7 10.4 %collective-permute-start.29 = (bf16[4,128,640]{2,1,0:T(8,128)(2,1)S(1)}, bf16[4,128,640]{2,1,0:T(8,128)(2,1)S(1)}, u32[]{:S(2)}, u32[]{:S(2)}) collective-permute-start(bf16[4,128,640]{2,1,0:T(8,128)(2,1)S(1)} %get-tuple-element.43), channel_id=1, source_target_pairs={{0,1},{1,0},{2,3},{3,2},{4,5},{5,4},{6,7},{7,6},{8,9},{9,8},{10,11... | collective-permute-start | bytes 1966088 | tf_op jit(solution)/shard_map/ppermute | solution.py:48
  119.8 7.2 %collective-permute-start.30 = (bf16[4,128,128]{2,1,0:T(8,128)(2,1)S(1)}, bf16[4,128,128]{2,1,0:T(8,128)(2,1)S(1)}, u32[]{:S(2)}, u32[]{:S(2)}) collective-permute-start(bf16[4,128,128]{2,1,0:T(8,128)(2,1)S(1)} %copy-done.21), channel_id=1, source_target_pairs={{0,192},{8,200},{16,208},{24,216},{32,224},{40,232},{48,240},{56,2... | collective-permute-start | bytes 393224 | tf_op jit(solution)/shard_map/ppermute | solution.py:32
  127.2 5.9 %collective-permute-start.28 = (bf16[128,640]{1,0:T(8,128)(2,1)S(1)}, bf16[128,640]{1,0:T(8,128)(2,1)S(1)}, u32[]{:S(2)}, u32[]{:S(2)}) collective-permute-start(bf16[128,640]{1,0:T(8,128)(2,1)S(1)} %fusion.6), channel_id=1, source_target_pairs={{0,1},{1,0},{2,3},{3,2},{4,5},{5,4},{6,7},{7,6},{8,9},{9,8},{10,11... | collective-permute-start | bytes 491528 | tf_op jit(solution)/shard_map/ppermute | solution.py:48
  133.1 9.7 %collective-permute-start.35 = (bf16[4,128,128]{2,1,0:T(8,128)(2,1)S(1)}, bf16[4,128,128]{2,1,0:T(8,128)(2,1)S(1)}, u32[]{:S(2)}, u32[]{:S(2)}) collective-permute-start(bf16[4,128,128]{2,1,0:T(8,128)(2,1)S(1)} %copy-done.19), channel_id=1, source_target_pairs={{0,128},{8,136},{16,144},{24,152},{32,160},{40,168},{48,176},{56,1... | collective-permute-start | bytes 393224 | tf_op jit(solution)/shard_map/ppermute | solution.py:32
  143.6 1.1 collective-permute-start.32
  144.8 2.3 %collective-permute-start.34 = (bf16[128,640]{1,0:T(8,128)(2,1)S(1)}, bf16[128,640]{1,0:T(8,128)(2,1)S(1)}, u32[]{:S(2)}, u32[]{:S(2)}) collective-permute-start(bf16[128,640]{1,0:T(8,128)(2,1)S(1)} %get-tuple-element.82), channel_id=1, source_target_pairs={{0,4},{1,5},{2,6},{3,7},{4,0},{5,1},{6,2},{7,3},{8,12},{9,13},{10,... | collective-permute-start | bytes 491528 | tf_op jit(solution)/shard_map/ppermute | solution.py:48
  147.5 5.7 %collective-permute-done.32 = bf16[128,640]{1,0:T(8,128)(2,1)S(1)} collective-permute-done((bf16[128,640]{1,0:T(8,128)(2,1)S(1)}, bf16[128,640]{1,0:T(8,128)(2,1)S(1)}, u32[]{:S(2)}, u32[]{:S(2)}) %collective-permute-start.32) | collective-permute-done | bytes 163872 | tf_op jit(solution)/shard_map/ppermute | solution.py:48
  155.4 2.9 %refill.1 = (bf16[6,128,128]{2,1,0:T(8,128)(2,1)}, bf16[6,128,128]{2,1,0:T(8,128)(2,1)}) custom-call(s32[2]{0:T(128)} %compare_select_fusion.25.source, bf16[6,128,128]{2,1,0:T(8,128)(2,1)} %bitcast.38, bf16[6,128,128]{2,1,0:T(8,128)(2,1)} %bitcast.40, bf16[4,128,128]{2,1,0:T(8,128)(2,1)} %get-tuple-element.49.refs_0_, bf16[4,128,128]{2,1,0:T(8,128)(2,1)} %copy-done.5, ...), custom_call_target="tpu_custom_call" | custom-call | tf_op jit(solution)/shard_map/refill/pallas_call | solution.py:450
  (170 shorter events, 19.9 us)
Async XLA Ops:
  0.7 21.8 %collective-permute-start.1 = (bf16[160,640]{1,0:T(8,128)(2,1)}, bf16[160,640]{1,0:T(8,128)(2,1)S(1)}, u32[]{:S(2)}, u32[]{:S(2)}) collective-permute-start(bf16[160,640]{1,0:T(8,128)(2,1)} %param.17), channel_id=1, source_target_pairs={{0,48},{8,56},{16,0},{24,8},{32,16},{40,24},{48,32},{56,40},{64,11... | collective-permute-start | bytes 614408 | tf_op jit(solution)/shard_map/ppermute | solution.py:32
  1.3 21.1 %collective-permute-start = (bf16[160,640]{1,0:T(8,128)(2,1)}, bf16[160,640]{1,0:T(8,128)(2,1)S(1)}, u32[]{:S(2)}, u32[]{:S(2)}) collective-permute-start(bf16[160,640]{1,0:T(8,128)(2,1)} %param.17), channel_id=1, source_target_pairs={{0,16},{8,24},{16,32},{24,40},{32,48},{40,56},{48,0},{56,8},{64,80... | collective-permute-start | bytes 614408 | tf_op jit(solution)/shard_map/ppermute | solution.py:32
  3.7 18.9 %collective-permute-start.2 = (bf16[160,640]{1,0:T(8,128)(2,1)}, bf16[160,640]{1,0:T(8,128)(2,1)S(1)}, u32[]{:S(2)}, u32[]{:S(2)}) collective-permute-start(bf16[160,640]{1,0:T(8,128)(2,1)} %param.17), channel_id=1, source_target_pairs={{0,32},{8,40},{16,48},{24,56},{32,0},{40,8},{48,16},{56,24},{64,96... | collective-permute-start | bytes 614408 | tf_op jit(solution)/shard_map/ppermute | solution.py:32
  5.8 13.0 %collective-permute-start.4 = (bf16[5,256,128]{2,1,0:T(8,128)(2,1)}, bf16[5,256,128]{2,1,0:T(8,128)(2,1)S(1)}, u32[]{:S(2)}, u32[]{:S(2)}) collective-permute-start(bf16[5,256,128]{2,1,0:T(8,128)(2,1)} %bitcast.47), channel_id=1, source_target_pairs={{0,192},{8,200},{16,208},{24,216},{32,224},{40,232},{48,240},{56,2... | collective-permute-start | bytes 983048 | tf_op jit(solution)/shard_map/ppermute | solution.py:32
  6.2 12.6 %collective-permute-start.3 = (bf16[5,256,128]{2,1,0:T(8,128)(2,1)}, bf16[5,256,128]{2,1,0:T(8,128)(2,1)S(1)}, u32[]{:S(2)}, u32[]{:S(2)}) collective-permute-start(bf16[5,256,128]{2,1,0:T(8,128)(2,1)} %bitcast.48), channel_id=1, source_target_pairs={{0,64},{8,72},{16,80},{24,88},{32,96},{40,104},{48,112},{56,120},{... | collective-permute-start | bytes 983048 | tf_op jit(solution)/shard_map/ppermute | solution.py:32
  18.8 10.2 %collective-permute-start.14 = (bf16[5,256,128]{2,1,0:T(8,128)(2,1)S(1)}, bf16[5,256,128]{2,1,0:T(8,128)(2,1)S(1)}, u32[]{:S(2)}, u32[]{:S(2)}) collective-permute-start(bf16[5,256,128]{2,1,0:T(8,128)(2,1)S(1)} %bitcast.50), channel_id=1, source_target_pairs={{0,128},{8,136},{16,144},{24,152},{32,160},{40,168},{48,176},{56,1... | collective-permute-start | bytes 983048 | tf_op jit(solution)/shard_map/ppermute | solution.py:32
  22.8 11.8 %collective-permute-start.8 = (bf16[12,128,128]{2,1,0:T(8,128)(2,1)S(1)}, bf16[12,128,128]{2,1,0:T(8,128)(2,1)S(1)}, u32[]{:S(2)}, u32[]{:S(2)}) collective-permute-start(bf16[12,128,128]{2,1,0:T(8,128)(2,1)S(1)} %copy-done), channel_id=1, source_target_pairs={{0,48},{8,56},{16,0},{24,8},{32,16},{40,24},{48,32},{56,40},{64,11... | collective-permute-start | bytes 1179656 | tf_op jit(solution)/shard_map/ppermute | solution.py:32
  26.9 14.5 %collective-permute-start.6 = (bf16[12,128,128]{2,1,0:T(8,128)(2,1)S(1)}, bf16[12,128,128]{2,1,0:T(8,128)(2,1)S(1)}, u32[]{:S(2)}, u32[]{:S(2)}) collective-permute-start(bf16[12,128,128]{2,1,0:T(8,128)(2,1)S(1)} %copy-done), channel_id=1, source_target_pairs={{0,16},{8,24},{16,32},{24,40},{32,48},{40,56},{48,0},{56,8},{64,80... | collective-permute-start | bytes 1179656 | tf_op jit(solution)/shard_map/ppermute | solution.py:32
  29.7 21.2 %collective-permute-start.21 = (bf16[4,160,640]{2,1,0:T(8,128)(2,1)S(1)}, bf16[4,160,640]{2,1,0:T(8,128)(2,1)S(1)}, u32[]{:S(2)}, u32[]{:S(2)}) collective-permute-start(bf16[4,160,640]{2,1,0:T(8,128)(2,1)S(1)} %pad_maximum_fusion.refs_4_), channel_id=1, source_target_pairs={{0,192},{8,200},{16,208},{24,216},{32,224},{40,232},{48,240},{56,2... | collective-permute-start | bytes 2457608 | tf_op jit(solution)/shard_map/ppermute | solution.py:32
  31.2 20.3 %collective-permute-start.19 = (bf16[4,160,640]{2,1,0:T(8,128)(2,1)S(1)}, bf16[4,160,640]{2,1,0:T(8,128)(2,1)S(1)}, u32[]{:S(2)}, u32[]{:S(2)}) collective-permute-start(bf16[4,160,640]{2,1,0:T(8,128)(2,1)S(1)} %pad_maximum_fusion.refs_4_), channel_id=1, source_target_pairs={{0,64},{8,72},{16,80},{24,88},{32,96},{40,104},{48,112},{56,120},{... | collective-permute-start | bytes 2457608 | tf_op jit(solution)/shard_map/ppermute | solution.py:32
  34.6 13.5 %collective-permute-start.11 = (bf16[6,128,128]{2,1,0:T(8,128)(2,1)S(1)}, bf16[6,128,128]{2,1,0:T(8,128)(2,1)S(1)}, u32[]{:S(2)}, u32[]{:S(2)}) collective-permute-start(bf16[6,128,128]{2,1,0:T(8,128)(2,1)S(1)} %slice.37), channel_id=1, source_target_pairs={{0,48},{8,56},{16,0},{24,8},{32,16},{40,24},{48,32},{56,40},{64,11... | collective-permute-start | bytes 589832 | tf_op jit(solution)/shard_map/ppermute | solution.py:32
  41.4 9.5 %collective-permute-start.10 = (bf16[6,128,128]{2,1,0:T(8,128)(2,1)S(1)}, bf16[6,128,128]{2,1,0:T(8,128)(2,1)}, u32[]{:S(2)}, u32[]{:S(2)}) collective-permute-start(bf16[6,128,128]{2,1,0:T(8,128)(2,1)S(1)} %slice.36), channel_id=1, source_target_pairs={{0,16},{8,24},{16,32},{24,40},{32,48},{40,56},{48,0},{56,8},{64,80... | collective-permute-start | bytes 589832 | tf_op jit(solution)/shard_map/ppermute | solution.py:32
  41.5 10.9 %collective-permute-start.5 = (bf16[12,128,128]{2,1,0:T(8,128)(2,1)S(1)}, bf16[12,128,128]{2,1,0:T(8,128)(2,1)}, u32[]{:S(2)}, u32[]{:S(2)}) collective-permute-start(bf16[12,128,128]{2,1,0:T(8,128)(2,1)S(1)} %copy-done), channel_id=1, source_target_pairs={{0,8},{8,0},{16,24},{24,16},{32,40},{40,32},{48,56},{56,48},{64,72... | collective-permute-start | bytes 1179656 | tf_op jit(solution)/shard_map/ppermute | solution.py:32
  48.2 5.5 %collective-permute-start.9 = (bf16[12,128,128]{2,1,0:T(8,128)(2,1)}, bf16[12,128,128]{2,1,0:T(8,128)(2,1)}, u32[]{:S(2)}, u32[]{:S(2)}) collective-permute-start(bf16[12,128,128]{2,1,0:T(8,128)(2,1)} %copy-done.8), channel_id=1, source_target_pairs={{0,8},{8,0},{16,24},{24,16},{32,40},{40,32},{48,56},{56,48},{64,72... | collective-permute-start | bytes 1179656 | tf_op jit(solution)/shard_map/ppermute | solution.py:32
  52.4 39.5 %collective-permute-start.23 = (bf16[4,160,640]{2,1,0:T(8,128)(2,1)S(1)}, bf16[4,160,640]{2,1,0:T(8,128)(2,1)S(1)}, u32[]{:S(2)}, u32[]{:S(2)}) collective-permute-start(bf16[4,160,640]{2,1,0:T(8,128)(2,1)S(1)} %pad_maximum_fusion.refs_4_), channel_id=1, source_target_pairs={{0,128},{8,136},{16,144},{24,152},{32,160},{40,168},{48,176},{56,1... | collective-permute-start | bytes 2457608 | tf_op jit(solution)/shard_map/ppermute | solution.py:32
  67.3 14.6 %collective-permute-start.15 = (bf16[2,656,128]{2,1,0:T(8,128)(2,1)}, bf16[2,656,128]{2,1,0:T(8,128)(2,1)S(1)}, u32[]{:S(2)}, u32[]{:S(2)}) collective-permute-start(bf16[2,656,128]{2,1,0:T(8,128)(2,1)} %get-tuple-element.32), channel_id=1, source_target_pairs={{0,192},{8,200},{16,208},{24,216},{32,224},{40,232},{48,240},{56,2... | collective-permute-start | bytes 1007624 | tf_op jit(solution)/shard_map/ppermute | solution.py:32
  69.9 21.7 %collective-permute-start.16 = (bf16[2,656,128]{2,1,0:T(8,128)(2,1)}, bf16[2,656,128]{2,1,0:T(8,128)(2,1)S(1)}, u32[]{:S(2)}, u32[]{:S(2)}) collective-permute-start(bf16[2,656,128]{2,1,0:T(8,128)(2,1)} %get-tuple-element.33), channel_id=1, source_target_pairs={{0,64},{8,72},{16,80},{24,88},{32,96},{40,104},{48,112},{56,120},{... | collective-permute-start | bytes 1007624 | tf_op jit(solution)/shard_map/ppermute | solution.py:32
  69.9 22.0 %collective-permute-start.17 = (bf16[2,656,128]{2,1,0:T(8,128)(2,1)}, bf16[2,656,128]{2,1,0:T(8,128)(2,1)S(1)}, u32[]{:S(2)}, u32[]{:S(2)}) collective-permute-start(bf16[2,656,128]{2,1,0:T(8,128)(2,1)} %get-tuple-element.34), channel_id=1, source_target_pairs={{0,128},{8,136},{16,144},{24,152},{32,160},{40,168},{48,176},{56,1... | collective-permute-start | bytes 1007624 | tf_op jit(solution)/shard_map/ppermute | solution.py:32
  76.0 18.3 %collective-permute-start.18 = (bf16[4,160,640]{2,1,0:T(8,128)(2,1)S(1)}, bf16[4,160,640]{2,1,0:T(8,128)(2,1)}, u32[]{:S(2)}, u32[]{:S(2)}) collective-permute-start(bf16[4,160,640]{2,1,0:T(8,128)(2,1)S(1)} %pad_maximum_fusion.refs_4_), channel_id=1, source_target_pairs={{0,8},{8,0},{16,24},{24,16},{32,40},{40,32},{48,56},{56,48},{64,72... | collective-permute-start | bytes 2457608 | tf_op jit(solution)/shard_map/ppermute | solution.py:32
  81.9 12.4 %collective-permute-start.22 = (bf16[4,160,640]{2,1,0:T(8,128)(2,1)S(1)}, bf16[4,160,640]{2,1,0:T(8,128)(2,1)}, u32[]{:S(2)}, u32[]{:S(2)}) collective-permute-start(bf16[4,160,640]{2,1,0:T(8,128)(2,1)S(1)} %collective-permute-done.21.refs_8_), channel_id=1, source_target_pairs={{0,8},{8,0},{16,24},{24,16},{32,40},{40,32},{48,56},{56,48},{64,72... | collective-permute-start | bytes 2457608 | tf_op jit(solution)/shard_map/ppermute | solution.py:32
  91.9 4.3 %collective-permute-start.24 = (bf16[4,160,640]{2,1,0:T(8,128)(2,1)S(1)}, bf16[4,160,640]{2,1,0:T(8,128)(2,1)}, u32[]{:S(2)}, u32[]{:S(2)}) collective-permute-start(bf16[4,160,640]{2,1,0:T(8,128)(2,1)S(1)} %collective-permute-done.23.refs_10_), channel_id=1, source_target_pairs={{0,8},{8,0},{16,24},{24,16},{32,40},{40,32},{48,56},{56,48},{64,72... | collective-permute-start | bytes 2457608 | tf_op jit(solution)/shard_map/ppermute | solution.py:32
  103.4 16.3 %collective-permute-start.25 = (bf16[2,128,640]{2,1,0:T(8,128)(2,1)S(1)}, bf16[2,128,640]{2,1,0:T(8,128)(2,1)S(1)}, u32[]{:S(2)}, u32[]{:S(2)}) collective-permute-start(bf16[2,128,640]{2,1,0:T(8,128)(2,1)S(1)} %get-tuple-element.39), channel_id=1, source_target_pairs={{0,2},{1,3},{2,4},{3,5},{4,6},{5,7},{6,0},{7,1},{8,10},{9,11},{10,... | collective-permute-start | bytes 983048 | tf_op jit(solution)/shard_map/ppermute | solution.py:48
  105.0 22.0 %collective-permute-start.26 = (bf16[2,128,640]{2,1,0:T(8,128)(2,1)S(1)}, bf16[2,128,640]{2,1,0:T(8,128)(2,1)S(1)}, u32[]{:S(2)}, u32[]{:S(2)}) collective-permute-start(bf16[2,128,640]{2,1,0:T(8,128)(2,1)S(1)} %get-tuple-element.40), channel_id=1, source_target_pairs={{0,6},{1,7},{2,0},{3,1},{4,2},{5,3},{6,4},{7,5},{8,14},{9,15},{10,... | collective-permute-start | bytes 983048 | tf_op jit(solution)/shard_map/ppermute | solution.py:48
  106.7 20.3 %collective-permute-start.27 = (bf16[2,128,640]{2,1,0:T(8,128)(2,1)S(1)}, bf16[2,128,640]{2,1,0:T(8,128)(2,1)S(1)}, u32[]{:S(2)}, u32[]{:S(2)}) collective-permute-start(bf16[2,128,640]{2,1,0:T(8,128)(2,1)S(1)} %get-tuple-element.41), channel_id=1, source_target_pairs={{0,4},{1,5},{2,6},{3,7},{4,0},{5,1},{6,2},{7,3},{8,12},{9,13},{10,... | collective-permute-start | bytes 983048 | tf_op jit(solution)/shard_map/ppermute | solution.py:48
  108.7 34.1 %collective-permute-start.29 = (bf16[4,128,640]{2,1,0:T(8,128)(2,1)S(1)}, bf16[4,128,640]{2,1,0:T(8,128)(2,1)S(1)}, u32[]{:S(2)}, u32[]{:S(2)}) collective-permute-start(bf16[4,128,640]{2,1,0:T(8,128)(2,1)S(1)} %get-tuple-element.43), channel_id=1, source_target_pairs={{0,1},{1,0},{2,3},{3,2},{4,5},{5,4},{6,7},{7,6},{8,9},{9,8},{10,11... | collective-permute-start | bytes 1966088 | tf_op jit(solution)/shard_map/ppermute | solution.py:48
  119.8 13.3 %collective-permute-start.30 = (bf16[4,128,128]{2,1,0:T(8,128)(2,1)S(1)}, bf16[4,128,128]{2,1,0:T(8,128)(2,1)S(1)}, u32[]{:S(2)}, u32[]{:S(2)}) collective-permute-start(bf16[4,128,128]{2,1,0:T(8,128)(2,1)S(1)} %copy-done.21), channel_id=1, source_target_pairs={{0,192},{8,200},{16,208},{24,216},{32,224},{40,232},{48,240},{56,2... | collective-permute-start | bytes 393224 | tf_op jit(solution)/shard_map/ppermute | solution.py:32
  127.0 16.0 %collective-permute-start.31 = (bf16[4,128,128]{2,1,0:T(8,128)(2,1)S(1)}, bf16[4,128,128]{2,1,0:T(8,128)(2,1)S(1)}, u32[]{:S(2)}, u32[]{:S(2)}) collective-permute-start(bf16[4,128,128]{2,1,0:T(8,128)(2,1)S(1)} %copy-done.20), channel_id=1, source_target_pairs={{0,64},{8,72},{16,80},{24,88},{32,96},{40,104},{48,112},{56,120},{... | collective-permute-start | bytes 393224 | tf_op jit(solution)/shard_map/ppermute | solution.py:32
  127.2 20.3 %collective-permute-start.28 = (bf16[128,640]{1,0:T(8,128)(2,1)S(1)}, bf16[128,640]{1,0:T(8,128)(2,1)S(1)}, u32[]{:S(2)}, u32[]{:S(2)}) collective-permute-start(bf16[128,640]{1,0:T(8,128)(2,1)S(1)} %fusion.6), channel_id=1, source_target_pairs={{0,1},{1,0},{2,3},{3,2},{4,5},{5,4},{6,7},{7,6},{8,9},{9,8},{10,11... | collective-permute-start | bytes 491528 | tf_op jit(solution)/shard_map/ppermute | solution.py:48
  133.1 21.6 %collective-permute-start.35 = (bf16[4,128,128]{2,1,0:T(8,128)(2,1)S(1)}, bf16[4,128,128]{2,1,0:T(8,128)(2,1)S(1)}, u32[]{:S(2)}, u32[]{:S(2)}) collective-permute-start(bf16[4,128,128]{2,1,0:T(8,128)(2,1)S(1)} %copy-done.19), channel_id=1, source_target_pairs={{0,128},{8,136},{16,144},{24,152},{32,160},{40,168},{48,176},{56,1... | collective-permute-start | bytes 393224 | tf_op jit(solution)/shard_map/ppermute | solution.py:32
  143.6 9.6 %collective-permute-start.32 = (bf16[128,640]{1,0:T(8,128)(2,1)S(1)}, bf16[128,640]{1,0:T(8,128)(2,1)S(1)}, u32[]{:S(2)}, u32[]{:S(2)}) collective-permute-start(bf16[128,640]{1,0:T(8,128)(2,1)S(1)} %get-tuple-element.81), channel_id=1, source_target_pairs={{0,2},{1,3},{2,4},{3,5},{4,6},{5,7},{6,0},{7,1},{8,10},{9,11},{10,... | collective-permute-start | bytes 491528 | tf_op jit(solution)/shard_map/ppermute | solution.py:48
  144.8 8.4 %collective-permute-start.34 = (bf16[128,640]{1,0:T(8,128)(2,1)S(1)}, bf16[128,640]{1,0:T(8,128)(2,1)S(1)}, u32[]{:S(2)}, u32[]{:S(2)}) collective-permute-start(bf16[128,640]{1,0:T(8,128)(2,1)S(1)} %get-tuple-element.82), channel_id=1, source_target_pairs={{0,4},{1,5},{2,6},{3,7},{4,0},{5,1},{6,2},{7,3},{8,12},{9,13},{10,... | collective-permute-start | bytes 491528 | tf_op jit(solution)/shard_map/ppermute | solution.py:48
  147.1 6.8 %collective-permute-start.33 = (bf16[128,640]{1,0:T(8,128)(2,1)S(1)}, bf16[128,640]{1,0:T(8,128)(2,1)S(1)}, u32[]{:S(2)}, u32[]{:S(2)}) collective-permute-start(bf16[128,640]{1,0:T(8,128)(2,1)S(1)} %get-tuple-element.83), channel_id=1, source_target_pairs={{0,6},{1,7},{2,0},{3,1},{4,2},{5,3},{6,4},{7,5},{8,14},{9,15},{10,... | collective-permute-start | bytes 491528 | tf_op jit(solution)/shard_map/ppermute | solution.py:48
  (27 other events, 267.9 us)

commit v8 on v7

--- a/solution.py
+++ b/solution.py
@@ -269,9 +269,9 @@
         result[i, wide : wide + 16, :] = stats.astype(jnp.bfloat16)
         return unused
 
+    lax.fori_loop(0, nq * per, one_block, 0)
     backs = []
-    for r in reversed(range(nq)):
-        lax.fori_loop(r * per, (r + 1) * per, one_block, 0)
+    for r in range(nq):
         backs.append(
             pltpu.make_async_copy(result.at[pl.ds(r * per, per)], out_refs[r], out_sem.at[r])
         )

time: 161 us -> 150 us (0.932)
  the two profiles are of different devices: /device:TPU:168 before, /device:TPU:6 now
where the time goes in v8:
time: 150 us; the launch traced here: 147 us
  waiting for transfers between devices  54.6 us (36%)
  starting transfers between devices  46.6 us (31%)
  Pallas kernels  27.9 us (19%)
  other arithmetic  13.3 us (9%)
  local copies, waits for them, and re-layouts  3.7 us (2%)
    ppermute x28, starting transfers between devices, shift(): return lax.ppermute(value, 'blk', blk_perm(dy, dz, dc))  38.8 us
    ppermute x28, waiting for transfers between devices, shift(): return lax.ppermute(value, 'blk', blk_perm(dy, dz, dc))  35.2 us
    ppermute x8, waiting for transfers between devices, head_shift(): return lax.ppermute(value, 'head', pairs)  19.4 us
    pallas_call x1, Pallas kernels, attend(): pl.pallas_call(functools.partial(attend_kernel, log_scale, nkv, nq), out_...  15.9 us
    ppermute x8, starting transfers between devices, head_shift(): return lax.ppermute(value, 'head', pairs)  7.87 us
    pallas_call x1, Pallas kernels, finish(): pl.pallas_call(functools.partial(finish_kernel, heads, nparts, nw), out_s...  7.22 us
    reduce_sum x2, other arithmetic, table_entry(): return jnp.sum(jnp.where(match, block_table[None], 0), axis=(1, 2))  3.89 us
  transfers between devices with their start and end apart: 36, of which 15 were waited for; matrix products, arithmetic and copies ran while one was open for 10% of the time, Pallas kernels for 12%

profile of v8, /device:TPU:6, one launch (start us, length us, event | category | flops | bytes accessed | tf_op | source)
XLA Modules:
  0.0 147.5 jit_solution(15721232749570496020)
XLA Ops:
  0.7 6.4 %collective-permute-start.1 = (bf16[160,640]{1,0:T(8,128)(2,1)}, bf16[160,640]{1,0:T(8,128)(2,1)S(1)}, u32[]{:S(2)}, u32[]{:S(2)}) collective-permute-start(bf16[160,640]{1,0:T(8,128)(2,1)} %param.17), channel_id=1, source_target_pairs={{0,48},{8,56},{16,0},{24,8},{32,16},{40,24},{48,32},{56,40},{64,11... | collective-permute-start | bytes 614408 | tf_op jit(solution)/shard_map/ppermute | solution.py:32
  7.0 3.8 %collective-permute-start.2 = (bf16[160,640]{1,0:T(8,128)(2,1)}, bf16[160,640]{1,0:T(8,128)(2,1)S(1)}, u32[]{:S(2)}, u32[]{:S(2)}) collective-permute-start(bf16[160,640]{1,0:T(8,128)(2,1)} %param.17), channel_id=1, source_target_pairs={{0,32},{8,40},{16,48},{24,56},{32,0},{40,8},{48,16},{56,24},{64,96... | collective-permute-start | bytes 614408 | tf_op jit(solution)/shard_map/ppermute | solution.py:32
  10.9 3.0 %collective-permute-start.4 = (bf16[5,256,128]{2,1,0:T(8,128)(2,1)}, bf16[5,256,128]{2,1,0:T(8,128)(2,1)S(1)}, u32[]{:S(2)}, u32[]{:S(2)}) collective-permute-start(bf16[5,256,128]{2,1,0:T(8,128)(2,1)} %bitcast.47), channel_id=1, source_target_pairs={{0,192},{8,200},{16,208},{24,216},{32,224},{40,232},{48,240},{56,2... | collective-permute-start | bytes 983048 | tf_op jit(solution)/shard_map/ppermute | solution.py:32
  17.2 2.6 %select_reduce_fusion.1 = (s32[48]{0:T(128)S(1)}, s32[48]{0:T(128)S(1)}) fusion(s32[8,64]{1,0:T(8,128)} %param.20, pred[48,64]{1,0:T(8,128)(4,1)S(1)} %iota_compare_fusion.2, pred[48,8]{1,0:T(8,128)(4,1)S(1)} %copy.19, s32[8,64]{1,0:T(8,128)S(1)} %add_add_fusion, pred[8,64]{1,0:T(8,128)(4,1)S(1)} %iota_compare_fusion.8, s32[48]{0:T(128)S(1)} %add.594), kind=kLoop, calls=%fused_computation.13 | loop fusion | flops 171936 | bytes 8640 | tf_op jit(solution)/shard_map/reduce_sum | solution.py:75
  23.0 1.8 %pack.1.refs_0_ = bf16[12,128,128]{2,1,0:T(8,128)(2,1)} custom-call(bf16[6,128,128]{2,1,0:T(8,128)(2,1)} %bitcast.37, bf16[6,128,128]{2,1,0:T(8,128)(2,1)} %bitcast.39, bf16[2,128,128]{2,1,0:T(8,128)(2,1)} %bitcast.45, bf16[2,128,128]{2,1,0:T(8,128)(2,1)} %bitcast.46), custom_call_target="tpu_custom_call" | custom-call | tf_op jit(solution)/shard_map/pack/pallas_call | solution.py:100
  24.9 2.3 %collective-permute-start.14 = (bf16[5,256,128]{2,1,0:T(8,128)(2,1)S(1)}, bf16[5,256,128]{2,1,0:T(8,128)(2,1)S(1)}, u32[]{:S(2)}, u32[]{:S(2)}) collective-permute-start(bf16[5,256,128]{2,1,0:T(8,128)(2,1)S(1)} %bitcast.50), channel_id=1, source_target_pairs={{0,128},{8,136},{16,144},{24,152},{32,160},{40,168},{48,176},{56,1... | collective-permute-start | bytes 983048 | tf_op jit(solution)/shard_map/ppermute | solution.py:32
  27.4 3.2 %collective-permute-start.8 = (bf16[12,128,128]{2,1,0:T(8,128)(2,1)S(1)}, bf16[12,128,128]{2,1,0:T(8,128)(2,1)S(1)}, u32[]{:S(2)}, u32[]{:S(2)}) collective-permute-start(bf16[12,128,128]{2,1,0:T(8,128)(2,1)S(1)} %copy-done), channel_id=1, source_target_pairs={{0,48},{8,56},{16,0},{24,8},{32,16},{40,24},{48,32},{56,40},{64,11... | collective-permute-start | bytes 1179656 | tf_op jit(solution)/shard_map/ppermute | solution.py:32
  31.2 3.6 %collective-permute-done.14.refs_13_ = bf16[5,256,128]{2,1,0:T(8,128)(2,1)S(1)} collective-permute-done((bf16[5,256,128]{2,1,0:T(8,128)(2,1)S(1)}, bf16[5,256,128]{2,1,0:T(8,128)(2,1)S(1)}, u32[]{:S(2)}, u32[]{:S(2)}) %collective-permute-start.14) | collective-permute-done | bytes 327712 | tf_op jit(solution)/shard_map/ppermute | solution.py:32
  35.6 2.9 %collective-permute-start.21 = (bf16[4,160,640]{2,1,0:T(8,128)(2,1)S(1)}, bf16[4,160,640]{2,1,0:T(8,128)(2,1)S(1)}, u32[]{:S(2)}, u32[]{:S(2)}) collective-permute-start(bf16[4,160,640]{2,1,0:T(8,128)(2,1)S(1)} %pad_maximum_fusion.refs_4_), channel_id=1, source_target_pairs={{0,192},{8,200},{16,208},{24,216},{32,224},{40,232},{48,240},{56,2... | collective-permute-start | bytes 2457608 | tf_op jit(solution)/shard_map/ppermute | solution.py:32
  39.2 10.0 %collective-permute-done.8.refs_4_ = bf16[12,128,128]{2,1,0:T(8,128)(2,1)S(1)} collective-permute-done((bf16[12,128,128]{2,1,0:T(8,128)(2,1)S(1)}, bf16[12,128,128]{2,1,0:T(8,128)(2,1)S(1)}, u32[]{:S(2)}, u32[]{:S(2)}) %collective-permute-start.8) | collective-permute-done | bytes 393248 | tf_op jit(solution)/shard_map/ppermute | solution.py:32
  49.2 2.8 %collective-permute-start.11 = (bf16[6,128,128]{2,1,0:T(8,128)(2,1)S(1)}, bf16[6,128,128]{2,1,0:T(8,128)(2,1)S(1)}, u32[]{:S(2)}, u32[]{:S(2)}) collective-permute-start(bf16[6,128,128]{2,1,0:T(8,128)(2,1)S(1)} %slice.37), channel_id=1, source_target_pairs={{0,48},{8,56},{16,0},{24,8},{32,16},{40,24},{48,32},{56,40},{64,11... | collective-permute-start | bytes 589832 | tf_op jit(solution)/shard_map/ppermute | solution.py:32
  52.4 2.6 %collective-permute-start.10 = (bf16[6,128,128]{2,1,0:T(8,128)(2,1)S(1)}, bf16[6,128,128]{2,1,0:T(8,128)(2,1)}, u32[]{:S(2)}, u32[]{:S(2)}) collective-permute-start(bf16[6,128,128]{2,1,0:T(8,128)(2,1)S(1)} %slice.36), channel_id=1, source_target_pairs={{0,16},{8,24},{16,32},{24,40},{32,48},{40,56},{48,0},{56,8},{64,80... | collective-permute-start | bytes 589832 | tf_op jit(solution)/shard_map/ppermute | solution.py:32
  55.2 4.8 %collective-permute-done.11.refs_7_ = bf16[6,128,128]{2,1,0:T(8,128)(2,1)S(1)} collective-permute-done((bf16[6,128,128]{2,1,0:T(8,128)(2,1)S(1)}, bf16[6,128,128]{2,1,0:T(8,128)(2,1)S(1)}, u32[]{:S(2)}, u32[]{:S(2)}) %collective-permute-start.11) | collective-permute-done | bytes 196640 | tf_op jit(solution)/shard_map/ppermute | solution.py:32
  62.3 1.6 %collective-permute-start.23 = (bf16[4,160,640]{2,1,0:T(8,128)(2,1)S(1)}, bf16[4,160,640]{2,1,0:T(8,128)(2,1)S(1)}, u32[]{:S(2)}, u32[]{:S(2)}) collective-permute-start(bf16[4,160,640]{2,1,0:T(8,128)(2,1)S(1)} %pad_maximum_fusion.refs_4_), channel_id=1, source_target_pairs={{0,128},{8,136},{16,144},{24,152},{32,160},{40,168},{48,176},{56,1... | collective-permute-start | bytes 2457608 | tf_op jit(solution)/shard_map/ppermute | solution.py:32
  64.1 15.9 %attend.1 = (bf16[2,656,128]{2,1,0:T(8,128)(2,1)}, bf16[2,656,128]{2,1,0:T(8,128)(2,1)}, bf16[2,656,128]{2,1,0:T(8,128)(2,1)}, bf16[2,656,128]{2,1,0:T(8,128)(2,...) custom-call(s32[8]{0:T(128)} %copy-done.13, ...), custom_call_target="tpu_custom_call" | custom-call | flops 5000000000 | bytes 8000000 | tf_op jit(solution)/shard_map/attend/pallas_call | solution.py:295
  80.1 2.0 %collective-permute-start.16 = (bf16[2,656,128]{2,1,0:T(8,128)(2,1)}, bf16[2,656,128]{2,1,0:T(8,128)(2,1)S(1)}, u32[]{:S(2)}, u32[]{:S(2)}) collective-permute-start(bf16[2,656,128]{2,1,0:T(8,128)(2,1)} %get-tuple-element.33), channel_id=1, source_target_pairs={{0,64},{8,72},{16,80},{24,88},{32,96},{40,104},{48,112},{56,120},{... | collective-permute-start | bytes 1007624 | tf_op jit(solution)/shard_map/ppermute | solution.py:32
  82.1 2.8 %collective-permute-start.17 = (bf16[2,656,128]{2,1,0:T(8,128)(2,1)}, bf16[2,656,128]{2,1,0:T(8,128)(2,1)S(1)}, u32[]{:S(2)}, u32[]{:S(2)}) collective-permute-start(bf16[2,656,128]{2,1,0:T(8,128)(2,1)} %get-tuple-element.34), channel_id=1, source_target_pairs={{0,128},{8,136},{16,144},{24,152},{32,160},{40,168},{48,176},{56,1... | collective-permute-start | bytes 1007624 | tf_op jit(solution)/shard_map/ppermute | solution.py:32
  85.4 5.5 %collective-permute-done.15.refs_1_ = bf16[2,656,128]{2,1,0:T(8,128)(2,1)S(1)} collective-permute-done((bf16[2,656,128]{2,1,0:T(8,128)(2,1)}, bf16[2,656,128]{2,1,0:T(8,128)(2,1)S(1)}, u32[]{:S(2)}, u32[]{:S(2)}) %collective-permute-start.15) | collective-permute-done | bytes 335904 | tf_op jit(solution)/shard_map/ppermute | solution.py:32
  92.3 8.8 %collective-permute-done.17.refs_3_ = bf16[2,656,128]{2,1,0:T(8,128)(2,1)S(1)} collective-permute-done((bf16[2,656,128]{2,1,0:T(8,128)(2,1)}, bf16[2,656,128]{2,1,0:T(8,128)(2,1)S(1)}, u32[]{:S(2)}, u32[]{:S(2)}) %collective-permute-start.17) | collective-permute-done | bytes 335904 | tf_op jit(solution)/shard_map/ppermute | solution.py:32
  102.1 1.3 select_reduce_fusion
  103.8 7.2 %finish.1 = (bf16[2,128,640]{2,1,0:T(8,128)(2,1)S(1)}, bf16[2,128,640]{2,1,0:T(8,128)(2,1)S(1)}, bf16[2,128,640]{2,1,0:T(8,128)(2,1)S(1)}, bf16[2,128,640]{2,1,0...) custom-call(s32[32]{0:T(128)S(1)} %fusion.31.pieces, ...), custom_call_target="tpu_custom_call" | custom-call | flops 2000000000 | bytes 12000000 | tf_op jit(solution)/shard_map/finish/pallas_call | solution.py:393
  111.6 1.5 %collective-permute-start.26 = (bf16[2,128,640]{2,1,0:T(8,128)(2,1)S(1)}, bf16[2,128,640]{2,1,0:T(8,128)(2,1)S(1)}, u32[]{:S(2)}, u32[]{:S(2)}) collective-permute-start(bf16[2,128,640]{2,1,0:T(8,128)(2,1)S(1)} %get-tuple-element.40), channel_id=1, source_target_pairs={{0,6},{1,7},{2,0},{3,1},{4,2},{5,3},{6,4},{7,5},{8,14},{9,15},{10,... | collective-permute-start | bytes 983048 | tf_op jit(solution)/shard_map/ppermute | solution.py:48
  113.2 1.4 collective-permute-start.27
  115.4 6.3 %collective-permute-done.25 = bf16[2,128,640]{2,1,0:T(8,128)(2,1)S(1)} collective-permute-done((bf16[2,128,640]{2,1,0:T(8,128)(2,1)S(1)}, bf16[2,128,640]{2,1,0:T(8,128)(2,1)S(1)}, u32[]{:S(2)}, u32[]{:S(2)}) %collective-permute-start.25) | collective-permute-done | bytes 327712 | tf_op jit(solution)/shard_map/ppermute | solution.py:48
  121.7 2.0 %collective-permute-start.31 = (bf16[4,128,128]{2,1,0:T(8,128)(2,1)S(1)}, bf16[4,128,128]{2,1,0:T(8,128)(2,1)S(1)}, u32[]{:S(2)}, u32[]{:S(2)}) collective-permute-start(bf16[4,128,128]{2,1,0:T(8,128)(2,1)S(1)} %copy-done.20), channel_id=1, source_target_pairs={{0,64},{8,72},{16,80},{24,88},{32,96},{40,104},{48,112},{56,120},{... | collective-permute-start | bytes 393224 | tf_op jit(solution)/shard_map/ppermute | solution.py:32
  123.7 5.6 %collective-permute-done.26 = bf16[2,128,640]{2,1,0:T(8,128)(2,1)S(1)} collective-permute-done((bf16[2,128,640]{2,1,0:T(8,128)(2,1)S(1)}, bf16[2,128,640]{2,1,0:T(8,128)(2,1)S(1)}, u32[]{:S(2)}, u32[]{:S(2)}) %collective-permute-start.26) | collective-permute-done | bytes 327712 | tf_op jit(solution)/shard_map/ppermute | solution.py:48
  131.6 2.1 %collective-permute-start.32 = (bf16[128,640]{1,0:T(8,128)(2,1)S(1)}, bf16[128,640]{1,0:T(8,128)(2,1)S(1)}, u32[]{:S(2)}, u32[]{:S(2)}) collective-permute-start(bf16[128,640]{1,0:T(8,128)(2,1)S(1)} %get-tuple-element.81), channel_id=1, source_target_pairs={{0,2},{1,3},{2,4},{3,5},{4,6},{5,7},{6,0},{7,1},{8,10},{9,11},{10,... | collective-permute-start | bytes 491528 | tf_op jit(solution)/shard_map/ppermute | solution.py:48
  133.7 2.1 %collective-permute-start.34 = (bf16[128,640]{1,0:T(8,128)(2,1)S(1)}, bf16[128,640]{1,0:T(8,128)(2,1)S(1)}, u32[]{:S(2)}, u32[]{:S(2)}) collective-permute-start(bf16[128,640]{1,0:T(8,128)(2,1)S(1)} %get-tuple-element.82), channel_id=1, source_target_pairs={{0,4},{1,5},{2,6},{3,7},{4,0},{5,1},{6,2},{7,3},{8,12},{9,13},{10,... | collective-permute-start | bytes 491528 | tf_op jit(solution)/shard_map/ppermute | solution.py:48
  135.8 3.4 %collective-permute-done.32 = bf16[128,640]{1,0:T(8,128)(2,1)S(1)} collective-permute-done((bf16[128,640]{1,0:T(8,128)(2,1)S(1)}, bf16[128,640]{1,0:T(8,128)(2,1)S(1)}, u32[]{:S(2)}, u32[]{:S(2)}) %collective-permute-start.32) | collective-permute-done | bytes 163872 | tf_op jit(solution)/shard_map/ppermute | solution.py:48
  139.2 2.0 %collective-permute-done.34 = bf16[128,640]{1,0:T(8,128)(2,1)S(1)} collective-permute-done((bf16[128,640]{1,0:T(8,128)(2,1)S(1)}, bf16[128,640]{1,0:T(8,128)(2,1)S(1)}, u32[]{:S(2)}, u32[]{:S(2)}) %collective-permute-start.34) | collective-permute-done | bytes 163872 | tf_op jit(solution)/shard_map/ppermute | solution.py:48
  141.2 1.7 %collective-permute-done.33 = bf16[128,640]{1,0:T(8,128)(2,1)S(1)} collective-permute-done((bf16[128,640]{1,0:T(8,128)(2,1)S(1)}, bf16[128,640]{1,0:T(8,128)(2,1)S(1)}, u32[]{:S(2)}, u32[]{:S(2)}) %collective-permute-start.33) | collective-permute-done | bytes 163872 | tf_op jit(solution)/shard_map/ppermute | solution.py:48
  144.4 2.9 %refill.1 = (bf16[6,128,128]{2,1,0:T(8,128)(2,1)}, bf16[6,128,128]{2,1,0:T(8,128)(2,1)}) custom-call(s32[2]{0:T(128)} %compare_select_fusion.25.source, bf16[6,128,128]{2,1,0:T(8,128)(2,1)} %bitcast.38, bf16[6,128,128]{2,1,0:T(8,128)(2,1)} %bitcast.40, bf16[4,128,128]{2,1,0:T(8,128)(2,1)} %get-tuple-element.49.refs_0_, bf16[4,128,128]{2,1,0:T(8,128)(2,1)} %copy-done.5, ...), custom_call_target="tpu_custom_call" | custom-call | tf_op jit(solution)/shard_map/refill/pallas_call | solution.py:450
  (170 shorter events, 20.1 us)
Async XLA Ops:
  0.7 26.5 %collective-permute-start.1 = (bf16[160,640]{1,0:T(8,128)(2,1)}, bf16[160,640]{1,0:T(8,128)(2,1)S(1)}, u32[]{:S(2)}, u32[]{:S(2)}) collective-permute-start(bf16[160,640]{1,0:T(8,128)(2,1)} %param.17), channel_id=1, source_target_pairs={{0,48},{8,56},{16,0},{24,8},{32,16},{40,24},{48,32},{56,40},{64,11... | collective-permute-start | bytes 614408 | tf_op jit(solution)/shard_map/ppermute | solution.py:32
  7.0 20.2 %collective-permute-start = (bf16[160,640]{1,0:T(8,128)(2,1)}, bf16[160,640]{1,0:T(8,128)(2,1)S(1)}, u32[]{:S(2)}, u32[]{:S(2)}) collective-permute-start(bf16[160,640]{1,0:T(8,128)(2,1)} %param.17), channel_id=1, source_target_pairs={{0,16},{8,24},{16,32},{24,40},{32,48},{40,56},{48,0},{56,8},{64,80... | collective-permute-start | bytes 614408 | tf_op jit(solution)/shard_map/ppermute | solution.py:32
  7.0 20.2 %collective-permute-start.2 = (bf16[160,640]{1,0:T(8,128)(2,1)}, bf16[160,640]{1,0:T(8,128)(2,1)S(1)}, u32[]{:S(2)}, u32[]{:S(2)}) collective-permute-start(bf16[160,640]{1,0:T(8,128)(2,1)} %param.17), channel_id=1, source_target_pairs={{0,32},{8,40},{16,48},{24,56},{32,0},{40,8},{48,16},{56,24},{64,96... | collective-permute-start | bytes 614408 | tf_op jit(solution)/shard_map/ppermute | solution.py:32
  10.9 14.0 %collective-permute-start.4 = (bf16[5,256,128]{2,1,0:T(8,128)(2,1)}, bf16[5,256,128]{2,1,0:T(8,128)(2,1)S(1)}, u32[]{:S(2)}, u32[]{:S(2)}) collective-permute-start(bf16[5,256,128]{2,1,0:T(8,128)(2,1)} %bitcast.47), channel_id=1, source_target_pairs={{0,192},{8,200},{16,208},{24,216},{32,224},{40,232},{48,240},{56,2... | collective-permute-start | bytes 983048 | tf_op jit(solution)/shard_map/ppermute | solution.py:32
  13.9 11.0 %collective-permute-start.3 = (bf16[5,256,128]{2,1,0:T(8,128)(2,1)}, bf16[5,256,128]{2,1,0:T(8,128)(2,1)S(1)}, u32[]{:S(2)}, u32[]{:S(2)}) collective-permute-start(bf16[5,256,128]{2,1,0:T(8,128)(2,1)} %bitcast.48), channel_id=1, source_target_pairs={{0,64},{8,72},{16,80},{24,88},{32,96},{40,104},{48,112},{56,120},{... | collective-permute-start | bytes 983048 | tf_op jit(solution)/shard_map/ppermute | solution.py:32
  24.9 9.9 %collective-permute-start.14 = (bf16[5,256,128]{2,1,0:T(8,128)(2,1)S(1)}, bf16[5,256,128]{2,1,0:T(8,128)(2,1)S(1)}, u32[]{:S(2)}, u32[]{:S(2)}) collective-permute-start(bf16[5,256,128]{2,1,0:T(8,128)(2,1)S(1)} %bitcast.50), channel_id=1, source_target_pairs={{0,128},{8,136},{16,144},{24,152},{32,160},{40,168},{48,176},{56,1... | collective-permute-start | bytes 983048 | tf_op jit(solution)/shard_map/ppermute | solution.py:32
  27.4 21.8 %collective-permute-start.8 = (bf16[12,128,128]{2,1,0:T(8,128)(2,1)S(1)}, bf16[12,128,128]{2,1,0:T(8,128)(2,1)S(1)}, u32[]{:S(2)}, u32[]{:S(2)}) collective-permute-start(bf16[12,128,128]{2,1,0:T(8,128)(2,1)S(1)} %copy-done), channel_id=1, source_target_pairs={{0,48},{8,56},{16,0},{24,8},{32,16},{40,24},{48,32},{56,40},{64,11... | collective-permute-start | bytes 1179656 | tf_op jit(solution)/shard_map/ppermute | solution.py:32
  30.6 21.8 %collective-permute-start.6 = (bf16[12,128,128]{2,1,0:T(8,128)(2,1)S(1)}, bf16[12,128,128]{2,1,0:T(8,128)(2,1)S(1)}, u32[]{:S(2)}, u32[]{:S(2)}) collective-permute-start(bf16[12,128,128]{2,1,0:T(8,128)(2,1)S(1)} %copy-done), channel_id=1, source_target_pairs={{0,16},{8,24},{16,32},{24,40},{32,48},{40,56},{48,0},{56,8},{64,80... | collective-permute-start | bytes 1179656 | tf_op jit(solution)/shard_map/ppermute | solution.py:32
  35.6 25.2 %collective-permute-start.21 = (bf16[4,160,640]{2,1,0:T(8,128)(2,1)S(1)}, bf16[4,160,640]{2,1,0:T(8,128)(2,1)S(1)}, u32[]{:S(2)}, u32[]{:S(2)}) collective-permute-start(bf16[4,160,640]{2,1,0:T(8,128)(2,1)S(1)} %pad_maximum_fusion.refs_4_), channel_id=1, source_target_pairs={{0,192},{8,200},{16,208},{24,216},{32,224},{40,232},{48,240},{56,2... | collective-permute-start | bytes 2457608 | tf_op jit(solution)/shard_map/ppermute | solution.py:32
  38.5 22.9 %collective-permute-start.19 = (bf16[4,160,640]{2,1,0:T(8,128)(2,1)S(1)}, bf16[4,160,640]{2,1,0:T(8,128)(2,1)S(1)}, u32[]{:S(2)}, u32[]{:S(2)}) collective-permute-start(bf16[4,160,640]{2,1,0:T(8,128)(2,1)S(1)} %pad_maximum_fusion.refs_4_), channel_id=1, source_target_pairs={{0,64},{8,72},{16,80},{24,88},{32,96},{40,104},{48,112},{56,120},{... | collective-permute-start | bytes 2457608 | tf_op jit(solution)/shard_map/ppermute | solution.py:32
  49.2 10.8 %collective-permute-start.11 = (bf16[6,128,128]{2,1,0:T(8,128)(2,1)S(1)}, bf16[6,128,128]{2,1,0:T(8,128)(2,1)S(1)}, u32[]{:S(2)}, u32[]{:S(2)}) collective-permute-start(bf16[6,128,128]{2,1,0:T(8,128)(2,1)S(1)} %slice.37), channel_id=1, source_target_pairs={{0,48},{8,56},{16,0},{24,8},{32,16},{40,24},{48,32},{56,40},{64,11... | collective-permute-start | bytes 589832 | tf_op jit(solution)/shard_map/ppermute | solution.py:32
  52.4 8.4 %collective-permute-start.10 = (bf16[6,128,128]{2,1,0:T(8,128)(2,1)S(1)}, bf16[6,128,128]{2,1,0:T(8,128)(2,1)}, u32[]{:S(2)}, u32[]{:S(2)}) collective-permute-start(bf16[6,128,128]{2,1,0:T(8,128)(2,1)S(1)} %slice.36), channel_id=1, source_target_pairs={{0,16},{8,24},{16,32},{24,40},{32,48},{40,56},{48,0},{56,8},{64,80... | collective-permute-start | bytes 589832 | tf_op jit(solution)/shard_map/ppermute | solution.py:32
  55.0 7.2 %collective-permute-start.5 = (bf16[12,128,128]{2,1,0:T(8,128)(2,1)S(1)}, bf16[12,128,128]{2,1,0:T(8,128)(2,1)}, u32[]{:S(2)}, u32[]{:S(2)}) collective-permute-start(bf16[12,128,128]{2,1,0:T(8,128)(2,1)S(1)} %copy-done), channel_id=1, source_target_pairs={{0,8},{8,0},{16,24},{24,16},{32,40},{40,32},{48,56},{56,48},{64,72... | collective-permute-start | bytes 1179656 | tf_op jit(solution)/shard_map/ppermute | solution.py:32
  60.0 4.0 %collective-permute-start.9 = (bf16[12,128,128]{2,1,0:T(8,128)(2,1)}, bf16[12,128,128]{2,1,0:T(8,128)(2,1)}, u32[]{:S(2)}, u32[]{:S(2)}) collective-permute-start(bf16[12,128,128]{2,1,0:T(8,128)(2,1)} %copy-done.8), channel_id=1, source_target_pairs={{0,8},{8,0},{16,24},{24,16},{32,40},{40,32},{48,56},{56,48},{64,72... | collective-permute-start | bytes 1179656 | tf_op jit(solution)/shard_map/ppermute | solution.py:32
  62.3 38.8 %collective-permute-start.23 = (bf16[4,160,640]{2,1,0:T(8,128)(2,1)S(1)}, bf16[4,160,640]{2,1,0:T(8,128)(2,1)S(1)}, u32[]{:S(2)}, u32[]{:S(2)}) collective-permute-start(bf16[4,160,640]{2,1,0:T(8,128)(2,1)S(1)} %pad_maximum_fusion.refs_4_), channel_id=1, source_target_pairs={{0,128},{8,136},{16,144},{24,152},{32,160},{40,168},{48,176},{56,1... | collective-permute-start | bytes 2457608 | tf_op jit(solution)/shard_map/ppermute | solution.py:32
  80.0 10.9 %collective-permute-start.15 = (bf16[2,656,128]{2,1,0:T(8,128)(2,1)}, bf16[2,656,128]{2,1,0:T(8,128)(2,1)S(1)}, u32[]{:S(2)}, u32[]{:S(2)}) collective-permute-start(bf16[2,656,128]{2,1,0:T(8,128)(2,1)} %get-tuple-element.32), channel_id=1, source_target_pairs={{0,192},{8,200},{16,208},{24,216},{32,224},{40,232},{48,240},{56,2... | collective-permute-start | bytes 1007624 | tf_op jit(solution)/shard_map/ppermute | solution.py:32
  80.1 12.1 %collective-permute-start.16 = (bf16[2,656,128]{2,1,0:T(8,128)(2,1)}, bf16[2,656,128]{2,1,0:T(8,128)(2,1)S(1)}, u32[]{:S(2)}, u32[]{:S(2)}) collective-permute-start(bf16[2,656,128]{2,1,0:T(8,128)(2,1)} %get-tuple-element.33), channel_id=1, source_target_pairs={{0,64},{8,72},{16,80},{24,88},{32,96},{40,104},{48,112},{56,120},{... | collective-permute-start | bytes 1007624 | tf_op jit(solution)/shard_map/ppermute | solution.py:32
  82.1 18.9 %collective-permute-start.17 = (bf16[2,656,128]{2,1,0:T(8,128)(2,1)}, bf16[2,656,128]{2,1,0:T(8,128)(2,1)S(1)}, u32[]{:S(2)}, u32[]{:S(2)}) collective-permute-start(bf16[2,656,128]{2,1,0:T(8,128)(2,1)} %get-tuple-element.34), channel_id=1, source_target_pairs={{0,128},{8,136},{16,144},{24,152},{32,160},{40,168},{48,176},{56,1... | collective-permute-start | bytes 1007624 | tf_op jit(solution)/shard_map/ppermute | solution.py:32
  85.0 18.4 %collective-permute-start.18 = (bf16[4,160,640]{2,1,0:T(8,128)(2,1)S(1)}, bf16[4,160,640]{2,1,0:T(8,128)(2,1)}, u32[]{:S(2)}, u32[]{:S(2)}) collective-permute-start(bf16[4,160,640]{2,1,0:T(8,128)(2,1)S(1)} %pad_maximum_fusion.refs_4_), channel_id=1, source_target_pairs={{0,8},{8,0},{16,24},{24,16},{32,40},{40,32},{48,56},{56,48},{64,72... | collective-permute-start | bytes 2457608 | tf_op jit(solution)/shard_map/ppermute | solution.py:32
  90.9 12.5 %collective-permute-start.22 = (bf16[4,160,640]{2,1,0:T(8,128)(2,1)S(1)}, bf16[4,160,640]{2,1,0:T(8,128)(2,1)}, u32[]{:S(2)}, u32[]{:S(2)}) collective-permute-start(bf16[4,160,640]{2,1,0:T(8,128)(2,1)S(1)} %collective-permute-done.21.refs_8_), channel_id=1, source_target_pairs={{0,8},{8,0},{16,24},{24,16},{32,40},{40,32},{48,56},{56,48},{64,72... | collective-permute-start | bytes 2457608 | tf_op jit(solution)/shard_map/ppermute | solution.py:32
  92.1 11.3 %collective-permute-start.20 = (bf16[4,160,640]{2,1,0:T(8,128)(2,1)S(1)}, bf16[4,160,640]{2,1,0:T(8,128)(2,1)}, u32[]{:S(2)}, u32[]{:S(2)}) collective-permute-start(bf16[4,160,640]{2,1,0:T(8,128)(2,1)S(1)} %collective-permute-done.19.refs_6_), channel_id=1, source_target_pairs={{0,8},{8,0},{16,24},{24,16},{32,40},{40,32},{48,56},{56,48},{64,72... | collective-permute-start | bytes 2457608 | tf_op jit(solution)/shard_map/ppermute | solution.py:32
  111.1 10.6 %collective-permute-start.25 = (bf16[2,128,640]{2,1,0:T(8,128)(2,1)S(1)}, bf16[2,128,640]{2,1,0:T(8,128)(2,1)S(1)}, u32[]{:S(2)}, u32[]{:S(2)}) collective-permute-start(bf16[2,128,640]{2,1,0:T(8,128)(2,1)S(1)} %get-tuple-element.39), channel_id=1, source_target_pairs={{0,2},{1,3},{2,4},{3,5},{4,6},{5,7},{6,0},{7,1},{8,10},{9,11},{10,... | collective-permute-start | bytes 983048 | tf_op jit(solution)/shard_map/ppermute | solution.py:48
  111.6 17.7 %collective-permute-start.26 = (bf16[2,128,640]{2,1,0:T(8,128)(2,1)S(1)}, bf16[2,128,640]{2,1,0:T(8,128)(2,1)S(1)}, u32[]{:S(2)}, u32[]{:S(2)}) collective-permute-start(bf16[2,128,640]{2,1,0:T(8,128)(2,1)S(1)} %get-tuple-element.40), channel_id=1, source_target_pairs={{0,6},{1,7},{2,0},{3,1},{4,2},{5,3},{6,4},{7,5},{8,14},{9,15},{10,... | collective-permute-start | bytes 983048 | tf_op jit(solution)/shard_map/ppermute | solution.py:48
  113.2 16.2 %collective-permute-start.27 = (bf16[2,128,640]{2,1,0:T(8,128)(2,1)S(1)}, bf16[2,128,640]{2,1,0:T(8,128)(2,1)S(1)}, u32[]{:S(2)}, u32[]{:S(2)}) collective-permute-start(bf16[2,128,640]{2,1,0:T(8,128)(2,1)S(1)} %get-tuple-element.41), channel_id=1, source_target_pairs={{0,4},{1,5},{2,6},{3,7},{4,0},{5,1},{6,2},{7,3},{8,12},{9,13},{10,... | collective-permute-start | bytes 983048 | tf_op jit(solution)/shard_map/ppermute | solution.py:48
  114.7 16.0 %collective-permute-start.29 = (bf16[4,128,640]{2,1,0:T(8,128)(2,1)S(1)}, bf16[4,128,640]{2,1,0:T(8,128)(2,1)S(1)}, u32[]{:S(2)}, u32[]{:S(2)}) collective-permute-start(bf16[4,128,640]{2,1,0:T(8,128)(2,1)S(1)} %get-tuple-element.43), channel_id=1, source_target_pairs={{0,1},{1,0},{2,3},{3,2},{4,5},{5,4},{6,7},{7,6},{8,9},{9,8},{10,11... | collective-permute-start | bytes 1966088 | tf_op jit(solution)/shard_map/ppermute | solution.py:48
  121.7 7.9 %collective-permute-start.30 = (bf16[4,128,128]{2,1,0:T(8,128)(2,1)S(1)}, bf16[4,128,128]{2,1,0:T(8,128)(2,1)S(1)}, u32[]{:S(2)}, u32[]{:S(2)}) collective-permute-start(bf16[4,128,128]{2,1,0:T(8,128)(2,1)S(1)} %copy-done.21), channel_id=1, source_target_pairs={{0,192},{8,200},{16,208},{24,216},{32,224},{40,232},{48,240},{56,2... | collective-permute-start | bytes 393224 | tf_op jit(solution)/shard_map/ppermute | solution.py:32
  121.7 9.2 %collective-permute-start.31 = (bf16[4,128,128]{2,1,0:T(8,128)(2,1)S(1)}, bf16[4,128,128]{2,1,0:T(8,128)(2,1)S(1)}, u32[]{:S(2)}, u32[]{:S(2)}) collective-permute-start(bf16[4,128,128]{2,1,0:T(8,128)(2,1)S(1)} %copy-done.20), channel_id=1, source_target_pairs={{0,64},{8,72},{16,80},{24,88},{32,96},{40,104},{48,112},{56,120},{... | collective-permute-start | bytes 393224 | tf_op jit(solution)/shard_map/ppermute | solution.py:32
  129.5 6.2 %collective-permute-start.28 = (bf16[128,640]{1,0:T(8,128)(2,1)S(1)}, bf16[128,640]{1,0:T(8,128)(2,1)S(1)}, u32[]{:S(2)}, u32[]{:S(2)}) collective-permute-start(bf16[128,640]{1,0:T(8,128)(2,1)S(1)} %fusion.6), channel_id=1, source_target_pairs={{0,1},{1,0},{2,3},{3,2},{4,5},{5,4},{6,7},{7,6},{8,9},{9,8},{10,11... | collective-permute-start | bytes 491528 | tf_op jit(solution)/shard_map/ppermute | solution.py:48
  129.6 14.1 %collective-permute-start.35 = (bf16[4,128,128]{2,1,0:T(8,128)(2,1)S(1)}, bf16[4,128,128]{2,1,0:T(8,128)(2,1)S(1)}, u32[]{:S(2)}, u32[]{:S(2)}) collective-permute-start(bf16[4,128,128]{2,1,0:T(8,128)(2,1)S(1)} %copy-done.19), channel_id=1, source_target_pairs={{0,128},{8,136},{16,144},{24,152},{32,160},{40,168},{48,176},{56,1... | collective-permute-start | bytes 393224 | tf_op jit(solution)/shard_map/ppermute | solution.py:32
  131.6 7.7 %collective-permute-start.32 = (bf16[128,640]{1,0:T(8,128)(2,1)S(1)}, bf16[128,640]{1,0:T(8,128)(2,1)S(1)}, u32[]{:S(2)}, u32[]{:S(2)}) collective-permute-start(bf16[128,640]{1,0:T(8,128)(2,1)S(1)} %get-tuple-element.81), channel_id=1, source_target_pairs={{0,2},{1,3},{2,4},{3,5},{4,6},{5,7},{6,0},{7,1},{8,10},{9,11},{10,... | collective-permute-start | bytes 491528 | tf_op jit(solution)/shard_map/ppermute | solution.py:48
  133.7 7.5 %collective-permute-start.34 = (bf16[128,640]{1,0:T(8,128)(2,1)S(1)}, bf16[128,640]{1,0:T(8,128)(2,1)S(1)}, u32[]{:S(2)}, u32[]{:S(2)}) collective-permute-start(bf16[128,640]{1,0:T(8,128)(2,1)S(1)} %get-tuple-element.82), channel_id=1, source_target_pairs={{0,4},{1,5},{2,6},{3,7},{4,0},{5,1},{6,2},{7,3},{8,12},{9,13},{10,... | collective-permute-start | bytes 491528 | tf_op jit(solution)/shard_map/ppermute | solution.py:48
  135.8 7.1 %collective-permute-start.33 = (bf16[128,640]{1,0:T(8,128)(2,1)S(1)}, bf16[128,640]{1,0:T(8,128)(2,1)S(1)}, u32[]{:S(2)}, u32[]{:S(2)}) collective-permute-start(bf16[128,640]{1,0:T(8,128)(2,1)S(1)} %get-tuple-element.83), channel_id=1, source_target_pairs={{0,6},{1,7},{2,0},{3,1},{4,2},{5,3},{6,4},{7,5},{8,14},{9,15},{10,... | collective-permute-start | bytes 491528 | tf_op jit(solution)/shard_map/ppermute | solution.py:48
  (27 other events, 243.6 us)
